TPU v7x, 256 devices: a whole 4x4x8 slice. The times are simulated.
256 devices in a mesh: shard: 32 (over z, y), dp: 8 (over x, core).
Axes of the slice: x: 4, y: 4, z: 8, core: 2. Of those that a mesh axis runs over, the one named last changes fastest.
Arguments:
- cold_table: bfloat16 [65536, 256], P('shard'), may hold values from -6 to 6
- cold_accum: float32 [65536], P('shard'), may hold values from 0.005 to 0.5
- dither_bits: int32 [65536, 256], P('shard'), may hold values from 0 to 65280
- hot_table: float32 [1024, 256], replicated, may hold values from -6 to 6
- hot_accum: float32 [1024], replicated, may hold values from 1 to 100
- w_flat: bfloat16 [4096, 512], replicated, may hold values from -0.09375 to 0.09375
- w_inter: bfloat16 [256, 512], replicated, may hold values from -0.09375 to 0.09375
- hidden_bias: float32 [512], replicated, may hold values from -1 to 1
- w_out: float32 [512], replicated, may hold values from -0.25 to 0.25
- targets: float32 [131072], P(('shard', 'dp')), may hold values from 0 to 1
- hot_ids: int32 [131072, 8], P(('shard', 'dp')), may hold values from 0 to 1023
- cold_slots: int32 [131072, 8], P(('shard', 'dp')), may hold values from 0 to 2047, as said below
- requests: int32 [16384, 64], P(('shard', 'dp')), may hold values from 0 to 2047, as said below
- counts: int32 [512, 32], P(('shard', 'dp')), may hold values from 1 to 64, as said below
Outputs:
- cold_out: bfloat16 [65536, 256], P('shard')
- cold_accum_out: float32 [65536], P('shard')
- hot_out: float32 [1024, 256], replicated
- hot_accum_out: float32 [1024], replicated
Inputs may be any that keep to these rules, and one draw needn't show every extreme that they name: `requests`: in each row of 64 entries (one device, micro-batch and shard) the entries name distinct rows of that shard's 2048; only the first counts-many are live, the rest name arbitrary rows. `counts`: in every draw, each device has in each micro-batch a shard with exactly 64 live slots. `cold_slots`: index into its device's request rows of that micro-batch, shard * 64 + slot; always a live slot, and every live slot is named by some lookup.
All inputs are finite; a program needn't handle non-finite values.
Results may differ from a plain program's by a relative error of at most 0.001.
The roundings to bfloat16 on the way count: a program that leaves them out, or rounds other values in their place, can miss the bound.
Values may be sent and summed in bfloat16 or wider, within the bound.
No kernel may reach another device: no remote copies, remote signals or barrier semaphores. Data moves between devices by JAX's collectives and lax.ppermute only.
A program may use at most 128 MiB of HBM per device.

v0:
```python
import jax
import jax.numpy as jnp
from jax import lax
from jax.sharding import PartitionSpec as P

MB = 2
BATCH = 256


learn_rate = 0.3


def backprop(stacked, targets, w_flat, w_inter, hidden_bias, w_out):
    row_count, feature_count, row_width = stacked.shape
    flattened = stacked.reshape(row_count, feature_count * row_width)
    pair_dots = (
        jnp.einsum("sfe,sge->sfg", stacked, stacked, preferred_element_type=jnp.float32)
        * row_width ** (-0.5)
    ).astype(jnp.bfloat16)
    pre_act = jnp.dot(flattened, w_flat, preferred_element_type=jnp.float32)
    pre_act = pre_act + jnp.dot(
        pair_dots.reshape(row_count, feature_count * feature_count),
        w_inter,
        preferred_element_type=jnp.float32,
    )
    pre_act = pre_act + hidden_bias
    gated = jax.nn.sigmoid(pre_act)
    logits = jnp.sum(pre_act * gated * w_out, axis=-1)
    residual = jax.nn.sigmoid(logits) - targets
    slopes = (residual[:, None] * w_out * gated * (1.0 + pre_act * (1.0 - gated))).astype(
        jnp.bfloat16
    )
    back_flat = jnp.dot(slopes, w_flat.T, preferred_element_type=jnp.float32)
    back_pairs = jnp.dot(slopes, w_inter.T, preferred_element_type=jnp.float32).reshape(
        row_count, feature_count, feature_count
    )
    mirror = ((back_pairs + jnp.swapaxes(back_pairs, 1, 2)) * row_width ** (-0.5)).astype(
        jnp.bfloat16
    )
    return back_flat.reshape(row_count, feature_count, row_width) + jnp.einsum(
        "sfg,sge->sfe", mirror, stacked, preferred_element_type=jnp.float32
    )


def adagrad_rows(table_rows, accum, gradient):
    accum_new = accum + jnp.mean(gradient * gradient, axis=-1)
    updated = table_rows - learn_rate * gradient / jnp.sqrt(accum_new)[:, None]
    return (updated, accum_new)


def requantize(updated, bits, touched):
    grid_step = jnp.max(jnp.abs(updated), axis=-1, keepdims=True) / 8.0
    dither = bits.astype(jnp.float32) * (1.0 / 65280.0) - 0.5
    return jnp.where(touched[:, None], updated + grid_step * dither, updated).astype(jnp.bfloat16)


def on_device(
    cold_table,
    cold_accum,
    dither_bits,
    hot_table,
    hot_accum,
    w_flat,
    w_inter,
    hidden_bias,
    w_out,
    targets,
    hot_ids,
    cold_slots,
    requests,
    counts,
):
    shards = lax.axis_size("shard")
    capacity = requests.shape[1]
    row_count = cold_table.shape[0]
    row_width = cold_table.shape[1]
    hot_count = hot_table.shape[0]
    cold_feats = cold_slots.shape[1]
    hot_grad = jnp.zeros((hot_count, row_width), jnp.float32)
    cold_grad = jnp.zeros((row_count, row_width), jnp.float32)
    touched = jnp.zeros((row_count,), jnp.float32)
    for micro_index in range(MB):
        asked_rows = requests[micro_index * shards : (micro_index + 1) * shards]
        requested = lax.all_to_all(asked_rows, "shard", split_axis=0, concat_axis=0, tiled=True)
        fetched_rows = lax.all_to_all(
            cold_table[requested], "shard", split_axis=0, concat_axis=0, tiled=True
        )
        first = micro_index * BATCH
        slot_part = cold_slots[first : first + BATCH]
        hot_part = hot_ids[first : first + BATCH]
        cold_vectors = fetched_rows.reshape(shards * capacity, row_width)[slot_part]
        stacked = jnp.concatenate([cold_vectors, hot_table[hot_part].astype(jnp.bfloat16)], axis=1)
        gradients = backprop(
            stacked, targets[first : first + BATCH], w_flat, w_inter, hidden_bias, w_out
        )
        slot_grad = jax.ops.segment_sum(
            gradients[:, :cold_feats].reshape(-1, row_width),
            slot_part.reshape(-1),
            num_segments=shards * capacity,
        )
        hot_term = jax.ops.segment_sum(
            gradients[:, cold_feats:].reshape(-1, row_width),
            hot_part.reshape(-1),
            num_segments=hot_count,
        )
        slot_grad, hot_term = (slot_grad.reshape(shards, capacity, row_width), hot_term)
        hot_grad = hot_grad + hot_term
        owner_grad, count_in = (
            lax.all_to_all(
                slot_grad.astype(jnp.bfloat16), "shard", split_axis=0, concat_axis=0, tiled=True
            ).astype(slot_grad.dtype),
            lax.all_to_all(counts[micro_index], "shard", split_axis=0, concat_axis=0, tiled=True),
        )
        cold_grad = cold_grad + jax.ops.segment_sum(
            owner_grad.reshape(-1, row_width), requested.reshape(-1), num_segments=row_count
        )
        live_mask = (jnp.arange(capacity, dtype=jnp.int32)[None, :] < count_in[:, None]).astype(
            jnp.float32
        )
        touched = touched + jax.ops.segment_sum(
            live_mask.reshape(-1), requested.reshape(-1), num_segments=row_count
        )
    summed_grad, summed_hits = (
        lax.psum(cold_grad.astype(jnp.bfloat16), "dp").astype(jnp.float32),
        lax.psum(touched.astype(jnp.bfloat16), "dp").astype(jnp.float32),
    )
    averaged = summed_grad / jnp.maximum(summed_hits, 1.0)[:, None]
    updated, cold_accum_out = adagrad_rows(cold_table.astype(jnp.float32), cold_accum, averaged)
    cold_out = requantize(updated, dither_bits, summed_hits > 0.5)
    total_hot = lax.psum(hot_grad, ("shard", "dp"))
    hot_out, hot_accum_out = adagrad_rows(hot_table, hot_accum, total_hot)
    return (cold_out, cold_accum_out, hot_out, hot_accum_out)


def solution(mesh):
    return jax.shard_map(
        on_device,
        mesh=mesh,
        in_specs=(
            P("shard", None),
            P("shard"),
            P("shard", None),
            P(),
            P(),
            P(),
            P(),
            P(),
            P(),
            P(("shard", "dp")),
            P(("shard", "dp"), None),
            P(("shard", "dp"), None),
            P(("shard", "dp"), None),
            P(("shard", "dp"), None),
        ),
        out_specs=(P("shard", None), P("shard"), P(), P()),
        check_vma=False,
    )
```

profile of v0, /device:TPU:8, one launch (start us, length us, event | category | flops | bytes accessed | tf_op | source)
XLA Modules:
  0.0 695.5 jit_solution(9611974366071185003)
XLA Ops:
  8.0 1.4 fusion.31
  9.4 20.0 %all_to_all.62 = s32[32,1,64]{2,1,0:T(1,128)S(1)} all-to-all(s32[32,1,64]{2,1,0:T(1,128)S(1)} %bitcast.113), channel_id=1, replica_groups=mesh['shard'=32,'dp'=8] {'shard'}, dimensions={0} | all-to-all | bytes 16384 | tf_op jit(solution)/shard_map/all_to_all | solution.py:84
  29.4 4.9 all-to-all-start
  34.5 9.9 %gather_fusion.3 = bf16[2048,256]{1,0:T(8,128)(2,1)} fusion(bf16[2048,256]{1,0:T(8,128)(2,1)} %param.14, s32[2048]{0:T(1024)S(1)} %broadcast_clamp_fusion.3), kind=kCustom, calls=%fused_computation.3 | custom fusion | bytes 2105344 | tf_op jit(solution)/shard_map/gather | solution.py:86
  44.3 10.0 %all-to-all-start.6 = ((bf16[32,64,256]{2,1,0:T(8,128)(2,1)}), bf16[32,64,256]{2,1,0:T(8,128)(2,1)S(1)}, u32[]{:S(2)}, u32[]{:S(2)}) async-start(bf16[32,64,256]{2,1,0:T(8,128)(2,1)} %bitcast.16), calls=%async_computation.6 | async-start | bytes 2097152 | tf_op jit(solution)/shard_map/all_to_all | solution.py:85
  54.5 9.1 %gather_fusion = bf16[2048,256]{1,0:T(8,128)(2,1)} fusion(bf16[2048,256]{1,0:T(8,128)(2,1)S(1)} %copy-done.2, s32[2048]{0:T(1024)S(1)} %broadcast_clamp_fusion.5), kind=kCustom, calls=%fused_computation | custom fusion | bytes 2105344 | tf_op jit(solution)/shard_map/gather | solution.py:86
  63.5 17.2 %all-to-all-done.6 = bf16[32,64,256]{2,1,0:T(8,128)(2,1)S(1)} async-done(((bf16[32,64,256]{2,1,0:T(8,128)(2,1)}), bf16[32,64,256]{2,1,0:T(8,128)(2,1)S(1)}, u32[]{:S(2)}, u32[]{:S(2)}) %all-to-all-start.6) | async-done | bytes 1048608 | tf_op jit(solution)/shard_map/all_to_all | solution.py:85
  80.7 5.6 all-to-all-start.4
  88.4 0.8 copy.69
  89.9 0.8 copy.75
  93.0 1.3 fusion.32
  94.3 0.8 copy.70
  98.1 8.4 %gather_fusion.5 = bf16[2048,256]{1,0:T(8,128)(2,1)} fusion(f32[1024,256]{1,0:T(8,128)S(1)} %copy-done.1, s32[2048]{0:T(1024)S(1)} %broadcast_clamp_fusion), kind=kCustom, calls=%fused_computation.5 | custom fusion | bytes 2105344 | tf_op jit(solution)/shard_map/gather | solution.py:92
  106.5 8.5 %gather_fusion.2 = bf16[2048,256]{1,0:T(8,128)(2,1)} fusion(f32[1024,256]{1,0:T(8,128)S(1)} %copy-done.1, s32[2048]{0:T(1024)S(1)} %broadcast_clamp_fusion.1), kind=kCustom, calls=%fused_computation.2 | custom fusion | bytes 2105344 | tf_op jit(solution)/shard_map/gather | solution.py:92
  115.0 9.0 %gather_fusion.4 = bf16[2048,256]{1,0:T(8,128)(2,1)} fusion(bf16[2048,256]{1,0:T(8,128)(2,1)S(1)} %bitcast.86, s32[2048]{0:T(1024)S(1)} %broadcast_clamp_fusion.2), kind=kCustom, calls=%fused_computation.4 | custom fusion | bytes 2105344 | tf_op jit(solution)/shard_map/gather | solution.py:91
  124.1 4.4 fusion.27
  128.5 1.5 pad_maximum_fusion.1
  129.9 10.2 %all-to-all-start.3 = ((s32[32,1,1]{2,1,0:T(1,128)}), s32[32,1,1]{2,1,0:T(1,128)}, u32[]{:S(2)}, u32[]{:S(2)}) async-start(s32[32,1,1]{2,1,0:T(1,128)} %copy.67), calls=%async_computation.3 | async-start | bytes 32768 | tf_op jit(solution)/shard_map/all_to_all | solution.py:112
  140.1 9.9 %gather_fusion.1 = bf16[2048,256]{1,0:T(8,128)(2,1)} fusion(bf16[2048,256]{1,0:T(8,128)(2,1)} %bitcast.6, s32[2048]{0:T(1024)S(1)} %broadcast_clamp_fusion.4), kind=kCustom, calls=%fused_computation.1 | custom fusion | bytes 2105344 | tf_op jit(solution)/shard_map/gather | solution.py:91
  150.0 4.3 fusion.28
  154.3 1.5 pad_maximum_fusion
  155.8 3.2 copy.77
  159.0 1.0 multiply_convert_fusion.2
  160.0 3.9 copy.84
  163.9 3.2 copy.71
  167.1 1.0 multiply_convert_fusion.3
  168.1 2.7 copy.82
  170.9 2.8 fusion.37
  173.7 1.2 fusion.34
  176.0 1.0 multiply_convert_fusion
  177.3 3.2 fusion.35
  180.6 1.9 copy.73
  182.5 5.9 copy.83
  188.4 10.1 %all-to-all-start.1 = ((s32[32,1,1]{2,1,0:T(1,128)}), s32[32,1,1]{2,1,0:T(1,128)S(1)}, u32[]{:S(2)}, u32[]{:S(2)}) async-start(s32[32,1,1]{2,1,0:T(1,128)} %copy.66), calls=%async_computation.1 | async-start | bytes 32768 | tf_op jit(solution)/shard_map/all_to_all | solution.py:112
  198.5 5.8 bitcast_add_fusion.1
  204.3 13.5 %scatter_custom_fusion.2 = f32[2048,256]{1,0:T(8,128)} fusion(s32[2048]{0:T(1024)} %reshape.252, f32[256,16,256]{2,1,0:T(8,128)} %bitcast_add_fusion.1, f32[]{:T(128)} %constant.13.clone.1), kind=kCustom, calls=%fused_computation.25 | custom fusion | flops 524288 | bytes 4194816 | tf_op jit(solution)/shard_map/scatter-add | solution.py:96
  217.8 2.7 convert_element_type.84
  220.4 9.8 %all-to-all-start.5 = ((bf16[32,64,256]{2,1,0:T(8,128)(2,1)}), bf16[32,64,256]{2,1,0:T(8,128)(2,1)}, u32[]{:S(2)}, u32[]{:S(2)}) async-start(bf16[32,64,256]{2,1,0:T(8,128)(2,1)} %bitcast.104), calls=%async_computation.5 | async-start | bytes 2097152 | tf_op jit(solution)/shard_map/all_to_all | solution.py:109
  230.3 0.8 copy.74
  231.8 1.2 fusion.39
  233.2 1.9 copy.79
  235.1 3.6 fusion.38
  238.7 1.8 copy.85
  240.4 2.9 bitcast_add_fusion
  243.4 13.6 %scatter_custom_fusion.4 = f32[2048,256]{1,0:T(8,128)} fusion(s32[2048]{0:T(1024)} %reshape.268, f32[256,16,256]{2,1,0:T(8,128)} %bitcast_add_fusion, f32[]{:T(128)} %constant.13.clone.1), kind=kCustom, calls=%fused_computation.23 | custom fusion | flops 524288 | bytes 4194816 | tf_op jit(solution)/shard_map/scatter-add | solution.py:96
  256.9 2.7 convert_element_type.90
  259.6 10.0 %all-to-all-start.7 = ((bf16[32,64,256]{2,1,0:T(8,128)(2,1)}), bf16[32,64,256]{2,1,0:T(8,128)(2,1)}, u32[]{:S(2)}, u32[]{:S(2)}) async-start(bf16[32,64,256]{2,1,0:T(8,128)(2,1)} %bitcast.24), calls=%async_computation.7 | async-start | bytes 2097152 | tf_op jit(solution)/shard_map/all_to_all | solution.py:109
  270.6 1.4 reduce.3
  275.0 11.3 %scatter_custom_fusion.1 = f32[2048]{0:T(1024)S(1)} fusion(s32[2048]{0:T(1024)S(1)} %reshape.244, f32[2048]{0:T(1024)S(1)} %reshape.246, f32[]{:T(128)} %constant.13.clone.1), kind=kCustom, calls=%fused_computation.87 | custom fusion | flops 2048 | bytes 8196 | tf_op jit(solution)/shard_map/scatter-add | solution.py:120
  286.3 11.3 %scatter_custom_fusion = f32[2048]{0:T(1024)S(1)} fusion(s32[2048]{0:T(1024)S(1)} %reshape.236, f32[2048]{0:T(1024)S(1)} %reshape.238, f32[]{:T(128)} %constant.13.clone.1), kind=kCustom, calls=%fused_computation.89 | custom fusion | flops 2048 | bytes 8196 | tf_op jit(solution)/shard_map/scatter-add | solution.py:120
  297.6 12.4 %scatter_custom_fusion.6 = f32[1024,256]{1,0:T(8,128)S(1)} fusion(s32[2048]{0:T(1024)S(1)} %reshape.284, f32[256,16,256]{2,1,0:T(8,128)} %bitcast_add_fusion.1, f32[]{:T(128)} %constant.13.clone.1), kind=kCustom, calls=%fused_computation.21 | custom fusion | flops 524288 | bytes 3146240 | tf_op jit(solution)/shard_map/scatter-add | solution.py:101
  310.0 13.1 %scatter_custom_fusion.7 = f32[1024,256]{1,0:T(8,128)} fusion(s32[2048]{0:T(1024)S(1)} %reshape.292, f32[256,16,256]{2,1,0:T(8,128)} %bitcast_add_fusion, f32[]{:T(128)} %constant.13.clone.1), kind=kCustom, calls=%fused_computation.19 | custom fusion | flops 524288 | bytes 3146240 | tf_op jit(solution)/shard_map/scatter-add | solution.py:101
  323.1 2.3 add.148
  325.5 12.4 %psum.21 = bf16[2048]{0:T(1024)(128)(2,1)S(1)} all-reduce(bf16[2048]{0:T(1024)(128)(2,1)S(1)} %add_convert_fusion.1), channel_id=1, replica_groups=mesh['shard'=32,'dp'=8] {'dp'}, use_global_device_ids=true, to_apply=%region_2.0 | all-reduce | flops 2048 | bytes 8192 | tf_op jit(solution)/shard_map/psum | solution.py:125
  337.9 247.4 %all-reduce.5.cloned.1.call-done = f32[1024,256]{1,0:T(8,128)} async-done(((f32[1024,256]{1,0:T(8,128)}), f32[1024,256]{1,0:T(8,128)}) %all-reduce.5.cloned.1.call-update) | async-done | bytes 1048592 | tf_op jit(solution)/shard_map/psum | solution.py:130
  585.4 1.4 multiply_reduce_fusion.1
  586.8 12.5 %scatter_custom_fusion.3 = f32[2048,256]{1,0:T(8,128)} fusion(s32[2048]{0:T(1024)S(1)} %reshape.236, bf16[2048,256]{1,0:T(8,128)(2,1)} %bitcast.28, f32[]{:T(128)} %constant.13.clone.1), kind=kCustom, calls=%fused_computation.30 | custom fusion | flops 1048576 | bytes 3145732 | tf_op jit(solution)/shard_map/scatter-add | solution.py:114
  599.3 12.3 %scatter_custom_fusion.5 = f32[2048,256]{1,0:T(8,128)} fusion(s32[2048]{0:T(1024)S(1)} %reshape.244, bf16[2048,256]{1,0:T(8,128)(2,1)} %bitcast.29, f32[]{:T(128)} %constant.13.clone.1), kind=kCustom, calls=%fused_computation.28 | custom fusion | flops 1048576 | bytes 3145732 | tf_op jit(solution)/shard_map/scatter-add | solution.py:114
  611.7 3.5 add_convert_fusion
  615.8 1.2 divide_subtract_fusion.1
  617.0 64.7 %all-reduce.3.cloned.1.call-done = bf16[2048,256]{1,0:T(8,128)(2,1)} async-done(((bf16[2048,256]{1,0:T(8,128)(2,1)}), bf16[2048,256]{1,0:T(8,128)(2,1)}) %all-reduce.3.cloned.1.call-update) | async-done | bytes 1048592 | tf_op jit(solution)/shard_map/psum | solution.py:124
  681.7 1.9 multiply_reduce_fusion
  684.2 2.2 abs_reduce_fusion
  686.4 1.5 fusion
  (114 shorter events, 15.7 us)
Async XLA Ops:
  8.0 167.0 %copy-start = (bf16[256,512]{1,0:T(8,128)(2,1)S(1)}, bf16[256,512]{1,0:T(8,128)(2,1)}, u32[]{:S(2)}) copy-start(bf16[256,512]{1,0:T(8,128)(2,1)} %param.20) | copy-start | bytes 786436
  29.4 14.9 %copy-start.12 = (s32[32,1,64]{2,1,0:T(1,128)}, s32[32,1,64]{2,1,0:T(1,128)S(1)}, u32[]{:S(2)}) copy-start(s32[32,1,64]{2,1,0:T(1,128)S(1)} %all_to_all.62) | copy-start | bytes 24580
  29.4 14.9 %all-to-all-start = ((s32[32,1,64]{2,1,0:T(1,128)}), s32[32,1,64]{2,1,0:T(1,128)S(1)}, u32[]{:S(2)}, u32[]{:S(2)}) async-start(s32[32,1,64]{2,1,0:T(1,128)} %bitcast), calls=%async_computation | async-start | bytes 32768 | tf_op jit(solution)/shard_map/all_to_all | solution.py:84
  44.3 10.1 %copy-start.2 = (bf16[2048,256]{1,0:T(8,128)(2,1)S(1)}, bf16[2048,256]{1,0:T(8,128)(2,1)}, u32[]{:S(2)}) copy-start(bf16[2048,256]{1,0:T(8,128)(2,1)} %param.14) | copy-start | bytes 3145732
  44.3 36.4 %all-to-all-start.6 = ((bf16[32,64,256]{2,1,0:T(8,128)(2,1)}), bf16[32,64,256]{2,1,0:T(8,128)(2,1)S(1)}, u32[]{:S(2)}, u32[]{:S(2)}) async-start(bf16[32,64,256]{2,1,0:T(8,128)(2,1)} %bitcast.16), calls=%async_computation.6 | async-start | bytes 2097152 | tf_op jit(solution)/shard_map/all_to_all | solution.py:85
  63.5 22.8 %copy-start.27 = (s32[2,32]{1,0:T(2,128)S(1)}, s32[2,32]{1,0:T(2,128)}, u32[]{:S(2)}) copy-start(s32[2,32]{1,0:T(2,128)} %param.27) | copy-start | bytes 772
  63.5 24.2 %copy-start.21 = (s32[512,8]{0,1:T(8,128)S(1)}, s32[512,8]{0,1:T(8,128)}, u32[]{:S(2)}) copy-start(s32[512,8]{0,1:T(8,128)} %param.25) | copy-start | bytes 49156
  63.5 34.5 %copy-start.1 = (f32[1024,256]{1,0:T(8,128)S(1)}, f32[1024,256]{1,0:T(8,128)}, u32[]{:S(2)}) copy-start(f32[1024,256]{1,0:T(8,128)} %param.17) | copy-start | bytes 3145732
  80.7 49.2 %all-to-all-start.4 = ((bf16[32,64,256]{2,1,0:T(8,128)(2,1)}), bf16[32,64,256]{2,1,0:T(8,128)(2,1)}, u32[]{:S(2)}, u32[]{:S(2)}) async-start(bf16[32,64,256]{2,1,0:T(8,128)(2,1)} %bitcast.103), calls=%async_computation.4 | async-start | bytes 2097152 | tf_op jit(solution)/shard_map/all_to_all | solution.py:85
  98.1 8.4 %copy-start.18 = (s32[2048]{0:T(1024)S(1)}, s32[2048]{0:T(1024)}, u32[]{:S(2)}) copy-start(s32[2048]{0:T(1024)} %reshape.204) | copy-start | bytes 24580
  106.5 8.5 %copy-start.16 = (s32[2048]{0:T(1024)S(1)}, s32[2048]{0:T(1024)}, u32[]{:S(2)}) copy-start(s32[2048]{0:T(1024)} %reshape.196) | copy-start | bytes 24580
  106.5 8.5 %copy-start.17 = (s32[2048]{0:T(1024)S(1)}, s32[2048]{0:T(1024)}, u32[]{:S(2)}) copy-start(s32[2048]{0:T(1024)} %reshape.220) | copy-start | bytes 24580
  124.0 4.4 copy-start.4
  124.0 4.4 copy-start.5
  129.9 58.5 %all-to-all-start.3 = ((s32[32,1,1]{2,1,0:T(1,128)}), s32[32,1,1]{2,1,0:T(1,128)}, u32[]{:S(2)}, u32[]{:S(2)}) async-start(s32[32,1,1]{2,1,0:T(1,128)} %copy.67), calls=%async_computation.3 | async-start | bytes 32768 | tf_op jit(solution)/shard_map/all_to_all | solution.py:112
  150.0 4.3 copy-start.7
  150.0 4.3 copy-start.8
  168.0 2.8 copy-start.3
  173.7 1.3 copy-start.24
  173.7 1.5 copy-start.25
  175.3 0.7 copy-start.26
  188.4 32.1 %all-to-all-start.1 = ((s32[32,1,1]{2,1,0:T(1,128)}), s32[32,1,1]{2,1,0:T(1,128)S(1)}, u32[]{:S(2)}, u32[]{:S(2)}) async-start(s32[32,1,1]{2,1,0:T(1,128)} %copy.66), calls=%async_computation.1 | async-start | bytes 32768 | tf_op jit(solution)/shard_map/all_to_all | solution.py:112
  220.4 9.8 %copy-start.14 = (s32[32,1,1]{2,1,0:T(1,128)}, s32[32,1,1]{2,1,0:T(1,128)S(1)}, u32[]{:S(2)}) copy-start(s32[32,1,1]{2,1,0:T(1,128)S(1)} %all-to-all-done.1) | copy-start | bytes 388
  220.4 39.2 %all-to-all-start.5 = ((bf16[32,64,256]{2,1,0:T(8,128)(2,1)}), bf16[32,64,256]{2,1,0:T(8,128)(2,1)}, u32[]{:S(2)}, u32[]{:S(2)}) async-start(bf16[32,64,256]{2,1,0:T(8,128)(2,1)} %bitcast.104), calls=%async_computation.5 | async-start | bytes 2097152 | tf_op jit(solution)/shard_map/all_to_all | solution.py:109
  238.6 1.8 copy-start.6
  238.6 1.8 copy-start.10
  256.9 13.1 %copy-start.20 = (s32[256,8]{0,1:T(8,128)S(1)}, s32[256,8]{0,1:T(8,128)}, u32[]{:S(2)}) copy-start(s32[256,8]{0,1:T(8,128)} %get-tuple-element.14) | copy-start | bytes 24580
  256.9 13.4 %copy-start.19 = (s32[256,8]{0,1:T(8,128)S(1)}, s32[256,8]{0,1:T(8,128)}, u32[]{:S(2)}) copy-start(s32[256,8]{0,1:T(8,128)} %get-tuple-element.17) | copy-start | bytes 24580
  259.6 12.5 %copy-start.15 = (s32[32,1,1]{2,1,0:T(1,128)S(1)}, s32[32,1,1]{2,1,0:T(1,128)}, u32[]{:S(2)}) copy-start(s32[32,1,1]{2,1,0:T(1,128)} %copy-done.14) | copy-start | bytes 388
  259.6 13.8 %copy-start.13 = (s32[32,1,64]{2,1,0:T(1,128)S(1)}, s32[32,1,64]{2,1,0:T(1,128)}, u32[]{:S(2)}) copy-start(s32[32,1,64]{2,1,0:T(1,128)} %copy-done.12) | copy-start | bytes 24580
  259.6 339.7 %all-to-all-start.7 = ((bf16[32,64,256]{2,1,0:T(8,128)(2,1)}), bf16[32,64,256]{2,1,0:T(8,128)(2,1)}, u32[]{:S(2)}, u32[]{:S(2)}) async-start(bf16[32,64,256]{2,1,0:T(8,128)(2,1)} %bitcast.24), calls=%async_computation.7 | async-start | bytes 2097152 | tf_op jit(solution)/shard_map/all_to_all | solution.py:109
  269.6 315.7 %all-reduce.5.cloned.1.call-start = ((), (), s32[]{:S(2)}) async-start(), calls=%async_computation.9 | async-start | bytes 2097152 | tf_op jit(solution)/shard_map/psum | solution.py:130
  325.4 356.2 %all-reduce.3.cloned.1.call-start = ((), (), s32[]{:S(2)}) async-start(), calls=%async_computation.8 | async-start | bytes 2097152 | tf_op jit(solution)/shard_map/psum | solution.py:124
  611.7 3.5 copy-start.23
  611.7 4.1 copy-start.9
  615.8 67.8 %copy-start.22 = (f32[2048]{0:T(1024)S(1)}, f32[2048]{0:T(1024)}, u32[]{:S(2)}) copy-start(f32[2048]{0:T(1024)} %param.15) | copy-start | bytes 24580
  684.2 2.2 copy-start.11
Sparse Core Ops, SparseCore 0:
  325.5 259.7 all-reduce.4
Sparse Core Ops, SparseCore 1:
  615.3 66.3 all-reduce.2
where the time goes:
time: 702 us; the launch traced here: 696 us
  waiting for transfers between devices  329 us (47%)
  other arithmetic  133 us (19%)
  local copies, waits for them, and re-layouts  92.7 us (13%)
  starting transfers between devices  61.1 us (9%)
  blocking collectives  32.5 us (5%)
  matrix products  30.5 us (4%)
  between operations  16.2 us (2%)
    psum x1, waiting for transfers between devices, on_device(): total_hot = lax.psum(hot_grad, ('shard', 'dp'))  247 us
    psum x1, waiting for transfers between devices, on_device(): lax.psum(cold_grad.astype(jnp.bfloat16), 'dp').astype(jnp.float32)  64.7 us
    scatter-add x2, other arithmetic, on_device(): jax.ops.segment_sum(gradients[:, :cold_feats].reshape(-1, row_width), slo...  27.1 us
    scatter-add x2, other arithmetic, on_device(): jax.ops.segment_sum(gradients[:, cold_feats:].reshape(-1, row_width), hot...  25.5 us
    scatter-add x2, other arithmetic, on_device(): jax.ops.segment_sum(owner_grad.reshape(-1, row_width), requested.reshape(...  24.8 us
    scatter-add x2, other arithmetic, on_device(): jax.ops.segment_sum(live_mask.reshape(-1), requested.reshape(-1), num_seg...  22.6 us
    all_to_all x2, starting transfers between devices, on_device(): lax.all_to_all(counts[micro_index], 'shard', split_axis=0, concat_axis=0,...  20.3 us
    all_to_all x1, blocking collectives, on_device(): lax.all_to_all(asked_rows, 'shard', split_axis=0, concat_axis=0, tiled=True)  20 us
  transfers between devices with their start and end apart: 9, of which 3 were waited for; matrix products, arithmetic and copies ran while one was open for 33% of the time, Pallas kernels for 0%

commit v1 on v0

v1 whole, which is shorter than its diff:
```python
import jax
import jax.numpy as jnp
from jax import lax
from jax.experimental import pallas as pl
from jax.experimental.pallas import tpu as pltpu
from jax.sharding import PartitionSpec as P

MB = 2
BATCH = 256
GROUP = 16
FEATS = 16
F_COLD = 8

learn_rate = 0.3

BF = jnp.bfloat16
F32 = jnp.float32

NT = (((1,), (1,)), ((), ()))


def iota(shape, axis):
    return lax.broadcasted_iota(jnp.int32, shape, axis)


def params(limit_mib):
    return pltpu.CompilerParams(vmem_limit_bytes=limit_mib << 20)


def one_hot(ids, shape, axis, base):
    return jnp.where(iota(shape, axis) + base == ids, 1.0, 0.0)


def fetch_kernel(ids_col, table, rows, hits, hot):
    slots = rows.shape[0]
    count = table.shape[0]
    block = 512
    hits[...] = jnp.zeros_like(hits)

    def step(i, carry):
        at = pl.multiple_of(i * block, block)
        ids = ids_col[pl.ds(at, block), :]
        for k in range(count // 256):
            match = one_hot(ids, (block, 256), 1, k * 256)
            hot[:, k * 256 : (k + 1) * 256] = match.astype(BF)
            hits[:, k * 256 : (k + 1) * 256] += jnp.sum(match, axis=0, keepdims=True)
        rows[pl.ds(at, block), :] = jnp.dot(
            hot[...], table[...], preferred_element_type=F32
        ).astype(BF)
        return carry

    lax.fori_loop(0, slots // block, step, 0)


def fetch_rows(ids_col, table):
    slots, width = ids_col.shape[0], table.shape[1]
    return pl.pallas_call(
        fetch_kernel,
        out_shape=(
            jax.ShapeDtypeStruct((slots, width), BF),
            jax.ShapeDtypeStruct((1, table.shape[0]), F32),
        ),
        scratch_shapes=[pltpu.VMEM((512, table.shape[0]), BF)],
        compiler_params=params(32),
        name="fetch_rows",
    )(ids_col, table)


def step_kernel(
    fetched,
    hotb,
    cold_col,
    hot_col,
    cold_row,
    hot_row,
    targets,
    w_flat,
    w_inter,
    w_inter_t,
    bias,
    w_out,
    hot_prev,
    slot_grad,
    hot_grad,
    x,
    a,
    pairs,
    back,
    mirror,
    g_hi,
    g_lo,
    h_hi,
    h_lo,
    match,
    slopes,
):
    width = fetched.shape[1]
    samples = targets.shape[0]
    groups = samples // GROUP
    lane_group = FEATS * GROUP
    half = F_COLD * GROUP
    scale = width ** (-0.5)
    block = 512
    per_block = block // half

    sq = (lane_group, lane_group)
    i_hi = iota(sq, 0) >> 4
    i_lo = iota(sq, 0) & 15
    j_hi = iota(sq, 1) >> 4
    j_lo = iota(sq, 1) & 15

    def gather(source, col, offset):
        count = source.shape[0]

        def body(b, carry):
            at = pl.multiple_of(b * block, block)
            ids = col[pl.ds(at, block), :]
            for k in range(count // 256):
                match[:, k * 256 : (k + 1) * 256] = one_hot(
                    ids, (block, 256), 1, k * 256
                ).astype(BF)
            picked = jnp.dot(
                match[:, :count], source[...], preferred_element_type=F32
            ).astype(BF)
            for q in range(per_block):
                dst = pl.multiple_of((b * per_block + q) * lane_group + offset, half)
                x[pl.ds(dst, half), :] = picked[q * half : (q + 1) * half]
            return carry

        lax.fori_loop(0, col.shape[0] // block, body, 0)

    gather(fetched, cold_col, 0)
    gather(hotb, hot_col, half)

    spread = jnp.where(i_hi == j_lo, 1.0, 0.0).astype(BF)
    spread_t = jnp.where(i_lo == j_hi, 1.0, 0.0).astype(BF)

    def dots(g, carry):
        rows = pl.ds(pl.multiple_of(g * lane_group, lane_group), lane_group)
        part = pl.ds(pl.multiple_of(g * GROUP, GROUP), GROUP)
        xg = x[rows, :]
        for f in range(FEATS):
            a[part, f * width : (f + 1) * width] = xg[f * GROUP : (f + 1) * GROUP]
        gram = lax.dot_general(xg, xg, NT, preferred_element_type=F32) * scale
        own = jnp.where(i_lo == j_lo, gram, 0.0).astype(BF)
        wide = jnp.dot(own, spread, preferred_element_type=F32)
        wide = jnp.where(i_hi == j_hi, wide, 0.0)
        pairs[part, :] = jnp.sum(
            wide.reshape(FEATS, GROUP, lane_group), axis=0
        ).astype(BF)
        return carry

    lax.fori_loop(0, groups, dots, 0)

    pre = jnp.dot(a[...], w_flat[...], preferred_element_type=F32)
    pre = pre + jnp.dot(pairs[...], w_inter[...], preferred_element_type=F32)
    pre = pre + bias[...]
    gated = jax.nn.sigmoid(pre)
    logits = jnp.sum(pre * gated * w_out[...], axis=-1, keepdims=True)
    residual = jax.nn.sigmoid(logits) - targets[...]
    slopes[...] = (residual * w_out[...] * gated * (1.0 + pre * (1.0 - gated))).astype(BF)

    def flat_back(f, carry):
        rows = pl.ds(pl.multiple_of(f * width, width), width)
        back[f] = lax.dot_general(
            slopes[...], w_flat[rows, :], NT, preferred_element_type=F32
        )
        return carry

    lax.fori_loop(0, FEATS, flat_back, 0)
    both = lax.dot_general(slopes[...], w_inter[...], NT, preferred_element_type=F32)
    both = both + lax.dot_general(slopes[...], w_inter_t[...], NT, preferred_element_type=F32)
    mirror[...] = (both * scale).astype(BF)

    def grads(g, carry):
        rows = pl.ds(pl.multiple_of(g * lane_group, lane_group), lane_group)
        part = pl.ds(pl.multiple_of(g * GROUP, GROUP), GROUP)
        mine = mirror[part, :].astype(F32)
        tall = jnp.broadcast_to(mine[None], (FEATS, GROUP, lane_group)).reshape(sq)
        tall = jnp.where(i_hi == j_hi, tall, 0.0).astype(BF)
        wide = jnp.dot(tall, spread_t, preferred_element_type=F32)
        wide = jnp.where(i_lo == j_lo, wide, 0.0).astype(BF)
        total = jnp.dot(wide, x[rows, :], preferred_element_type=F32)
        flat = back[:, part, :].reshape(lane_group, width)
        total = total + flat
        hi = total.astype(BF)
        lo = (total - hi.astype(F32)).astype(BF)
        dst = pl.ds(pl.multiple_of(g * half, half), half)
        g_hi[dst, :] = hi[:half]
        g_lo[dst, :] = lo[:half]
        h_hi[dst, :] = hi[half:]
        h_lo[dst, :] = lo[half:]
        return carry

    lax.fori_loop(0, groups, grads, 0)

    lookups = cold_row.shape[1]

    def scatter(ids_row, hi, lo, write, count):
        def body(b, carry):
            at = pl.multiple_of(b * block, block)
            for k in range(lookups // 256):
                ids = ids_row[:, k * 256 : (k + 1) * 256]
                match[:, k * 256 : (k + 1) * 256] = one_hot(
                    ids - at, (block, 256), 0, 0
                ).astype(BF)
            total = jnp.dot(match[...], hi[...], preferred_element_type=F32)
            total = total + jnp.dot(match[...], lo[...], preferred_element_type=F32)
            write(pl.ds(at, block), total)
            return carry

        lax.fori_loop(0, count // block, body, 0)

    def write_hot(rows, total):
        if hot_prev is None:
            hot_grad[rows, :] = total
        else:
            hot_grad[rows, :] = total + hot_prev[rows, :]

    def write_slot(rows, total):
        slot_grad[rows, :] = total.astype(BF)

    scatter(cold_row, g_hi, g_lo, write_slot, slot_grad.shape[0])
    scatter(hot_row, h_hi, h_lo, write_hot, hot_grad.shape[0])


def first_step_kernel(*refs):
    step_kernel(*refs[:12], None, *refs[12:])


def backprop(args, hot_prev, slots, hot_count):
    width = args[0].shape[1]
    samples = args[6].shape[0]
    hidden = args[7].shape[1]
    lookups = samples * F_COLD
    wide = FEATS * width
    kernel = step_kernel if hot_prev is not None else first_step_kernel
    extra = () if hot_prev is None else (hot_prev,)
    return pl.pallas_call(
        kernel,
        out_shape=(
            jax.ShapeDtypeStruct((slots, width), BF),
            jax.ShapeDtypeStruct((hot_count, width), F32),
        ),
        scratch_shapes=[
            pltpu.VMEM((samples * FEATS, width), BF),
            pltpu.VMEM((samples, wide), BF),
            pltpu.VMEM((samples, FEATS * FEATS), BF),
            pltpu.VMEM((FEATS, samples, width), F32),
            pltpu.VMEM((samples, FEATS * FEATS), BF),
            pltpu.VMEM((lookups, width), BF),
            pltpu.VMEM((lookups, width), BF),
            pltpu.VMEM((lookups, width), BF),
            pltpu.VMEM((lookups, width), BF),
            pltpu.VMEM((512, 2048), BF),
            pltpu.VMEM((samples, hidden), BF),
        ],
        compiler_params=params(48),
        name="train_step",
    )(*args, *extra)


def owner_body(ids_row, grads, match, write):
    block = 512
    slots = grads.shape[0]
    rows = 2048

    def body(b, carry):
        at = pl.multiple_of(b * block, block)
        for k in range(slots // 256):
            ids = ids_row[:, k * 256 : (k + 1) * 256]
            match[:, k * 256 : (k + 1) * 256] = one_hot(
                ids - at, (block, 256), 0, 0
            ).astype(BF)
        write(b, at, jnp.dot(match[...], grads[...], preferred_element_type=F32))
        return carry

    lax.fori_loop(0, rows // block, body, 0)


def owner_first_kernel(ids_row, grads, out, match):
    def write(b, at, total):
        out[pl.ds(at, 512), :] = total

    owner_body(ids_row, grads, match, write)


def owner_second_kernel(ids_row, grads, prev, hits0, hits1, out, match):
    def write(b, at, total):
        total = (total + prev[pl.ds(at, 512), :]).astype(BF)
        out[b * 2, :256, :] = total[:256]
        out[b * 2 + 1, :256, :] = total[256:]

    owner_body(ids_row, grads, match, write)
    hits = hits0[...] + hits1[...]
    for p in range(out.shape[0]):
        mine = hits[:, p * 256 : (p + 1) * 256]
        out[p, 256:, :] = jnp.broadcast_to(mine, (16, 256)).astype(BF)


def owner_first(ids_row, grads):
    return pl.pallas_call(
        owner_first_kernel,
        out_shape=jax.ShapeDtypeStruct((2048, grads.shape[1]), F32),
        scratch_shapes=[pltpu.VMEM((512, 2048), BF)],
        compiler_params=params(32),
        name="owner_first",
    )(ids_row, grads)


def owner_second(ids_row, grads, prev, hits0, hits1):
    return pl.pallas_call(
        owner_second_kernel,
        out_shape=jax.ShapeDtypeStruct((8, 272, 256), BF),
        scratch_shapes=[pltpu.VMEM((512, 2048), BF)],
        compiler_params=params(32),
        name="owner_second",
    )(ids_row, grads, prev, hits0, hits1)


def to_col(row, eye):
    return jnp.sum(jnp.where(eye, row, 0.0), axis=1, keepdims=True)


def to_row(col, eye):
    return jnp.sum(jnp.where(eye, col, 0.0), axis=0, keepdims=True)


def cold_update_kernel(parts, table, accum, bits, out):
    eye = iota((256, 256), 0) == iota((256, 256), 1)
    total = parts[0].astype(F32)
    for p in range(1, parts.shape[0]):
        total = total + parts[p].astype(F32)
    grad = total[:256]
    touched = to_col(total[256:257], eye)
    averaged = grad / jnp.maximum(touched, 1.0)
    mean = jnp.mean(averaged * averaged, axis=-1, keepdims=True)
    accum_new = to_col(accum[...], eye) + mean
    updated = table[...].astype(F32) - learn_rate * averaged / jnp.sqrt(accum_new)
    grid_step = jnp.max(jnp.abs(updated), axis=-1, keepdims=True) / 8.0
    dither = bits[...].astype(F32) * (1.0 / 65280.0) - 0.5
    out[:256, :] = jnp.where(touched > 0.5, updated + grid_step * dither, updated).astype(BF)
    row = to_row(accum_new, eye)
    high = row.astype(BF)
    rest = row - high.astype(F32)
    middle = rest.astype(BF)
    low = rest - middle.astype(F32)
    at = iota((16, 256), 0)
    packed = jnp.where(
        at == 0, high.astype(F32), jnp.where(at == 1, middle.astype(F32), low)
    )
    out[256:, :] = packed.astype(BF)


def cold_update(parts, table, accum, bits):
    return pl.pallas_call(
        cold_update_kernel,
        out_shape=jax.ShapeDtypeStruct((272, 256), BF),
        compiler_params=params(32),
        name="cold_update",
    )(parts, table, accum, bits)


def adagrad_rows(table_rows, accum, gradient):
    accum_new = accum + jnp.mean(gradient * gradient, axis=-1)
    updated = table_rows - learn_rate * gradient / jnp.sqrt(accum_new)[:, None]
    return (updated, accum_new)


def exchange(value, axis):
    return lax.all_to_all(value, axis, split_axis=0, concat_axis=0, tiled=True)


def on_device(
    cold_table,
    cold_accum,
    dither_bits,
    hot_table,
    hot_accum,
    w_flat,
    w_inter,
    hidden_bias,
    w_out,
    targets,
    hot_ids,
    cold_slots,
    requests,
    counts,
):
    shards = lax.axis_size("shard")
    dps = lax.axis_size("dp")
    capacity = requests.shape[1]
    row_count, row_width = cold_table.shape
    hot_count = hot_table.shape[0]
    slots = shards * capacity

    live = jnp.arange(capacity, dtype=jnp.int32) < counts[:, :, None]
    asked = jnp.where(live, requests.reshape(MB, shards, capacity), -1)
    asked = asked.transpose(1, 0, 2).reshape(shards, MB * capacity)
    wanted = exchange(asked, "shard")
    wanted = [wanted[:, m * capacity : (m + 1) * capacity].reshape(slots) for m in range(MB)]

    def arrange(ids, m):
        part = ids[m * BATCH : (m + 1) * BATCH].reshape(BATCH // GROUP, GROUP, F_COLD)
        return part.transpose(0, 2, 1).reshape(-1)

    hot_bf = hot_table.astype(BF)
    inter_t = w_inter.reshape(FEATS, FEATS, -1).transpose(1, 0, 2).reshape(w_inter.shape)

    served = [fetch_rows(wanted[m].reshape(slots, 1), cold_table) for m in range(MB)]
    fetched = [
        exchange(served[m][0].reshape(shards, capacity, row_width), "shard").reshape(
            slots, row_width
        )
        for m in range(MB)
    ]
    hot_grad = None
    owned = []
    for m in range(MB):
        cold_at = arrange(cold_slots, m)
        hot_at = arrange(hot_ids, m)
        args = (
            fetched[m],
            hot_bf,
            cold_at.reshape(-1, 1),
            hot_at.reshape(-1, 1),
            cold_at.reshape(1, -1),
            hot_at.reshape(1, -1),
            targets[m * BATCH : (m + 1) * BATCH].reshape(-1, 1),
            w_flat,
            w_inter,
            inter_t,
            hidden_bias.reshape(1, -1),
            w_out.reshape(1, -1),
        )
        slot_grad, hot_grad = backprop(args, hot_grad, slots, hot_count)
        owned.append(
            exchange(slot_grad.reshape(shards, capacity, row_width), "shard").reshape(
                slots, row_width
            )
        )

    shard_at = lax.axis_index("shard")
    dp_at = lax.axis_index("dp")
    hot_part = hot_count // dps
    hot_own = hot_part // shards
    hot_sum = jnp.sum(exchange(hot_grad.reshape(dps, hot_part, row_width), "dp"), axis=0)
    hot_sum = jnp.sum(
        exchange(hot_sum.reshape(shards, hot_own, row_width), "shard"), axis=0
    )
    first_hot = dp_at * hot_part + shard_at * hot_own
    hot_new, hot_accum_new = adagrad_rows(
        lax.dynamic_slice(hot_table, (first_hot, 0), (hot_own, row_width)),
        lax.dynamic_slice(hot_accum, (first_hot,), (hot_own,)),
        hot_sum,
    )
    hot_pack = jnp.concatenate(
        [hot_new, jnp.broadcast_to(hot_accum_new[:, None], (hot_own, 128))], axis=1
    )
    hot_all = exchange(jnp.broadcast_to(hot_pack[None], (shards,) + hot_pack.shape), "shard")
    hot_all = hot_all.reshape(hot_part, row_width + 128)
    accum_rows = jnp.broadcast_to(
        jnp.pad(hot_all[:, row_width], (0, row_width - hot_part))[None], (8, row_width)
    )
    hot_all = jnp.concatenate([hot_all[:, :row_width], accum_rows], axis=0)
    hot_all = lax.all_gather(hot_all, "dp", axis=0, tiled=False)
    hot_out = hot_all[:, :hot_part].reshape(hot_count, row_width)
    hot_accum_out = hot_all[:, hot_part, :hot_part].reshape(hot_count)

    cold_part = row_count // dps
    first = owner_first(wanted[0].reshape(1, slots), owned[0])
    parts = owner_second(
        wanted[1].reshape(1, slots), owned[1], first, served[0][1], served[1][1]
    )
    parts = exchange(parts, "dp")
    first_cold = dp_at * cold_part
    packed = cold_update(
        parts,
        lax.dynamic_slice(cold_table, (first_cold, 0), (cold_part, row_width)),
        lax.dynamic_slice(cold_accum, (first_cold,), (cold_part,)).reshape(1, -1),
        lax.dynamic_slice(dither_bits, (first_cold, 0), (cold_part, row_width)),
    )
    cold_all = lax.all_gather(packed, "dp", axis=0, tiled=False)
    cold_out = cold_all[:, :cold_part].reshape(row_count, row_width)
    pieces = cold_all[:, cold_part : cold_part + 3].astype(F32)
    cold_accum_out = ((pieces[:, 2] + pieces[:, 1]) + pieces[:, 0]).reshape(row_count)
    return (cold_out, cold_accum_out, hot_out, hot_accum_out)


def solution(mesh):
    return jax.shard_map(
        on_device,
        mesh=mesh,
        in_specs=(
            P("shard", None),
            P("shard"),
            P("shard", None),
            P(),
            P(),
            P(),
            P(),
            P(),
            P(),
            P(("shard", "dp")),
            P(("shard", "dp"), None),
            P(("shard", "dp"), None),
            P(("shard", "dp"), None),
            P(("shard", "dp"), None),
        ),
        out_specs=(P("shard", None), P("shard"), P(), P()),
        check_vma=False,
    )
```

time: 702 us -> 356 us (0.51)
  waiting for transfers between devices: 329 us -> 77.6 us
  other arithmetic: 133 us -> 8.02 us
  Pallas kernels: 0 us -> 85.6 us
  blocking collectives: 32.5 us -> 86.2 us
  local copies, waits for them, and re-layouts: 92.7 us -> 50 us
  matrix products: 30.5 us -> 0 us
  starting transfers between devices: 61.1 us -> 31.2 us
    psum x2 -> x0, waiting for transfers between devices: 312 us -> none  [the longest x1 247 us: on_device(): total_hot = lax.psum(hot_grad, ('shard', 'dp'))]
    scatter-add x8 -> x0, other arithmetic: 100 us -> none  [the longest x2 27.1 us: on_device(): jax.ops.segment_sum(gradients[:, :cold_feats].reshape(-1, row_width), slo...]
    pallas_call x0 -> x7, Pallas kernels: none -> 85.6 us  [the longest x2 68.1 us: backprop(): pl.pallas_call(kernel, out_shape=(jax.ShapeDtypeStruct((slots, width), BF...]
    all_to_all x1 -> x4, blocking collectives: 20 us -> 86.2 us  [exchange(): return lax.all_to_all(value, axis, split_axis=0, concat_axis=0, tiled=True)]
    gather x6 -> x0, local copies, waits for them, and re-layouts: 54.7 us -> none  [the longest x2 18.9 us: on_device(): cold_table[requested]]
    all_to_all x7 -> x5, waiting for transfers between devices: 17.2 us -> 60.3 us  [exchange(): return lax.all_to_all(value, axis, split_axis=0, concat_axis=0, tiled=True)]
    dot_general x12 -> x0, matrix products: 30.5 us -> none  [the longest x2 8.74 us: backprop(): jnp.einsum('sfe,sge->sfg', stacked, stacked, preferred_element_type=jnp.f...]
    all_to_all x7 -> x5, starting transfers between devices: 60.7 us -> 31.1 us  [exchange(): return lax.all_to_all(value, axis, split_axis=0, concat_axis=0, tiled=True)]
  transfers between devices with their start and end apart: 9 -> 7, of which waited for: 3 -> 5; matrix products, arithmetic and copies ran while one was open for 33% -> 6% of each run, Pallas kernels for 0% -> 13%
where the time goes in v1:
time: 356 us; the launch traced here: 353 us
  blocking collectives  86.2 us (24%)
  Pallas kernels  85.6 us (24%)
  waiting for transfers between devices  77.6 us (22%)
  local copies, waits for them, and re-layouts  50 us (14%)
  starting transfers between devices  31.2 us (9%)
  between operations  14.5 us (4%)
  other arithmetic  8.02 us (2%)
    all_to_all x4, blocking collectives, exchange(): return lax.all_to_all(value, axis, split_axis=0, concat_axis=0, tiled=True)  86.2 us
    pallas_call x2, Pallas kernels, backprop(): pl.pallas_call(kernel, out_shape=(jax.ShapeDtypeStruct((slots, width), BF...  68.1 us
    all_to_all x5, waiting for transfers between devices, exchange(): return lax.all_to_all(value, axis, split_axis=0, concat_axis=0, tiled=True)  60.3 us
    all_to_all x5, starting transfers between devices, exchange(): return lax.all_to_all(value, axis, split_axis=0, concat_axis=0, tiled=True)  31.1 us
    unnamed x75, local copies, waits for them, and re-layouts  26 us
    all_gather x1, waiting for transfers between devices, on_device(): cold_all = lax.all_gather(packed, 'dp', axis=0, tiled=False)  17.3 us
    pallas_call x2, Pallas kernels, fetch_rows(): pl.pallas_call(fetch_kernel, out_shape=(jax.ShapeDtypeStruct((slots, widt...  8.33 us
  transfers between devices with their start and end apart: 7, of which 5 were waited for; matrix products, arithmetic and copies ran while one was open for 6% of the time, Pallas kernels for 13%

profile of v1, /device:TPU:8, one launch (start us, length us, event | category | flops | bytes accessed | tf_op | source)
XLA Modules:
  0.0 353.1 jit_solution(8916378882592540557)
XLA Ops:
  7.2 0.9 copy.84
  8.1 0.9 fusion
  9.1 20.1 %all_to_all.52 = s32[32,1,128]{2,1,0:T(1,128)S(1)} all-to-all(s32[32,1,128]{2,1,0:T(1,128)S(1)} %all_to_all.32), channel_id=1, replica_groups=mesh['shard'=32,'dp'=8] {'shard'}, dimensions={0} | all-to-all | bytes 32768 | tf_op jit(solution)/shard_map/all_to_all | solution.py:371
  29.2 2.0 reshape_reshape.51.ids_col
  31.2 1.2 copy-done.9
  32.4 4.2 %fetch_rows.3 = (bf16[2048,256]{1,0:T(8,128)(2,1)S(1)}, f32[1,2048]{1,0:T(1,128)S(1)}) custom-call(s32[2048,1]{1,0:T(8,128)S(1)} %copy-done.9, bf16[2048,256]{1,0:T(8,128)(2,1)S(1)} %copy-done.3), custom_call_target="tpu_custom_call" | custom-call | tf_op jit(solution)/shard_map/fetch_rows/pallas_call | solution.py:57
  36.6 1.0 copy-done.19
  38.2 5.7 %all-to-all-start.2 = ((bf16[32,64,256]{2,1,0:T(8,128)(2,1)}), bf16[32,64,256]{2,1,0:T(8,128)(2,1)}, u32[]{:S(2)}, u32[]{:S(2)}) async-start(bf16[32,64,256]{2,1,0:T(8,128)(2,1)} %bitcast.55), calls=%async_computation.2 | async-start | bytes 2097152 | tf_op jit(solution)/shard_map/all_to_all | solution.py:371
  43.9 2.0 reshape_reshape.48.ids_col
  45.9 1.2 copy-done.10
  47.1 4.2 %fetch_rows.2 = (bf16[2048,256]{1,0:T(8,128)(2,1)S(1)}, f32[1,2048]{1,0:T(1,128)S(1)}) custom-call(s32[2048,1]{1,0:T(8,128)S(1)} %copy-done.10, bf16[2048,256]{1,0:T(8,128)(2,1)S(1)} %copy-done.3), custom_call_target="tpu_custom_call" | custom-call | tf_op jit(solution)/shard_map/fetch_rows/pallas_call | solution.py:57
  51.3 1.0 copy-done.18
  52.8 18.1 %all-to-all-done.2 = bf16[32,64,256]{2,1,0:T(8,128)(2,1)} async-done(((bf16[32,64,256]{2,1,0:T(8,128)(2,1)}), bf16[32,64,256]{2,1,0:T(8,128)(2,1)}, u32[]{:S(2)}, u32[]{:S(2)}) %all-to-all-start.2) | async-done | bytes 1048608 | tf_op jit(solution)/shard_map/all_to_all | solution.py:371
  70.9 5.6 %all-to-all-start.1 = ((bf16[32,64,256]{2,1,0:T(8,128)(2,1)}), bf16[32,64,256]{2,1,0:T(8,128)(2,1)}, u32[]{:S(2)}, u32[]{:S(2)}) async-start(bf16[32,64,256]{2,1,0:T(8,128)(2,1)} %bitcast.54), calls=%async_computation.1 | async-start | bytes 2097152 | tf_op jit(solution)/shard_map/all_to_all | solution.py:371
  76.7 1.6 reshape_reshape.52.refs_2_
  78.5 1.6 reshape_reshape.53.refs_3_
  80.1 0.7 reshape_reshape.46.refs_5_
  80.9 1.6 reshape_reshape.49.cold_col
  82.7 1.6 reshape_reshape.50.hot_col
  85.0 2.1 convert_element_type.8.refs_1_.hotb
  87.0 0.9 copy.89
  88.5 0.8 copy.95.refs_6_
  89.3 0.8 copy.98.targets
  90.1 1.0 copy-done.4
  91.1 1.2 copy-done.11
  92.4 0.9 copy-done.13
  93.3 0.9 copy-done.20
  94.2 0.7 copy-done.21
  96.3 33.8 %train_step.2 = (bf16[2048,256]{1,0:T(8,128)(2,1)S(1)}, f32[1024,256]{1,0:T(8,128)S(1)}) custom-call(bf16[2048,256]{1,0:T(8,128)(2,1)} %bitcast.14.refs_0_, bf16[1024,256]{1,0:T(8,128)(2,1)S(1)} %copy-done.4, s32[2048,1]{1,0:T(8,128)S(1)} %copy-done.11, s32[2048,1]{1,0:T(8,128)} %reshape_reshape.53.refs_3_, s32[1,2048]{1,0:T(1,128)S(1)} %reshape_reshape.45.refs_4_, ...), custom_call_target="tpu_custom_call" | custom-call | tf_op jit(solution)/shard_map/train_step/pallas_call | solution.py:239
  130.1 1.0 copy-done.15
  131.1 1.0 copy-done.17
  132.1 1.0 copy-done.5
  133.1 1.2 copy-done.7
  134.3 0.9 copy-done.14
  135.3 0.7 copy-done.22
  137.3 34.3 %train_step.3 = (bf16[2048,256]{1,0:T(8,128)(2,1)S(1)}, f32[1024,256]{1,0:T(8,128)S(1)}) custom-call(bf16[2048,256]{1,0:T(8,128)(2,1)} %bitcast.4.fetched, bf16[1024,256]{1,0:T(8,128)(2,1)S(1)} %copy-done.5, s32[2048,1]{1,0:T(8,128)S(1)} %copy-done.7, s32[2048,1]{1,0:T(8,128)} %reshape_reshape.50.hot_col, s32[1,2048]{1,0:T(1,128)S(1)} %reshape_reshape.40.cold_row, ...), custom_call_target="tpu_custom_call" | custom-call | tf_op jit(solution)/shard_map/train_step/pallas_call | solution.py:239
  171.6 1.0 copy-done.16
  172.6 20.2 %all_to_all.53 = f32[8,128,256]{2,1,0:T(8,128)} all-to-all(f32[8,128,256]{2,1,0:T(8,128)S(1)} %bitcast.56), channel_id=1, replica_groups=mesh['shard'=32,'dp'=8] {'dp'}, dimensions={0} | all-to-all | bytes 2097152 | tf_op jit(solution)/shard_map/all_to_all | solution.py:371
  192.8 1.3 reduce_sum.27
  194.1 0.7 reshape.122
  194.8 9.8 %all-to-all-start.7 = ((f32[32,4,256]{2,1,0:T(4,128)}), f32[32,4,256]{2,1,0:T(4,128)S(1)}, u32[]{:S(2)}, u32[]{:S(2)}) async-start(f32[32,4,256]{2,1,0:T(4,128)} %reshape.122), calls=%async_computation.7 | async-start | bytes 262144 | tf_op jit(solution)/shard_map/all_to_all | solution.py:371
  204.6 8.9 %all-to-all-done.7 = f32[32,4,256]{2,1,0:T(4,128)S(1)} async-done(((f32[32,4,256]{2,1,0:T(4,128)}), f32[32,4,256]{2,1,0:T(4,128)S(1)}, u32[]{:S(2)}, u32[]{:S(2)}) %all-to-all-start.7) | async-done | bytes 131104 | tf_op jit(solution)/shard_map/all_to_all | solution.py:371
  213.6 0.8 fusion.1
  214.3 0.8 divide_subtract_fusion
  215.2 14.1 %all_to_all.54 = f32[32,4,384]{2,1,0:T(4,128)S(1)} all-to-all(f32[32,4,384]{2,1,0:T(4,128)S(1)} %broadcast_in_dim.12), channel_id=1, replica_groups=mesh['shard'=32,'dp'=8] {'shard'}, dimensions={0} | all-to-all | bytes 393216 | tf_op jit(solution)/shard_map/all_to_all | solution.py:371
  229.3 31.9 %all_to_all.55 = bf16[32,64,256]{2,1,0:T(8,128)(2,1)} all-to-all(bf16[32,64,256]{2,1,0:T(8,128)(2,1)} %bitcast.53), channel_id=1, replica_groups=mesh['shard'=32,'dp'=8] {'shard'}, dimensions={0} | all-to-all | bytes 2097152 | tf_op jit(solution)/shard_map/all_to_all | solution.py:371
  261.2 5.8 %all-to-all-start.3 = ((bf16[32,64,256]{2,1,0:T(8,128)(2,1)}), bf16[32,64,256]{2,1,0:T(8,128)(2,1)}, u32[]{:S(2)}, u32[]{:S(2)}) async-start(bf16[32,64,256]{2,1,0:T(8,128)(2,1)} %bitcast.52), calls=%async_computation.3 | async-start | bytes 2097152 | tf_op jit(solution)/shard_map/all_to_all | solution.py:371
  267.9 0.8 reshape_reshape.47.ids_row
  268.8 1.2 copy-done.8
  270.1 2.8 owner_first.1.prev
  272.9 1.3 copy-done.1
  274.2 17.5 %all-to-all-done.3 = bf16[32,64,256]{2,1,0:T(8,128)(2,1)} async-done(((bf16[32,64,256]{2,1,0:T(8,128)(2,1)}), bf16[32,64,256]{2,1,0:T(8,128)(2,1)}, u32[]{:S(2)}, u32[]{:S(2)}) %all-to-all-start.3) | async-done | bytes 1048608 | tf_op jit(solution)/shard_map/all_to_all | solution.py:371
  291.8 1.6 copy-done.2
  293.4 4.1 %owner_second.1 = bf16[8,272,256]{2,1,0:T(8,128)(2,1)S(1)} custom-call(s32[1,2048]{1,0:T(1,128)S(1)} %reshape_reshape.36.ids_row, bf16[2048,256]{1,0:T(8,128)(2,1)} %bitcast.20.grads, f32[2048,256]{1,0:T(8,128)S(1)} %copy-done.2, f32[1,2048]{1,0:T(1,128)S(1)} %copy-done.24, f32[1,2048]{1,0:T(1,128)S(1)} %copy-done.26), custom_call_target="tpu_custom_call" | custom-call | tf_op jit(solution)/shard_map/owner_second/pallas_call | solution.py:312
  297.5 1.0 copy-done.6
  298.5 4.3 %all-to-all-start.5 = ((bf16[8,272,256]{2,1,0:T(8,128)(2,1)}), bf16[8,272,256]{2,1,0:T(8,128)(2,1)}, u32[]{:S(2)}, u32[]{:S(2)}) async-start(bf16[8,272,256]{2,1,0:T(8,128)(2,1)} %copy-done.6), calls=%async_computation.5 | async-start | bytes 2228224 | tf_op jit(solution)/shard_map/all_to_all | solution.py:371
  302.8 0.8 dynamic_slice.16
  303.6 15.8 %all-to-all-done.5.parts = bf16[8,272,256]{2,1,0:T(8,128)(2,1)} async-done(((bf16[8,272,256]{2,1,0:T(8,128)(2,1)}), bf16[8,272,256]{2,1,0:T(8,128)(2,1)}, u32[]{:S(2)}, u32[]{:S(2)}) %all-to-all-start.5) | async-done | bytes 1114144 | tf_op jit(solution)/shard_map/all_to_all | solution.py:371
  319.4 2.3 cold_update.1
  321.7 2.3 slice.77
  324.0 1.4 slice.78
  325.3 17.3 %all-gather.5.cloned.1.call-done = bf16[2176,256]{1,0:T(8,128)(2,1)} async-done(((bf16[272,256]{1,0:T(8,128)(2,1)}), bf16[2176,256]{1,0:T(8,128)(2,1)}) %all-gather.5.cloned.1.call-update) | async-done | bytes 1114128 | tf_op jit(solution)/shard_map/all_gather | solution.py:483
  342.6 2.3 slice.70
  344.9 0.8 slice_convert_fusion
  (91 shorter events, 8.0 us)
Async XLA Ops:
  7.2 296.4 %copy-start = (s32[2048,256]{1,0:T(8,128)S(1)}, s32[2048,256]{1,0:T(8,128)}, u32[]{:S(2)}) copy-start(s32[2048,256]{1,0:T(8,128)} %param.16) | copy-start | bytes 6291460
  7.2 24.0 %copy-start.3 = (bf16[2048,256]{1,0:T(8,128)(2,1)S(1)}, bf16[2048,256]{1,0:T(8,128)(2,1)}, u32[]{:S(2)}) copy-start(bf16[2048,256]{1,0:T(8,128)(2,1)} %table.3) | copy-start | bytes 3145732
  29.2 7.4 %copy-start.33 = (s32[32,64]{1,0:T(8,128)}, s32[32,64]{1,0:T(8,128)S(1)}, u32[]{:S(2)}) copy-start(s32[32,64]{1,0:T(8,128)S(1)} %get-tuple-element.26) | copy-start | bytes 24580
  29.2 14.7 %copy-start.31 = (s32[32,64]{1,0:T(8,128)}, s32[32,64]{1,0:T(8,128)S(1)}, u32[]{:S(2)}) copy-start(s32[32,64]{1,0:T(8,128)S(1)} %get-tuple-element.27) | copy-start | bytes 24580
  31.2 1.2 copy-start.9
  36.6 1.0 copy-start.19
  37.6 0.6 copy-start.23
  38.2 32.7 %all-to-all-start.2 = ((bf16[32,64,256]{2,1,0:T(8,128)(2,1)}), bf16[32,64,256]{2,1,0:T(8,128)(2,1)}, u32[]{:S(2)}, u32[]{:S(2)}) async-start(bf16[32,64,256]{2,1,0:T(8,128)(2,1)} %bitcast.55), calls=%async_computation.2 | async-start | bytes 2097152 | tf_op jit(solution)/shard_map/all_to_all | solution.py:371
  45.9 1.2 copy-start.10
  51.3 1.0 copy-start.18
  52.3 0.6 copy-start.25
  52.8 23.7 %copy-start.34 = (s32[512,8]{0,1:T(8,128)S(1)}, s32[512,8]{0,1:T(8,128)}, u32[]{:S(2)}) copy-start(s32[512,8]{0,1:T(8,128)} %param.25) | copy-start | bytes 49156
  70.9 61.1 %all-to-all-start.1 = ((bf16[32,64,256]{2,1,0:T(8,128)(2,1)}), bf16[32,64,256]{2,1,0:T(8,128)(2,1)}, u32[]{:S(2)}, u32[]{:S(2)}) async-start(bf16[32,64,256]{2,1,0:T(8,128)(2,1)} %bitcast.54), calls=%async_computation.1 | async-start | bytes 2097152 | tf_op jit(solution)/shard_map/all_to_all | solution.py:371
  76.6 1.8 copy-start.35
  82.7 4.4 %copy-start.12 = (bf16[256,512]{1,0:T(8,128)(2,1)S(1)}, bf16[256,512]{1,0:T(8,128)(2,1)}, u32[]{:S(2)}) copy-start(bf16[256,512]{1,0:T(8,128)(2,1)} %w_inter.1) | copy-start | bytes 786436
  84.3 3.6 %copy-start.36 = (f32[512]{0:T(512)S(1)}, f32[512]{0:T(512)}, u32[]{:S(2)}) copy-start(f32[512]{0:T(512)} %param.23) | copy-start | bytes 6148
  90.1 1.0 copy-start.4
  91.1 1.2 copy-start.11
  92.4 0.9 copy-start.13
  93.3 0.9 copy-start.20
  94.2 0.7 copy-start.21
  94.9 0.7 copy-start.27
  95.6 0.7 copy-start.29
  130.1 1.0 copy-start.15
  131.1 1.0 copy-start.17
  132.1 1.0 copy-start.5
  133.1 1.2 copy-start.7
  134.3 0.9 copy-start.14
  135.3 0.7 copy-start.22
  136.0 0.7 copy-start.28
  136.6 0.7 copy-start.30
  171.6 1.0 copy-start.16
  194.8 18.6 %all-to-all-start.7 = ((f32[32,4,256]{2,1,0:T(4,128)}), f32[32,4,256]{2,1,0:T(4,128)S(1)}, u32[]{:S(2)}, u32[]{:S(2)}) async-start(f32[32,4,256]{2,1,0:T(4,128)} %reshape.122), calls=%async_computation.7 | async-start | bytes 262144 | tf_op jit(solution)/shard_map/all_to_all | solution.py:371
  261.2 7.5 %copy-start.32 = (s32[32,64]{1,0:T(8,128)S(1)}, s32[32,64]{1,0:T(8,128)}, u32[]{:S(2)}) copy-start(s32[32,64]{1,0:T(8,128)} %copy-done.31) | copy-start | bytes 24580
  261.2 30.6 %all-to-all-start.3 = ((bf16[32,64,256]{2,1,0:T(8,128)(2,1)}), bf16[32,64,256]{2,1,0:T(8,128)(2,1)}, u32[]{:S(2)}, u32[]{:S(2)}) async-start(bf16[32,64,256]{2,1,0:T(8,128)(2,1)} %bitcast.52), calls=%async_computation.3 | async-start | bytes 2097152 | tf_op jit(solution)/shard_map/all_to_all | solution.py:371
  267.0 54.7 %all-gather.7.cloned.1.call-start = ((), (), s32[]{:S(2)}) async-start(), calls=%async_computation.10 | async-start | bytes 1253376 | tf_op jit(solution)/shard_map/all_gather | solution.py:466
  268.8 1.2 copy-start.8
  270.0 21.7 %copy-start.24 = (f32[1,2048]{1,0:T(1,128)S(1)}, f32[1,2048]{1,0:T(1,128)}, u32[]{:S(2)}) copy-start(f32[1,2048]{1,0:T(1,128)} %copy-done.23) | copy-start | bytes 24580
  270.0 21.7 %copy-start.26 = (f32[1,2048]{1,0:T(1,128)S(1)}, f32[1,2048]{1,0:T(1,128)}, u32[]{:S(2)}) copy-start(f32[1,2048]{1,0:T(1,128)} %copy-done.25) | copy-start | bytes 24580
  272.9 1.3 copy-start.1
  291.8 1.6 copy-start.2
  297.5 1.0 copy-start.6
  298.5 20.9 %all-to-all-start.5 = ((bf16[8,272,256]{2,1,0:T(8,128)(2,1)}), bf16[8,272,256]{2,1,0:T(8,128)(2,1)}, u32[]{:S(2)}, u32[]{:S(2)}) async-start(bf16[8,272,256]{2,1,0:T(8,128)(2,1)} %copy-done.6), calls=%async_computation.5 | async-start | bytes 2228224 | tf_op jit(solution)/shard_map/all_to_all | solution.py:371
  302.7 39.9 %all-gather.5.cloned.1.call-start = ((), (), s32[]{:S(2)}) async-start(), calls=%async_computation.9 | async-start | bytes 1253376 | tf_op jit(solution)/shard_map/all_gather | solution.py:483
Sparse Core Ops, SparseCore 0:
  269.6 24.9 all-gather.6
  321.8 20.7 all-gather.4

commit v2 on v0

v2 whole, which is shorter than its diff:
```python
import jax
import jax.numpy as jnp
from jax import lax
from jax.experimental import pallas as pl
from jax.experimental.pallas import tpu as pltpu
from jax.sharding import PartitionSpec as P


MB = 2
GROUP = 16
FEATS = 16
F_COLD = 8
BF = jnp.bfloat16
F32 = jnp.float32
NT = (((1,), (1,)), ((), ()))
HBM = pl.BlockSpec(memory_space=pltpu.HBM)
VMEM = pl.BlockSpec(memory_space=pltpu.VMEM)
SMEM = pl.BlockSpec(memory_space=pltpu.SMEM)
N_DP = 8
learn_rate = 0.3
UNROLL = 4


def iota(shape, axis):
    return lax.broadcasted_iota(jnp.int32, shape, axis)


def as_one(same):
    return jnp.where(same, jnp.ones(same.shape, BF), jnp.zeros(same.shape, BF))


def params(limit_mib):
    return pltpu.CompilerParams(vmem_limit_bytes=limit_mib << 20)


def load_all(pairs, sems):
    copies = [pltpu.make_async_copy(s, d, sems.at[i]) for i, (s, d) in enumerate(pairs)]
    for c in copies:
        c.start()
    return copies


def match_rows(ids, match, at, count):
    lanes = iota((GROUP, count), 1).astype(jnp.int16)
    for f in range(F_COLD):
        mine = jnp.broadcast_to(ids[:, f : f + 1], (GROUP, 128)).astype(jnp.int16)
        same = lanes == jnp.concatenate([mine] * (count // 128), axis=1)
        match[pl.ds(at + f * GROUP, GROUP), :count] = as_one(same)


def hot_rows_kernel(hot_ids, table, out, ids, src, match, res, sems):
    copies = load_all([(hot_ids, ids), (table, src)], sems)
    for c in copies:
        c.wait()
    source = src[...].astype(BF)
    half = F_COLD * GROUP
    block = 4
    steps = ids.shape[0] // GROUP // block

    def body(b, carry):
        for q in range(block):
            part = pl.ds(pl.multiple_of((b * block + q) * GROUP, GROUP), GROUP)
            match_rows(ids[part, :], match, q * half, source.shape[0])
        rows = pl.ds(pl.multiple_of(b * block * half, block * half), block * half)
        res[rows, :] = jnp.dot(match[...], source, preferred_element_type=F32).astype(BF)
        return carry

    lax.fori_loop(0, steps, body, 0)
    done = pltpu.make_async_copy(res, out, sems.at[2])
    done.start()
    done.wait()


def hot_rows(hot_ids, table):
    count, width = table.shape
    rows = hot_ids.shape[0] * F_COLD
    return pl.pallas_call(
        hot_rows_kernel,
        in_specs=[HBM, HBM],
        out_specs=HBM,
        out_shape=jax.ShapeDtypeStruct((rows, width), BF),
        scratch_shapes=[
            pltpu.VMEM(hot_ids.shape, jnp.int32),
            pltpu.VMEM(table.shape, F32),
            pltpu.VMEM((512, count), BF),
            pltpu.VMEM((rows, width), BF),
            pltpu.SemaphoreType.DMA((3,)),
        ],
        compiler_params=params(32),
        name="hot_rows",
    )(hot_ids, table)


def step_kernel(m, *refs):
    (
        fetched_h, xh_h, slots_h, slots_t_h, targets_h, flat_h, inter_h, bias_h, w_out_h,
        slot_grad, hot_hi, hot_lo,
        fetched, x, slots, slots_t, targets, w_flat, w_inter, bias, w_out,
        a, pairs, back, mirror, g_hi, g_lo, h_hi, h_lo, match, slopes, sems,
    ) = refs
    width = fetched.shape[1]
    samples = targets.shape[1]
    groups = samples // GROUP
    lane_group = FEATS * GROUP
    half = F_COLD * GROUP
    scale = width ** (-0.5)
    block = 4
    first = m * samples

    head = load_all(
        [
            (slots_h.at[pl.ds(first, samples), :], slots),
            (fetched_h, fetched),
        ],
        sems,
    )
    hot_copies = [
        pltpu.make_async_copy(
            xh_h.at[pl.ds((m * groups + g) * half, half), :],
            x.at[pl.ds(g * lane_group + half, half), :],
            sems.at[2],
        )
        for g in range(groups)
    ]
    for c in hot_copies:
        c.start()
    tail = load_all(
        [
            (flat_h, w_flat),
            (inter_h, w_inter),
            (bias_h, bias),
            (w_out_h, w_out),
            (targets_h.at[:, pl.ds(first, samples)], targets),
            (slots_t_h.at[:, pl.ds(first, samples)], slots_t),
        ],
        sems.at[pl.ds(3, 6)],
    )

    sq = (lane_group, lane_group)
    i_hi = iota(sq, 0) >> 4
    i_lo = iota(sq, 0) & 15
    j_hi = iota(sq, 1) >> 4
    j_lo = iota(sq, 1) & 15
    spread = jnp.where(i_hi == j_lo, 1.0, 0.0).astype(BF)
    spread_t = jnp.where(i_lo == j_hi, 1.0, 0.0).astype(BF)
    swap = jnp.where((i_hi == j_lo) & (i_lo == j_hi), 1.0, 0.0).astype(BF)

    for c in head:
        c.wait()

    def gather(b, carry):
        for q in range(block):
            part = pl.ds(pl.multiple_of((b * block + q) * GROUP, GROUP), GROUP)
            match_rows(slots[part, :], match, q * half, fetched.shape[0])
        picked = jnp.dot(match[...], fetched[...], preferred_element_type=F32).astype(BF)
        for q in range(block):
            dst = pl.multiple_of((b * block + q) * lane_group, lane_group)
            x[pl.ds(dst, half), :] = picked[q * half : (q + 1) * half]
        return carry

    lax.fori_loop(0, groups // block, gather, 0)
    for c in hot_copies:
        c.wait()

    def dots(i, carry):
        for u in range(UNROLL):
            g = i * UNROLL + u
            rows = pl.ds(pl.multiple_of(g * lane_group, lane_group), lane_group)
            part = pl.ds(pl.multiple_of(g * GROUP, GROUP), GROUP)
            xg = x[rows, :]
            for f in range(FEATS):
                a[part, f * width : (f + 1) * width] = xg[f * GROUP : (f + 1) * GROUP]
            gram = lax.dot_general(xg, xg, NT, preferred_element_type=F32) * scale
            own = jnp.where(i_lo == j_lo, gram, 0.0).astype(BF)
            wide = jnp.dot(own, spread, preferred_element_type=F32)
            wide = jnp.where(i_hi == j_hi, wide, 0.0)
            pairs[part, :] = jnp.sum(
                wide.reshape(FEATS, GROUP, lane_group), axis=0
            ).astype(BF)
        return carry

    lax.fori_loop(0, groups // UNROLL, dots, 0)
    for c in tail:
        c.wait()

    pre = jnp.dot(a[...], w_flat[...], preferred_element_type=F32)
    pre = pre + jnp.dot(pairs[...], w_inter[...], preferred_element_type=F32)
    pre = pre + bias[...]
    gated = jax.nn.sigmoid(pre)
    logits = jnp.sum(pre * gated * w_out[...], axis=-1, keepdims=True)
    eye = iota((samples, samples), 0) == iota((samples, samples), 1)
    target = jnp.sum(jnp.where(eye, targets[...], 0.0), axis=1, keepdims=True)
    residual = jax.nn.sigmoid(logits) - target
    slopes[...] = (residual * w_out[...] * gated * (1.0 + pre * (1.0 - gated))).astype(BF)

    inter_t = jnp.dot(swap, w_inter[...], preferred_element_type=F32).astype(BF)
    both = lax.dot_general(slopes[...], w_inter[...], NT, preferred_element_type=F32)
    both = both + lax.dot_general(slopes[...], inter_t, NT, preferred_element_type=F32)
    mirror[...] = (both * scale).astype(BF)

    def flat_back(f, carry):
        rows = pl.ds(pl.multiple_of(f * width, width), width)
        back[f] = lax.dot_general(
            slopes[...], w_flat[rows, :], NT, preferred_element_type=F32
        )
        return carry

    lax.fori_loop(0, FEATS, flat_back, 0)

    def grads(i, carry):
        for u in range(UNROLL):
            g = i * UNROLL + u
            rows = pl.ds(pl.multiple_of(g * lane_group, lane_group), lane_group)
            part = pl.ds(pl.multiple_of(g * GROUP, GROUP), GROUP)
            mine = mirror[part, :].astype(F32)
            tall = jnp.broadcast_to(mine[None], (FEATS, GROUP, lane_group)).reshape(sq)
            tall = jnp.where(i_hi == j_hi, tall, 0.0).astype(BF)
            wide = jnp.dot(tall, spread_t, preferred_element_type=F32)
            wide = jnp.where(i_lo == j_lo, wide, 0.0).astype(BF)
            total = jnp.dot(wide, x[rows, :], preferred_element_type=F32)
            total = total + back[:, part, :].reshape(lane_group, width)
            hi = total.astype(BF)
            lo = (total - hi.astype(F32)).astype(BF)
            for f in range(F_COLD):
                dst = pl.ds(pl.multiple_of(f * samples + g * GROUP, GROUP), GROUP)
                at = f * GROUP
                g_hi[dst, :] = hi[at : at + GROUP]
                g_lo[dst, :] = lo[at : at + GROUP]
                h_hi[dst, :] = hi[half + at : half + at + GROUP]
                h_lo[dst, :] = lo[half + at : half + at + GROUP]
        return carry

    lax.fori_loop(0, groups // UNROLL, grads, 0)
    outs = load_all([(h_hi, hot_hi), (h_lo, hot_lo)], sems.at[pl.ds(0, 2)])

    rows_blk = 512

    def scatter(b, carry):
        at = pl.multiple_of(b * rows_blk, rows_blk)
        subs = iota((rows_blk, samples), 0).astype(jnp.int16)
        for f in range(F_COLD):
            mine = jnp.broadcast_to(slots_t[f : f + 1, :] - at, (16, samples)).astype(jnp.int16)
            same = subs == jnp.concatenate([mine] * (rows_blk // 16), axis=0)
            match[:, f * samples : (f + 1) * samples] = as_one(same)
        total = jnp.dot(match[...], g_hi[...], preferred_element_type=F32)
        total = total + jnp.dot(match[...], g_lo[...], preferred_element_type=F32)
        fetched[pl.ds(at, rows_blk), :] = total.astype(BF)
        pltpu.make_async_copy(
            fetched.at[pl.ds(at, rows_blk), :], slot_grad.at[pl.ds(at, rows_blk), :], sems.at[3 + b]
        ).start()
        return carry

    n_out = slot_grad.shape[0] // rows_blk
    lax.fori_loop(0, n_out, scatter, 0)
    for b in range(n_out):
        pltpu.make_async_copy(
            fetched.at[pl.ds(b * rows_blk, rows_blk), :],
            slot_grad.at[pl.ds(b * rows_blk, rows_blk), :],
            sems.at[3 + b],
        ).wait()
    for c in outs:
        c.wait()


def backprop(m, fetched, xh, slots, slots_t, targets, w_flat, w_inter, bias, w_out):
    count, width = fetched.shape
    samples = slots.shape[0] // MB
    hidden = w_flat.shape[1]
    lookups = samples * F_COLD
    wide = FEATS * width
    rows = jax.ShapeDtypeStruct((lookups, width), BF)
    return pl.pallas_call(
        lambda *refs: step_kernel(m, *refs),
        in_specs=[HBM] * 9,
        out_specs=(HBM,) * 3,
        out_shape=(jax.ShapeDtypeStruct((count, width), BF), rows, rows),
        scratch_shapes=[
            pltpu.VMEM((count, width), BF),
            pltpu.VMEM((samples * FEATS, width), BF),
            pltpu.VMEM((samples, F_COLD), jnp.int32),
            pltpu.VMEM((F_COLD, samples), jnp.int32),
            pltpu.VMEM((1, samples), F32),
            pltpu.VMEM(w_flat.shape, BF),
            pltpu.VMEM(w_inter.shape, BF),
            pltpu.VMEM((1, hidden), F32),
            pltpu.VMEM((1, hidden), F32),
            pltpu.VMEM((samples, wide), BF),
            pltpu.VMEM((samples, FEATS * FEATS), BF),
            pltpu.VMEM((FEATS, samples, width), F32),
            pltpu.VMEM((samples, FEATS * FEATS), BF),
            pltpu.VMEM((lookups, width), BF),
            pltpu.VMEM((lookups, width), BF),
            pltpu.VMEM((lookups, width), BF),
            pltpu.VMEM((lookups, width), BF),
            pltpu.VMEM((512, 2048), BF),
            pltpu.VMEM((samples, hidden), BF),
            pltpu.SemaphoreType.DMA((9,)),
        ],
        compiler_params=params(48),
        name="train_step",
    )(fetched, xh, slots, slots_t, targets, w_flat, w_inter, bias, w_out)


def hot_scatter_kernel(at_ref, ids_h, hi0, lo0, hi1, lo1, *refs):
    outs = refs[:N_DP]
    ids, h0, l0, h1, l1, match, res, sems = refs[N_DP:]
    copies = load_all([(ids_h, ids), (hi0, h0), (lo0, l0), (hi1, h1), (lo1, l1)], sems)
    samples = ids.shape[1] // MB
    block = 256
    subs = iota((block, samples), 0).astype(jnp.int16)
    for c in copies:
        c.wait()

    def body(b, carry):
        at = pl.multiple_of(b * block, block)
        total = None
        for m, parts in enumerate(((h0, l0), (h1, l1))):
            for f in range(F_COLD):
                row = ids[f : f + 1, m * samples : (m + 1) * samples] - at
                mine = jnp.broadcast_to(row, (16, samples)).astype(jnp.int16)
                same = subs == jnp.concatenate([mine] * (block // 16), axis=0)
                match[m, :, f * samples : (f + 1) * samples] = as_one(same)
            for part in parts:
                term = jnp.dot(match[m], part[...], preferred_element_type=F32)
                total = term if total is None else total + term
        res[pl.ds(at, block), :] = total
        return carry

    lax.fori_loop(0, res.shape[0] // block, body, 0)
    size = res.shape[0] // N_DP
    done = []
    for k in range(N_DP):
        chunk = (at_ref[0] + k) & (N_DP - 1)
        src = res.at[pl.ds(pl.multiple_of(chunk * size, size), size), :]
        done.append(pltpu.make_async_copy(src, outs[k], sems.at[k]))
        done[-1].start()
    for c in done:
        c.wait()


def hot_scatter(dp_at, ids, hi0, lo0, hi1, lo1, count):
    rows, width = hi0.shape
    return pl.pallas_call(
        hot_scatter_kernel,
        in_specs=[SMEM] + [HBM] * 5,
        out_specs=(HBM,) * N_DP,
        out_shape=(jax.ShapeDtypeStruct((count // N_DP, width), F32),) * N_DP,
        scratch_shapes=[pltpu.VMEM(ids.shape, jnp.int32)]
        + [pltpu.VMEM((rows, width), BF)] * 4
        + [
            pltpu.VMEM((MB, 256, rows), BF),
            pltpu.VMEM((count, width), F32),
            pltpu.SemaphoreType.DMA((N_DP,)),
        ],
        compiler_params=params(32),
        name="hot_scatter",
    )(dp_at, ids, hi0, lo0, hi1, lo1)


def serve_kernel(m, with_hits, wanted, table, rows, *refs):
    if with_hits:
        hits, match, res, count_acc, sems = refs
    else:
        match, res, sems = refs
    shards, lanes = wanted.shape
    capacity = lanes // MB
    count = table.shape[0]
    per = 8
    block = per * capacity
    ids = jnp.concatenate([wanted[...], jnp.zeros((lanes - shards, lanes), jnp.int32)], axis=0)
    turned = ids.T
    names = iota((capacity, count), 1).astype(jnp.int16)
    if with_hits:
        count_acc[...] = jnp.zeros_like(count_acc)

    def ones_of(part, mb, j):
        col = part[mb * capacity : (mb + 1) * capacity, j : j + 1]
        mine = jnp.broadcast_to(col, (capacity, 128)).astype(jnp.int16)
        return as_one(names == jnp.concatenate([mine] * (count // 128), axis=1))

    def add_hits(one):
        tall = one[0:16] + one[16:32] + one[32:48] + one[48:64]
        count_acc[...] += tall

    def body(b, carry):
        part = pltpu.roll(turned, lanes - b * per, 1)
        for j in range(per):
            one = ones_of(part, m, j)
            match[j * capacity : (j + 1) * capacity, :] = one
            if with_hits:
                add_hits(one)
                for other in range(MB):
                    if other != m:
                        add_hits(ones_of(part, other, j))
        at = pl.ds(pl.multiple_of(b * block, block), block)
        res[at, :] = jnp.dot(match[...], table[...], preferred_element_type=F32).astype(BF)
        pltpu.make_async_copy(res.at[at, :], rows.at[at, :], sems.at[b]).start()
        return carry

    steps = shards // per
    lax.fori_loop(0, steps, body, 0)
    if with_hits:
        hits[...] = jnp.sum(count_acc[...].astype(F32), axis=0, keepdims=True)
    for b in range(steps):
        at = pl.ds(b * block, block)
        pltpu.make_async_copy(res.at[at, :], rows.at[at, :], sems.at[b]).wait()


def serve(m, with_hits, wanted, table):
    shards, lanes = wanted.shape
    capacity = lanes // MB
    slots = shards * capacity
    count, width = table.shape
    rows = jax.ShapeDtypeStruct((slots, width), BF)
    extra = [pltpu.VMEM((16, count), BF)] if with_hits else []
    return pl.pallas_call(
        lambda *refs: serve_kernel(m, with_hits, *refs),
        in_specs=[VMEM, VMEM],
        out_specs=(HBM, VMEM) if with_hits else HBM,
        out_shape=(rows, jax.ShapeDtypeStruct((1, count), F32)) if with_hits else rows,
        scratch_shapes=[pltpu.VMEM((512, count), BF), pltpu.VMEM((slots, width), BF)]
        + extra
        + [pltpu.SemaphoreType.DMA((shards // 8,))],
        compiler_params=params(24),
        name="serve_rows",
    )(wanted, table)


def id_tiles(wanted, m):
    ids = wanted[...]
    other = pltpu.roll(ids, 64, 1)
    left, right = (ids, other) if m == 0 else (other, ids)
    low = iota((1, 128), 1) < 64
    return [
        jnp.where(low, left[2 * i : 2 * i + 1], right[2 * i + 1 : 2 * i + 2])
        for i in range(ids.shape[0] // 2)
    ]


def owner_match(tiles, base, match, subs):
    size = match.shape[0]
    for i, tile in enumerate(tiles):
        mine = jnp.broadcast_to(tile - base, (16, 128)).astype(jnp.int16)
        same = subs == jnp.concatenate([mine] * (size // 16), axis=0)
        match[:, i * 128 : (i + 1) * 128] = as_one(same)


def owner_first_kernel(wanted, grads_h, out, grads, match, res, sems):
    load = pltpu.make_async_copy(grads_h, grads, sems.at[0])
    load.start()
    block = match.shape[0]
    tiles = id_tiles(wanted, 0)
    subs = iota((block, 128), 0).astype(jnp.int16)
    load.wait()

    def body(b, carry):
        at = pl.multiple_of(b * block, block)
        owner_match(tiles, at, match, subs)
        res[pl.ds(at, block), :] = jnp.dot(match[...], grads[...], preferred_element_type=F32)
        return carry

    lax.fori_loop(0, res.shape[0] // block, body, 0)
    done = pltpu.make_async_copy(res, out, sems.at[1])
    done.start()
    done.wait()


def owner_first(wanted, grads, count):
    slots, width = grads.shape
    return pl.pallas_call(
        owner_first_kernel,
        in_specs=[VMEM, HBM],
        out_specs=HBM,
        out_shape=jax.ShapeDtypeStruct((count, width), F32),
        scratch_shapes=[
            pltpu.VMEM((slots, width), BF),
            pltpu.VMEM((512, slots), BF),
            pltpu.VMEM((count, width), F32),
            pltpu.SemaphoreType.DMA((2,)),
        ],
        compiler_params=params(24),
        name="owner_first",
    )(wanted, grads)


def owner_second_kernel(at_ref, wanted, hits, grads_h, prev_h, *refs):
    outs = refs[:N_DP]
    grads, prev, match, res, sems = refs[N_DP:]
    size = match.shape[0]
    load = pltpu.make_async_copy(grads_h, grads, sems.at[0])
    load.start()
    load_prev = pltpu.make_async_copy(prev_h, prev, sems.at[1])
    load_prev.start()
    tiles = id_tiles(wanted, 1)
    subs = iota((size, 128), 0).astype(jnp.int16)
    for k in range(N_DP):
        chunk = (at_ref[0] + k) & (N_DP - 1)
        at = pl.multiple_of(chunk * size, size)
        owner_match(tiles, at, match, subs)
        if k == 0:
            load.wait()
        total = jnp.dot(match[...], grads[...], preferred_element_type=F32)
        if k == 0:
            load_prev.wait()
        total = total + prev[pl.ds(at, size), :]
        res[k, :size, :] = total.astype(BF)
        mine = hits[pl.ds(chunk, 1), :]
        res[k, size:, :] = jnp.broadcast_to(mine, (16, size)).astype(BF)
        pltpu.make_async_copy(res.at[k], outs[k], sems.at[2 + k]).start()
    for k in range(N_DP):
        pltpu.make_async_copy(res.at[k], outs[k], sems.at[2 + k]).wait()


def owner_second(dp_at, wanted, hits, grads, prev):
    slots, width = grads.shape
    count = prev.shape[0]
    size = count // N_DP
    return pl.pallas_call(
        owner_second_kernel,
        in_specs=[SMEM, VMEM, VMEM, HBM, HBM],
        out_specs=(HBM,) * N_DP,
        out_shape=(jax.ShapeDtypeStruct((size + 16, width), BF),) * N_DP,
        scratch_shapes=[
            pltpu.VMEM((slots, width), BF),
            pltpu.VMEM((count, width), F32),
            pltpu.VMEM((size, slots), BF),
            pltpu.VMEM((N_DP, size + 16, width), BF),
            pltpu.SemaphoreType.DMA((2 + N_DP,)),
        ],
        compiler_params=params(24),
        name="owner_second",
    )(dp_at, wanted, hits, grads, prev)


def to_col(row, eye):
    return jnp.sum(jnp.where(eye, row, 0.0), axis=1, keepdims=True)


def to_row(col, eye):
    return jnp.sum(jnp.where(eye, col, 0.0), axis=0, keepdims=True)


def adagrad(table, accum, grad):
    accum_new = accum + jnp.mean(grad * grad, axis=-1, keepdims=True)
    return table - learn_rate * grad / jnp.sqrt(accum_new), accum_new


def cold_update_kernel(at_ref, table_h, accum_h, bits_h, *refs):
    parts_h = refs[:N_DP]
    out = refs[N_DP]
    parts, table, accum, bits, res, sems = refs[N_DP + 1 :]
    size = table.shape[0]
    at = pl.multiple_of(at_ref[0] * size, size)
    copies = load_all(
        [(parts_h[k], parts.at[k]) for k in range(N_DP)]
        + [
            (table_h.at[pl.ds(at, size), :], table),
            (accum_h, accum),
            (bits_h.at[pl.ds(at, size), :], bits),
        ],
        sems,
    )
    eye = iota((size, size), 0) == iota((size, size), 1)
    for c in copies:
        c.wait()
    total = parts[0].astype(F32)
    for k in range(1, N_DP):
        total = total + parts[k].astype(F32)
    touched = to_col(total[size : size + 1], eye)
    averaged = total[:size] / jnp.maximum(touched, 1.0)
    old = to_col(accum[pl.ds(at_ref[0], 1), :], eye)
    updated, accum_new = adagrad(table[...].astype(F32), old, averaged)
    grid_step = jnp.max(jnp.abs(updated), axis=-1, keepdims=True) / 8.0
    dither = bits[...].astype(F32) * (1.0 / 65280.0) - 0.5
    res[:size, :] = jnp.where(touched > 0.5, updated + grid_step * dither, updated).astype(BF)
    row = to_row(accum_new, eye)
    high = row.astype(BF).astype(F32)
    middle = (row - high).astype(BF).astype(F32)
    low = (row - high) - middle
    which = iota((16, size), 0)
    packed = jnp.where(which == 0, high, jnp.where(which == 1, middle, low))
    res[size:, :] = packed.astype(BF)
    done = pltpu.make_async_copy(res, out, sems.at[0])
    done.start()
    done.wait()


def cold_update(dp_at, table, accum, bits, parts):
    width = table.shape[1]
    size = table.shape[0] // N_DP
    packed = parts[0].shape
    return pl.pallas_call(
        cold_update_kernel,
        in_specs=[SMEM] + [HBM] * (3 + N_DP),
        out_specs=HBM,
        out_shape=jax.ShapeDtypeStruct(packed, BF),
        scratch_shapes=[
            pltpu.VMEM((N_DP,) + packed, BF),
            pltpu.VMEM((size, width), BF),
            pltpu.VMEM(accum.shape, F32),
            pltpu.VMEM((size, width), jnp.int32),
            pltpu.VMEM(packed, BF),
            pltpu.SemaphoreType.DMA((N_DP + 3,)),
        ],
        compiler_params=params(24),
        name="cold_update",
    )(dp_at, table, accum, bits, *parts)


def cold_join_kernel(at_ref, *refs):
    parts = refs[:N_DP]
    out, accum_out, pieces, sems = refs[N_DP:]
    size = out.shape[0] // N_DP
    copies = []
    for k in range(N_DP):
        chunk = (at_ref[0] - k) & (N_DP - 1)
        dst = out.at[pl.ds(pl.multiple_of(chunk * size, size), size), :]
        copies.append(pltpu.make_async_copy(parts[k].at[pl.ds(0, size), :], dst, sems.at[k]))
        copies.append(
            pltpu.make_async_copy(
                parts[k].at[pl.ds(size, 16), :], pieces.at[chunk], sems.at[N_DP + k]
            )
        )
    for c in copies:
        c.start()
    for c in copies:
        c.wait()
    for p in range(N_DP):
        rows = pieces[p].astype(F32)
        accum_out[p : p + 1, :] = (rows[2:3] + rows[1:2]) + rows[0:1]


def cold_join(dp_at, parts):
    width = parts[0].shape[1]
    size = parts[0].shape[0] - 16
    return pl.pallas_call(
        cold_join_kernel,
        in_specs=[SMEM] + [HBM] * N_DP,
        out_specs=(HBM, VMEM),
        out_shape=(
            jax.ShapeDtypeStruct((N_DP * size, width), BF),
            jax.ShapeDtypeStruct((N_DP, size), F32),
        ),
        scratch_shapes=[
            pltpu.VMEM((N_DP, 16, width), BF),
            pltpu.SemaphoreType.DMA((2 * N_DP,)),
        ],
        compiler_params=params(16),
        name="cold_join",
    )(dp_at, *parts)


def sum_parts_kernel(*refs):
    parts_h = refs[:N_DP]
    out, parts, sems = refs[N_DP:]
    copies = load_all([(parts_h[k], parts.at[k]) for k in range(N_DP)], sems)
    for c in copies:
        c.wait()
    out[...] = jnp.sum(parts[...], axis=0)


def sum_parts(parts):
    shape = parts[0].shape
    return pl.pallas_call(
        sum_parts_kernel,
        in_specs=[HBM] * N_DP,
        out_specs=VMEM,
        out_shape=jax.ShapeDtypeStruct(shape, F32),
        scratch_shapes=[
            pltpu.VMEM((N_DP,) + shape, F32),
            pltpu.SemaphoreType.DMA((N_DP,)),
        ],
        compiler_params=params(16),
        name="sum_parts",
    )(*parts)


def hot_update_kernel(at_ref, table_h, accum_h, *refs):
    grads_h = refs[:N_DP]
    out, accum_out, table, accum, grads, res, sems = refs[N_DP:]
    size = grads.shape[1]
    copies = load_all(
        [(table_h, table), (accum_h, accum)]
        + [(grads_h[k], grads.at[k]) for k in range(N_DP)],
        sems,
    )
    eye = iota((size, size), 0) == iota((size, size), 1)
    for c in copies:
        c.wait()
    for k in range(N_DP):
        chunk = (at_ref[0] - k) & (N_DP - 1)
        rows = pl.ds(pl.multiple_of(chunk * size, size), size)
        old = to_col(accum[pl.ds(chunk, 1), :], eye)
        updated, accum_new = adagrad(table[rows, :], old, grads[k])
        res[rows, :] = updated
        accum_out[pl.ds(chunk, 1), :] = to_row(accum_new, eye)
    done = pltpu.make_async_copy(res, out, sems.at[0])
    done.start()
    done.wait()


def hot_update(dp_at, table, accum, grads):
    count, width = table.shape
    size = count // N_DP
    return pl.pallas_call(
        hot_update_kernel,
        in_specs=[SMEM] + [HBM] * (2 + N_DP),
        out_specs=(HBM, VMEM),
        out_shape=(
            jax.ShapeDtypeStruct((count, width), F32),
            jax.ShapeDtypeStruct((N_DP, size), F32),
        ),
        scratch_shapes=[
            pltpu.VMEM((count, width), F32),
            pltpu.VMEM((N_DP, size), F32),
            pltpu.VMEM((N_DP, size, width), F32),
            pltpu.VMEM((count, width), F32),
            pltpu.SemaphoreType.DMA((2 + N_DP,)),
        ],
        compiler_params=params(24),
        name="hot_update",
    )(dp_at, table, accum, *grads)


def exchange(value, axis):
    return lax.all_to_all(value, axis, split_axis=0, concat_axis=0, tiled=True)


def shift(value, k):
    return lax.ppermute(value, "dp", [(i, (i + k) % N_DP) for i in range(N_DP)])


def to_owners(parts):
    return [parts[0]] + [shift(parts[k], k) for k in range(1, N_DP)]


def to_all(part):
    return [part] + [shift(part, k) for k in range(1, N_DP)]


def step(
    cold_table,
    cold_accum,
    dither_bits,
    hot_table,
    hot_accum,
    w_flat,
    w_inter,
    hidden_bias,
    w_out,
    targets,
    hot_ids,
    cold_slots,
    requests,
    counts,
):
    shards = lax.axis_size("shard")
    capacity = requests.shape[1]
    row_count, row_width = cold_table.shape
    hot_count = hot_table.shape[0]
    slots = shards * capacity
    dp_at = lax.axis_index("dp").astype(jnp.int32).reshape(1)

    live = jnp.arange(capacity, dtype=jnp.int32) < counts[:, :, None]
    asked = jnp.where(live, requests.reshape(MB, shards, capacity), -1)
    asked = asked.transpose(1, 0, 2).reshape(shards, MB * capacity)
    wanted = exchange(asked, "shard")

    fetched = []
    for m in range(MB):
        rows = serve(m, m == 1, wanted, cold_table)
        if m == 1:
            rows, hits = rows
        rows = exchange(rows.reshape(shards, capacity, row_width), "shard")
        fetched.append(rows.reshape(slots, row_width))
    xh = hot_rows(hot_ids, hot_table)

    owned = []
    hot_parts = []
    for m in range(MB):
        slot_grad, *hot_part = backprop(
            m,
            fetched[m],
            xh,
            cold_slots,
            cold_slots.T,
            targets.reshape(1, -1),
            w_flat,
            w_inter,
            hidden_bias.reshape(1, -1),
            w_out.reshape(1, -1),
        )
        hot_parts += hot_part
        rows = exchange(slot_grad.reshape(shards, capacity, row_width), "shard")
        owned.append(rows.reshape(slots, row_width))

    hot_grads = hot_scatter(dp_at, hot_ids.T, *hot_parts, hot_count)
    hot_grads = to_owners(hot_grads)
    hot_sum = sum_parts(hot_grads)
    hot_size = hot_sum.shape[0]
    hot_sum = exchange(hot_sum.reshape(shards, hot_size // shards, row_width), "shard")
    hot_sum = jnp.sum(hot_sum, axis=0)
    hot_all = exchange(jnp.broadcast_to(hot_sum[None], (shards,) + hot_sum.shape), "shard")
    hot_all = to_all(hot_all.reshape(hot_size, row_width))
    hot_out, hot_accum_out = hot_update(
        dp_at, hot_table, hot_accum.reshape(N_DP, -1), hot_all
    )

    first = owner_first(wanted, owned[0], row_count)
    parts = owner_second(dp_at, wanted, hits.reshape(N_DP, -1), owned[1], first)
    parts = to_owners(parts)
    packed = cold_update(
        dp_at, cold_table, cold_accum.reshape(N_DP, -1), dither_bits, parts
    )
    parts = to_all(packed)
    cold_out, cold_accum_out = cold_join(dp_at, parts)
    return (cold_out, cold_accum_out.reshape(-1), hot_out, hot_accum_out.reshape(-1))


def solution(mesh):
    return jax.shard_map(
        step,
        mesh=mesh,
        in_specs=(
            P("shard", None),
            P("shard"),
            P("shard", None),
            P(),
            P(),
            P(),
            P(),
            P(),
            P(),
            P(("shard", "dp")),
            P(("shard", "dp"), None),
            P(("shard", "dp"), None),
            P(("shard", "dp"), None),
            P(("shard", "dp"), None),
        ),
        out_specs=(P("shard", None), P("shard"), P(), P()),
        check_vma=False,
    )
```

time: 702 us -> 259 us (0.37)
  waiting for transfers between devices: 329 us -> 48.3 us
  other arithmetic: 133 us -> 2.47 us
  Pallas kernels: 0 us -> 75.9 us
  local copies, waits for them, and re-layouts: 92.7 us -> 24.7 us
  matrix products: 30.5 us -> 0 us
  starting transfers between devices: 61.1 us -> 84.1 us
  between operations: 16.2 us -> 1.05 us
  blocking collectives: 32.5 us -> 20.1 us
    psum x2 -> x0, waiting for transfers between devices: 312 us -> none  [the longest x1 247 us: on_device(): total_hot = lax.psum(hot_grad, ('shard', 'dp'))]
    scatter-add x8 -> x0, other arithmetic: 100 us -> none  [the longest x2 27.1 us: on_device(): jax.ops.segment_sum(gradients[:, :cold_feats].reshape(-1, row_width), slo...]
    pallas_call x0 -> x12, Pallas kernels: none -> 75.9 us  [the longest x2 39.8 us: backprop(): pl.pallas_call(lambda *refs: step_kernel(m, *refs), in_specs=[HBM] * 9, o...]
    gather x6 -> x0, local copies, waits for them, and re-layouts: 54.7 us -> none  [the longest x2 18.9 us: on_device(): cold_table[requested]]
    ppermute x0 -> x28, starting transfers between devices: none -> 36.5 us  [shift(): return lax.ppermute(value, 'dp', [(i, (i + k) % N_DP) for i in range(N_DP)])]
    dot_general x12 -> x0, matrix products: 30.5 us -> none  [the longest x2 8.74 us: backprop(): jnp.einsum('sfe,sge->sfg', stacked, stacked, preferred_element_type=jnp.f...]
    ppermute x0 -> x28, waiting for transfers between devices: none -> 22.8 us  [shift(): return lax.ppermute(value, 'dp', [(i, (i + k) % N_DP) for i in range(N_DP)])]
    convert_element_type x12 -> x0, other arithmetic: 13.8 us -> none  [the longest x2 5.35 us: on_device(): slot_grad.astype(jnp.bfloat16)]
  transfers between devices with their start and end apart: 9 -> 34, of which waited for: 3 -> 14; matrix products, arithmetic and copies ran while one was open for 33% -> 2% of each run, Pallas kernels for 0% -> 28%
where the time goes in v2:
time: 259 us; the launch traced here: 257 us
  starting transfers between devices  84.1 us (32%)
  Pallas kernels  75.9 us (29%)
  waiting for transfers between devices  48.3 us (19%)
  local copies, waits for them, and re-layouts  24.7 us (10%)
  blocking collectives  20.1 us (8%)
    all_to_all x6, starting transfers between devices, exchange(): return lax.all_to_all(value, axis, split_axis=0, concat_axis=0, tiled=True)  47.7 us
    pallas_call x2, Pallas kernels, backprop(): pl.pallas_call(lambda *refs: step_kernel(m, *refs), in_specs=[HBM] * 9, o...  39.8 us
    ppermute x28, starting transfers between devices, shift(): return lax.ppermute(value, 'dp', [(i, (i + k) % N_DP) for i in range(N_DP)])  36.5 us
    all_to_all x6, waiting for transfers between devices, exchange(): return lax.all_to_all(value, axis, split_axis=0, concat_axis=0, tiled=True)  25.5 us
    ppermute x28, waiting for transfers between devices, shift(): return lax.ppermute(value, 'dp', [(i, (i + k) % N_DP) for i in range(N_DP)])  22.8 us
    unnamed x62, local copies, waits for them, and re-layouts  22.7 us
    all_to_all x1, blocking collectives, exchange(): return lax.all_to_all(value, axis, split_axis=0, concat_axis=0, tiled=True)  20.1 us
    pallas_call x2, Pallas kernels, serve(): pl.pallas_call(lambda *refs: serve_kernel(m, with_hits, *refs), in_specs=...  7.86 us
  transfers between devices with their start and end apart: 34, of which 14 were waited for; matrix products, arithmetic and copies ran while one was open for 2% of the time, Pallas kernels for 28%

profile of v2, /device:TPU:8, one launch (start us, length us, event | category | flops | bytes accessed | tf_op | source)
XLA Modules:
  0.0 256.6 jit_solution(17382269564105005321)
XLA Ops:
  2.4 20.1 %all_to_all.41 = s32[32,1,128]{2,1,0:T(1,128)S(1)} all-to-all(s32[32,1,128]{2,1,0:T(1,128)S(1)} %all_to_all.25), channel_id=1, replica_groups=mesh['shard'=32,'dp'=8] {'shard'}, dimensions={0} | all-to-all | bytes 32768 | tf_op jit(solution)/shard_map/all_to_all | solution.py:726
  22.4 1.2 copy-done.1
  23.6 4.1 %serve_rows.3 = bf16[2048,256]{1,0:T(8,128)(2,1)} custom-call(s32[32,128]{1,0:T(8,128)S(1)} %bitcast.29, bf16[2048,256]{1,0:T(8,128)(2,1)S(1)} %copy-done.1), custom_call_target="tpu_custom_call" | custom-call | tf_op jit(solution)/shard_map/serve_rows/pallas_call | solution.py:416
  27.7 5.0 %all-to-all-start.3 = ((bf16[32,64,256]{2,1,0:T(8,128)(2,1)}), bf16[32,64,256]{2,1,0:T(8,128)(2,1)S(1)}, u32[]{:S(2)}, u32[]{:S(2)}) async-start(bf16[32,64,256]{2,1,0:T(8,128)(2,1)} %bitcast.12), calls=%async_computation.3 | async-start | bytes 2097152 | tf_op jit(solution)/shard_map/all_to_all | solution.py:726
  32.8 3.8 %serve_rows.2 = (bf16[2048,256]{1,0:T(8,128)(2,1)S(1)}, f32[1,2048]{1,0:T(1,128)S(1)}) custom-call(s32[32,128]{1,0:T(8,128)S(1)} %bitcast.30, bf16[2048,256]{1,0:T(8,128)(2,1)S(1)} %copy-done.2), custom_call_target="tpu_custom_call" | custom-call | tf_op jit(solution)/shard_map/serve_rows/pallas_call | solution.py:416
  36.6 1.0 copy-done.17
  37.6 22.2 %all-to-all-done.3 = bf16[32,64,256]{2,1,0:T(8,128)(2,1)S(1)} async-done(((bf16[32,64,256]{2,1,0:T(8,128)(2,1)}), bf16[32,64,256]{2,1,0:T(8,128)(2,1)S(1)}, u32[]{:S(2)}, u32[]{:S(2)}) %all-to-all-start.3) | async-done | bytes 1048608 | tf_op jit(solution)/shard_map/all_to_all | solution.py:726
  59.8 5.6 %all-to-all-start.1 = ((bf16[32,64,256]{2,1,0:T(8,128)(2,1)}), bf16[32,64,256]{2,1,0:T(8,128)(2,1)S(1)}, u32[]{:S(2)}, u32[]{:S(2)}) async-start(bf16[32,64,256]{2,1,0:T(8,128)(2,1)} %bitcast.27), calls=%async_computation.1 | async-start | bytes 2097152 | tf_op jit(solution)/shard_map/all_to_all | solution.py:726
  66.4 1.2 copy-done.3
  67.6 0.9 copy-done.19
  68.6 4.2 %hot_rows.1.refs_1_ = bf16[4096,256]{1,0:T(8,128)(2,1)S(1)} custom-call(s32[512,8]{1,0:T(8,128)S(1)} %copy-done.19, f32[1024,256]{1,0:T(8,128)S(1)} %copy-done.3), custom_call_target="tpu_custom_call" | custom-call | tf_op jit(solution)/shard_map/hot_rows/pallas_call | solution.py:77
  72.8 1.3 copy-done
  74.2 19.9 %train_step.3 = (bf16[2048,256]{1,0:T(8,128)(2,1)S(1)}, bf16[2048,256]{1,0:T(8,128)(2,1)S(1)}, bf16[2048,256]{1,0:T(8,128)(2,1)S(1)}) custom-call(bf16[2048,256]{1,0:T(8,128)(2,1)S(1)} %bitcast.24, bf16[4096,256]{1,0:T(8,128)(2,1)} %copy-done, s32[512,8]{1,0:T(8,128)S(1)} %copy.26.refs_2_, s32[8,512]{1,0:T(8,128)S(1)} %bitcast.33, f32[1,512]{1,0:T(1,128)S(1)} %bitcast.37, ...), custom_call_target="tpu_custom_call" | custom-call | tf_op jit(solution)/shard_map/train_step/pallas_call | solution.py:272
  94.1 1.0 copy-done.6
  95.1 1.0 copy-done.8
  96.0 1.0 copy-done.18
  97.0 9.8 %all-to-all-start.4 = ((bf16[32,64,256]{2,1,0:T(8,128)(2,1)}), bf16[32,64,256]{2,1,0:T(8,128)(2,1)S(1)}, u32[]{:S(2)}, u32[]{:S(2)}) async-start(bf16[32,64,256]{2,1,0:T(8,128)(2,1)} %bitcast.28), calls=%async_computation.4 | async-start | bytes 2097152 | tf_op jit(solution)/shard_map/all_to_all | solution.py:726
  107.7 19.9 %train_step.2 = (bf16[2048,256]{1,0:T(8,128)(2,1)S(1)}, bf16[2048,256]{1,0:T(8,128)(2,1)S(1)}, bf16[2048,256]{1,0:T(8,128)(2,1)S(1)}) custom-call(bf16[2048,256]{1,0:T(8,128)(2,1)S(1)} %bitcast.23, bf16[4096,256]{1,0:T(8,128)(2,1)} %copy-done, s32[512,8]{1,0:T(8,128)S(1)} %copy.26.refs_2_, s32[8,512]{1,0:T(8,128)S(1)} %bitcast.34, f32[1,512]{1,0:T(1,128)S(1)} %bitcast.38, ...), custom_call_target="tpu_custom_call" | custom-call | tf_op jit(solution)/shard_map/train_step/pallas_call | solution.py:272
  127.6 1.0 copy-done.10
  128.7 1.0 copy-done.12
  129.7 1.0 copy-done.16
  130.6 2.1 all-to-all-done.4
  132.7 7.7 %all-to-all-start.2 = ((bf16[32,64,256]{2,1,0:T(8,128)(2,1)}), bf16[32,64,256]{2,1,0:T(8,128)(2,1)S(1)}, u32[]{:S(2)}, u32[]{:S(2)}) async-start(bf16[32,64,256]{2,1,0:T(8,128)(2,1)} %bitcast.26), calls=%async_computation.2 | async-start | bytes 2097152 | tf_op jit(solution)/shard_map/all_to_all | solution.py:726
  140.4 1.2 copy-done.7
  141.6 1.2 copy-done.9
  142.9 1.2 copy-done.11
  144.1 1.2 copy-done.13
  145.3 6.8 %hot_scatter.1 = (f32[128,256]{1,0:T(8,128)S(1)}, f32[128,256]{1,0:T(8,128)S(1)}, f32[128,256]{1,0:T(8,128)S(1)}, f32[128,256]{1,0:T(8,128)S(1)}, f32[128,256]{1...) custom-call(s32[1]{0:T(128)} %bitcast.at_ref, s32[8,512]{1,0:T(8,128)S(1)} %bitcast.35, ...), custom_call_target="tpu_custom_call" | custom-call | tf_op jit(solution)/shard_map/hot_scatter/pallas_call | solution.py:343
  152.1 1.6 collective-permute-start.15
  153.7 2.0 collective-permute-start.16
  155.7 2.0 collective-permute-start.17
  157.7 1.6 collective-permute-start.18
  159.4 1.4 collective-permute-start.19
  160.8 1.7 collective-permute-start.20
  162.5 2.5 collective-permute-done.16.refs_3_
  165.0 1.3 collective-permute-done.17.refs_4_
  166.4 1.4 collective-permute-done.19.refs_6_
  168.2 1.4 sum_parts.1
  170.3 9.8 %all-to-all-start.5 = ((f32[32,4,256]{2,1,0:T(4,128)}), f32[32,4,256]{2,1,0:T(4,128)}, u32[]{:S(2)}, u32[]{:S(2)}) async-start(f32[32,4,256]{2,1,0:T(4,128)} %reshape.94), calls=%async_computation.5 | async-start | bytes 262144 | tf_op jit(solution)/shard_map/all_to_all | solution.py:726
  181.4 3.2 %owner_first.1.prev_h = f32[2048,256]{1,0:T(8,128)S(1)} custom-call(s32[32,128]{1,0:T(8,128)S(1)} %bitcast.31, bf16[2048,256]{1,0:T(8,128)(2,1)S(1)} %bitcast.22), custom_call_target="tpu_custom_call" | custom-call | tf_op jit(solution)/shard_map/owner_first/pallas_call | solution.py:470
  184.6 5.7 %owner_second.1 = (bf16[272,256]{1,0:T(8,128)(2,1)S(1)}, bf16[272,256]{1,0:T(8,128)(2,1)S(1)}, bf16[272,256]{1,0:T(8,128)(2,1)}, bf16[272,256]{1,0:T(8,128)(2,1)...) custom-call(s32[1]{0:T(128)} %bitcast.at_ref, ...), custom_call_target="tpu_custom_call" | custom-call | tf_op jit(solution)/shard_map/owner_second/pallas_call | solution.py:518
  191.9 0.9 reduce_sum.9
  193.5 9.8 %all-to-all-start.6 = ((f32[32,4,256]{2,1,0:T(4,128)}), f32[32,4,256]{2,1,0:T(4,128)S(1)}, u32[]{:S(2)}, u32[]{:S(2)}) async-start(f32[32,4,256]{2,1,0:T(4,128)} %broadcast_in_dim.7), calls=%async_computation.6 | async-start | bytes 262144 | tf_op jit(solution)/shard_map/all_to_all | solution.py:726
  203.3 1.8 collective-permute-start.1
  205.1 2.4 collective-permute-start.3
  207.5 3.0 %collective-permute-start.4 = (bf16[272,256]{1,0:T(8,128)(2,1)}, bf16[272,256]{1,0:T(8,128)(2,1)S(1)}, u32[]{:S(2)}, u32[]{:S(2)}) collective-permute-start(bf16[272,256]{1,0:T(8,128)(2,1)} %get-tuple-element.41), channel_id=1, source_target_pairs={{0,5},{1,6},{2,7},{3,0},{4,1},{5,2},{6,3},{7,4},{8,13},{9,14},{10,... | collective-permute-start | bytes 417800 | tf_op jit(solution)/shard_map/ppermute | solution.py:730
  211.3 1.1 all-to-all-done.6
  213.2 3.8 %collective-permute-done.3.refs_4_ = bf16[272,256]{1,0:T(8,128)(2,1)S(1)} collective-permute-done((bf16[272,256]{1,0:T(8,128)(2,1)}, bf16[272,256]{1,0:T(8,128)(2,1)S(1)}, u32[]{:S(2)}, u32[]{:S(2)}) %collective-permute-start.3) | collective-permute-done | bytes 139296 | tf_op jit(solution)/shard_map/ppermute | solution.py:730
  217.5 1.5 collective-permute-done.5.refs_6_
  219.0 2.4 collective-permute-start.24
  221.5 1.6 copy-done.5
  223.1 2.3 cold_update.1.refs_0_
  225.4 1.2 collective-permute-start.10
  226.6 2.0 collective-permute-start.11
  229.3 2.4 collective-permute-start.26
  232.3 5.7 %collective-permute-done.25.refs_5_ = f32[128,256]{1,0:T(8,128)S(1)} collective-permute-done((f32[128,256]{1,0:T(8,128)S(1)}, f32[128,256]{1,0:T(8,128)S(1)}, u32[]{:S(2)}, u32[]{:S(2)}) %collective-permute-start.25) | collective-permute-done | bytes 131104 | tf_op jit(solution)/shard_map/ppermute | solution.py:730
  238.1 4.6 %collective-permute-start.12 = (bf16[272,256]{1,0:T(8,128)(2,1)S(1)}, bf16[272,256]{1,0:T(8,128)(2,1)S(1)}, u32[]{:S(2)}, u32[]{:S(2)}) collective-permute-start(bf16[272,256]{1,0:T(8,128)(2,1)S(1)} %cold_update.1.refs_0_), channel_id=1, source_target_pairs={{0,6},{1,7},{2,0},{3,1},{4,2},{5,3},{6,4},{7,5},{8,14},{9,15},{10,... | collective-permute-start | bytes 417800 | tf_op jit(solution)/shard_map/ppermute | solution.py:730
  242.6 1.5 collective-permute-start.13
  244.3 1.5 collective-permute-start.9
  245.8 3.6 %hot_update.1 = (f32[1024,256]{1,0:T(8,128)}, f32[8,128]{1,0:T(8,128)}) custom-call(s32[1]{0:T(128)} %bitcast.at_ref, f32[1024,256]{1,0:T(8,128)S(1)} %copy-done.4, f32[8,128]{1,0:T(8,128)S(1)} %bitcast.43, f32[128,256]{1,0:T(8,128)S(1)} %reshape.95.refs_0_, f32[128,256]{1,0:T(8,128)S(1)} %collective-permute-done.21.refs_1_, ...), custom_call_target="tpu_custom_call" | custom-call | tf_op jit(solution)/shard_map/hot_update/pallas_call | solution.py:705
  249.3 1.3 collective-permute-done.7.refs_1_
  250.7 1.3 collective-permute-done.8.refs_2_
  252.0 2.9 %collective-permute-done.9.refs_3_ = bf16[272,256]{1,0:T(8,128)(2,1)S(1)} collective-permute-done((bf16[272,256]{1,0:T(8,128)(2,1)S(1)}, bf16[272,256]{1,0:T(8,128)(2,1)S(1)}, u32[]{:S(2)}, u32[]{:S(2)}) %collective-permute-start.9) | collective-permute-done | bytes 139296 | tf_op jit(solution)/shard_map/ppermute | solution.py:730
  254.9 1.1 cold_join.1
  (89 shorter events, 12.4 us)
Async XLA Ops:
  22.4 1.2 copy-start.1
  23.6 9.2 %copy-start.2 = (bf16[2048,256]{1,0:T(8,128)(2,1)S(1)}, bf16[2048,256]{1,0:T(8,128)(2,1)}, u32[]{:S(2)}) copy-start(bf16[2048,256]{1,0:T(8,128)(2,1)} %table_h.2) | copy-start | bytes 3145732
  27.7 32.0 %all-to-all-start.3 = ((bf16[32,64,256]{2,1,0:T(8,128)(2,1)}), bf16[32,64,256]{2,1,0:T(8,128)(2,1)S(1)}, u32[]{:S(2)}, u32[]{:S(2)}) async-start(bf16[32,64,256]{2,1,0:T(8,128)(2,1)} %bitcast.12), calls=%async_computation.3 | async-start | bytes 2097152 | tf_op jit(solution)/shard_map/all_to_all | solution.py:726
  32.8 32.6 %copy-start.21 = (s32[512,8]{0,1:T(8,128)S(1)}, s32[512,8]{0,1:T(8,128)}, u32[]{:S(2)}) copy-start(s32[512,8]{0,1:T(8,128)} %param.24) | copy-start | bytes 49156
  32.8 33.4 %copy-start.20 = (s32[512,8]{0,1:T(8,128)S(1)}, s32[512,8]{0,1:T(8,128)}, u32[]{:S(2)}) copy-start(s32[512,8]{0,1:T(8,128)} %param.25) | copy-start | bytes 49156
  36.6 1.0 copy-start.17
  59.8 37.2 %all-to-all-start.1 = ((bf16[32,64,256]{2,1,0:T(8,128)(2,1)}), bf16[32,64,256]{2,1,0:T(8,128)(2,1)S(1)}, u32[]{:S(2)}, u32[]{:S(2)}) async-start(bf16[32,64,256]{2,1,0:T(8,128)(2,1)} %bitcast.27), calls=%async_computation.1 | async-start | bytes 2097152 | tf_op jit(solution)/shard_map/all_to_all | solution.py:726
  65.4 8.8 %copy-start.22 = (f32[512]{0:T(512)S(1)}, f32[512]{0:T(512)}, u32[]{:S(2)}) copy-start(f32[512]{0:T(512)} %param.23) | copy-start | bytes 6148
  65.4 8.8 %copy-start.23 = (f32[512]{0:T(512)S(1)}, f32[512]{0:T(512)}, u32[]{:S(2)}) copy-start(f32[512]{0:T(512)} %param.21) | copy-start | bytes 6148
  65.4 8.8 %copy-start.24 = (f32[512]{0:T(512)S(1)}, f32[512]{0:T(512)}, u32[]{:S(2)}) copy-start(f32[512]{0:T(512)} %param.22) | copy-start | bytes 6148
  66.4 1.2 copy-start.3
  67.6 0.9 copy-start.19
  68.6 5.6 %copy-start.14 = (bf16[256,512]{1,0:T(8,128)(2,1)S(1)}, bf16[256,512]{1,0:T(8,128)(2,1)}, u32[]{:S(2)}) copy-start(bf16[256,512]{1,0:T(8,128)(2,1)} %refs_6_.3) | copy-start | bytes 786436
  72.8 1.3 copy-start
  94.1 1.0 copy-start.6
  95.1 1.0 copy-start.8
  96.0 1.0 copy-start.18
  97.0 35.7 %all-to-all-start.4 = ((bf16[32,64,256]{2,1,0:T(8,128)(2,1)}), bf16[32,64,256]{2,1,0:T(8,128)(2,1)S(1)}, u32[]{:S(2)}, u32[]{:S(2)}) async-start(bf16[32,64,256]{2,1,0:T(8,128)(2,1)} %bitcast.28), calls=%async_computation.4 | async-start | bytes 2097152 | tf_op jit(solution)/shard_map/all_to_all | solution.py:726
  106.8 1.0 copy-start.15
  127.6 1.0 copy-start.10
  128.6 1.0 copy-start.12
  129.7 1.0 copy-start.16
  132.7 37.6 %all-to-all-start.2 = ((bf16[32,64,256]{2,1,0:T(8,128)(2,1)}), bf16[32,64,256]{2,1,0:T(8,128)(2,1)S(1)}, u32[]{:S(2)}, u32[]{:S(2)}) async-start(bf16[32,64,256]{2,1,0:T(8,128)(2,1)} %bitcast.26), calls=%async_computation.2 | async-start | bytes 2097152 | tf_op jit(solution)/shard_map/all_to_all | solution.py:726
  140.4 1.2 copy-start.7
  141.6 1.2 copy-start.9
  142.9 1.2 copy-start.11
  144.1 1.2 copy-start.13
  152.1 7.3 %collective-permute-start.14 = (f32[128,256]{1,0:T(8,128)S(1)}, f32[128,256]{1,0:T(8,128)S(1)}, u32[]{:S(2)}, u32[]{:S(2)}) collective-permute-start(f32[128,256]{1,0:T(8,128)S(1)} %get-tuple-element.51), channel_id=1, source_target_pairs={{0,1},{1,2},{2,3},{3,4},{4,5},{5,6},{6,7},{7,0},{8,9},{9,10},{10,1... | collective-permute-start | bytes 393224 | tf_op jit(solution)/shard_map/ppermute | solution.py:730
  152.1 8.7 %collective-permute-start.15 = (f32[128,256]{1,0:T(8,128)S(1)}, f32[128,256]{1,0:T(8,128)S(1)}, u32[]{:S(2)}, u32[]{:S(2)}) collective-permute-start(f32[128,256]{1,0:T(8,128)S(1)} %get-tuple-element.52), channel_id=1, source_target_pairs={{0,2},{1,3},{2,4},{3,5},{4,6},{5,7},{6,0},{7,1},{8,10},{9,11},{10,... | collective-permute-start | bytes 393224 | tf_op jit(solution)/shard_map/ppermute | solution.py:730
  153.7 11.4 %collective-permute-start.16 = (f32[128,256]{1,0:T(8,128)S(1)}, f32[128,256]{1,0:T(8,128)S(1)}, u32[]{:S(2)}, u32[]{:S(2)}) collective-permute-start(f32[128,256]{1,0:T(8,128)S(1)} %get-tuple-element.53), channel_id=1, source_target_pairs={{0,3},{1,4},{2,5},{3,6},{4,7},{5,0},{6,1},{7,2},{8,11},{9,12},{10,... | collective-permute-start | bytes 393224 | tf_op jit(solution)/shard_map/ppermute | solution.py:730
  155.7 10.7 %collective-permute-start.17 = (f32[128,256]{1,0:T(8,128)S(1)}, f32[128,256]{1,0:T(8,128)S(1)}, u32[]{:S(2)}, u32[]{:S(2)}) collective-permute-start(f32[128,256]{1,0:T(8,128)S(1)} %get-tuple-element.54), channel_id=1, source_target_pairs={{0,4},{1,5},{2,6},{3,7},{4,0},{5,1},{6,2},{7,3},{8,12},{9,13},{10,... | collective-permute-start | bytes 393224 | tf_op jit(solution)/shard_map/ppermute | solution.py:730
  157.7 8.6 %collective-permute-start.18 = (f32[128,256]{1,0:T(8,128)S(1)}, f32[128,256]{1,0:T(8,128)S(1)}, u32[]{:S(2)}, u32[]{:S(2)}) collective-permute-start(f32[128,256]{1,0:T(8,128)S(1)} %get-tuple-element.55), channel_id=1, source_target_pairs={{0,5},{1,6},{2,7},{3,0},{4,1},{5,2},{6,3},{7,4},{8,13},{9,14},{10,... | collective-permute-start | bytes 393224 | tf_op jit(solution)/shard_map/ppermute | solution.py:730
  159.4 8.4 %collective-permute-start.19 = (f32[128,256]{1,0:T(8,128)S(1)}, f32[128,256]{1,0:T(8,128)S(1)}, u32[]{:S(2)}, u32[]{:S(2)}) collective-permute-start(f32[128,256]{1,0:T(8,128)S(1)} %get-tuple-element.56), channel_id=1, source_target_pairs={{0,6},{1,7},{2,0},{3,1},{4,2},{5,3},{6,4},{7,5},{8,14},{9,15},{10,... | collective-permute-start | bytes 393224 | tf_op jit(solution)/shard_map/ppermute | solution.py:730
  160.8 7.4 %collective-permute-start.20 = (f32[128,256]{1,0:T(8,128)S(1)}, f32[128,256]{1,0:T(8,128)S(1)}, u32[]{:S(2)}, u32[]{:S(2)}) collective-permute-start(f32[128,256]{1,0:T(8,128)S(1)} %get-tuple-element.57), channel_id=1, source_target_pairs={{0,7},{1,0},{2,1},{3,2},{4,3},{5,4},{6,5},{7,6},{8,15},{9,8},{10,9... | collective-permute-start | bytes 393224 | tf_op jit(solution)/shard_map/ppermute | solution.py:730
  170.3 21.5 %all-to-all-start.5 = ((f32[32,4,256]{2,1,0:T(4,128)}), f32[32,4,256]{2,1,0:T(4,128)}, u32[]{:S(2)}, u32[]{:S(2)}) async-start(f32[32,4,256]{2,1,0:T(4,128)} %reshape.94), calls=%async_computation.5 | async-start | bytes 262144 | tf_op jit(solution)/shard_map/all_to_all | solution.py:726
  184.6 36.9 %copy-start.28 = (f32[2048]{0:T(1024)S(1)}, f32[2048]{0:T(1024)}, u32[]{:S(2)}) copy-start(f32[2048]{0:T(1024)} %param.15) | copy-start | bytes 24580
  190.3 0.7 copy-start.26
  190.9 0.7 copy-start.27
  191.6 18.9 %collective-permute-start = (bf16[272,256]{1,0:T(8,128)(2,1)S(1)}, bf16[272,256]{1,0:T(8,128)(2,1)S(1)}, u32[]{:S(2)}, u32[]{:S(2)}) collective-permute-start(bf16[272,256]{1,0:T(8,128)(2,1)S(1)} %get-tuple-element.37), channel_id=1, source_target_pairs={{0,1},{1,2},{2,3},{3,4},{4,5},{5,6},{6,7},{7,0},{8,9},{9,10},{10,1... | collective-permute-start | bytes 417800 | tf_op jit(solution)/shard_map/ppermute | solution.py:730
  193.5 18.9 %all-to-all-start.6 = ((f32[32,4,256]{2,1,0:T(4,128)}), f32[32,4,256]{2,1,0:T(4,128)S(1)}, u32[]{:S(2)}, u32[]{:S(2)}) async-start(f32[32,4,256]{2,1,0:T(4,128)} %broadcast_in_dim.7), calls=%async_computation.6 | async-start | bytes 262144 | tf_op jit(solution)/shard_map/all_to_all | solution.py:726
  203.3 8.0 %collective-permute-start.1 = (bf16[272,256]{1,0:T(8,128)(2,1)}, bf16[272,256]{1,0:T(8,128)(2,1)S(1)}, u32[]{:S(2)}, u32[]{:S(2)}) collective-permute-start(bf16[272,256]{1,0:T(8,128)(2,1)} %get-tuple-element.38), channel_id=1, source_target_pairs={{0,2},{1,3},{2,4},{3,5},{4,6},{5,7},{6,0},{7,1},{8,10},{9,11},{10,... | collective-permute-start | bytes 417800 | tf_op jit(solution)/shard_map/ppermute | solution.py:730
  205.1 7.9 %collective-permute-start.2 = (bf16[272,256]{1,0:T(8,128)(2,1)}, bf16[272,256]{1,0:T(8,128)(2,1)S(1)}, u32[]{:S(2)}, u32[]{:S(2)}) collective-permute-start(bf16[272,256]{1,0:T(8,128)(2,1)} %get-tuple-element.39), channel_id=1, source_target_pairs={{0,3},{1,4},{2,5},{3,6},{4,7},{5,0},{6,1},{7,2},{8,11},{9,12},{10,... | collective-permute-start | bytes 417800 | tf_op jit(solution)/shard_map/ppermute | solution.py:730
  205.1 12.0 %collective-permute-start.3 = (bf16[272,256]{1,0:T(8,128)(2,1)}, bf16[272,256]{1,0:T(8,128)(2,1)S(1)}, u32[]{:S(2)}, u32[]{:S(2)}) collective-permute-start(bf16[272,256]{1,0:T(8,128)(2,1)} %get-tuple-element.40), channel_id=1, source_target_pairs={{0,4},{1,5},{2,6},{3,7},{4,0},{5,1},{6,2},{7,3},{8,12},{9,13},{10,... | collective-permute-start | bytes 417800 | tf_op jit(solution)/shard_map/ppermute | solution.py:730
  207.5 9.6 %collective-permute-start.4 = (bf16[272,256]{1,0:T(8,128)(2,1)}, bf16[272,256]{1,0:T(8,128)(2,1)S(1)}, u32[]{:S(2)}, u32[]{:S(2)}) collective-permute-start(bf16[272,256]{1,0:T(8,128)(2,1)} %get-tuple-element.41), channel_id=1, source_target_pairs={{0,5},{1,6},{2,7},{3,0},{4,1},{5,2},{6,3},{7,4},{8,13},{9,14},{10,... | collective-permute-start | bytes 417800 | tf_op jit(solution)/shard_map/ppermute | solution.py:730
  210.5 8.6 %collective-permute-start.5 = (bf16[272,256]{1,0:T(8,128)(2,1)}, bf16[272,256]{1,0:T(8,128)(2,1)S(1)}, u32[]{:S(2)}, u32[]{:S(2)}) collective-permute-start(bf16[272,256]{1,0:T(8,128)(2,1)} %copy-done.27), channel_id=1, source_target_pairs={{0,6},{1,7},{2,0},{3,1},{4,2},{5,3},{6,4},{7,5},{8,14},{9,15},{10,... | collective-permute-start | bytes 417800 | tf_op jit(solution)/shard_map/ppermute | solution.py:730
  211.3 10.2 %collective-permute-start.6 = (bf16[272,256]{1,0:T(8,128)(2,1)}, bf16[272,256]{1,0:T(8,128)(2,1)S(1)}, u32[]{:S(2)}, u32[]{:S(2)}) collective-permute-start(bf16[272,256]{1,0:T(8,128)(2,1)} %copy-done.26), channel_id=1, source_target_pairs={{0,7},{1,0},{2,1},{3,2},{4,3},{5,4},{6,5},{7,6},{8,15},{9,8},{10,9... | collective-permute-start | bytes 417800 | tf_op jit(solution)/shard_map/ppermute | solution.py:730
  212.9 13.6 %collective-permute-start.21 = (f32[128,256]{1,0:T(8,128)S(1)}, f32[128,256]{1,0:T(8,128)S(1)}, u32[]{:S(2)}, u32[]{:S(2)}) collective-permute-start(f32[128,256]{1,0:T(8,128)S(1)} %reshape.95.refs_0_), channel_id=1, source_target_pairs={{0,1},{1,2},{2,3},{3,4},{4,5},{5,6},{6,7},{7,0},{8,9},{9,10},{10,1... | collective-permute-start | bytes 393224 | tf_op jit(solution)/shard_map/ppermute | solution.py:730
  217.1 11.6 %collective-permute-start.22 = (f32[128,256]{1,0:T(8,128)S(1)}, f32[128,256]{1,0:T(8,128)S(1)}, u32[]{:S(2)}, u32[]{:S(2)}) collective-permute-start(f32[128,256]{1,0:T(8,128)S(1)} %reshape.95.refs_0_), channel_id=1, source_target_pairs={{0,2},{1,3},{2,4},{3,5},{4,6},{5,7},{6,0},{7,1},{8,10},{9,11},{10,... | collective-permute-start | bytes 393224 | tf_op jit(solution)/shard_map/ppermute | solution.py:730
  217.1 12.2 %collective-permute-start.23 = (f32[128,256]{1,0:T(8,128)S(1)}, f32[128,256]{1,0:T(8,128)S(1)}, u32[]{:S(2)}, u32[]{:S(2)}) collective-permute-start(f32[128,256]{1,0:T(8,128)S(1)} %reshape.95.refs_0_), channel_id=1, source_target_pairs={{0,3},{1,4},{2,5},{3,6},{4,7},{5,0},{6,1},{7,2},{8,11},{9,12},{10,... | collective-permute-start | bytes 393224 | tf_op jit(solution)/shard_map/ppermute | solution.py:730
  219.0 12.6 %collective-permute-start.24 = (f32[128,256]{1,0:T(8,128)S(1)}, f32[128,256]{1,0:T(8,128)S(1)}, u32[]{:S(2)}, u32[]{:S(2)}) collective-permute-start(f32[128,256]{1,0:T(8,128)S(1)} %reshape.95.refs_0_), channel_id=1, source_target_pairs={{0,4},{1,5},{2,6},{3,7},{4,0},{5,1},{6,2},{7,3},{8,12},{9,13},{10,... | collective-permute-start | bytes 393224 | tf_op jit(solution)/shard_map/ppermute | solution.py:730
  221.5 1.6 copy-start.5
  223.1 22.7 %copy-start.4 = (f32[1024,256]{1,0:T(8,128)S(1)}, f32[1024,256]{1,0:T(8,128)}, u32[]{:S(2)}) copy-start(f32[1024,256]{1,0:T(8,128)} %table_h.3) | copy-start | bytes 3145732
  223.1 22.7 %copy-start.25 = (f32[1024]{0:T(1024)S(1)}, f32[1024]{0:T(1024)}, u32[]{:S(2)}) copy-start(f32[1024]{0:T(1024)} %param.18) | copy-start | bytes 12292
  225.4 18.8 %collective-permute-start.10 = (bf16[272,256]{1,0:T(8,128)(2,1)S(1)}, bf16[272,256]{1,0:T(8,128)(2,1)S(1)}, u32[]{:S(2)}, u32[]{:S(2)}) collective-permute-start(bf16[272,256]{1,0:T(8,128)(2,1)S(1)} %cold_update.1.refs_0_), channel_id=1, source_target_pairs={{0,4},{1,5},{2,6},{3,7},{4,0},{5,1},{6,2},{7,3},{8,12},{9,13},{10,... | collective-permute-start | bytes 417800 | tf_op jit(solution)/shard_map/ppermute | solution.py:730
  226.6 17.7 %collective-permute-start.11 = (bf16[272,256]{1,0:T(8,128)(2,1)S(1)}, bf16[272,256]{1,0:T(8,128)(2,1)S(1)}, u32[]{:S(2)}, u32[]{:S(2)}) collective-permute-start(bf16[272,256]{1,0:T(8,128)(2,1)S(1)} %cold_update.1.refs_0_), channel_id=1, source_target_pairs={{0,5},{1,6},{2,7},{3,0},{4,1},{5,2},{6,3},{7,4},{8,13},{9,14},{10,... | collective-permute-start | bytes 417800 | tf_op jit(solution)/shard_map/ppermute | solution.py:730
  228.6 9.4 %collective-permute-start.25 = (f32[128,256]{1,0:T(8,128)S(1)}, f32[128,256]{1,0:T(8,128)S(1)}, u32[]{:S(2)}, u32[]{:S(2)}) collective-permute-start(f32[128,256]{1,0:T(8,128)S(1)} %reshape.95.refs_0_), channel_id=1, source_target_pairs={{0,5},{1,6},{2,7},{3,0},{4,1},{5,2},{6,3},{7,4},{8,13},{9,14},{10,... | collective-permute-start | bytes 393224 | tf_op jit(solution)/shard_map/ppermute | solution.py:730
  229.3 13.3 %collective-permute-start.26 = (f32[128,256]{1,0:T(8,128)S(1)}, f32[128,256]{1,0:T(8,128)S(1)}, u32[]{:S(2)}, u32[]{:S(2)}) collective-permute-start(f32[128,256]{1,0:T(8,128)S(1)} %reshape.95.refs_0_), channel_id=1, source_target_pairs={{0,6},{1,7},{2,0},{3,1},{4,2},{5,3},{6,4},{7,5},{8,14},{9,15},{10,... | collective-permute-start | bytes 393224 | tf_op jit(solution)/shard_map/ppermute | solution.py:730
  231.7 12.5 %collective-permute-start.27 = (f32[128,256]{1,0:T(8,128)S(1)}, f32[128,256]{1,0:T(8,128)S(1)}, u32[]{:S(2)}, u32[]{:S(2)}) collective-permute-start(f32[128,256]{1,0:T(8,128)S(1)} %reshape.95.refs_0_), channel_id=1, source_target_pairs={{0,7},{1,0},{2,1},{3,2},{4,3},{5,4},{6,5},{7,6},{8,15},{9,8},{10,9... | collective-permute-start | bytes 393224 | tf_op jit(solution)/shard_map/ppermute | solution.py:730
  238.1 11.2 %collective-permute-start.12 = (bf16[272,256]{1,0:T(8,128)(2,1)S(1)}, bf16[272,256]{1,0:T(8,128)(2,1)S(1)}, u32[]{:S(2)}, u32[]{:S(2)}) collective-permute-start(bf16[272,256]{1,0:T(8,128)(2,1)S(1)} %cold_update.1.refs_0_), channel_id=1, source_target_pairs={{0,6},{1,7},{2,0},{3,1},{4,2},{5,3},{6,4},{7,5},{8,14},{9,15},{10,... | collective-permute-start | bytes 417800 | tf_op jit(solution)/shard_map/ppermute | solution.py:730
  242.6 6.7 %collective-permute-start.13 = (bf16[272,256]{1,0:T(8,128)(2,1)S(1)}, bf16[272,256]{1,0:T(8,128)(2,1)S(1)}, u32[]{:S(2)}, u32[]{:S(2)}) collective-permute-start(bf16[272,256]{1,0:T(8,128)(2,1)S(1)} %cold_update.1.refs_0_), channel_id=1, source_target_pairs={{0,7},{1,0},{2,1},{3,2},{4,3},{5,4},{6,5},{7,6},{8,15},{9,8},{10,9... | collective-permute-start | bytes 417800 | tf_op jit(solution)/shard_map/ppermute | solution.py:730
  244.1 6.5 %collective-permute-start.7 = (bf16[272,256]{1,0:T(8,128)(2,1)S(1)}, bf16[272,256]{1,0:T(8,128)(2,1)S(1)}, u32[]{:S(2)}, u32[]{:S(2)}) collective-permute-start(bf16[272,256]{1,0:T(8,128)(2,1)S(1)} %cold_update.1.refs_0_), channel_id=1, source_target_pairs={{0,1},{1,2},{2,3},{3,4},{4,5},{5,6},{6,7},{7,0},{8,9},{9,10},{10,1... | collective-permute-start | bytes 417800 | tf_op jit(solution)/shard_map/ppermute | solution.py:730
  244.2 7.8 %collective-permute-start.8 = (bf16[272,256]{1,0:T(8,128)(2,1)S(1)}, bf16[272,256]{1,0:T(8,128)(2,1)S(1)}, u32[]{:S(2)}, u32[]{:S(2)}) collective-permute-start(bf16[272,256]{1,0:T(8,128)(2,1)S(1)} %cold_update.1.refs_0_), channel_id=1, source_target_pairs={{0,2},{1,3},{2,4},{3,5},{4,6},{5,7},{6,0},{7,1},{8,10},{9,11},{10,... | collective-permute-start | bytes 417800 | tf_op jit(solution)/shard_map/ppermute | solution.py:730
  244.3 10.6 %collective-permute-start.9 = (bf16[272,256]{1,0:T(8,128)(2,1)S(1)}, bf16[272,256]{1,0:T(8,128)(2,1)S(1)}, u32[]{:S(2)}, u32[]{:S(2)}) collective-permute-start(bf16[272,256]{1,0:T(8,128)(2,1)S(1)} %cold_update.1.refs_0_), channel_id=1, source_target_pairs={{0,3},{1,4},{2,5},{3,6},{4,7},{5,0},{6,1},{7,2},{8,11},{9,12},{10,... | collective-permute-start | bytes 417800 | tf_op jit(solution)/shard_map/ppermute | solution.py:730

commit v3 on v2

--- a/solution.py
+++ b/solution.py
@@ -17,6 +17,7 @@
 VMEM = pl.BlockSpec(memory_space=pltpu.VMEM)
 SMEM = pl.BlockSpec(memory_space=pltpu.SMEM)
 N_DP = 8
+VMEM_LIMIT = (64 << 20) - (64 << 10)
 learn_rate = 0.3
 UNROLL = 4
 
@@ -29,8 +30,8 @@
     return jnp.where(same, jnp.ones(same.shape, BF), jnp.zeros(same.shape, BF))
 
 
-def params(limit_mib):
-    return pltpu.CompilerParams(vmem_limit_bytes=limit_mib << 20)
+def params():
+    return pltpu.CompilerParams(vmem_limit_bytes=VMEM_LIMIT)
 
 
 def load_all(pairs, sems):
@@ -86,7 +87,7 @@
             pltpu.VMEM((rows, width), BF),
             pltpu.SemaphoreType.DMA((3,)),
         ],
-        compiler_params=params(32),
+        compiler_params=params(),
         name="hot_rows",
     )(hot_ids, table)
 
@@ -296,7 +297,7 @@
             pltpu.VMEM((samples, hidden), BF),
             pltpu.SemaphoreType.DMA((9,)),
         ],
-        compiler_params=params(48),
+        compiler_params=params(),
         name="train_step",
     )(fetched, xh, slots, slots_t, targets, w_flat, w_inter, bias, w_out)
 
@@ -352,7 +353,7 @@
             pltpu.VMEM((count, width), F32),
             pltpu.SemaphoreType.DMA((N_DP,)),
         ],
-        compiler_params=params(32),
+        compiler_params=params(),
         name="hot_scatter",
     )(dp_at, ids, hi0, lo0, hi1, lo1)
 
@@ -421,7 +422,7 @@
         scratch_shapes=[pltpu.VMEM((512, count), BF), pltpu.VMEM((slots, width), BF)]
         + extra
         + [pltpu.SemaphoreType.DMA((shards // 8,))],
-        compiler_params=params(24),
+        compiler_params=params(),
         name="serve_rows",
     )(wanted, table)
 
@@ -478,7 +479,7 @@
             pltpu.VMEM((count, width), F32),
             pltpu.SemaphoreType.DMA((2,)),
         ],
-        compiler_params=params(24),
+        compiler_params=params(),
         name="owner_first",
     )(wanted, grads)
 
@@ -493,22 +494,24 @@
     load_prev.start()
     tiles = id_tiles(wanted, 1)
     subs = iota((size, 128), 0).astype(jnp.int16)
-    for k in range(N_DP):
+    load.wait()
+    load_prev.wait()
+
+    def body(k, carry):
         chunk = (at_ref[0] + k) & (N_DP - 1)
         at = pl.multiple_of(chunk * size, size)
         owner_match(tiles, at, match, subs)
-        if k == 0:
-            load.wait()
         total = jnp.dot(match[...], grads[...], preferred_element_type=F32)
-        if k == 0:
-            load_prev.wait()
         total = total + prev[pl.ds(at, size), :]
         res[k, :size, :] = total.astype(BF)
         mine = hits[pl.ds(chunk, 1), :]
         res[k, size:, :] = jnp.broadcast_to(mine, (16, size)).astype(BF)
-        pltpu.make_async_copy(res.at[k], outs[k], sems.at[2 + k]).start()
-    for k in range(N_DP):
-        pltpu.make_async_copy(res.at[k], outs[k], sems.at[2 + k]).wait()
+        return carry
+
+    lax.fori_loop(0, N_DP, body, 0)
+    done = load_all([(res.at[k], outs[k]) for k in range(N_DP)], sems)
+    for c in done:
+        c.wait()
 
 
 def owner_second(dp_at, wanted, hits, grads, prev):
@@ -527,7 +530,7 @@
             pltpu.VMEM((N_DP, size + 16, width), BF),
             pltpu.SemaphoreType.DMA((2 + N_DP,)),
         ],
-        compiler_params=params(24),
+        compiler_params=params(),
         name="owner_second",
     )(dp_at, wanted, hits, grads, prev)
 
@@ -602,7 +605,7 @@
             pltpu.VMEM(packed, BF),
             pltpu.SemaphoreType.DMA((N_DP + 3,)),
         ],
-        compiler_params=params(24),
+        compiler_params=params(),
         name="cold_update",
     )(dp_at, table, accum, bits, *parts)
 
@@ -645,7 +648,7 @@
             pltpu.VMEM((N_DP, 16, width), BF),
             pltpu.SemaphoreType.DMA((2 * N_DP,)),
         ],
-        compiler_params=params(16),
+        compiler_params=params(),
         name="cold_join",
     )(dp_at, *parts)
 
@@ -670,7 +673,7 @@
             pltpu.VMEM((N_DP,) + shape, F32),
             pltpu.SemaphoreType.DMA((N_DP,)),
         ],
-        compiler_params=params(16),
+        compiler_params=params(),
         name="sum_parts",
     )(*parts)
 
@@ -717,7 +720,7 @@
             pltpu.VMEM((count, width), F32),
             pltpu.SemaphoreType.DMA((2 + N_DP,)),
         ],
-        compiler_params=params(24),
+        compiler_params=params(),
         name="hot_update",
     )(dp_at, table, accum, *grads)
 

time: 259 us -> 293 us (1.13)
  Pallas kernels: 75.9 us -> 124 us
  local copies, waits for them, and re-layouts: 24.7 us -> 10.6 us
    pallas_call x1, Pallas kernels: 1.12 us -> 33.6 us  [cold_join(): pl.pallas_call(cold_join_kernel, in_specs=[SMEM] + [HBM] * N_DP, out_spec...]
    unnamed x62 -> x14, local copies, waits for them, and re-layouts: 22.7 us -> 5.1 us
    pallas_call x2, Pallas kernels: 7.86 us -> 11.5 us  [serve(): pl.pallas_call(lambda *refs: serve_kernel(m, with_hits, *refs), in_specs=...]
    pallas_call x1, Pallas kernels: 3.18 us -> 6.16 us  [owner_first(): pl.pallas_call(owner_first_kernel, in_specs=[VMEM, HBM], out_specs=HBM, o...]
    pallas_call x2, Pallas kernels: 39.8 us -> 42.7 us  [backprop(): pl.pallas_call(lambda *refs: step_kernel(m, *refs), in_specs=[HBM] * 9, o...]
  transfers between devices with their start and end apart: 34 -> 34, of which waited for: 14 -> 13; matrix products, arithmetic and copies ran while one was open for 2% -> 3% of each run, Pallas kernels for 28% -> 30%
where the time goes in v3:
time: 293 us; the launch traced here: 290 us
  Pallas kernels  124 us (42%)
  starting transfers between devices  83.1 us (28%)
  waiting for transfers between devices  47.3 us (16%)
  blocking collectives  20.2 us (7%)
  local copies, waits for them, and re-layouts  10.6 us (4%)
  other arithmetic  3.17 us (1%)
    all_to_all x6, starting transfers between devices, exchange(): return lax.all_to_all(value, axis, split_axis=0, concat_axis=0, tiled=True)  46.4 us
    pallas_call x2, Pallas kernels, backprop(): pl.pallas_call(lambda *refs: step_kernel(m, *refs), in_specs=[HBM] * 9, o...  42.7 us
    ppermute x28, starting transfers between devices, shift(): return lax.ppermute(value, 'dp', [(i, (i + k) % N_DP) for i in range(N_DP)])  36.7 us
    pallas_call x1, Pallas kernels, cold_join(): pl.pallas_call(cold_join_kernel, in_specs=[SMEM] + [HBM] * N_DP, out_spec...  33.6 us
    all_to_all x6, waiting for transfers between devices, exchange(): return lax.all_to_all(value, axis, split_axis=0, concat_axis=0, tiled=True)  25.7 us
    ppermute x28, waiting for transfers between devices, shift(): return lax.ppermute(value, 'dp', [(i, (i + k) % N_DP) for i in range(N_DP)])  21.6 us
    all_to_all x1, blocking collectives, exchange(): return lax.all_to_all(value, axis, split_axis=0, concat_axis=0, tiled=True)  20.2 us
    pallas_call x2, Pallas kernels, serve(): pl.pallas_call(lambda *refs: serve_kernel(m, with_hits, *refs), in_specs=...  11.5 us
  transfers between devices with their start and end apart: 34, of which 13 were waited for; matrix products, arithmetic and copies ran while one was open for 3% of the time, Pallas kernels for 30%

profile of v3, /device:TPU:8, one launch (start us, length us, event | category | flops | bytes accessed | tf_op | source)
XLA Modules:
  0.0 289.7 jit_solution(5475587126430568157)
XLA Ops:
  0.6 0.8 copy.23
  1.4 0.9 fusion
  2.4 20.2 %all_to_all.41 = s32[32,1,128]{2,1,0:T(1,128)} all-to-all(s32[32,1,128]{2,1,0:T(1,128)S(1)} %all_to_all.25), channel_id=1, replica_groups=mesh['shard'=32,'dp'=8] {'shard'}, dimensions={0} | all-to-all | bytes 32768 | tf_op jit(solution)/shard_map/all_to_all | solution.py:729
  22.5 5.3 %serve_rows.3 = bf16[2048,256]{1,0:T(8,128)(2,1)} custom-call(s32[32,128]{1,0:T(8,128)} %bitcast.26, bf16[2048,256]{1,0:T(8,128)(2,1)} %table_h.2), custom_call_target="tpu_custom_call" | custom-call | tf_op jit(solution)/shard_map/serve_rows/pallas_call | solution.py:417
  27.9 5.7 %all-to-all-start.3 = ((bf16[32,64,256]{2,1,0:T(8,128)(2,1)}), bf16[32,64,256]{2,1,0:T(8,128)(2,1)}, u32[]{:S(2)}, u32[]{:S(2)}) async-start(bf16[32,64,256]{2,1,0:T(8,128)(2,1)} %bitcast.22), calls=%async_computation.3 | async-start | bytes 2097152 | tf_op jit(solution)/shard_map/all_to_all | solution.py:729
  33.6 6.2 %serve_rows.2 = (bf16[2048,256]{1,0:T(8,128)(2,1)}, f32[1,2048]{1,0:T(1,128)}) custom-call(s32[32,128]{1,0:T(8,128)} %bitcast.27, bf16[2048,256]{1,0:T(8,128)(2,1)} %table_h.2), custom_call_target="tpu_custom_call" | custom-call | tf_op jit(solution)/shard_map/serve_rows/pallas_call | solution.py:417
  39.8 20.7 %all-to-all-done.3 = bf16[32,64,256]{2,1,0:T(8,128)(2,1)} async-done(((bf16[32,64,256]{2,1,0:T(8,128)(2,1)}), bf16[32,64,256]{2,1,0:T(8,128)(2,1)}, u32[]{:S(2)}, u32[]{:S(2)}) %all-to-all-start.3) | async-done | bytes 1048608 | tf_op jit(solution)/shard_map/all_to_all | solution.py:729
  60.5 5.6 %all-to-all-start.1 = ((bf16[32,64,256]{2,1,0:T(8,128)(2,1)}), bf16[32,64,256]{2,1,0:T(8,128)(2,1)}, u32[]{:S(2)}, u32[]{:S(2)}) async-start(bf16[32,64,256]{2,1,0:T(8,128)(2,1)} %bitcast.24), calls=%async_computation.1 | async-start | bytes 2097152 | tf_op jit(solution)/shard_map/all_to_all | solution.py:729
  66.1 0.8 copy.25.hot_ids
  66.9 0.9 copy.26.refs_2_
  67.8 6.6 %hot_rows.1.refs_1_ = bf16[4096,256]{1,0:T(8,128)(2,1)} custom-call(s32[512,8]{1,0:T(8,128)} %copy.25.hot_ids, f32[1024,256]{1,0:T(8,128)} %table_h.3), custom_call_target="tpu_custom_call" | custom-call | tf_op jit(solution)/shard_map/hot_rows/pallas_call | solution.py:78
  74.5 21.4 %train_step.3 = (bf16[2048,256]{1,0:T(8,128)(2,1)}, bf16[2048,256]{1,0:T(8,128)(2,1)}, bf16[2048,256]{1,0:T(8,128)(2,1)}) custom-call(bf16[2048,256]{1,0:T(8,128)(2,1)} %bitcast.13.refs_0_, bf16[4096,256]{1,0:T(8,128)(2,1)} %hot_rows.1.refs_1_, s32[512,8]{1,0:T(8,128)} %copy.26.refs_2_, s32[8,512]{1,0:T(8,128)} %bitcast.30, f32[1,512]{1,0:T(1,128)} %bitcast.36, ...), custom_call_target="tpu_custom_call" | custom-call | tf_op jit(solution)/shard_map/train_step/pallas_call | solution.py:273
  95.9 9.8 %all-to-all-start.4 = ((bf16[32,64,256]{2,1,0:T(8,128)(2,1)}), bf16[32,64,256]{2,1,0:T(8,128)(2,1)}, u32[]{:S(2)}, u32[]{:S(2)}) async-start(bf16[32,64,256]{2,1,0:T(8,128)(2,1)} %bitcast.25), calls=%async_computation.4 | async-start | bytes 2097152 | tf_op jit(solution)/shard_map/all_to_all | solution.py:729
  105.7 21.4 %train_step.2 = (bf16[2048,256]{1,0:T(8,128)(2,1)}, bf16[2048,256]{1,0:T(8,128)(2,1)}, bf16[2048,256]{1,0:T(8,128)(2,1)}) custom-call(bf16[2048,256]{1,0:T(8,128)(2,1)} %bitcast.5.refs_0_, bf16[4096,256]{1,0:T(8,128)(2,1)} %hot_rows.1.refs_1_, s32[512,8]{1,0:T(8,128)} %copy.26.refs_2_, s32[8,512]{1,0:T(8,128)} %bitcast.31, f32[1,512]{1,0:T(1,128)} %bitcast.37, ...), custom_call_target="tpu_custom_call" | custom-call | tf_op jit(solution)/shard_map/train_step/pallas_call | solution.py:273
  127.1 4.6 %all-to-all-done.4 = bf16[32,64,256]{2,1,0:T(8,128)(2,1)} async-done(((bf16[32,64,256]{2,1,0:T(8,128)(2,1)}), bf16[32,64,256]{2,1,0:T(8,128)(2,1)}, u32[]{:S(2)}, u32[]{:S(2)}) %all-to-all-start.4) | async-done | bytes 1048608 | tf_op jit(solution)/shard_map/all_to_all | solution.py:729
  131.7 5.6 %all-to-all-start.2 = ((bf16[32,64,256]{2,1,0:T(8,128)(2,1)}), bf16[32,64,256]{2,1,0:T(8,128)(2,1)}, u32[]{:S(2)}, u32[]{:S(2)}) async-start(bf16[32,64,256]{2,1,0:T(8,128)(2,1)} %bitcast.23), calls=%async_computation.2 | async-start | bytes 2097152 | tf_op jit(solution)/shard_map/all_to_all | solution.py:729
  137.3 8.2 %hot_scatter.1 = (f32[128,256]{1,0:T(8,128)}, f32[128,256]{1,0:T(8,128)}, f32[128,256]{1,0:T(8,128)}, f32[128,256]{1,0:T(8,128)}, f32[128,256]{1,0:T(8,128)}, /*...) custom-call(s32[1]{0:T(128)} %bitcast.at_ref, s32[8,512]{1,0:T(8,128)} %bitcast.32, ...), custom_call_target="tpu_custom_call" | custom-call | tf_op jit(solution)/shard_map/hot_scatter/pallas_call | solution.py:344
  145.6 1.6 collective-permute-start.15
  147.1 2.0 collective-permute-start.16
  149.2 2.0 collective-permute-start.17
  151.2 1.6 collective-permute-start.18
  152.8 1.4 collective-permute-start.19
  154.3 2.0 collective-permute-start.20
  156.3 2.5 collective-permute-done.16.refs_3_
  158.8 1.3 collective-permute-done.17.refs_4_
  160.1 1.4 collective-permute-done.19.refs_6_
  162.0 2.1 sum_parts.1
  164.0 1.6 reshape.94
  165.6 9.8 %all-to-all-start.5 = ((f32[32,4,256]{2,1,0:T(4,128)}), f32[32,4,256]{2,1,0:T(4,128)}, u32[]{:S(2)}, u32[]{:S(2)}) async-start(f32[32,4,256]{2,1,0:T(4,128)} %reshape.94), calls=%async_computation.5 | async-start | bytes 262144 | tf_op jit(solution)/shard_map/all_to_all | solution.py:729
  175.5 0.5 broadcast.5
  176.0 1.4 reduce.3
  177.3 0.6 reshape.80.hits
  177.9 6.2 %owner_first.1.prev_h = f32[2048,256]{1,0:T(8,128)} custom-call(s32[32,128]{1,0:T(8,128)} %bitcast.28, bf16[2048,256]{1,0:T(8,128)(2,1)} %bitcast.15.grads_h), custom_call_target="tpu_custom_call" | custom-call | tf_op jit(solution)/shard_map/owner_first/pallas_call | solution.py:471
  184.1 7.3 %owner_second.1 = (bf16[272,256]{1,0:T(8,128)(2,1)}, bf16[272,256]{1,0:T(8,128)(2,1)}, bf16[272,256]{1,0:T(8,128)(2,1)}, bf16[272,256]{1,0:T(8,128)(2,1)}, bf16[...) custom-call(s32[1]{0:T(128)} %bitcast.at_ref, ...), custom_call_target="tpu_custom_call" | custom-call | tf_op jit(solution)/shard_map/owner_second/pallas_call | solution.py:521
  191.7 0.9 reduce_sum.9
  192.7 0.7 broadcast_in_dim.7
  193.3 9.8 %all-to-all-start.6 = ((f32[32,4,256]{2,1,0:T(4,128)}), f32[32,4,256]{2,1,0:T(4,128)S(1)}, u32[]{:S(2)}, u32[]{:S(2)}) async-start(f32[32,4,256]{2,1,0:T(4,128)} %broadcast_in_dim.7), calls=%async_computation.6 | async-start | bytes 262144 | tf_op jit(solution)/shard_map/all_to_all | solution.py:729
  203.1 1.8 collective-permute-start.1
  204.9 2.5 collective-permute-start.3
  207.3 3.0 %collective-permute-start.4 = (bf16[272,256]{1,0:T(8,128)(2,1)}, bf16[272,256]{1,0:T(8,128)(2,1)}, u32[]{:S(2)}, u32[]{:S(2)}) collective-permute-start(bf16[272,256]{1,0:T(8,128)(2,1)} %get-tuple-element.41), channel_id=1, source_target_pairs={{0,5},{1,6},{2,7},{3,0},{4,1},{5,2},{6,3},{7,4},{8,13},{9,14},{10,... | collective-permute-start | bytes 417800 | tf_op jit(solution)/shard_map/ppermute | solution.py:733
  210.3 0.8 collective-permute-start.5
  211.2 0.7 copy-done.2
  212.3 0.7 reshape.95.refs_0_
  213.0 0.7 copy-done.3
  213.7 3.3 %collective-permute-done.3.refs_4_ = bf16[272,256]{1,0:T(8,128)(2,1)} collective-permute-done((bf16[272,256]{1,0:T(8,128)(2,1)}, bf16[272,256]{1,0:T(8,128)(2,1)}, u32[]{:S(2)}, u32[]{:S(2)}) %collective-permute-start.3) | collective-permute-done | bytes 139296 | tf_op jit(solution)/shard_map/ppermute | solution.py:733
  217.0 0.4 collective-permute-start.23
  217.5 1.5 collective-permute-done.5.refs_6_
  219.0 2.4 collective-permute-start.24
  221.4 1.3 reshape.78.accum_h
  222.7 2.6 cold_update.1.refs_0_
  225.3 1.2 collective-permute-start.10
  226.5 1.9 collective-permute-start.11
  228.7 2.9 %collective-permute-start.26 = (f32[128,256]{1,0:T(8,128)}, f32[128,256]{1,0:T(8,128)}, u32[]{:S(2)}, u32[]{:S(2)}) collective-permute-start(f32[128,256]{1,0:T(8,128)} %reshape.95.refs_0_), channel_id=1, source_target_pairs={{0,6},{1,7},{2,0},{3,1},{4,2},{5,3},{6,4},{7,5},{8,14},{9,15},{10,... | collective-permute-start | bytes 393224 | tf_op jit(solution)/shard_map/ppermute | solution.py:733
  231.6 0.7 collective-permute-start.27
  232.2 5.3 %collective-permute-done.25.refs_5_ = f32[128,256]{1,0:T(8,128)} collective-permute-done((f32[128,256]{1,0:T(8,128)}, f32[128,256]{1,0:T(8,128)}, u32[]{:S(2)}, u32[]{:S(2)}) %collective-permute-start.25) | collective-permute-done | bytes 131104 | tf_op jit(solution)/shard_map/ppermute | solution.py:733
  237.5 4.6 %collective-permute-start.12 = (bf16[272,256]{1,0:T(8,128)(2,1)}, bf16[272,256]{1,0:T(8,128)(2,1)}, u32[]{:S(2)}, u32[]{:S(2)}) collective-permute-start(bf16[272,256]{1,0:T(8,128)(2,1)} %cold_update.1.refs_0_), channel_id=1, source_target_pairs={{0,6},{1,7},{2,0},{3,1},{4,2},{5,3},{6,4},{7,5},{8,14},{9,15},{10,... | collective-permute-start | bytes 417800 | tf_op jit(solution)/shard_map/ppermute | solution.py:733
  242.1 1.9 collective-permute-start.13
  244.1 1.2 collective-permute-start.9
  245.3 3.6 %hot_update.1 = (f32[1024,256]{1,0:T(8,128)}, f32[8,128]{1,0:T(8,128)}) custom-call(s32[1]{0:T(128)} %bitcast.at_ref, f32[1024,256]{1,0:T(8,128)} %table_h.3, f32[8,128]{1,0:T(8,128)} %bitcast.42, f32[128,256]{1,0:T(8,128)} %reshape.95.refs_0_, f32[128,256]{1,0:T(8,128)} %collective-permute-done.21.refs_1_, f32[128,256]{1,0:T(8,128)} %collective-permute-done.22.refs_2_, ...), custom_call_target="tpu_custom_call" | custom-call | tf_op jit(solution)/shard_map/hot_update/pallas_call | solution.py:708
  249.0 1.8 collective-permute-done.7.refs_1_
  250.8 1.3 collective-permute-done.8.refs_2_
  252.1 2.6 collective-permute-done.9.refs_3_
  254.8 33.6 %cold_join.1 = (bf16[2048,256]{1,0:T(8,128)(2,1)}, f32[8,256]{1,0:T(8,128)}) custom-call(s32[1]{0:T(128)} %bitcast.at_ref, bf16[272,256]{1,0:T(8,128)(2,1)} %cold_update.1.refs_0_, bf16[272,256]{1,0:T(8,128)(2,1)} %collective-permute-done.7.refs_1_, bf16[272,256]{1,0:T(8,128)(2,1)} %collective-permute-done.8.refs_2_, ...), custom_call_target="tpu_custom_call" | custom-call | tf_op jit(solution)/shard_map/cold_join/pallas_call | solution.py:639
  288.4 1.3 copy.28
  (41 shorter events, 1.7 us)
Async XLA Ops:
  27.9 32.6 %all-to-all-start.3 = ((bf16[32,64,256]{2,1,0:T(8,128)(2,1)}), bf16[32,64,256]{2,1,0:T(8,128)(2,1)}, u32[]{:S(2)}, u32[]{:S(2)}) async-start(bf16[32,64,256]{2,1,0:T(8,128)(2,1)} %bitcast.22), calls=%async_computation.3 | async-start | bytes 2097152 | tf_op jit(solution)/shard_map/all_to_all | solution.py:729
  39.8 26.3 %copy-start.4 = (s32[512,8]{0,1:T(8,128)S(1)}, s32[512,8]{0,1:T(8,128)}, u32[]{:S(2)}) copy-start(s32[512,8]{0,1:T(8,128)} %param.24) | copy-start | bytes 49156
  39.8 27.2 %copy-start = (s32[512,8]{0,1:T(8,128)S(1)}, s32[512,8]{0,1:T(8,128)}, u32[]{:S(2)}) copy-start(s32[512,8]{0,1:T(8,128)} %param.25) | copy-start | bytes 49156
  60.5 35.4 %all-to-all-start.1 = ((bf16[32,64,256]{2,1,0:T(8,128)(2,1)}), bf16[32,64,256]{2,1,0:T(8,128)(2,1)}, u32[]{:S(2)}, u32[]{:S(2)}) async-start(bf16[32,64,256]{2,1,0:T(8,128)(2,1)} %bitcast.24), calls=%async_computation.1 | async-start | bytes 2097152 | tf_op jit(solution)/shard_map/all_to_all | solution.py:729
  95.9 35.8 %all-to-all-start.4 = ((bf16[32,64,256]{2,1,0:T(8,128)(2,1)}), bf16[32,64,256]{2,1,0:T(8,128)(2,1)}, u32[]{:S(2)}, u32[]{:S(2)}) async-start(bf16[32,64,256]{2,1,0:T(8,128)(2,1)} %bitcast.25), calls=%async_computation.4 | async-start | bytes 2097152 | tf_op jit(solution)/shard_map/all_to_all | solution.py:729
  131.7 34.0 %all-to-all-start.2 = ((bf16[32,64,256]{2,1,0:T(8,128)(2,1)}), bf16[32,64,256]{2,1,0:T(8,128)(2,1)}, u32[]{:S(2)}, u32[]{:S(2)}) async-start(bf16[32,64,256]{2,1,0:T(8,128)(2,1)} %bitcast.23), calls=%async_computation.2 | async-start | bytes 2097152 | tf_op jit(solution)/shard_map/all_to_all | solution.py:729
  145.5 7.3 %collective-permute-start.14 = (f32[128,256]{1,0:T(8,128)}, f32[128,256]{1,0:T(8,128)}, u32[]{:S(2)}, u32[]{:S(2)}) collective-permute-start(f32[128,256]{1,0:T(8,128)} %get-tuple-element.51), channel_id=1, source_target_pairs={{0,1},{1,2},{2,3},{3,4},{4,5},{5,6},{6,7},{7,0},{8,9},{9,10},{10,1... | collective-permute-start | bytes 393224 | tf_op jit(solution)/shard_map/ppermute | solution.py:733
  145.6 8.7 %collective-permute-start.15 = (f32[128,256]{1,0:T(8,128)}, f32[128,256]{1,0:T(8,128)}, u32[]{:S(2)}, u32[]{:S(2)}) collective-permute-start(f32[128,256]{1,0:T(8,128)} %get-tuple-element.52), channel_id=1, source_target_pairs={{0,2},{1,3},{2,4},{3,5},{4,6},{5,7},{6,0},{7,1},{8,10},{9,11},{10,... | collective-permute-start | bytes 393224 | tf_op jit(solution)/shard_map/ppermute | solution.py:733
  147.1 11.7 %collective-permute-start.16 = (f32[128,256]{1,0:T(8,128)}, f32[128,256]{1,0:T(8,128)}, u32[]{:S(2)}, u32[]{:S(2)}) collective-permute-start(f32[128,256]{1,0:T(8,128)} %get-tuple-element.53), channel_id=1, source_target_pairs={{0,3},{1,4},{2,5},{3,6},{4,7},{5,0},{6,1},{7,2},{8,11},{9,12},{10,... | collective-permute-start | bytes 393224 | tf_op jit(solution)/shard_map/ppermute | solution.py:733
  149.2 11.0 %collective-permute-start.17 = (f32[128,256]{1,0:T(8,128)}, f32[128,256]{1,0:T(8,128)}, u32[]{:S(2)}, u32[]{:S(2)}) collective-permute-start(f32[128,256]{1,0:T(8,128)} %get-tuple-element.54), channel_id=1, source_target_pairs={{0,4},{1,5},{2,6},{3,7},{4,0},{5,1},{6,2},{7,3},{8,12},{9,13},{10,... | collective-permute-start | bytes 393224 | tf_op jit(solution)/shard_map/ppermute | solution.py:733
  151.2 9.0 %collective-permute-start.18 = (f32[128,256]{1,0:T(8,128)}, f32[128,256]{1,0:T(8,128)}, u32[]{:S(2)}, u32[]{:S(2)}) collective-permute-start(f32[128,256]{1,0:T(8,128)} %get-tuple-element.55), channel_id=1, source_target_pairs={{0,5},{1,6},{2,7},{3,0},{4,1},{5,2},{6,3},{7,4},{8,13},{9,14},{10,... | collective-permute-start | bytes 393224 | tf_op jit(solution)/shard_map/ppermute | solution.py:733
  152.8 8.7 %collective-permute-start.19 = (f32[128,256]{1,0:T(8,128)}, f32[128,256]{1,0:T(8,128)}, u32[]{:S(2)}, u32[]{:S(2)}) collective-permute-start(f32[128,256]{1,0:T(8,128)} %get-tuple-element.56), channel_id=1, source_target_pairs={{0,6},{1,7},{2,0},{3,1},{4,2},{5,3},{6,4},{7,5},{8,14},{9,15},{10,... | collective-permute-start | bytes 393224 | tf_op jit(solution)/shard_map/ppermute | solution.py:733
  154.3 7.7 %collective-permute-start.20 = (f32[128,256]{1,0:T(8,128)}, f32[128,256]{1,0:T(8,128)}, u32[]{:S(2)}, u32[]{:S(2)}) collective-permute-start(f32[128,256]{1,0:T(8,128)} %get-tuple-element.57), channel_id=1, source_target_pairs={{0,7},{1,0},{2,1},{3,2},{4,3},{5,4},{6,5},{7,6},{8,15},{9,8},{10,9... | collective-permute-start | bytes 393224 | tf_op jit(solution)/shard_map/ppermute | solution.py:733
  165.6 26.1 %all-to-all-start.5 = ((f32[32,4,256]{2,1,0:T(4,128)}), f32[32,4,256]{2,1,0:T(4,128)}, u32[]{:S(2)}, u32[]{:S(2)}) async-start(f32[32,4,256]{2,1,0:T(4,128)} %reshape.94), calls=%async_computation.5 | async-start | bytes 262144 | tf_op jit(solution)/shard_map/all_to_all | solution.py:729
  191.4 18.9 %collective-permute-start = (bf16[272,256]{1,0:T(8,128)(2,1)}, bf16[272,256]{1,0:T(8,128)(2,1)S(1)}, u32[]{:S(2)}, u32[]{:S(2)}) collective-permute-start(bf16[272,256]{1,0:T(8,128)(2,1)} %get-tuple-element.37), channel_id=1, source_target_pairs={{0,1},{1,2},{2,3},{3,4},{4,5},{5,6},{6,7},{7,0},{8,9},{9,10},{10,1... | collective-permute-start | bytes 417800 | tf_op jit(solution)/shard_map/ppermute | solution.py:733
  193.3 18.9 %all-to-all-start.6 = ((f32[32,4,256]{2,1,0:T(4,128)}), f32[32,4,256]{2,1,0:T(4,128)S(1)}, u32[]{:S(2)}, u32[]{:S(2)}) async-start(f32[32,4,256]{2,1,0:T(4,128)} %broadcast_in_dim.7), calls=%async_computation.6 | async-start | bytes 262144 | tf_op jit(solution)/shard_map/all_to_all | solution.py:729
  203.1 8.0 %collective-permute-start.1 = (bf16[272,256]{1,0:T(8,128)(2,1)}, bf16[272,256]{1,0:T(8,128)(2,1)S(1)}, u32[]{:S(2)}, u32[]{:S(2)}) collective-permute-start(bf16[272,256]{1,0:T(8,128)(2,1)} %get-tuple-element.38), channel_id=1, source_target_pairs={{0,2},{1,3},{2,4},{3,5},{4,6},{5,7},{6,0},{7,1},{8,10},{9,11},{10,... | collective-permute-start | bytes 417800 | tf_op jit(solution)/shard_map/ppermute | solution.py:733
  204.9 8.1 %collective-permute-start.2 = (bf16[272,256]{1,0:T(8,128)(2,1)}, bf16[272,256]{1,0:T(8,128)(2,1)S(1)}, u32[]{:S(2)}, u32[]{:S(2)}) collective-permute-start(bf16[272,256]{1,0:T(8,128)(2,1)} %get-tuple-element.39), channel_id=1, source_target_pairs={{0,3},{1,4},{2,5},{3,6},{4,7},{5,0},{6,1},{7,2},{8,11},{9,12},{10,... | collective-permute-start | bytes 417800 | tf_op jit(solution)/shard_map/ppermute | solution.py:733
  204.9 12.1 %collective-permute-start.3 = (bf16[272,256]{1,0:T(8,128)(2,1)}, bf16[272,256]{1,0:T(8,128)(2,1)}, u32[]{:S(2)}, u32[]{:S(2)}) collective-permute-start(bf16[272,256]{1,0:T(8,128)(2,1)} %get-tuple-element.40), channel_id=1, source_target_pairs={{0,4},{1,5},{2,6},{3,7},{4,0},{5,1},{6,2},{7,3},{8,12},{9,13},{10,... | collective-permute-start | bytes 417800 | tf_op jit(solution)/shard_map/ppermute | solution.py:733
  207.3 9.7 %collective-permute-start.4 = (bf16[272,256]{1,0:T(8,128)(2,1)}, bf16[272,256]{1,0:T(8,128)(2,1)}, u32[]{:S(2)}, u32[]{:S(2)}) collective-permute-start(bf16[272,256]{1,0:T(8,128)(2,1)} %get-tuple-element.41), channel_id=1, source_target_pairs={{0,5},{1,6},{2,7},{3,0},{4,1},{5,2},{6,3},{7,4},{8,13},{9,14},{10,... | collective-permute-start | bytes 417800 | tf_op jit(solution)/shard_map/ppermute | solution.py:733
  210.3 2.7 copy-start.1
  210.3 8.7 %collective-permute-start.5 = (bf16[272,256]{1,0:T(8,128)(2,1)}, bf16[272,256]{1,0:T(8,128)(2,1)}, u32[]{:S(2)}, u32[]{:S(2)}) collective-permute-start(bf16[272,256]{1,0:T(8,128)(2,1)} %get-tuple-element.42), channel_id=1, source_target_pairs={{0,6},{1,7},{2,0},{3,1},{4,2},{5,3},{6,4},{7,5},{8,14},{9,15},{10,... | collective-permute-start | bytes 417800 | tf_op jit(solution)/shard_map/ppermute | solution.py:733
  211.1 0.7 copy-start.2
  211.8 10.9 %collective-permute-start.6 = (bf16[272,256]{1,0:T(8,128)(2,1)}, bf16[272,256]{1,0:T(8,128)(2,1)}, u32[]{:S(2)}, u32[]{:S(2)}) collective-permute-start(bf16[272,256]{1,0:T(8,128)(2,1)} %get-tuple-element.43), channel_id=1, source_target_pairs={{0,7},{1,0},{2,1},{3,2},{4,3},{5,4},{6,5},{7,6},{8,15},{9,8},{10,9... | collective-permute-start | bytes 417800 | tf_op jit(solution)/shard_map/ppermute | solution.py:733
  213.0 0.7 copy-start.3
  213.6 12.8 %collective-permute-start.21 = (f32[128,256]{1,0:T(8,128)}, f32[128,256]{1,0:T(8,128)}, u32[]{:S(2)}, u32[]{:S(2)}) collective-permute-start(f32[128,256]{1,0:T(8,128)} %reshape.95.refs_0_), channel_id=1, source_target_pairs={{0,1},{1,2},{2,3},{3,4},{4,5},{5,6},{6,7},{7,0},{8,9},{9,10},{10,1... | collective-permute-start | bytes 393224 | tf_op jit(solution)/shard_map/ppermute | solution.py:733
  217.0 11.4 %collective-permute-start.22 = (f32[128,256]{1,0:T(8,128)}, f32[128,256]{1,0:T(8,128)}, u32[]{:S(2)}, u32[]{:S(2)}) collective-permute-start(f32[128,256]{1,0:T(8,128)} %reshape.95.refs_0_), channel_id=1, source_target_pairs={{0,2},{1,3},{2,4},{3,5},{4,6},{5,7},{6,0},{7,1},{8,10},{9,11},{10,... | collective-permute-start | bytes 393224 | tf_op jit(solution)/shard_map/ppermute | solution.py:733
  217.0 11.6 %collective-permute-start.23 = (f32[128,256]{1,0:T(8,128)}, f32[128,256]{1,0:T(8,128)}, u32[]{:S(2)}, u32[]{:S(2)}) collective-permute-start(f32[128,256]{1,0:T(8,128)} %reshape.95.refs_0_), channel_id=1, source_target_pairs={{0,3},{1,4},{2,5},{3,6},{4,7},{5,0},{6,1},{7,2},{8,11},{9,12},{10,... | collective-permute-start | bytes 393224 | tf_op jit(solution)/shard_map/ppermute | solution.py:733
  219.0 12.6 %collective-permute-start.24 = (f32[128,256]{1,0:T(8,128)}, f32[128,256]{1,0:T(8,128)}, u32[]{:S(2)}, u32[]{:S(2)}) collective-permute-start(f32[128,256]{1,0:T(8,128)} %reshape.95.refs_0_), channel_id=1, source_target_pairs={{0,4},{1,5},{2,6},{3,7},{4,0},{5,1},{6,2},{7,3},{8,12},{9,13},{10,... | collective-permute-start | bytes 393224 | tf_op jit(solution)/shard_map/ppermute | solution.py:733
  225.3 18.7 %collective-permute-start.10 = (bf16[272,256]{1,0:T(8,128)(2,1)}, bf16[272,256]{1,0:T(8,128)(2,1)}, u32[]{:S(2)}, u32[]{:S(2)}) collective-permute-start(bf16[272,256]{1,0:T(8,128)(2,1)} %cold_update.1.refs_0_), channel_id=1, source_target_pairs={{0,4},{1,5},{2,6},{3,7},{4,0},{5,1},{6,2},{7,3},{8,12},{9,13},{10,... | collective-permute-start | bytes 417800 | tf_op jit(solution)/shard_map/ppermute | solution.py:733
  226.5 17.6 %collective-permute-start.11 = (bf16[272,256]{1,0:T(8,128)(2,1)}, bf16[272,256]{1,0:T(8,128)(2,1)}, u32[]{:S(2)}, u32[]{:S(2)}) collective-permute-start(bf16[272,256]{1,0:T(8,128)(2,1)} %cold_update.1.refs_0_), channel_id=1, source_target_pairs={{0,5},{1,6},{2,7},{3,0},{4,1},{5,2},{6,3},{7,4},{8,13},{9,14},{10,... | collective-permute-start | bytes 417800 | tf_op jit(solution)/shard_map/ppermute | solution.py:733
  228.4 9.1 %collective-permute-start.25 = (f32[128,256]{1,0:T(8,128)}, f32[128,256]{1,0:T(8,128)}, u32[]{:S(2)}, u32[]{:S(2)}) collective-permute-start(f32[128,256]{1,0:T(8,128)} %reshape.95.refs_0_), channel_id=1, source_target_pairs={{0,5},{1,6},{2,7},{3,0},{4,1},{5,2},{6,3},{7,4},{8,13},{9,14},{10,... | collective-permute-start | bytes 393224 | tf_op jit(solution)/shard_map/ppermute | solution.py:733
  228.7 13.4 %collective-permute-start.26 = (f32[128,256]{1,0:T(8,128)}, f32[128,256]{1,0:T(8,128)}, u32[]{:S(2)}, u32[]{:S(2)}) collective-permute-start(f32[128,256]{1,0:T(8,128)} %reshape.95.refs_0_), channel_id=1, source_target_pairs={{0,6},{1,7},{2,0},{3,1},{4,2},{5,3},{6,4},{7,5},{8,14},{9,15},{10,... | collective-permute-start | bytes 393224 | tf_op jit(solution)/shard_map/ppermute | solution.py:733
  231.6 12.4 %collective-permute-start.27 = (f32[128,256]{1,0:T(8,128)}, f32[128,256]{1,0:T(8,128)}, u32[]{:S(2)}, u32[]{:S(2)}) collective-permute-start(f32[128,256]{1,0:T(8,128)} %reshape.95.refs_0_), channel_id=1, source_target_pairs={{0,7},{1,0},{2,1},{3,2},{4,3},{5,4},{6,5},{7,6},{8,15},{9,8},{10,9... | collective-permute-start | bytes 393224 | tf_op jit(solution)/shard_map/ppermute | solution.py:733
  237.5 11.4 %collective-permute-start.12 = (bf16[272,256]{1,0:T(8,128)(2,1)}, bf16[272,256]{1,0:T(8,128)(2,1)}, u32[]{:S(2)}, u32[]{:S(2)}) collective-permute-start(bf16[272,256]{1,0:T(8,128)(2,1)} %cold_update.1.refs_0_), channel_id=1, source_target_pairs={{0,6},{1,7},{2,0},{3,1},{4,2},{5,3},{6,4},{7,5},{8,14},{9,15},{10,... | collective-permute-start | bytes 417800 | tf_op jit(solution)/shard_map/ppermute | solution.py:733
  242.1 6.9 %collective-permute-start.13 = (bf16[272,256]{1,0:T(8,128)(2,1)}, bf16[272,256]{1,0:T(8,128)(2,1)}, u32[]{:S(2)}, u32[]{:S(2)}) collective-permute-start(bf16[272,256]{1,0:T(8,128)(2,1)} %cold_update.1.refs_0_), channel_id=1, source_target_pairs={{0,7},{1,0},{2,1},{3,2},{4,3},{5,4},{6,5},{7,6},{8,15},{9,8},{10,9... | collective-permute-start | bytes 417800 | tf_op jit(solution)/shard_map/ppermute | solution.py:733
  244.0 6.8 %collective-permute-start.7 = (bf16[272,256]{1,0:T(8,128)(2,1)}, bf16[272,256]{1,0:T(8,128)(2,1)}, u32[]{:S(2)}, u32[]{:S(2)}) collective-permute-start(bf16[272,256]{1,0:T(8,128)(2,1)} %cold_update.1.refs_0_), channel_id=1, source_target_pairs={{0,1},{1,2},{2,3},{3,4},{4,5},{5,6},{6,7},{7,0},{8,9},{9,10},{10,1... | collective-permute-start | bytes 417800 | tf_op jit(solution)/shard_map/ppermute | solution.py:733
  244.0 8.1 %collective-permute-start.8 = (bf16[272,256]{1,0:T(8,128)(2,1)}, bf16[272,256]{1,0:T(8,128)(2,1)}, u32[]{:S(2)}, u32[]{:S(2)}) collective-permute-start(bf16[272,256]{1,0:T(8,128)(2,1)} %cold_update.1.refs_0_), channel_id=1, source_target_pairs={{0,2},{1,3},{2,4},{3,5},{4,6},{5,7},{6,0},{7,1},{8,10},{9,11},{10,... | collective-permute-start | bytes 417800 | tf_op jit(solution)/shard_map/ppermute | solution.py:733
  244.1 10.7 %collective-permute-start.9 = (bf16[272,256]{1,0:T(8,128)(2,1)}, bf16[272,256]{1,0:T(8,128)(2,1)}, u32[]{:S(2)}, u32[]{:S(2)}) collective-permute-start(bf16[272,256]{1,0:T(8,128)(2,1)} %cold_update.1.refs_0_), channel_id=1, source_target_pairs={{0,3},{1,4},{2,5},{3,6},{4,7},{5,0},{6,1},{7,2},{8,11},{9,12},{10,... | collective-permute-start | bytes 417800 | tf_op jit(solution)/shard_map/ppermute | solution.py:733

commit v4 on v3

--- a/solution.py
+++ b/solution.py
@@ -28,6 +28,11 @@
 
 def as_one(same):
     return jnp.where(same, jnp.ones(same.shape, BF), jnp.zeros(same.shape, BF))
+
+
+def chunk_of(at, i):
+    x = ((at >> 1) - (i & 3)) & 3
+    return x * 2 + ((at & 1) ^ (i >> 2))
 
 
 def params():
@@ -302,32 +307,45 @@
     )(fetched, xh, slots, slots_t, targets, w_flat, w_inter, bias, w_out)
 
 
-def hot_scatter_kernel(at_ref, ids_h, hi0, lo0, hi1, lo1, *refs):
-    outs = refs[:N_DP]
-    ids, h0, l0, h1, l1, match, res, sems = refs[N_DP:]
-    copies = load_all([(ids_h, ids), (hi0, h0), (lo0, l0), (hi1, h1), (lo1, l1)], sems)
+def hot_sums(m, ids, hi, lo, prev, match, res):
     samples = ids.shape[1] // MB
-    block = 256
+    block = match.shape[0]
     subs = iota((block, samples), 0).astype(jnp.int16)
-    for c in copies:
-        c.wait()
 
     def body(b, carry):
         at = pl.multiple_of(b * block, block)
-        total = None
-        for m, parts in enumerate(((h0, l0), (h1, l1))):
-            for f in range(F_COLD):
-                row = ids[f : f + 1, m * samples : (m + 1) * samples] - at
-                mine = jnp.broadcast_to(row, (16, samples)).astype(jnp.int16)
-                same = subs == jnp.concatenate([mine] * (block // 16), axis=0)
-                match[m, :, f * samples : (f + 1) * samples] = as_one(same)
-            for part in parts:
-                term = jnp.dot(match[m], part[...], preferred_element_type=F32)
-                total = term if total is None else total + term
+        for f in range(F_COLD):
+            row = ids[f : f + 1, m * samples : (m + 1) * samples] - at
+            mine = jnp.broadcast_to(row, (16, samples)).astype(jnp.int16)
+            same = subs == jnp.concatenate([mine] * (block // 16), axis=0)
+            match[:, f * samples : (f + 1) * samples] = as_one(same)
+        total = jnp.dot(match[...], hi[...], preferred_element_type=F32)
+        total = total + jnp.dot(match[...], lo[...], preferred_element_type=F32)
+        if prev is not None:
+            total = total + prev[pl.ds(at, block), :]
         res[pl.ds(at, block), :] = total
         return carry
 
     lax.fori_loop(0, res.shape[0] // block, body, 0)
+
+
+def hot_first_kernel(ids_h, hi_h, lo_h, out, ids, hi, lo, match, res, sems):
+    copies = load_all([(ids_h, ids), (hi_h, hi), (lo_h, lo)], sems)
+    for c in copies:
+        c.wait()
+    hot_sums(0, ids, hi, lo, None, match, res)
+    done = pltpu.make_async_copy(res, out, sems.at[0])
+    done.start()
+    done.wait()
+
+
+def hot_second_kernel(at_ref, ids_h, hi_h, lo_h, prev_h, *refs):
+    outs = refs[:N_DP]
+    ids, hi, lo, prev, match, res, sems = refs[N_DP:]
+    copies = load_all([(ids_h, ids), (hi_h, hi), (lo_h, lo), (prev_h, prev)], sems)
+    for c in copies:
+        c.wait()
+    hot_sums(1, ids, hi, lo, prev, match, res)
     size = res.shape[0] // N_DP
     done = []
     for k in range(N_DP):
@@ -339,23 +357,38 @@
         c.wait()
 
 
-def hot_scatter(dp_at, ids, hi0, lo0, hi1, lo1, count):
-    rows, width = hi0.shape
-    return pl.pallas_call(
-        hot_scatter_kernel,
-        in_specs=[SMEM] + [HBM] * 5,
+def hot_scatter(m, dp_at, ids, hi, lo, prev, count):
+    rows, width = hi.shape
+    scratch = [
+        pltpu.VMEM(ids.shape, jnp.int32),
+        pltpu.VMEM((rows, width), BF),
+        pltpu.VMEM((rows, width), BF),
+    ]
+    tail = [
+        pltpu.VMEM((256, rows), BF),
+        pltpu.VMEM((count, width), F32),
+        pltpu.SemaphoreType.DMA((N_DP,)),
+    ]
+    whole = jax.ShapeDtypeStruct((count, width), F32)
+    if m == 0:
+        return pl.pallas_call(
+            hot_first_kernel,
+            in_specs=[HBM] * 3,
+            out_specs=HBM,
+            out_shape=whole,
+            scratch_shapes=scratch + tail,
+            compiler_params=params(),
+            name="hot_first",
+        )(ids, hi, lo)
+    return pl.pallas_call(
+        hot_second_kernel,
+        in_specs=[SMEM] + [HBM] * 4,
         out_specs=(HBM,) * N_DP,
         out_shape=(jax.ShapeDtypeStruct((count // N_DP, width), F32),) * N_DP,
-        scratch_shapes=[pltpu.VMEM(ids.shape, jnp.int32)]
-        + [pltpu.VMEM((rows, width), BF)] * 4
-        + [
-            pltpu.VMEM((MB, 256, rows), BF),
-            pltpu.VMEM((count, width), F32),
-            pltpu.SemaphoreType.DMA((N_DP,)),
-        ],
-        compiler_params=params(),
-        name="hot_scatter",
-    )(dp_at, ids, hi0, lo0, hi1, lo1)
+        scratch_shapes=scratch + [pltpu.VMEM((count, width), F32)] + tail,
+        compiler_params=params(),
+        name="hot_second",
+    )(dp_at, ids, hi, lo, prev)
 
 
 def serve_kernel(m, with_hits, wanted, table, rows, *refs):
@@ -475,7 +508,7 @@
         out_shape=jax.ShapeDtypeStruct((count, width), F32),
         scratch_shapes=[
             pltpu.VMEM((slots, width), BF),
-            pltpu.VMEM((512, slots), BF),
+            pltpu.VMEM((256, slots), BF),
             pltpu.VMEM((count, width), F32),
             pltpu.SemaphoreType.DMA((2,)),
         ],
@@ -614,23 +647,18 @@
     parts = refs[:N_DP]
     out, accum_out, pieces, sems = refs[N_DP:]
     size = out.shape[0] // N_DP
-    copies = []
-    for k in range(N_DP):
-        chunk = (at_ref[0] - k) & (N_DP - 1)
+    copies = load_all([(parts[i], pieces.at[i]) for i in range(N_DP)], sems)
+    done = []
+    for i in range(N_DP):
+        copies[i].wait()
+        chunk = chunk_of(at_ref[0], i)
         dst = out.at[pl.ds(pl.multiple_of(chunk * size, size), size), :]
-        copies.append(pltpu.make_async_copy(parts[k].at[pl.ds(0, size), :], dst, sems.at[k]))
-        copies.append(
-            pltpu.make_async_copy(
-                parts[k].at[pl.ds(size, 16), :], pieces.at[chunk], sems.at[N_DP + k]
-            )
-        )
-    for c in copies:
-        c.start()
-    for c in copies:
-        c.wait()
-    for p in range(N_DP):
-        rows = pieces[p].astype(F32)
-        accum_out[p : p + 1, :] = (rows[2:3] + rows[1:2]) + rows[0:1]
+        done.append(pltpu.make_async_copy(pieces.at[i, pl.ds(0, size), :], dst, sems.at[N_DP + i]))
+        done[i].start()
+        rows = pieces[i, size:, :].astype(F32)
+        accum_out[pl.ds(chunk, 1), :] = (rows[2:3] + rows[1:2]) + rows[0:1]
+    for c in done:
+        c.wait()
 
 
 def cold_join(dp_at, parts):
@@ -645,7 +673,7 @@
             jax.ShapeDtypeStruct((N_DP, size), F32),
         ),
         scratch_shapes=[
-            pltpu.VMEM((N_DP, 16, width), BF),
+            pltpu.VMEM((N_DP,) + parts[0].shape, BF),
             pltpu.SemaphoreType.DMA((2 * N_DP,)),
         ],
         compiler_params=params(),
@@ -691,7 +719,7 @@
     for c in copies:
         c.wait()
     for k in range(N_DP):
-        chunk = (at_ref[0] - k) & (N_DP - 1)
+        chunk = chunk_of(at_ref[0], k)
         rows = pl.ds(pl.multiple_of(chunk * size, size), size)
         old = to_col(accum[pl.ds(chunk, 1), :], eye)
         updated, accum_new = adagrad(table[rows, :], old, grads[k])
@@ -738,7 +766,12 @@
 
 
 def to_all(part):
-    return [part] + [shift(part, k) for k in range(1, N_DP)]
+    along = [part]
+    for k in range(1, 4):
+        perm = [(i, ((i // 2 + k) % 4) * 2 + i % 2) for i in range(N_DP)]
+        along.append(lax.ppermute(part, "dp", perm))
+    partner = [(i, i ^ 1) for i in range(N_DP)]
+    return along + [lax.ppermute(value, "dp", partner) for value in along]
 
 
 def step(
@@ -797,14 +830,16 @@
         rows = exchange(slot_grad.reshape(shards, capacity, row_width), "shard")
         owned.append(rows.reshape(slots, row_width))
 
-    hot_grads = hot_scatter(dp_at, hot_ids.T, *hot_parts, hot_count)
+    hot_grads = hot_scatter(0, dp_at, hot_ids.T, *hot_parts[:2], None, hot_count)
+    hot_grads = hot_scatter(1, dp_at, hot_ids.T, *hot_parts[2:], hot_grads, hot_count)
     hot_grads = to_owners(hot_grads)
-    hot_sum = sum_parts(hot_grads)
-    hot_size = hot_sum.shape[0]
-    hot_sum = exchange(hot_sum.reshape(shards, hot_size // shards, row_width), "shard")
-    hot_sum = jnp.sum(hot_sum, axis=0)
-    hot_all = exchange(jnp.broadcast_to(hot_sum[None], (shards,) + hot_sum.shape), "shard")
-    hot_all = to_all(hot_all.reshape(hot_size, row_width))
+    hot_all = sum_parts(hot_grads)
+    step_bit = 1
+    while step_bit < shards:
+        perm = [(i, i ^ step_bit) for i in range(shards)]
+        hot_all = hot_all + lax.ppermute(hot_all, "shard", perm)
+        step_bit *= 2
+    hot_all = to_all(hot_all)
     hot_out, hot_accum_out = hot_update(
         dp_at, hot_table, hot_accum.reshape(N_DP, -1), hot_all
     )

time: 293 us -> 263 us (0.90)
  Pallas kernels: 124 us -> 97.3 us
  waiting for transfers between devices: 47.3 us -> 56.3 us
  starting transfers between devices: 83.1 us -> 74.7 us
  local copies, waits for them, and re-layouts: 10.6 us -> 6.27 us
    pallas_call x1, Pallas kernels: 33.6 us -> 2.7 us  [cold_join(): pl.pallas_call(cold_join_kernel, in_specs=[SMEM] + [HBM] * N_DP, out_spec...]
    ppermute x0 -> x19, starting transfers between devices: none -> 25.8 us  [the longest x5 12 us: step(): hot_all = hot_all + lax.ppermute(hot_all, 'shard', perm)]
    ppermute x0 -> x19, waiting for transfers between devices: none -> 24.6 us  [the longest x5 16.9 us: step(): hot_all = hot_all + lax.ppermute(hot_all, 'shard', perm)]
    all_to_all x6 -> x4, starting transfers between devices: 46.4 us -> 26.8 us  [exchange(): return lax.all_to_all(value, axis, split_axis=0, concat_axis=0, tiled=True)]
    ppermute x28 -> x14, waiting for transfers between devices: 21.6 us -> 6.37 us  [shift(): return lax.ppermute(value, 'dp', [(i, (i + k) % N_DP) for i in range(N_DP)])]
    ppermute x28 -> x14, starting transfers between devices: 36.7 us -> 22.2 us  [shift(): return lax.ppermute(value, 'dp', [(i, (i + k) % N_DP) for i in range(N_DP)])]
    add x0 -> x5, other arithmetic: none -> 3.2 us  [step(): hot_all = hot_all + lax.ppermute(hot_all, 'shard', perm)]
    pallas_call x1 -> x2, Pallas kernels: 8.24 us -> 11.3 us  [the longest x1 5.78 us: hot_scatter(): pl.pallas_call(hot_second_kernel, in_specs=[SMEM] + [HBM] * 4, out_specs=...]
  transfers between devices with their start and end apart: 34 -> 37, of which waited for: 13 -> 15; matrix products, arithmetic and copies ran while one was open for 3% -> 3% of each run, Pallas kernels for 30% -> 31%
where the time goes in v4:
time: 263 us; the launch traced here: 261 us
  Pallas kernels  97.3 us (37%)
  starting transfers between devices  74.7 us (28%)
  waiting for transfers between devices  56.3 us (21%)
  blocking collectives  20.2 us (8%)
  local copies, waits for them, and re-layouts  6.27 us (2%)
  other arithmetic  5.42 us (2%)
    pallas_call x2, Pallas kernels, backprop(): pl.pallas_call(lambda *refs: step_kernel(m, *refs), in_specs=[HBM] * 9, o...  42.7 us
    all_to_all x4, starting transfers between devices, exchange(): return lax.all_to_all(value, axis, split_axis=0, concat_axis=0, tiled=True)  26.8 us
    all_to_all x4, waiting for transfers between devices, exchange(): return lax.all_to_all(value, axis, split_axis=0, concat_axis=0, tiled=True)  25.3 us
    ppermute x14, starting transfers between devices, shift(): return lax.ppermute(value, 'dp', [(i, (i + k) % N_DP) for i in range(N_DP)])  22.2 us
    all_to_all x1, blocking collectives, exchange(): return lax.all_to_all(value, axis, split_axis=0, concat_axis=0, tiled=True)  20.2 us
    ppermute x5, waiting for transfers between devices, step(): hot_all = hot_all + lax.ppermute(hot_all, 'shard', perm)  16.9 us
    ppermute x5, starting transfers between devices, step(): hot_all = hot_all + lax.ppermute(hot_all, 'shard', perm)  12 us
    pallas_call x2, Pallas kernels, serve(): pl.pallas_call(lambda *refs: serve_kernel(m, with_hits, *refs), in_specs=...  11.5 us
  transfers between devices with their start and end apart: 37, of which 15 were waited for; matrix products, arithmetic and copies ran while one was open for 3% of the time, Pallas kernels for 31%

profile of v4, /device:TPU:8, one launch (start us, length us, event | category | flops | bytes accessed | tf_op | source)
XLA Modules:
  0.0 261.1 jit_solution(12413477992380836110)
XLA Ops:
  0.6 0.8 copy.23
  1.4 0.9 fusion
  2.4 20.2 %all_to_all.31 = s32[32,1,128]{2,1,0:T(1,128)} all-to-all(s32[32,1,128]{2,1,0:T(1,128)S(1)} %all_to_all.19), channel_id=1, replica_groups=mesh['shard'=32,'dp'=8] {'shard'}, dimensions={0} | all-to-all | bytes 32768 | tf_op jit(solution)/shard_map/all_to_all | solution.py:757
  22.5 5.3 %serve_rows.3 = bf16[2048,256]{1,0:T(8,128)(2,1)} custom-call(s32[32,128]{1,0:T(8,128)} %bitcast.26, bf16[2048,256]{1,0:T(8,128)(2,1)} %table_h.2), custom_call_target="tpu_custom_call" | custom-call | tf_op jit(solution)/shard_map/serve_rows/pallas_call | solution.py:450
  27.9 5.7 %all-to-all-start.3 = ((bf16[32,64,256]{2,1,0:T(8,128)(2,1)}), bf16[32,64,256]{2,1,0:T(8,128)(2,1)}, u32[]{:S(2)}, u32[]{:S(2)}) async-start(bf16[32,64,256]{2,1,0:T(8,128)(2,1)} %bitcast.22), calls=%async_computation.3 | async-start | bytes 2097152 | tf_op jit(solution)/shard_map/all_to_all | solution.py:757
  33.6 6.2 %serve_rows.2 = (bf16[2048,256]{1,0:T(8,128)(2,1)}, f32[1,2048]{1,0:T(1,128)}) custom-call(s32[32,128]{1,0:T(8,128)} %bitcast.27, bf16[2048,256]{1,0:T(8,128)(2,1)} %table_h.2), custom_call_target="tpu_custom_call" | custom-call | tf_op jit(solution)/shard_map/serve_rows/pallas_call | solution.py:450
  39.8 20.7 %all-to-all-done.3 = bf16[32,64,256]{2,1,0:T(8,128)(2,1)} async-done(((bf16[32,64,256]{2,1,0:T(8,128)(2,1)}), bf16[32,64,256]{2,1,0:T(8,128)(2,1)}, u32[]{:S(2)}, u32[]{:S(2)}) %all-to-all-start.3) | async-done | bytes 1048608 | tf_op jit(solution)/shard_map/all_to_all | solution.py:757
  60.5 5.6 %all-to-all-start.1 = ((bf16[32,64,256]{2,1,0:T(8,128)(2,1)}), bf16[32,64,256]{2,1,0:T(8,128)(2,1)}, u32[]{:S(2)}, u32[]{:S(2)}) async-start(bf16[32,64,256]{2,1,0:T(8,128)(2,1)} %bitcast.24), calls=%async_computation.1 | async-start | bytes 2097152 | tf_op jit(solution)/shard_map/all_to_all | solution.py:757
  66.1 0.8 copy.25.hot_ids
  66.9 0.9 copy.26.refs_2_
  67.8 6.6 %hot_rows.1.refs_1_ = bf16[4096,256]{1,0:T(8,128)(2,1)} custom-call(s32[512,8]{1,0:T(8,128)} %copy.25.hot_ids, f32[1024,256]{1,0:T(8,128)} %table_h.3), custom_call_target="tpu_custom_call" | custom-call | tf_op jit(solution)/shard_map/hot_rows/pallas_call | solution.py:83
  74.4 21.4 %train_step.3 = (bf16[2048,256]{1,0:T(8,128)(2,1)}, bf16[2048,256]{1,0:T(8,128)(2,1)}, bf16[2048,256]{1,0:T(8,128)(2,1)}) custom-call(bf16[2048,256]{1,0:T(8,128)(2,1)} %bitcast.13.refs_0_, bf16[4096,256]{1,0:T(8,128)(2,1)} %hot_rows.1.refs_1_, s32[512,8]{1,0:T(8,128)} %copy.26.refs_2_, s32[8,512]{1,0:T(8,128)} %bitcast.30, f32[1,512]{1,0:T(1,128)} %bitcast.37, ...), custom_call_target="tpu_custom_call" | custom-call | tf_op jit(solution)/shard_map/train_step/pallas_call | solution.py:278
  95.8 9.8 %all-to-all-start.4 = ((bf16[32,64,256]{2,1,0:T(8,128)(2,1)}), bf16[32,64,256]{2,1,0:T(8,128)(2,1)}, u32[]{:S(2)}, u32[]{:S(2)}) async-start(bf16[32,64,256]{2,1,0:T(8,128)(2,1)} %bitcast.25), calls=%async_computation.4 | async-start | bytes 2097152 | tf_op jit(solution)/shard_map/all_to_all | solution.py:757
  105.7 21.3 %train_step.2 = (bf16[2048,256]{1,0:T(8,128)(2,1)}, bf16[2048,256]{1,0:T(8,128)(2,1)}, bf16[2048,256]{1,0:T(8,128)(2,1)}) custom-call(bf16[2048,256]{1,0:T(8,128)(2,1)} %bitcast.5.refs_0_, bf16[4096,256]{1,0:T(8,128)(2,1)} %hot_rows.1.refs_1_, s32[512,8]{1,0:T(8,128)} %copy.26.refs_2_, s32[8,512]{1,0:T(8,128)} %bitcast.31, f32[1,512]{1,0:T(1,128)} %bitcast.38, ...), custom_call_target="tpu_custom_call" | custom-call | tf_op jit(solution)/shard_map/train_step/pallas_call | solution.py:278
  127.0 4.6 %all-to-all-done.4 = bf16[32,64,256]{2,1,0:T(8,128)(2,1)} async-done(((bf16[32,64,256]{2,1,0:T(8,128)(2,1)}), bf16[32,64,256]{2,1,0:T(8,128)(2,1)}, u32[]{:S(2)}, u32[]{:S(2)}) %all-to-all-start.4) | async-done | bytes 1048608 | tf_op jit(solution)/shard_map/all_to_all | solution.py:757
  131.6 5.6 %all-to-all-start.2 = ((bf16[32,64,256]{2,1,0:T(8,128)(2,1)}), bf16[32,64,256]{2,1,0:T(8,128)(2,1)}, u32[]{:S(2)}, u32[]{:S(2)}) async-start(bf16[32,64,256]{2,1,0:T(8,128)(2,1)} %bitcast.23), calls=%async_computation.2 | async-start | bytes 2097152 | tf_op jit(solution)/shard_map/all_to_all | solution.py:757
  137.3 5.5 %hot_first.1.prev_h = f32[1024,256]{1,0:T(8,128)} custom-call(s32[8,512]{1,0:T(8,128)} %bitcast.32, bf16[2048,256]{1,0:T(8,128)(2,1)} %get-tuple-element.48.hi_h, bf16[2048,256]{1,0:T(8,128)(2,1)} %get-tuple-element.49.lo_h), custom_call_target="tpu_custom_call" | custom-call | tf_op jit(solution)/shard_map/hot_first/pallas_call | solution.py:374
  142.8 5.8 %hot_second.1 = (f32[128,256]{1,0:T(8,128)}, f32[128,256]{1,0:T(8,128)}, f32[128,256]{1,0:T(8,128)}, f32[128,256]{1,0:T(8,128)}, f32[128,256]{1,0:T(8,128)}, /*i...) custom-call(s32[1]{0:T(128)} %bitcast.at_ref, s32[8,512]{1,0:T(8,128)} %bitcast.33, ...), custom_call_target="tpu_custom_call" | custom-call | tf_op jit(solution)/shard_map/hot_second/pallas_call | solution.py:383
  148.6 1.6 collective-permute-start.15
  150.1 2.0 collective-permute-start.16
  152.2 2.0 collective-permute-start.17
  154.2 1.6 collective-permute-start.18
  155.8 1.4 collective-permute-start.19
  157.3 2.0 collective-permute-start.20
  159.3 2.5 collective-permute-done.16.refs_3_
  161.8 1.3 collective-permute-done.17.refs_4_
  163.1 1.4 collective-permute-done.19.refs_6_
  165.0 2.1 sum_parts.1
  167.4 6.1 %collective-permute-done.21 = f32[128,256]{1,0:T(8,128)S(1)} collective-permute-done((f32[128,256]{1,0:T(8,128)}, f32[128,256]{1,0:T(8,128)S(1)}, u32[]{:S(2)}, u32[]{:S(2)}) %collective-permute-start.21) | collective-permute-done | bytes 131104 | tf_op jit(solution)/shard_map/ppermute | solution.py:840
  173.6 0.9 add.15
  174.5 2.2 collective-permute-start.22
  176.6 4.8 %collective-permute-done.22 = f32[128,256]{1,0:T(8,128)S(1)} collective-permute-done((f32[128,256]{1,0:T(8,128)S(1)}, f32[128,256]{1,0:T(8,128)S(1)}, u32[]{:S(2)}, u32[]{:S(2)}) %collective-permute-start.22) | collective-permute-done | bytes 131104 | tf_op jit(solution)/shard_map/ppermute | solution.py:840
  181.5 1.6 collective-permute-start.23
  183.0 3.5 %collective-permute-done.23 = f32[128,256]{1,0:T(8,128)S(1)} collective-permute-done((f32[128,256]{1,0:T(8,128)S(1)}, f32[128,256]{1,0:T(8,128)S(1)}, u32[]{:S(2)}, u32[]{:S(2)}) %collective-permute-start.23) | collective-permute-done | bytes 131104 | tf_op jit(solution)/shard_map/ppermute | solution.py:840
  186.6 2.5 collective-permute-start.24
  189.0 0.5 broadcast.4
  189.5 1.4 reduce.3
  190.9 0.6 reshape.73.hits
  191.5 2.4 collective-permute-done.24
  193.9 0.7 add.18
  194.6 7.0 %owner_first.1.prev_h = f32[2048,256]{1,0:T(8,128)} custom-call(s32[32,128]{1,0:T(8,128)} %bitcast.28, bf16[2048,256]{1,0:T(8,128)(2,1)} %bitcast.15.grads_h), custom_call_target="tpu_custom_call" | custom-call | tf_op jit(solution)/shard_map/owner_first/pallas_call | solution.py:504
  201.6 7.3 %owner_second.1 = (bf16[272,256]{1,0:T(8,128)(2,1)}, bf16[272,256]{1,0:T(8,128)(2,1)}, bf16[272,256]{1,0:T(8,128)(2,1)}, bf16[272,256]{1,0:T(8,128)(2,1)}, bf16[...) custom-call(s32[1]{0:T(128)} %bitcast.at_ref, ...), custom_call_target="tpu_custom_call" | custom-call | tf_op jit(solution)/shard_map/owner_second/pallas_call | solution.py:554
  208.9 5.5 %collective-permute-start.25 = (f32[128,256]{1,0:T(8,128)}, f32[128,256]{1,0:T(8,128)S(1)}, u32[]{:S(2)}, u32[]{:S(2)}) collective-permute-start(f32[128,256]{1,0:T(8,128)} %add.18), channel_id=1, source_target_pairs={{0,128},{8,136},{16,144},{24,152},{32,160},{40,168},{48,176},{56,1... | collective-permute-start | bytes 393224 | tf_op jit(solution)/shard_map/ppermute | solution.py:840
  214.4 1.9 collective-permute-start.1
  216.2 1.4 collective-permute-start.2
  217.6 2.4 collective-permute-start.3
  220.0 4.1 %collective-permute-start.4 = (bf16[272,256]{1,0:T(8,128)(2,1)}, bf16[272,256]{1,0:T(8,128)(2,1)}, u32[]{:S(2)}, u32[]{:S(2)}) collective-permute-start(bf16[272,256]{1,0:T(8,128)(2,1)} %get-tuple-element.41), channel_id=1, source_target_pairs={{0,5},{1,6},{2,7},{3,0},{4,1},{5,2},{6,3},{7,4},{8,13},{9,14},{10,... | collective-permute-start | bytes 417800 | tf_op jit(solution)/shard_map/ppermute | solution.py:761
  224.2 1.4 collective-permute-start.5
  225.8 1.6 add.19.refs_0_
  227.4 0.6 collective-permute-start.26
  228.0 0.7 collective-permute-done.3.refs_4_
  228.7 1.2 collective-permute-start.27
  229.9 3.5 %collective-permute-start.28 = (f32[128,256]{1,0:T(8,128)}, f32[128,256]{1,0:T(8,128)}, u32[]{:S(2)}, u32[]{:S(2)}) collective-permute-start(f32[128,256]{1,0:T(8,128)} %add.19.refs_0_), channel_id=1, source_target_pairs={{0,6},{1,7},{2,0},{3,1},{4,2},{5,3},{6,4},{7,5},{8,14},{9,15},{10,... | collective-permute-start | bytes 393224 | tf_op jit(solution)/shard_map/ppermute | solution.py:772
  233.4 2.0 collective-permute-start.29
  235.3 1.3 reshape.71.accum_h
  236.7 2.6 cold_update.1.refs_0_
  239.3 5.1 %collective-permute-start.8 = (bf16[272,256]{1,0:T(8,128)(2,1)}, bf16[272,256]{1,0:T(8,128)(2,1)}, u32[]{:S(2)}, u32[]{:S(2)}) collective-permute-start(bf16[272,256]{1,0:T(8,128)(2,1)} %cold_update.1.refs_0_), channel_id=1, source_target_pairs={{0,4},{1,5},{2,6},{3,7},{4,0},{5,1},{6,2},{7,3},{8,12},{9,13},{10,... | collective-permute-start | bytes 417800 | tf_op jit(solution)/shard_map/ppermute | solution.py:772
  245.0 1.2 collective-permute-done.30.refs_5_
  246.3 0.8 collective-permute-done.7.refs_1_
  247.1 4.2 %collective-permute-done.8.refs_2_ = bf16[272,256]{1,0:T(8,128)(2,1)} collective-permute-done((bf16[272,256]{1,0:T(8,128)(2,1)}, bf16[272,256]{1,0:T(8,128)(2,1)}, u32[]{:S(2)}, u32[]{:S(2)}) %collective-permute-start.8) | collective-permute-done | bytes 139296 | tf_op jit(solution)/shard_map/ppermute | solution.py:772
  251.9 1.6 collective-permute-done.32.refs_7_
  253.5 3.6 %hot_update.1 = (f32[1024,256]{1,0:T(8,128)}, f32[8,128]{1,0:T(8,128)}) custom-call(s32[1]{0:T(128)} %bitcast.at_ref, f32[1024,256]{1,0:T(8,128)} %table_h.3, f32[8,128]{1,0:T(8,128)} %bitcast.43, f32[128,256]{1,0:T(8,128)} %add.19.refs_0_, f32[128,256]{1,0:T(8,128)} %collective-permute-done.26.refs_1_, f32[128,256]{1,0:T(8,128)} %collective-permute-done.27.refs_2_, ...), custom_call_target="tpu_custom_call" | custom-call | tf_op jit(solution)/shard_map/hot_update/pallas_call | solution.py:736
  257.1 2.7 %cold_join.1 = (bf16[2048,256]{1,0:T(8,128)(2,1)}, f32[8,256]{1,0:T(8,128)}) custom-call(s32[1]{0:T(128)} %bitcast.at_ref, bf16[272,256]{1,0:T(8,128)(2,1)} %cold_update.1.refs_0_, bf16[272,256]{1,0:T(8,128)(2,1)} %collective-permute-done.7.refs_1_, bf16[272,256]{1,0:T(8,128)(2,1)} %collective-permute-done.8.refs_2_, ...), custom_call_target="tpu_custom_call" | custom-call | tf_op jit(solution)/shard_map/cold_join/pallas_call | solution.py:667
  259.8 1.3 copy.28
  (43 shorter events, 2.6 us)
Async XLA Ops:
  27.9 32.6 %all-to-all-start.3 = ((bf16[32,64,256]{2,1,0:T(8,128)(2,1)}), bf16[32,64,256]{2,1,0:T(8,128)(2,1)}, u32[]{:S(2)}, u32[]{:S(2)}) async-start(bf16[32,64,256]{2,1,0:T(8,128)(2,1)} %bitcast.22), calls=%async_computation.3 | async-start | bytes 2097152 | tf_op jit(solution)/shard_map/all_to_all | solution.py:757
  39.7 26.3 %copy-start.1 = (s32[512,8]{0,1:T(8,128)S(1)}, s32[512,8]{0,1:T(8,128)}, u32[]{:S(2)}) copy-start(s32[512,8]{0,1:T(8,128)} %param.24) | copy-start | bytes 49156
  39.8 27.2 %copy-start = (s32[512,8]{0,1:T(8,128)S(1)}, s32[512,8]{0,1:T(8,128)}, u32[]{:S(2)}) copy-start(s32[512,8]{0,1:T(8,128)} %param.25) | copy-start | bytes 49156
  60.5 35.4 %all-to-all-start.1 = ((bf16[32,64,256]{2,1,0:T(8,128)(2,1)}), bf16[32,64,256]{2,1,0:T(8,128)(2,1)}, u32[]{:S(2)}, u32[]{:S(2)}) async-start(bf16[32,64,256]{2,1,0:T(8,128)(2,1)} %bitcast.24), calls=%async_computation.1 | async-start | bytes 2097152 | tf_op jit(solution)/shard_map/all_to_all | solution.py:757
  95.8 35.8 %all-to-all-start.4 = ((bf16[32,64,256]{2,1,0:T(8,128)(2,1)}), bf16[32,64,256]{2,1,0:T(8,128)(2,1)}, u32[]{:S(2)}, u32[]{:S(2)}) async-start(bf16[32,64,256]{2,1,0:T(8,128)(2,1)} %bitcast.25), calls=%async_computation.4 | async-start | bytes 2097152 | tf_op jit(solution)/shard_map/all_to_all | solution.py:757
  131.6 69.9 %all-to-all-start.2 = ((bf16[32,64,256]{2,1,0:T(8,128)(2,1)}), bf16[32,64,256]{2,1,0:T(8,128)(2,1)}, u32[]{:S(2)}, u32[]{:S(2)}) async-start(bf16[32,64,256]{2,1,0:T(8,128)(2,1)} %bitcast.23), calls=%async_computation.2 | async-start | bytes 2097152 | tf_op jit(solution)/shard_map/all_to_all | solution.py:757
  148.5 7.3 %collective-permute-start.14 = (f32[128,256]{1,0:T(8,128)}, f32[128,256]{1,0:T(8,128)}, u32[]{:S(2)}, u32[]{:S(2)}) collective-permute-start(f32[128,256]{1,0:T(8,128)} %get-tuple-element.51), channel_id=1, source_target_pairs={{0,1},{1,2},{2,3},{3,4},{4,5},{5,6},{6,7},{7,0},{8,9},{9,10},{10,1... | collective-permute-start | bytes 393224 | tf_op jit(solution)/shard_map/ppermute | solution.py:761
  148.6 8.7 %collective-permute-start.15 = (f32[128,256]{1,0:T(8,128)}, f32[128,256]{1,0:T(8,128)}, u32[]{:S(2)}, u32[]{:S(2)}) collective-permute-start(f32[128,256]{1,0:T(8,128)} %get-tuple-element.52), channel_id=1, source_target_pairs={{0,2},{1,3},{2,4},{3,5},{4,6},{5,7},{6,0},{7,1},{8,10},{9,11},{10,... | collective-permute-start | bytes 393224 | tf_op jit(solution)/shard_map/ppermute | solution.py:761
  150.1 11.7 %collective-permute-start.16 = (f32[128,256]{1,0:T(8,128)}, f32[128,256]{1,0:T(8,128)}, u32[]{:S(2)}, u32[]{:S(2)}) collective-permute-start(f32[128,256]{1,0:T(8,128)} %get-tuple-element.53), channel_id=1, source_target_pairs={{0,3},{1,4},{2,5},{3,6},{4,7},{5,0},{6,1},{7,2},{8,11},{9,12},{10,... | collective-permute-start | bytes 393224 | tf_op jit(solution)/shard_map/ppermute | solution.py:761
  152.2 11.0 %collective-permute-start.17 = (f32[128,256]{1,0:T(8,128)}, f32[128,256]{1,0:T(8,128)}, u32[]{:S(2)}, u32[]{:S(2)}) collective-permute-start(f32[128,256]{1,0:T(8,128)} %get-tuple-element.54), channel_id=1, source_target_pairs={{0,4},{1,5},{2,6},{3,7},{4,0},{5,1},{6,2},{7,3},{8,12},{9,13},{10,... | collective-permute-start | bytes 393224 | tf_op jit(solution)/shard_map/ppermute | solution.py:761
  154.2 9.0 %collective-permute-start.18 = (f32[128,256]{1,0:T(8,128)}, f32[128,256]{1,0:T(8,128)}, u32[]{:S(2)}, u32[]{:S(2)}) collective-permute-start(f32[128,256]{1,0:T(8,128)} %get-tuple-element.55), channel_id=1, source_target_pairs={{0,5},{1,6},{2,7},{3,0},{4,1},{5,2},{6,3},{7,4},{8,13},{9,14},{10,... | collective-permute-start | bytes 393224 | tf_op jit(solution)/shard_map/ppermute | solution.py:761
  155.8 8.7 %collective-permute-start.19 = (f32[128,256]{1,0:T(8,128)}, f32[128,256]{1,0:T(8,128)}, u32[]{:S(2)}, u32[]{:S(2)}) collective-permute-start(f32[128,256]{1,0:T(8,128)} %get-tuple-element.56), channel_id=1, source_target_pairs={{0,6},{1,7},{2,0},{3,1},{4,2},{5,3},{6,4},{7,5},{8,14},{9,15},{10,... | collective-permute-start | bytes 393224 | tf_op jit(solution)/shard_map/ppermute | solution.py:761
  157.3 7.7 %collective-permute-start.20 = (f32[128,256]{1,0:T(8,128)}, f32[128,256]{1,0:T(8,128)}, u32[]{:S(2)}, u32[]{:S(2)}) collective-permute-start(f32[128,256]{1,0:T(8,128)} %get-tuple-element.57), channel_id=1, source_target_pairs={{0,7},{1,0},{2,1},{3,2},{4,3},{5,4},{6,5},{7,6},{8,15},{9,8},{10,9... | collective-permute-start | bytes 393224 | tf_op jit(solution)/shard_map/ppermute | solution.py:761
  167.0 6.5 %collective-permute-start.21 = (f32[128,256]{1,0:T(8,128)}, f32[128,256]{1,0:T(8,128)S(1)}, u32[]{:S(2)}, u32[]{:S(2)}) collective-permute-start(f32[128,256]{1,0:T(8,128)} %sum_parts.1), channel_id=1, source_target_pairs={{0,8},{8,0},{16,24},{24,16},{32,40},{40,32},{48,56},{56,48},{64,72... | collective-permute-start | bytes 393224 | tf_op jit(solution)/shard_map/ppermute | solution.py:840
  174.5 7.0 %collective-permute-start.22 = (f32[128,256]{1,0:T(8,128)S(1)}, f32[128,256]{1,0:T(8,128)S(1)}, u32[]{:S(2)}, u32[]{:S(2)}) collective-permute-start(f32[128,256]{1,0:T(8,128)S(1)} %add.15), channel_id=1, source_target_pairs={{0,16},{8,24},{16,0},{24,8},{32,48},{40,56},{48,32},{56,40},{64,80... | collective-permute-start | bytes 393224 | tf_op jit(solution)/shard_map/ppermute | solution.py:840
  181.5 5.1 %collective-permute-start.23 = (f32[128,256]{1,0:T(8,128)S(1)}, f32[128,256]{1,0:T(8,128)S(1)}, u32[]{:S(2)}, u32[]{:S(2)}) collective-permute-start(f32[128,256]{1,0:T(8,128)S(1)} %add.16), channel_id=1, source_target_pairs={{0,32},{8,40},{16,48},{24,56},{32,0},{40,8},{48,16},{56,24},{64,96... | collective-permute-start | bytes 393224 | tf_op jit(solution)/shard_map/ppermute | solution.py:840
  186.6 7.4 %collective-permute-start.24 = (f32[128,256]{1,0:T(8,128)S(1)}, f32[128,256]{1,0:T(8,128)S(1)}, u32[]{:S(2)}, u32[]{:S(2)}) collective-permute-start(f32[128,256]{1,0:T(8,128)S(1)} %add.17), channel_id=1, source_target_pairs={{0,64},{8,72},{16,80},{24,88},{32,96},{40,104},{48,112},{56,120},{... | collective-permute-start | bytes 393224 | tf_op jit(solution)/shard_map/ppermute | solution.py:840
  208.9 15.3 %collective-permute-start = (bf16[272,256]{1,0:T(8,128)(2,1)}, bf16[272,256]{1,0:T(8,128)(2,1)}, u32[]{:S(2)}, u32[]{:S(2)}) collective-permute-start(bf16[272,256]{1,0:T(8,128)(2,1)} %get-tuple-element.37), channel_id=1, source_target_pairs={{0,1},{1,2},{2,3},{3,4},{4,5},{5,6},{6,7},{7,0},{8,9},{9,10},{10,1... | collective-permute-start | bytes 417800 | tf_op jit(solution)/shard_map/ppermute | solution.py:761
  208.9 11.1 %collective-permute-start.25 = (f32[128,256]{1,0:T(8,128)}, f32[128,256]{1,0:T(8,128)S(1)}, u32[]{:S(2)}, u32[]{:S(2)}) collective-permute-start(f32[128,256]{1,0:T(8,128)} %add.18), channel_id=1, source_target_pairs={{0,128},{8,136},{16,144},{24,152},{32,160},{40,168},{48,176},{56,1... | collective-permute-start | bytes 393224 | tf_op jit(solution)/shard_map/ppermute | solution.py:840
  214.4 11.2 %collective-permute-start.1 = (bf16[272,256]{1,0:T(8,128)(2,1)}, bf16[272,256]{1,0:T(8,128)(2,1)}, u32[]{:S(2)}, u32[]{:S(2)}) collective-permute-start(bf16[272,256]{1,0:T(8,128)(2,1)} %get-tuple-element.38), channel_id=1, source_target_pairs={{0,2},{1,3},{2,4},{3,5},{4,6},{5,7},{6,0},{7,1},{8,10},{9,11},{10,... | collective-permute-start | bytes 417800 | tf_op jit(solution)/shard_map/ppermute | solution.py:761
  216.2 11.1 %collective-permute-start.2 = (bf16[272,256]{1,0:T(8,128)(2,1)}, bf16[272,256]{1,0:T(8,128)(2,1)}, u32[]{:S(2)}, u32[]{:S(2)}) collective-permute-start(bf16[272,256]{1,0:T(8,128)(2,1)} %get-tuple-element.39), channel_id=1, source_target_pairs={{0,3},{1,4},{2,5},{3,6},{4,7},{5,0},{6,1},{7,2},{8,11},{9,12},{10,... | collective-permute-start | bytes 417800 | tf_op jit(solution)/shard_map/ppermute | solution.py:761
  217.6 11.0 %collective-permute-start.3 = (bf16[272,256]{1,0:T(8,128)(2,1)}, bf16[272,256]{1,0:T(8,128)(2,1)}, u32[]{:S(2)}, u32[]{:S(2)}) collective-permute-start(bf16[272,256]{1,0:T(8,128)(2,1)} %get-tuple-element.40), channel_id=1, source_target_pairs={{0,4},{1,5},{2,6},{3,7},{4,0},{5,1},{6,2},{7,3},{8,12},{9,13},{10,... | collective-permute-start | bytes 417800 | tf_op jit(solution)/shard_map/ppermute | solution.py:761
  220.0 9.8 %collective-permute-start.4 = (bf16[272,256]{1,0:T(8,128)(2,1)}, bf16[272,256]{1,0:T(8,128)(2,1)}, u32[]{:S(2)}, u32[]{:S(2)}) collective-permute-start(bf16[272,256]{1,0:T(8,128)(2,1)} %get-tuple-element.41), channel_id=1, source_target_pairs={{0,5},{1,6},{2,7},{3,0},{4,1},{5,2},{6,3},{7,4},{8,13},{9,14},{10,... | collective-permute-start | bytes 417800 | tf_op jit(solution)/shard_map/ppermute | solution.py:761
  224.2 9.2 %collective-permute-start.5 = (bf16[272,256]{1,0:T(8,128)(2,1)}, bf16[272,256]{1,0:T(8,128)(2,1)}, u32[]{:S(2)}, u32[]{:S(2)}) collective-permute-start(bf16[272,256]{1,0:T(8,128)(2,1)} %get-tuple-element.42), channel_id=1, source_target_pairs={{0,6},{1,7},{2,0},{3,1},{4,2},{5,3},{6,4},{7,5},{8,14},{9,15},{10,... | collective-permute-start | bytes 417800 | tf_op jit(solution)/shard_map/ppermute | solution.py:761
  225.6 11.1 %collective-permute-start.6 = (bf16[272,256]{1,0:T(8,128)(2,1)}, bf16[272,256]{1,0:T(8,128)(2,1)}, u32[]{:S(2)}, u32[]{:S(2)}) collective-permute-start(bf16[272,256]{1,0:T(8,128)(2,1)} %get-tuple-element.43), channel_id=1, source_target_pairs={{0,7},{1,0},{2,1},{3,2},{4,3},{5,4},{6,5},{7,6},{8,15},{9,8},{10,9... | collective-permute-start | bytes 417800 | tf_op jit(solution)/shard_map/ppermute | solution.py:761
  227.4 11.9 %collective-permute-start.26 = (f32[128,256]{1,0:T(8,128)}, f32[128,256]{1,0:T(8,128)}, u32[]{:S(2)}, u32[]{:S(2)}) collective-permute-start(f32[128,256]{1,0:T(8,128)} %add.19.refs_0_), channel_id=1, source_target_pairs={{0,2},{1,3},{2,4},{3,5},{4,6},{5,7},{6,0},{7,1},{8,10},{9,11},{10,... | collective-permute-start | bytes 393224 | tf_op jit(solution)/shard_map/ppermute | solution.py:772
  228.7 15.7 %collective-permute-start.27 = (f32[128,256]{1,0:T(8,128)}, f32[128,256]{1,0:T(8,128)}, u32[]{:S(2)}, u32[]{:S(2)}) collective-permute-start(f32[128,256]{1,0:T(8,128)} %add.19.refs_0_), channel_id=1, source_target_pairs={{0,4},{1,5},{2,6},{3,7},{4,0},{5,1},{6,2},{7,3},{8,12},{9,13},{10,... | collective-permute-start | bytes 393224 | tf_op jit(solution)/shard_map/ppermute | solution.py:772
  229.9 14.6 %collective-permute-start.28 = (f32[128,256]{1,0:T(8,128)}, f32[128,256]{1,0:T(8,128)}, u32[]{:S(2)}, u32[]{:S(2)}) collective-permute-start(f32[128,256]{1,0:T(8,128)} %add.19.refs_0_), channel_id=1, source_target_pairs={{0,6},{1,7},{2,0},{3,1},{4,2},{5,3},{6,4},{7,5},{8,14},{9,15},{10,... | collective-permute-start | bytes 393224 | tf_op jit(solution)/shard_map/ppermute | solution.py:772
  233.4 11.2 %collective-permute-start.29 = (f32[128,256]{1,0:T(8,128)}, f32[128,256]{1,0:T(8,128)}, u32[]{:S(2)}, u32[]{:S(2)}) collective-permute-start(f32[128,256]{1,0:T(8,128)} %add.19.refs_0_), channel_id=1, source_target_pairs={{0,1},{1,0},{2,3},{3,2},{4,5},{5,4},{6,7},{7,6},{8,9},{9,8},{10,11... | collective-permute-start | bytes 393224 | tf_op jit(solution)/shard_map/ppermute | solution.py:774
  239.2 7.9 %collective-permute-start.7 = (bf16[272,256]{1,0:T(8,128)(2,1)}, bf16[272,256]{1,0:T(8,128)(2,1)}, u32[]{:S(2)}, u32[]{:S(2)}) collective-permute-start(bf16[272,256]{1,0:T(8,128)(2,1)} %cold_update.1.refs_0_), channel_id=1, source_target_pairs={{0,2},{1,3},{2,4},{3,5},{4,6},{5,7},{6,0},{7,1},{8,10},{9,11},{10,... | collective-permute-start | bytes 417800 | tf_op jit(solution)/shard_map/ppermute | solution.py:772
  239.3 11.9 %collective-permute-start.8 = (bf16[272,256]{1,0:T(8,128)(2,1)}, bf16[272,256]{1,0:T(8,128)(2,1)}, u32[]{:S(2)}, u32[]{:S(2)}) collective-permute-start(bf16[272,256]{1,0:T(8,128)(2,1)} %cold_update.1.refs_0_), channel_id=1, source_target_pairs={{0,4},{1,5},{2,6},{3,7},{4,0},{5,1},{6,2},{7,3},{8,12},{9,13},{10,... | collective-permute-start | bytes 417800 | tf_op jit(solution)/shard_map/ppermute | solution.py:772
  244.4 6.9 %collective-permute-start.9 = (bf16[272,256]{1,0:T(8,128)(2,1)}, bf16[272,256]{1,0:T(8,128)(2,1)}, u32[]{:S(2)}, u32[]{:S(2)}) collective-permute-start(bf16[272,256]{1,0:T(8,128)(2,1)} %cold_update.1.refs_0_), channel_id=1, source_target_pairs={{0,6},{1,7},{2,0},{3,1},{4,2},{5,3},{6,4},{7,5},{8,14},{9,15},{10,... | collective-permute-start | bytes 417800 | tf_op jit(solution)/shard_map/ppermute | solution.py:772
  244.4 1.8 collective-permute-start.30
  244.5 7.2 %collective-permute-start.31 = (f32[128,256]{1,0:T(8,128)}, f32[128,256]{1,0:T(8,128)}, u32[]{:S(2)}, u32[]{:S(2)}) collective-permute-start(f32[128,256]{1,0:T(8,128)} %collective-permute-done.27.refs_2_), channel_id=1, source_target_pairs={{0,1},{1,0},{2,3},{3,2},{4,5},{5,4},{6,7},{7,6},{8,9},{9,8},{10,11... | collective-permute-start | bytes 393224 | tf_op jit(solution)/shard_map/ppermute | solution.py:774
  246.2 10.9 %collective-permute-start.10 = (bf16[272,256]{1,0:T(8,128)(2,1)}, bf16[272,256]{1,0:T(8,128)(2,1)}, u32[]{:S(2)}, u32[]{:S(2)}) collective-permute-start(bf16[272,256]{1,0:T(8,128)(2,1)} %cold_update.1.refs_0_), channel_id=1, source_target_pairs={{0,1},{1,0},{2,3},{3,2},{4,5},{5,4},{6,7},{7,6},{8,9},{9,8},{10,11... | collective-permute-start | bytes 417800 | tf_op jit(solution)/shard_map/ppermute | solution.py:774
  247.1 10.0 %collective-permute-start.11 = (bf16[272,256]{1,0:T(8,128)(2,1)}, bf16[272,256]{1,0:T(8,128)(2,1)}, u32[]{:S(2)}, u32[]{:S(2)}) collective-permute-start(bf16[272,256]{1,0:T(8,128)(2,1)} %collective-permute-done.7.refs_1_), channel_id=1, source_target_pairs={{0,1},{1,0},{2,3},{3,2},{4,5},{5,4},{6,7},{7,6},{8,9},{9,8},{10,11... | collective-permute-start | bytes 417800 | tf_op jit(solution)/shard_map/ppermute | solution.py:774
  251.2 5.9 %collective-permute-start.12 = (bf16[272,256]{1,0:T(8,128)(2,1)}, bf16[272,256]{1,0:T(8,128)(2,1)}, u32[]{:S(2)}, u32[]{:S(2)}) collective-permute-start(bf16[272,256]{1,0:T(8,128)(2,1)} %collective-permute-done.8.refs_2_), channel_id=1, source_target_pairs={{0,1},{1,0},{2,3},{3,2},{4,5},{5,4},{6,7},{7,6},{8,9},{9,8},{10,11... | collective-permute-start | bytes 417800 | tf_op jit(solution)/shard_map/ppermute | solution.py:774
  251.3 5.9 %collective-permute-start.13 = (bf16[272,256]{1,0:T(8,128)(2,1)}, bf16[272,256]{1,0:T(8,128)(2,1)}, u32[]{:S(2)}, u32[]{:S(2)}) collective-permute-start(bf16[272,256]{1,0:T(8,128)(2,1)} %collective-permute-done.9.refs_3_), channel_id=1, source_target_pairs={{0,1},{1,0},{2,3},{3,2},{4,5},{5,4},{6,7},{7,6},{8,9},{9,8},{10,11... | collective-permute-start | bytes 417800 | tf_op jit(solution)/shard_map/ppermute | solution.py:774
  251.8 1.7 collective-permute-start.32

commit v5 on v3

--- a/solution.py
+++ b/solution.py
@@ -17,7 +17,8 @@
 VMEM = pl.BlockSpec(memory_space=pltpu.VMEM)
 SMEM = pl.BlockSpec(memory_space=pltpu.SMEM)
 N_DP = 8
-VMEM_LIMIT = (64 << 20) - (64 << 10)
+N_X = 4
+VMEM_LIMIT = 64 << 20
 learn_rate = 0.3
 UNROLL = 4
 
@@ -30,8 +31,17 @@
     return jnp.where(same, jnp.ones(same.shape, BF), jnp.zeros(same.shape, BF))
 
 
+def chunk_of(at, i):
+    x = ((at >> 1) - (i & 3)) & 3
+    return x * 2 + ((at & 1) ^ (i >> 2))
+
+
 def params():
     return pltpu.CompilerParams(vmem_limit_bytes=VMEM_LIMIT)
+
+
+def small_params():
+    return pltpu.CompilerParams(vmem_limit_bytes=20 << 20)
 
 
 def load_all(pairs, sems):
@@ -49,7 +59,7 @@
         match[pl.ds(at + f * GROUP, GROUP), :count] = as_one(same)
 
 
-def hot_rows_kernel(hot_ids, table, out, ids, src, match, res, sems):
+def hot_rows_kernel(hot_ids, table, later, out, ids, src, match, res, sems):
     copies = load_all([(hot_ids, ids), (table, src)], sems)
     for c in copies:
         c.wait()
@@ -72,12 +82,12 @@
     done.wait()
 
 
-def hot_rows(hot_ids, table):
+def hot_rows(hot_ids, table, later):
     count, width = table.shape
     rows = hot_ids.shape[0] * F_COLD
     return pl.pallas_call(
         hot_rows_kernel,
-        in_specs=[HBM, HBM],
+        in_specs=[HBM] * 3,
         out_specs=HBM,
         out_shape=jax.ShapeDtypeStruct((rows, width), BF),
         scratch_shapes=[
@@ -89,7 +99,7 @@
         ],
         compiler_params=params(),
         name="hot_rows",
-    )(hot_ids, table)
+    )(hot_ids, table, later)
 
 
 def step_kernel(m, *refs):
@@ -303,14 +313,14 @@
 
 
 def hot_scatter_kernel(at_ref, ids_h, hi0, lo0, hi1, lo1, *refs):
-    outs = refs[:N_DP]
-    ids, h0, l0, h1, l1, match, res, sems = refs[N_DP:]
+    outs = refs[:N_X]
+    other, ids, h0, l0, h1, l1, match, res, sems = refs[N_X:]
     copies = load_all([(ids_h, ids), (hi0, h0), (lo0, l0), (hi1, h1), (lo1, l1)], sems)
     samples = ids.shape[1] // MB
-    block = 256
+    block = match.shape[1]
+    size = res.shape[0] // N_DP
     subs = iota((block, samples), 0).astype(jnp.int16)
-    for c in copies:
-        c.wait()
+    copies[0].wait()
 
     def body(b, carry):
         at = pl.multiple_of(b * block, block)
@@ -321,22 +331,38 @@
                 mine = jnp.broadcast_to(row, (16, samples)).astype(jnp.int16)
                 same = subs == jnp.concatenate([mine] * (block // 16), axis=0)
                 match[m, :, f * samples : (f + 1) * samples] = as_one(same)
+
+            @pl.when(b == 0)
+            def _():
+                copies[1 + 2 * m].wait()
+                copies[2 + 2 * m].wait()
+
             for part in parts:
                 term = jnp.dot(match[m], part[...], preferred_element_type=F32)
                 total = term if total is None else total + term
         res[pl.ds(at, block), :] = total
+        for q in range(block // size):
+            chunk = b * (block // size) + q
+            src = res.at[pl.ds(pl.multiple_of(chunk * size, size), size), :]
+            place = ((chunk >> 1) - (at_ref[0] >> 1)) & (N_X - 1)
+            mine = (chunk & 1) == (at_ref[0] & 1)
+            for k in range(N_X):
+
+                @pl.when(mine & (place == k))
+                def _():
+                    pltpu.make_async_copy(src, outs[k], sems.at[5 + k]).start()
+
+            @pl.when(jnp.logical_not(mine))
+            def _():
+                pltpu.make_async_copy(src, other.at[place], sems.at[5 + N_X + place]).start()
+
         return carry
 
     lax.fori_loop(0, res.shape[0] // block, body, 0)
-    size = res.shape[0] // N_DP
-    done = []
-    for k in range(N_DP):
-        chunk = (at_ref[0] + k) & (N_DP - 1)
-        src = res.at[pl.ds(pl.multiple_of(chunk * size, size), size), :]
-        done.append(pltpu.make_async_copy(src, outs[k], sems.at[k]))
-        done[-1].start()
-    for c in done:
-        c.wait()
+    for k in range(N_X):
+        src = res.at[pl.ds(0, size), :]
+        pltpu.make_async_copy(src, outs[k], sems.at[5 + k]).wait()
+        pltpu.make_async_copy(src, other.at[k], sems.at[5 + N_X + k]).wait()
 
 
 def hot_scatter(dp_at, ids, hi0, lo0, hi1, lo1, count):
@@ -344,25 +370,28 @@
     return pl.pallas_call(
         hot_scatter_kernel,
         in_specs=[SMEM] + [HBM] * 5,
-        out_specs=(HBM,) * N_DP,
-        out_shape=(jax.ShapeDtypeStruct((count // N_DP, width), F32),) * N_DP,
+        out_specs=(HBM,) * (N_X + 1),
+        out_shape=(jax.ShapeDtypeStruct((count // N_DP, width), F32),) * N_X
+        + (jax.ShapeDtypeStruct((N_X, count // N_DP, width), F32),),
         scratch_shapes=[pltpu.VMEM(ids.shape, jnp.int32)]
         + [pltpu.VMEM((rows, width), BF)] * 4
         + [
             pltpu.VMEM((MB, 256, rows), BF),
             pltpu.VMEM((count, width), F32),
-            pltpu.SemaphoreType.DMA((N_DP,)),
+            pltpu.SemaphoreType.DMA((5 + N_DP,)),
         ],
         compiler_params=params(),
         name="hot_scatter",
     )(dp_at, ids, hi0, lo0, hi1, lo1)
 
 
-def serve_kernel(m, with_hits, wanted, table, rows, *refs):
+def serve_kernel(m, with_hits, wanted, table_h, rows, *refs):
     if with_hits:
-        hits, match, res, count_acc, sems = refs
+        hits, table, match, res, count_acc, sems = refs
     else:
-        match, res, sems = refs
+        table, match, res, sems = refs
+    load = pltpu.make_async_copy(table_h, table, sems.at[0])
+    load.start()
     shards, lanes = wanted.shape
     capacity = lanes // MB
     count = table.shape[0]
@@ -394,17 +423,25 @@
                     if other != m:
                         add_hits(ones_of(part, other, j))
         at = pl.ds(pl.multiple_of(b * block, block), block)
+
+        @pl.when(b == 0)
+        def _():
+            load.wait()
+
         res[at, :] = jnp.dot(match[...], table[...], preferred_element_type=F32).astype(BF)
-        pltpu.make_async_copy(res.at[at, :], rows.at[at, :], sems.at[b]).start()
+        pltpu.make_async_copy(res.at[at, :], rows.at[at, :], sems.at[1 + b]).start()
         return carry
 
     steps = shards // per
     lax.fori_loop(0, steps, body, 0)
     if with_hits:
-        hits[...] = jnp.sum(count_acc[...].astype(F32), axis=0, keepdims=True)
+        total = jnp.sum(count_acc[...].astype(F32), axis=0, keepdims=True)
+        size = count // N_DP
+        for p in range(N_DP):
+            hits[p : p + 1, :] = total[:, p * size : (p + 1) * size]
     for b in range(steps):
         at = pl.ds(b * block, block)
-        pltpu.make_async_copy(res.at[at, :], rows.at[at, :], sems.at[b]).wait()
+        pltpu.make_async_copy(res.at[at, :], rows.at[at, :], sems.at[1 + b]).wait()
 
 
 def serve(m, with_hits, wanted, table):
@@ -416,12 +453,18 @@
     extra = [pltpu.VMEM((16, count), BF)] if with_hits else []
     return pl.pallas_call(
         lambda *refs: serve_kernel(m, with_hits, *refs),
-        in_specs=[VMEM, VMEM],
+        in_specs=[VMEM, HBM],
         out_specs=(HBM, VMEM) if with_hits else HBM,
-        out_shape=(rows, jax.ShapeDtypeStruct((1, count), F32)) if with_hits else rows,
-        scratch_shapes=[pltpu.VMEM((512, count), BF), pltpu.VMEM((slots, width), BF)]
+        out_shape=(rows, jax.ShapeDtypeStruct((N_DP, count // N_DP), F32))
+        if with_hits
+        else rows,
+        scratch_shapes=[
+            pltpu.VMEM(table.shape, BF),
+            pltpu.VMEM((512, count), BF),
+            pltpu.VMEM((slots, width), BF),
+        ]
         + extra
-        + [pltpu.SemaphoreType.DMA((shards // 8,))],
+        + [pltpu.SemaphoreType.DMA((1 + shards // 8,))],
         compiler_params=params(),
         name="serve_rows",
     )(wanted, table)
@@ -452,18 +495,25 @@
     block = match.shape[0]
     tiles = id_tiles(wanted, 0)
     subs = iota((block, 128), 0).astype(jnp.int16)
-    load.wait()
+    steps = res.shape[0] // block
 
     def body(b, carry):
         at = pl.multiple_of(b * block, block)
         owner_match(tiles, at, match, subs)
-        res[pl.ds(at, block), :] = jnp.dot(match[...], grads[...], preferred_element_type=F32)
+
+        @pl.when(b == 0)
+        def _():
+            load.wait()
+
+        rows = pl.ds(at, block)
+        res[rows, :] = jnp.dot(match[...], grads[...], preferred_element_type=F32)
+        pltpu.make_async_copy(res.at[rows, :], out.at[rows, :], sems.at[1 + b]).start()
         return carry
 
-    lax.fori_loop(0, res.shape[0] // block, body, 0)
-    done = pltpu.make_async_copy(res, out, sems.at[1])
-    done.start()
-    done.wait()
+    lax.fori_loop(0, steps, body, 0)
+    for b in range(steps):
+        rows = pl.ds(b * block, block)
+        pltpu.make_async_copy(res.at[rows, :], out.at[rows, :], sems.at[1 + b]).wait()
 
 
 def owner_first(wanted, grads, count):
@@ -475,9 +525,9 @@
         out_shape=jax.ShapeDtypeStruct((count, width), F32),
         scratch_shapes=[
             pltpu.VMEM((slots, width), BF),
-            pltpu.VMEM((512, slots), BF),
+            pltpu.VMEM((256, slots), BF),
             pltpu.VMEM((count, width), F32),
-            pltpu.SemaphoreType.DMA((2,)),
+            pltpu.SemaphoreType.DMA((1 + count // 256,)),
         ],
         compiler_params=params(),
         name="owner_first",
@@ -485,8 +535,8 @@
 
 
 def owner_second_kernel(at_ref, wanted, hits, grads_h, prev_h, *refs):
-    outs = refs[:N_DP]
-    grads, prev, match, res, sems = refs[N_DP:]
+    outs = refs[:N_X]
+    other, grads, prev, match, res, sems = refs[N_X:]
     size = match.shape[0]
     load = pltpu.make_async_copy(grads_h, grads, sems.at[0])
     load.start()
@@ -494,24 +544,45 @@
     load_prev.start()
     tiles = id_tiles(wanted, 1)
     subs = iota((size, 128), 0).astype(jnp.int16)
-    load.wait()
-    load_prev.wait()
 
     def body(k, carry):
-        chunk = (at_ref[0] + k) & (N_DP - 1)
+        x = ((at_ref[0] >> 1) + k) & (N_X - 1)
+        chunk = x * 2 + ((at_ref[0] & 1) ^ (1 - (k >> 2)))
         at = pl.multiple_of(chunk * size, size)
         owner_match(tiles, at, match, subs)
+
+        @pl.when(k == 0)
+        def _():
+            load.wait()
+
         total = jnp.dot(match[...], grads[...], preferred_element_type=F32)
+
+        @pl.when(k == 0)
+        def _():
+            load_prev.wait()
+
         total = total + prev[pl.ds(at, size), :]
         res[k, :size, :] = total.astype(BF)
         mine = hits[pl.ds(chunk, 1), :]
         res[k, size:, :] = jnp.broadcast_to(mine, (16, size)).astype(BF)
+
+        @pl.when(k < N_X)
+        def _():
+            place = k & (N_X - 1)
+            pltpu.make_async_copy(res.at[k], other.at[place], sems.at[2 + k]).start()
+
+        for j in range(N_X):
+
+            @pl.when(k == N_X + j)
+            def _():
+                pltpu.make_async_copy(res.at[k], outs[j], sems.at[2 + k]).start()
+
         return carry
 
     lax.fori_loop(0, N_DP, body, 0)
-    done = load_all([(res.at[k], outs[k]) for k in range(N_DP)], sems)
-    for c in done:
-        c.wait()
+    for j in range(N_X):
+        pltpu.make_async_copy(res.at[j], other.at[j], sems.at[2 + j]).wait()
+        pltpu.make_async_copy(res.at[N_X + j], outs[j], sems.at[2 + N_X + j]).wait()
 
 
 def owner_second(dp_at, wanted, hits, grads, prev):
@@ -521,8 +592,9 @@
     return pl.pallas_call(
         owner_second_kernel,
         in_specs=[SMEM, VMEM, VMEM, HBM, HBM],
-        out_specs=(HBM,) * N_DP,
-        out_shape=(jax.ShapeDtypeStruct((size + 16, width), BF),) * N_DP,
+        out_specs=(HBM,) * (N_X + 1),
+        out_shape=(jax.ShapeDtypeStruct((size + 16, width), BF),) * N_X
+        + (jax.ShapeDtypeStruct((N_X, size + 16, width), BF),),
         scratch_shapes=[
             pltpu.VMEM((slots, width), BF),
             pltpu.VMEM((count, width), F32),
@@ -548,89 +620,92 @@
     return table - learn_rate * grad / jnp.sqrt(accum_new), accum_new
 
 
-def cold_update_kernel(at_ref, table_h, accum_h, bits_h, *refs):
-    parts_h = refs[:N_DP]
-    out = refs[N_DP]
-    parts, table, accum, bits, res, sems = refs[N_DP + 1 :]
+def pick_kernel(at_ref, table_h, bits_h, table_out, bits_out, table, bits, sems):
     size = table.shape[0]
-    at = pl.multiple_of(at_ref[0] * size, size)
-    copies = load_all(
-        [(parts_h[k], parts.at[k]) for k in range(N_DP)]
-        + [
-            (table_h.at[pl.ds(at, size), :], table),
-            (accum_h, accum),
-            (bits_h.at[pl.ds(at, size), :], bits),
+    rows = pl.ds(pl.multiple_of(at_ref[0] * size, size), size)
+    for pairs in (
+        [(table_h.at[rows, :], table), (bits_h.at[rows, :], bits)],
+        [(table, table_out), (bits, bits_out)],
+    ):
+        for c in load_all(pairs, sems):
+            c.wait()
+
+
+def pick(dp_at, table, bits):
+    shape = (table.shape[0] // N_DP, table.shape[1])
+    return pl.pallas_call(
+        pick_kernel,
+        in_specs=[SMEM, HBM, HBM],
+        out_specs=(HBM, HBM),
+        out_shape=(
+            jax.ShapeDtypeStruct(shape, table.dtype),
+            jax.ShapeDtypeStruct(shape, bits.dtype),
+        ),
+        scratch_shapes=[
+            pltpu.VMEM(shape, table.dtype),
+            pltpu.VMEM(shape, bits.dtype),
+            pltpu.SemaphoreType.DMA((2,)),
         ],
-        sems,
-    )
+        compiler_params=params(),
+        name="pick_rows",
+    )(dp_at, table, bits)
+
+
+def cold_update_kernel(at_ref, table, accum, bits, *refs):
+    parts = refs[:N_X]
+    out = refs[N_X]
+    size = table.shape[0]
     eye = iota((size, size), 0) == iota((size, size), 1)
-    for c in copies:
-        c.wait()
-    total = parts[0].astype(F32)
-    for k in range(1, N_DP):
-        total = total + parts[k].astype(F32)
+    total = parts[0][...].astype(F32)
+    for k in range(1, N_X):
+        total = total + parts[k][...].astype(F32)
     touched = to_col(total[size : size + 1], eye)
     averaged = total[:size] / jnp.maximum(touched, 1.0)
-    old = to_col(accum[pl.ds(at_ref[0], 1), :], eye)
+    at = at_ref[0] * 2
+    old = jnp.concatenate([accum[pl.ds(at, 1), :], accum[pl.ds(at + 1, 1), :]], axis=1)
+    old = to_col(old, eye)
     updated, accum_new = adagrad(table[...].astype(F32), old, averaged)
     grid_step = jnp.max(jnp.abs(updated), axis=-1, keepdims=True) / 8.0
     dither = bits[...].astype(F32) * (1.0 / 65280.0) - 0.5
-    res[:size, :] = jnp.where(touched > 0.5, updated + grid_step * dither, updated).astype(BF)
+    out[:size, :] = jnp.where(touched > 0.5, updated + grid_step * dither, updated).astype(BF)
     row = to_row(accum_new, eye)
     high = row.astype(BF).astype(F32)
     middle = (row - high).astype(BF).astype(F32)
     low = (row - high) - middle
     which = iota((16, size), 0)
     packed = jnp.where(which == 0, high, jnp.where(which == 1, middle, low))
-    res[size:, :] = packed.astype(BF)
-    done = pltpu.make_async_copy(res, out, sems.at[0])
-    done.start()
-    done.wait()
+    out[size:, :] = packed.astype(BF)
 
 
 def cold_update(dp_at, table, accum, bits, parts):
-    width = table.shape[1]
-    size = table.shape[0] // N_DP
-    packed = parts[0].shape
     return pl.pallas_call(
         cold_update_kernel,
-        in_specs=[SMEM] + [HBM] * (3 + N_DP),
-        out_specs=HBM,
-        out_shape=jax.ShapeDtypeStruct(packed, BF),
-        scratch_shapes=[
-            pltpu.VMEM((N_DP,) + packed, BF),
-            pltpu.VMEM((size, width), BF),
-            pltpu.VMEM(accum.shape, F32),
-            pltpu.VMEM((size, width), jnp.int32),
-            pltpu.VMEM(packed, BF),
-            pltpu.SemaphoreType.DMA((N_DP + 3,)),
-        ],
-        compiler_params=params(),
+        in_specs=[SMEM] + [VMEM] * (3 + N_X),
+        out_specs=VMEM,
+        out_shape=jax.ShapeDtypeStruct(parts[0].shape, BF),
+        compiler_params=small_params(),
         name="cold_update",
     )(dp_at, table, accum, bits, *parts)
 
 
 def cold_join_kernel(at_ref, *refs):
     parts = refs[:N_DP]
-    out, accum_out, pieces, sems = refs[N_DP:]
+    out, accum_out, sems = refs[N_DP:]
     size = out.shape[0] // N_DP
-    copies = []
-    for k in range(N_DP):
-        chunk = (at_ref[0] - k) & (N_DP - 1)
+    done = []
+    for i in range(N_DP):
+        chunk = chunk_of(at_ref[0], i)
         dst = out.at[pl.ds(pl.multiple_of(chunk * size, size), size), :]
-        copies.append(pltpu.make_async_copy(parts[k].at[pl.ds(0, size), :], dst, sems.at[k]))
-        copies.append(
-            pltpu.make_async_copy(
-                parts[k].at[pl.ds(size, 16), :], pieces.at[chunk], sems.at[N_DP + k]
-            )
-        )
-    for c in copies:
-        c.start()
-    for c in copies:
+        done.append(pltpu.make_async_copy(parts[i].at[pl.ds(0, size), :], dst, sems.at[i]))
+        done[i].start()
+    for i in range(N_DP):
+        chunk = chunk_of(at_ref[0], i)
+        rows = parts[i][size:, :].astype(F32)
+        row = (rows[2:3] + rows[1:2]) + rows[0:1]
+        accum_out[pl.ds(chunk * 2, 1), :] = row[:, :128]
+        accum_out[pl.ds(chunk * 2 + 1, 1), :] = row[:, 128:]
+    for c in done:
         c.wait()
-    for p in range(N_DP):
-        rows = pieces[p].astype(F32)
-        accum_out[p : p + 1, :] = (rows[2:3] + rows[1:2]) + rows[0:1]
 
 
 def cold_join(dp_at, parts):
@@ -638,68 +713,86 @@
     size = parts[0].shape[0] - 16
     return pl.pallas_call(
         cold_join_kernel,
-        in_specs=[SMEM] + [HBM] * N_DP,
+        in_specs=[SMEM] + [VMEM] * N_DP,
         out_specs=(HBM, VMEM),
         out_shape=(
             jax.ShapeDtypeStruct((N_DP * size, width), BF),
-            jax.ShapeDtypeStruct((N_DP, size), F32),
+            jax.ShapeDtypeStruct((N_DP * size // 128, 128), F32),
         ),
+        scratch_shapes=[pltpu.SemaphoreType.DMA((N_DP,))],
+        compiler_params=small_params(),
+        name="cold_join",
+    )(dp_at, *parts)
+
+
+def pair_sum_kernel(*refs):
+    mine_h = refs[:N_X]
+    other_h = refs[N_X]
+    outs = refs[N_X + 1 : 2 * N_X + 1]
+    mine, other, sems = refs[2 * N_X + 1 :]
+    copies = load_all([(mine_h[k], mine.at[k]) for k in range(N_X)] + [(other_h, other)], sems)
+    for c in copies:
+        c.wait()
+    mine[...] = (mine[...].astype(F32) + other[...].astype(F32)).astype(mine.dtype)
+    done = load_all([(mine.at[k], outs[k]) for k in range(N_X)], sems)
+    for c in done:
+        c.wait()
+
+
+def pair_sum(mine, other):
+    outs = tuple(jax.ShapeDtypeStruct(part.shape, part.dtype) for part in mine)
+    return pl.pallas_call(
+        pair_sum_kernel,
+        in_specs=[HBM] * (N_X + 1),
+        out_specs=(HBM,) * N_X,
+        out_shape=outs,
         scratch_shapes=[
-            pltpu.VMEM((N_DP, 16, width), BF),
-            pltpu.SemaphoreType.DMA((2 * N_DP,)),
+            pltpu.VMEM(other.shape, other.dtype),
+            pltpu.VMEM(other.shape, other.dtype),
+            pltpu.SemaphoreType.DMA((N_X + 1,)),
         ],
         compiler_params=params(),
-        name="cold_join",
-    )(dp_at, *parts)
+        name="pair_sum",
+    )(*mine, other)
 
 
 def sum_parts_kernel(*refs):
-    parts_h = refs[:N_DP]
-    out, parts, sems = refs[N_DP:]
-    copies = load_all([(parts_h[k], parts.at[k]) for k in range(N_DP)], sems)
-    for c in copies:
-        c.wait()
-    out[...] = jnp.sum(parts[...], axis=0)
+    parts = refs[:N_X]
+    out = refs[N_X]
+    out[...] = (parts[0][...] + parts[1][...]) + (parts[2][...] + parts[3][...])
 
 
 def sum_parts(parts):
-    shape = parts[0].shape
     return pl.pallas_call(
         sum_parts_kernel,
-        in_specs=[HBM] * N_DP,
+        in_specs=[VMEM] * N_X,
         out_specs=VMEM,
-        out_shape=jax.ShapeDtypeStruct(shape, F32),
-        scratch_shapes=[
-            pltpu.VMEM((N_DP,) + shape, F32),
-            pltpu.SemaphoreType.DMA((N_DP,)),
-        ],
-        compiler_params=params(),
+        out_shape=jax.ShapeDtypeStruct(parts[0].shape, F32),
+        compiler_params=small_params(),
         name="sum_parts",
     )(*parts)
 
 
 def hot_update_kernel(at_ref, table_h, accum_h, *refs):
-    grads_h = refs[:N_DP]
-    out, accum_out, table, accum, grads, res, sems = refs[N_DP:]
-    size = grads.shape[1]
-    copies = load_all(
-        [(table_h, table), (accum_h, accum)]
-        + [(grads_h[k], grads.at[k]) for k in range(N_DP)],
-        sems,
-    )
+    grads = refs[:N_DP]
+    out, accum_out, table, accum, res, sems = refs[N_DP:]
+    size = grads[0].shape[0]
+    copies = load_all([(table_h, table), (accum_h, accum)], sems)
     eye = iota((size, size), 0) == iota((size, size), 1)
     for c in copies:
         c.wait()
+    done = []
     for k in range(N_DP):
-        chunk = (at_ref[0] - k) & (N_DP - 1)
+        chunk = chunk_of(at_ref[0], k)
         rows = pl.ds(pl.multiple_of(chunk * size, size), size)
         old = to_col(accum[pl.ds(chunk, 1), :], eye)
-        updated, accum_new = adagrad(table[rows, :], old, grads[k])
+        updated, accum_new = adagrad(table[rows, :], old, grads[k][...])
         res[rows, :] = updated
         accum_out[pl.ds(chunk, 1), :] = to_row(accum_new, eye)
-    done = pltpu.make_async_copy(res, out, sems.at[0])
-    done.start()
-    done.wait()
+        done.append(pltpu.make_async_copy(res.at[rows, :], out.at[rows, :], sems.at[2 + k]))
+        done[k].start()
+    for c in done:
+        c.wait()
 
 
 def hot_update(dp_at, table, accum, grads):
@@ -707,7 +800,7 @@
     size = count // N_DP
     return pl.pallas_call(
         hot_update_kernel,
-        in_specs=[SMEM] + [HBM] * (2 + N_DP),
+        in_specs=[SMEM] + [HBM] * 2 + [VMEM] * N_DP,
         out_specs=(HBM, VMEM),
         out_shape=(
             jax.ShapeDtypeStruct((count, width), F32),
@@ -716,11 +809,10 @@
         scratch_shapes=[
             pltpu.VMEM((count, width), F32),
             pltpu.VMEM((N_DP, size), F32),
-            pltpu.VMEM((N_DP, size, width), F32),
             pltpu.VMEM((count, width), F32),
             pltpu.SemaphoreType.DMA((2 + N_DP,)),
         ],
-        compiler_params=params(),
+        compiler_params=small_params(),
         name="hot_update",
     )(dp_at, table, accum, *grads)
 
@@ -729,16 +821,25 @@
     return lax.all_to_all(value, axis, split_axis=0, concat_axis=0, tiled=True)
 
 
-def shift(value, k):
-    return lax.ppermute(value, "dp", [(i, (i + k) % N_DP) for i in range(N_DP)])
+def along_x(value, k):
+    perm = [(i, ((i // 2 + k) % N_X) * 2 + i % 2) for i in range(N_DP)]
+    return lax.ppermute(value, "dp", perm)
+
+
+def to_partner(value):
+    return lax.ppermute(value, "dp", [(i, i ^ 1) for i in range(N_DP)])
 
 
 def to_owners(parts):
-    return [parts[0]] + [shift(parts[k], k) for k in range(1, N_DP)]
+    *mine, other = parts
+    other = to_partner(other)
+    mine = pair_sum(mine, other)
+    return [mine[0]] + [along_x(mine[k], k) for k in range(1, N_X)]
 
 
 def to_all(part):
-    return [part] + [shift(part, k) for k in range(1, N_DP)]
+    along = [part] + [along_x(part, k) for k in range(1, N_X)]
+    return along + [to_partner(value) for value in along]
 
 
 def step(
@@ -776,7 +877,8 @@
             rows, hits = rows
         rows = exchange(rows.reshape(shards, capacity, row_width), "shard")
         fetched.append(rows.reshape(slots, row_width))
-    xh = hot_rows(hot_ids, hot_table)
+    own_table, own_bits = pick(dp_at, cold_table, dither_bits)
+    xh = hot_rows(hot_ids, hot_table, cold_slots)
 
     owned = []
     hot_parts = []
@@ -799,22 +901,21 @@
 
     hot_grads = hot_scatter(dp_at, hot_ids.T, *hot_parts, hot_count)
     hot_grads = to_owners(hot_grads)
-    hot_sum = sum_parts(hot_grads)
-    hot_size = hot_sum.shape[0]
-    hot_sum = exchange(hot_sum.reshape(shards, hot_size // shards, row_width), "shard")
-    hot_sum = jnp.sum(hot_sum, axis=0)
-    hot_all = exchange(jnp.broadcast_to(hot_sum[None], (shards,) + hot_sum.shape), "shard")
-    hot_all = to_all(hot_all.reshape(hot_size, row_width))
+    hot_all = sum_parts(hot_grads)
+    step_bit = 1
+    while step_bit < shards:
+        perm = [(i, i ^ step_bit) for i in range(shards)]
+        hot_all = hot_all + lax.ppermute(hot_all, "shard", perm)
+        step_bit *= 2
+    hot_all = to_all(hot_all)
     hot_out, hot_accum_out = hot_update(
         dp_at, hot_table, hot_accum.reshape(N_DP, -1), hot_all
     )
 
     first = owner_first(wanted, owned[0], row_count)
-    parts = owner_second(dp_at, wanted, hits.reshape(N_DP, -1), owned[1], first)
+    parts = owner_second(dp_at, wanted, hits, owned[1], first)
     parts = to_owners(parts)
-    packed = cold_update(
-        dp_at, cold_table, cold_accum.reshape(N_DP, -1), dither_bits, parts
-    )
+    packed = cold_update(dp_at, own_table, cold_accum.reshape(-1, 128), own_bits, parts)
     parts = to_all(packed)
     cold_out, cold_accum_out = cold_join(dp_at, parts)
     return (cold_out, cold_accum_out.reshape(-1), hot_out, hot_accum_out.reshape(-1))

time: 293 us -> 255 us (0.87)
  starting transfers between devices: 83.1 us -> 58.6 us
  Pallas kernels: 124 us -> 108 us
    pallas_call x5 -> x8, Pallas kernels: 48.5 us -> 19.9 us  [the longest x1 6.64 us: hot_rows(): pl.pallas_call(hot_rows_kernel, in_specs=[HBM] * 3, out_specs=HBM, out_sh...]
    all_to_all x6 -> x4, starting transfers between devices: 46.4 us -> 26.8 us  [exchange(): return lax.all_to_all(value, axis, split_axis=0, concat_axis=0, tiled=True)]
    unnamed x14 -> x29, local copies, waits for them, and re-layouts: 5.1 us -> 11.8 us
    ppermute x28 -> x27, starting transfers between devices: 36.7 us -> 31.8 us  [the longest x12 17.9 us: along_x(): return lax.ppermute(value, 'dp', perm)]
    pallas_call x1, Pallas kernels: 8.24 us -> 13.1 us  [hot_scatter(): pl.pallas_call(hot_scatter_kernel, in_specs=[SMEM] + [HBM] * 5, out_specs...]
    reshape x4 -> x0, local copies, waits for them, and re-layouts: 4.21 us -> none  [the longest x1 1.6 us: step(): hot_sum.reshape(shards, hot_size // shards, row_width)]
    ppermute x28 -> x27, waiting for transfers between devices: 21.6 us -> 25.3 us  [the longest x5 16.1 us: step(): hot_all = hot_all + lax.ppermute(hot_all, 'shard', perm)]
    pallas_call x2, Pallas kernels: 11.5 us -> 14.8 us  [serve(): pl.pallas_call(lambda *refs: serve_kernel(m, with_hits, *refs), in_specs=...]
  transfers between devices with their start and end apart: 34 -> 31, of which waited for: 13 -> 12; matrix products, arithmetic and copies ran while one was open for 3% -> 2% of each run, Pallas kernels for 30% -> 40%
where the time goes in v5:
time: 255 us; the launch traced here: 252 us
  Pallas kernels  108 us (42%)
  starting transfers between devices  58.6 us (23%)
  waiting for transfers between devices  49 us (19%)
  blocking collectives  20 us (8%)
  local copies, waits for them, and re-layouts  11.9 us (5%)
  other arithmetic  3.21 us (1%)
    pallas_call x2, Pallas kernels, backprop(): pl.pallas_call(lambda *refs: step_kernel(m, *refs), in_specs=[HBM] * 9, o...  42.7 us
    all_to_all x4, starting transfers between devices, exchange(): return lax.all_to_all(value, axis, split_axis=0, concat_axis=0, tiled=True)  26.8 us
    all_to_all x4, waiting for transfers between devices, exchange(): return lax.all_to_all(value, axis, split_axis=0, concat_axis=0, tiled=True)  23.7 us
    all_to_all x1, blocking collectives, exchange(): return lax.all_to_all(value, axis, split_axis=0, concat_axis=0, tiled=True)  20 us
    ppermute x12, starting transfers between devices, along_x(): return lax.ppermute(value, 'dp', perm)  17.9 us
    ppermute x5, waiting for transfers between devices, step(): hot_all = hot_all + lax.ppermute(hot_all, 'shard', perm)  16.1 us
    pallas_call x2, Pallas kernels, serve(): pl.pallas_call(lambda *refs: serve_kernel(m, with_hits, *refs), in_specs=...  14.8 us
    pallas_call x1, Pallas kernels, hot_scatter(): pl.pallas_call(hot_scatter_kernel, in_specs=[SMEM] + [HBM] * 5, out_specs...  13.1 us
  transfers between devices with their start and end apart: 31, of which 12 were waited for; matrix products, arithmetic and copies ran while one was open for 2% of the time, Pallas kernels for 40%

profile of v5, /device:TPU:8, one launch (start us, length us, event | category | flops | bytes accessed | tf_op | source)
XLA Modules:
  0.0 252.0 jit_solution(4159967898399705085)
XLA Ops:
  0.6 0.8 copy.24
  1.4 0.9 fusion
  2.4 20.0 %all_to_all.31 = s32[32,1,128]{2,1,0:T(1,128)} all-to-all(s32[32,1,128]{2,1,0:T(1,128)S(1)} %all_to_all.19), channel_id=1, replica_groups=mesh['shard'=32,'dp'=8] {'shard'}, dimensions={0} | all-to-all | bytes 32768 | tf_op jit(solution)/shard_map/all_to_all | solution.py:821
  22.4 6.6 %serve_rows.3 = bf16[2048,256]{1,0:T(8,128)(2,1)} custom-call(s32[32,128]{1,0:T(8,128)} %bitcast.28, bf16[2048,256]{1,0:T(8,128)(2,1)} %refs_1_.3), custom_call_target="tpu_custom_call" | custom-call | tf_op jit(solution)/shard_map/serve_rows/pallas_call | solution.py:454
  29.0 5.7 %all-to-all-start.3 = ((bf16[32,64,256]{2,1,0:T(8,128)(2,1)}), bf16[32,64,256]{2,1,0:T(8,128)(2,1)}, u32[]{:S(2)}, u32[]{:S(2)}) async-start(bf16[32,64,256]{2,1,0:T(8,128)(2,1)} %bitcast.24), calls=%async_computation.3 | async-start | bytes 2097152 | tf_op jit(solution)/shard_map/all_to_all | solution.py:821
  34.7 8.2 %serve_rows.2 = (bf16[2048,256]{1,0:T(8,128)(2,1)}, f32[8,256]{1,0:T(8,128)}) custom-call(s32[32,128]{1,0:T(8,128)} %bitcast.29, bf16[2048,256]{1,0:T(8,128)(2,1)} %refs_1_.3), custom_call_target="tpu_custom_call" | custom-call | tf_op jit(solution)/shard_map/serve_rows/pallas_call | solution.py:454
  42.9 18.9 %all-to-all-done.3 = bf16[32,64,256]{2,1,0:T(8,128)(2,1)} async-done(((bf16[32,64,256]{2,1,0:T(8,128)(2,1)}), bf16[32,64,256]{2,1,0:T(8,128)(2,1)}, u32[]{:S(2)}, u32[]{:S(2)}) %all-to-all-start.3) | async-done | bytes 1048608 | tf_op jit(solution)/shard_map/all_to_all | solution.py:821
  61.9 5.6 %all-to-all-start.1 = ((bf16[32,64,256]{2,1,0:T(8,128)(2,1)}), bf16[32,64,256]{2,1,0:T(8,128)(2,1)}, u32[]{:S(2)}, u32[]{:S(2)}) async-start(bf16[32,64,256]{2,1,0:T(8,128)(2,1)} %bitcast.26), calls=%async_computation.1 | async-start | bytes 2097152 | tf_op jit(solution)/shard_map/all_to_all | solution.py:821
  67.5 0.8 copy.27.later.refs_2_
  68.4 0.8 copy.26.hot_ids
  69.2 6.6 %hot_rows.1.refs_1_ = bf16[4096,256]{1,0:T(8,128)(2,1)} custom-call(s32[512,8]{1,0:T(8,128)} %copy.26.hot_ids, f32[1024,256]{1,0:T(8,128)} %table_h.3, s32[512,8]{1,0:T(8,128)} %copy.27.later.refs_2_), custom_call_target="tpu_custom_call" | custom-call | tf_op jit(solution)/shard_map/hot_rows/pallas_call | solution.py:88
  75.9 21.4 %train_step.3 = (bf16[2048,256]{1,0:T(8,128)(2,1)}, bf16[2048,256]{1,0:T(8,128)(2,1)}, bf16[2048,256]{1,0:T(8,128)(2,1)}) custom-call(bf16[2048,256]{1,0:T(8,128)(2,1)} %bitcast.14.refs_0_, bf16[4096,256]{1,0:T(8,128)(2,1)} %hot_rows.1.refs_1_, s32[512,8]{1,0:T(8,128)} %copy.27.later.refs_2_, s32[8,512]{1,0:T(8,128)} %bitcast.32, f32[1,512]{1,0:T(1,128)} %bitcast.36, ...), custom_call_target="tpu_custom_call" | custom-call | tf_op jit(solution)/shard_map/train_step/pallas_call | solution.py:283
  97.2 9.9 %all-to-all-start.4 = ((bf16[32,64,256]{2,1,0:T(8,128)(2,1)}), bf16[32,64,256]{2,1,0:T(8,128)(2,1)}, u32[]{:S(2)}, u32[]{:S(2)}) async-start(bf16[32,64,256]{2,1,0:T(8,128)(2,1)} %bitcast.27), calls=%async_computation.4 | async-start | bytes 2097152 | tf_op jit(solution)/shard_map/all_to_all | solution.py:821
  107.1 21.3 %train_step.2 = (bf16[2048,256]{1,0:T(8,128)(2,1)}, bf16[2048,256]{1,0:T(8,128)(2,1)}, bf16[2048,256]{1,0:T(8,128)(2,1)}) custom-call(bf16[2048,256]{1,0:T(8,128)(2,1)} %bitcast.6.refs_0_, bf16[4096,256]{1,0:T(8,128)(2,1)} %hot_rows.1.refs_1_, s32[512,8]{1,0:T(8,128)} %copy.27.later.refs_2_, s32[8,512]{1,0:T(8,128)} %bitcast.33, f32[1,512]{1,0:T(1,128)} %bitcast.37, ...), custom_call_target="tpu_custom_call" | custom-call | tf_op jit(solution)/shard_map/train_step/pallas_call | solution.py:283
  128.5 4.8 %all-to-all-done.4 = bf16[32,64,256]{2,1,0:T(8,128)(2,1)} async-done(((bf16[32,64,256]{2,1,0:T(8,128)(2,1)}), bf16[32,64,256]{2,1,0:T(8,128)(2,1)}, u32[]{:S(2)}, u32[]{:S(2)}) %all-to-all-start.4) | async-done | bytes 1048608 | tf_op jit(solution)/shard_map/all_to_all | solution.py:821
  133.2 5.6 %all-to-all-start.2 = ((bf16[32,64,256]{2,1,0:T(8,128)(2,1)}), bf16[32,64,256]{2,1,0:T(8,128)(2,1)}, u32[]{:S(2)}, u32[]{:S(2)}) async-start(bf16[32,64,256]{2,1,0:T(8,128)(2,1)} %bitcast.25), calls=%async_computation.2 | async-start | bytes 2097152 | tf_op jit(solution)/shard_map/all_to_all | solution.py:821
  138.9 13.1 %hot_scatter.1 = (f32[128,256]{1,0:T(8,128)}, f32[128,256]{1,0:T(8,128)}, f32[128,256]{1,0:T(8,128)}, f32[128,256]{1,0:T(8,128)}, f32[4,128,256]{2,1,0:T(8,128)}) custom-call(s32[1]{0:T(128)} %bitcast.at_ref, s32[8,512]{1,0:T(8,128)} %bitcast.34, bf16[2048,256]{1,0:T(8,128)(2,1)} %get-tuple-element.53.hi0, bf16[2048,256]{1,0:T(8,128)(2,1)} %get-tuple-element.54.lo0, ...), custom_call_target="tpu_custom_call" | custom-call | tf_op jit(solution)/shard_map/hot_scatter/pallas_call | solution.py:370
  152.0 2.2 collective-permute-done.11.refs_4_
  154.3 2.2 pair_sum.3
  156.5 1.6 collective-permute-start.12
  158.1 2.7 %collective-permute-start.13 = (f32[128,256]{1,0:T(8,128)}, f32[128,256]{1,0:T(8,128)}, u32[]{:S(2)}, u32[]{:S(2)}) collective-permute-start(f32[128,256]{1,0:T(8,128)} %get-tuple-element.64), channel_id=1, source_target_pairs={{0,4},{1,5},{2,6},{3,7},{4,0},{5,1},{6,2},{7,3},{8,12},{9,13},{10,... | collective-permute-start | bytes 393224 | tf_op jit(solution)/shard_map/ppermute | solution.py:826
  160.8 1.4 collective-permute-start.14
  162.2 8.0 %owner_first.1.prev_h = f32[2048,256]{1,0:T(8,128)} custom-call(s32[32,128]{1,0:T(8,128)} %bitcast.30, bf16[2048,256]{1,0:T(8,128)(2,1)} %bitcast.16.grads_h), custom_call_target="tpu_custom_call" | custom-call | tf_op jit(solution)/shard_map/owner_first/pallas_call | solution.py:521
  170.2 9.6 %owner_second.1 = (bf16[272,256]{1,0:T(8,128)(2,1)}, bf16[272,256]{1,0:T(8,128)(2,1)}, bf16[272,256]{1,0:T(8,128)(2,1)}, bf16[272,256]{1,0:T(8,128)(2,1)}, bf16[4,272,256]{2,1,0:T(8,128)(2,1)}) custom-call(s32[1]{0:T(128)} %bitcast.at_ref, s32[32,128]{1,0:T(8,128)} %bitcast.31, f32[8,256]{1,0:T(8,128)} %get-tuple-element.38.hits, ...), custom_call_target="tpu_custom_call" | custom-call | tf_op jit(solution)/shard_map/owner_second/pallas_call | solution.py:592
  179.9 0.9 copy-done.7
  180.8 1.1 sum_parts.1
  182.3 5.6 %collective-permute-done.15 = f32[128,256]{1,0:T(8,128)S(1)} collective-permute-done((f32[128,256]{1,0:T(8,128)S(1)}, f32[128,256]{1,0:T(8,128)S(1)}, u32[]{:S(2)}, u32[]{:S(2)}) %collective-permute-start.15) | collective-permute-done | bytes 131104 | tf_op jit(solution)/shard_map/ppermute | solution.py:908
  187.9 2.2 collective-permute-start.16
  190.0 4.5 %collective-permute-done.16 = f32[128,256]{1,0:T(8,128)S(1)} collective-permute-done((f32[128,256]{1,0:T(8,128)S(1)}, f32[128,256]{1,0:T(8,128)S(1)}, u32[]{:S(2)}, u32[]{:S(2)}) %collective-permute-start.16) | collective-permute-done | bytes 131104 | tf_op jit(solution)/shard_map/ppermute | solution.py:908
  194.5 1.8 collective-permute-start.17
  196.3 3.5 %collective-permute-done.17 = f32[128,256]{1,0:T(8,128)S(1)} collective-permute-done((f32[128,256]{1,0:T(8,128)S(1)}, f32[128,256]{1,0:T(8,128)S(1)}, u32[]{:S(2)}, u32[]{:S(2)}) %collective-permute-start.17) | collective-permute-done | bytes 131104 | tf_op jit(solution)/shard_map/ppermute | solution.py:908
  199.8 0.7 add.17
  200.5 2.4 collective-permute-start.18
  202.8 2.3 pair_sum.2
  205.1 0.7 collective-permute-start.1
  205.8 2.3 collective-permute-done.18
  208.1 1.0 add.18
  209.0 5.5 %collective-permute-start.19 = (f32[128,256]{1,0:T(8,128)S(1)}, f32[128,256]{1,0:T(8,128)S(1)}, u32[]{:S(2)}, u32[]{:S(2)}) collective-permute-start(f32[128,256]{1,0:T(8,128)S(1)} %add.18), channel_id=1, source_target_pairs={{0,128},{8,136},{16,144},{24,152},{32,160},{40,168},{48,176},{56,1... | collective-permute-start | bytes 393224 | tf_op jit(solution)/shard_map/ppermute | solution.py:908
  215.1 2.7 %collective-permute-start.3 = (bf16[272,256]{1,0:T(8,128)(2,1)}, bf16[272,256]{1,0:T(8,128)(2,1)}, u32[]{:S(2)}, u32[]{:S(2)}) collective-permute-start(bf16[272,256]{1,0:T(8,128)(2,1)} %get-tuple-element.50), channel_id=1, source_target_pairs={{0,6},{1,7},{2,0},{3,1},{4,2},{5,3},{6,4},{7,5},{8,14},{9,15},{10,... | collective-permute-start | bytes 417800 | tf_op jit(solution)/shard_map/ppermute | solution.py:826
  218.1 0.7 add.19.refs_0_
  218.8 0.6 collective-permute-start.20
  219.3 1.7 collective-permute-start.21
  221.0 0.7 copy-done.3
  221.7 1.0 collective-permute-start.22
  222.7 0.6 copy-done.5
  223.3 1.8 pick_rows.1
  225.1 0.9 copy-done.1
  226.1 0.9 copy-done.2
  227.0 0.9 copy-done.4
  227.9 0.9 copy-done.6
  228.8 0.9 copy-done.8
  229.7 0.7 copy-done.9
  230.4 1.3 cold_update.1.refs_0_
  231.7 1.5 collective-permute-start.6
  233.2 0.6 collective-permute-start.4
  233.8 2.9 %collective-permute-start.5 = (bf16[272,256]{1,0:T(8,128)(2,1)S(1)}, bf16[272,256]{1,0:T(8,128)(2,1)S(1)}, u32[]{:S(2)}, u32[]{:S(2)}) collective-permute-start(bf16[272,256]{1,0:T(8,128)(2,1)S(1)} %cold_update.1.refs_0_), channel_id=1, source_target_pairs={{0,4},{1,5},{2,6},{3,7},{4,0},{5,1},{6,2},{7,3},{8,12},{9,13},{10,... | collective-permute-start | bytes 417800 | tf_op jit(solution)/shard_map/ppermute | solution.py:826
  237.2 1.0 collective-permute-done.24.refs_5_
  238.8 1.9 collective-permute-done.4.refs_1_
  240.7 2.8 %collective-permute-done.5.refs_2_ = bf16[272,256]{1,0:T(8,128)(2,1)S(1)} collective-permute-done((bf16[272,256]{1,0:T(8,128)(2,1)S(1)}, bf16[272,256]{1,0:T(8,128)(2,1)S(1)}, u32[]{:S(2)}, u32[]{:S(2)}) %collective-permute-start.5) | collective-permute-done | bytes 139296 | tf_op jit(solution)/shard_map/ppermute | solution.py:826
  244.0 1.2 collective-permute-done.26.refs_7_
  245.2 1.2 copy-done
  246.4 0.7 copy-done.10
  247.1 3.1 %hot_update.1 = (f32[1024,256]{1,0:T(8,128)}, f32[8,128]{1,0:T(8,128)}) custom-call(s32[1]{0:T(128)} %bitcast.at_ref, f32[1024,256]{1,0:T(8,128)S(1)} %copy-done, f32[8,128]{1,0:T(8,128)S(1)} %bitcast.23, f32[128,256]{1,0:T(8,128)} %add.19.refs_0_, f32[128,256]{1,0:T(8,128)} %collective-permute-done.20.refs_1_, f32[128,256]{1,0:T(8,128)} %collective-permute-done.21.refs_2_, ...), custom_call_target="tpu_custom_call" | custom-call | tf_op jit(solution)/shard_map/hot_update/pallas_call | solution.py:801
  250.2 1.6 cold_join.1
  (50 shorter events, 3.1 us)
Async XLA Ops:
  29.0 32.9 %all-to-all-start.3 = ((bf16[32,64,256]{2,1,0:T(8,128)(2,1)}), bf16[32,64,256]{2,1,0:T(8,128)(2,1)}, u32[]{:S(2)}, u32[]{:S(2)}) async-start(bf16[32,64,256]{2,1,0:T(8,128)(2,1)} %bitcast.24), calls=%async_computation.3 | async-start | bytes 2097152 | tf_op jit(solution)/shard_map/all_to_all | solution.py:821
  42.9 24.6 %copy-start.11 = (s32[512,8]{0,1:T(8,128)S(1)}, s32[512,8]{0,1:T(8,128)}, u32[]{:S(2)}) copy-start(s32[512,8]{0,1:T(8,128)} %param.25) | copy-start | bytes 49156
  42.9 25.4 %copy-start.12 = (s32[512,8]{0,1:T(8,128)S(1)}, s32[512,8]{0,1:T(8,128)}, u32[]{:S(2)}) copy-start(s32[512,8]{0,1:T(8,128)} %param.24) | copy-start | bytes 49156
  61.9 35.3 %all-to-all-start.1 = ((bf16[32,64,256]{2,1,0:T(8,128)(2,1)}), bf16[32,64,256]{2,1,0:T(8,128)(2,1)}, u32[]{:S(2)}, u32[]{:S(2)}) async-start(bf16[32,64,256]{2,1,0:T(8,128)(2,1)} %bitcast.26), calls=%async_computation.1 | async-start | bytes 2097152 | tf_op jit(solution)/shard_map/all_to_all | solution.py:821
  97.2 36.0 %all-to-all-start.4 = ((bf16[32,64,256]{2,1,0:T(8,128)(2,1)}), bf16[32,64,256]{2,1,0:T(8,128)(2,1)}, u32[]{:S(2)}, u32[]{:S(2)}) async-start(bf16[32,64,256]{2,1,0:T(8,128)(2,1)} %bitcast.27), calls=%async_computation.4 | async-start | bytes 2097152 | tf_op jit(solution)/shard_map/all_to_all | solution.py:821
  133.2 37.0 %all-to-all-start.2 = ((bf16[32,64,256]{2,1,0:T(8,128)(2,1)}), bf16[32,64,256]{2,1,0:T(8,128)(2,1)}, u32[]{:S(2)}, u32[]{:S(2)}) async-start(bf16[32,64,256]{2,1,0:T(8,128)(2,1)} %bitcast.25), calls=%async_computation.2 | async-start | bytes 2097152 | tf_op jit(solution)/shard_map/all_to_all | solution.py:821
  151.9 2.3 collective-permute-start.11
  156.5 23.4 %collective-permute-start.12 = (f32[128,256]{1,0:T(8,128)}, f32[128,256]{1,0:T(8,128)}, u32[]{:S(2)}, u32[]{:S(2)}) collective-permute-start(f32[128,256]{1,0:T(8,128)} %get-tuple-element.63), channel_id=1, source_target_pairs={{0,2},{1,3},{2,4},{3,5},{4,6},{5,7},{6,0},{7,1},{8,10},{9,11},{10,... | collective-permute-start | bytes 393224 | tf_op jit(solution)/shard_map/ppermute | solution.py:826
  158.1 21.9 %collective-permute-start.13 = (f32[128,256]{1,0:T(8,128)}, f32[128,256]{1,0:T(8,128)}, u32[]{:S(2)}, u32[]{:S(2)}) collective-permute-start(f32[128,256]{1,0:T(8,128)} %get-tuple-element.64), channel_id=1, source_target_pairs={{0,4},{1,5},{2,6},{3,7},{4,0},{5,1},{6,2},{7,3},{8,12},{9,13},{10,... | collective-permute-start | bytes 393224 | tf_op jit(solution)/shard_map/ppermute | solution.py:826
  160.8 19.2 %collective-permute-start.14 = (f32[128,256]{1,0:T(8,128)}, f32[128,256]{1,0:T(8,128)}, u32[]{:S(2)}, u32[]{:S(2)}) collective-permute-start(f32[128,256]{1,0:T(8,128)} %get-tuple-element.65), channel_id=1, source_target_pairs={{0,6},{1,7},{2,0},{3,1},{4,2},{5,3},{6,4},{7,5},{8,14},{9,15},{10,... | collective-permute-start | bytes 393224 | tf_op jit(solution)/shard_map/ppermute | solution.py:826
  179.8 23.0 %collective-permute-start = (bf16[4,272,256]{2,1,0:T(8,128)(2,1)}, bf16[4,272,256]{2,1,0:T(8,128)(2,1)}, u32[]{:S(2)}, u32[]{:S(2)}) collective-permute-start(bf16[4,272,256]{2,1,0:T(8,128)(2,1)} %get-tuple-element.46), channel_id=1, source_target_pairs={{0,1},{1,0},{2,3},{3,2},{4,5},{5,4},{6,7},{7,6},{8,9},{9,8},{10,11... | collective-permute-start | bytes 1671176 | tf_op jit(solution)/shard_map/ppermute | solution.py:830
  179.9 0.9 copy-start.7
  181.9 6.0 %collective-permute-start.15 = (f32[128,256]{1,0:T(8,128)S(1)}, f32[128,256]{1,0:T(8,128)S(1)}, u32[]{:S(2)}, u32[]{:S(2)}) collective-permute-start(f32[128,256]{1,0:T(8,128)S(1)} %sum_parts.1), channel_id=1, source_target_pairs={{0,8},{8,0},{16,24},{24,16},{32,40},{40,32},{48,56},{56,48},{64,72... | collective-permute-start | bytes 393224 | tf_op jit(solution)/shard_map/ppermute | solution.py:908
  187.9 6.6 %collective-permute-start.16 = (f32[128,256]{1,0:T(8,128)S(1)}, f32[128,256]{1,0:T(8,128)S(1)}, u32[]{:S(2)}, u32[]{:S(2)}) collective-permute-start(f32[128,256]{1,0:T(8,128)S(1)} %add.15), channel_id=1, source_target_pairs={{0,16},{8,24},{16,0},{24,8},{32,48},{40,56},{48,32},{56,40},{64,80... | collective-permute-start | bytes 393224 | tf_op jit(solution)/shard_map/ppermute | solution.py:908
  194.5 5.3 %collective-permute-start.17 = (f32[128,256]{1,0:T(8,128)S(1)}, f32[128,256]{1,0:T(8,128)S(1)}, u32[]{:S(2)}, u32[]{:S(2)}) collective-permute-start(f32[128,256]{1,0:T(8,128)S(1)} %add.16), channel_id=1, source_target_pairs={{0,32},{8,40},{16,48},{24,56},{32,0},{40,8},{48,16},{56,24},{64,96... | collective-permute-start | bytes 393224 | tf_op jit(solution)/shard_map/ppermute | solution.py:908
  200.5 7.6 %collective-permute-start.18 = (f32[128,256]{1,0:T(8,128)}, f32[128,256]{1,0:T(8,128)}, u32[]{:S(2)}, u32[]{:S(2)}) collective-permute-start(f32[128,256]{1,0:T(8,128)} %add.17), channel_id=1, source_target_pairs={{0,64},{8,72},{16,80},{24,88},{32,96},{40,104},{48,112},{56,120},{... | collective-permute-start | bytes 393224 | tf_op jit(solution)/shard_map/ppermute | solution.py:908
  205.1 15.9 %collective-permute-start.1 = (bf16[272,256]{1,0:T(8,128)(2,1)}, bf16[272,256]{1,0:T(8,128)(2,1)S(1)}, u32[]{:S(2)}, u32[]{:S(2)}) collective-permute-start(bf16[272,256]{1,0:T(8,128)(2,1)} %get-tuple-element.48), channel_id=1, source_target_pairs={{0,2},{1,3},{2,4},{3,5},{4,6},{5,7},{6,0},{7,1},{8,10},{9,11},{10,... | collective-permute-start | bytes 417800 | tf_op jit(solution)/shard_map/ppermute | solution.py:826
  209.0 9.1 %collective-permute-start.19 = (f32[128,256]{1,0:T(8,128)S(1)}, f32[128,256]{1,0:T(8,128)S(1)}, u32[]{:S(2)}, u32[]{:S(2)}) collective-permute-start(f32[128,256]{1,0:T(8,128)S(1)} %add.18), channel_id=1, source_target_pairs={{0,128},{8,136},{16,144},{24,152},{32,160},{40,168},{48,176},{56,1... | collective-permute-start | bytes 393224 | tf_op jit(solution)/shard_map/ppermute | solution.py:908
  214.6 8.1 %collective-permute-start.2 = (bf16[272,256]{1,0:T(8,128)(2,1)}, bf16[272,256]{1,0:T(8,128)(2,1)S(1)}, u32[]{:S(2)}, u32[]{:S(2)}) collective-permute-start(bf16[272,256]{1,0:T(8,128)(2,1)} %get-tuple-element.49), channel_id=1, source_target_pairs={{0,4},{1,5},{2,6},{3,7},{4,0},{5,1},{6,2},{7,3},{8,12},{9,13},{10,... | collective-permute-start | bytes 417800 | tf_op jit(solution)/shard_map/ppermute | solution.py:826
  215.1 10.1 %collective-permute-start.3 = (bf16[272,256]{1,0:T(8,128)(2,1)}, bf16[272,256]{1,0:T(8,128)(2,1)}, u32[]{:S(2)}, u32[]{:S(2)}) collective-permute-start(bf16[272,256]{1,0:T(8,128)(2,1)} %get-tuple-element.50), channel_id=1, source_target_pairs={{0,6},{1,7},{2,0},{3,1},{4,2},{5,3},{6,4},{7,5},{8,14},{9,15},{10,... | collective-permute-start | bytes 417800 | tf_op jit(solution)/shard_map/ppermute | solution.py:826
  218.8 14.4 %collective-permute-start.20 = (f32[128,256]{1,0:T(8,128)}, f32[128,256]{1,0:T(8,128)}, u32[]{:S(2)}, u32[]{:S(2)}) collective-permute-start(f32[128,256]{1,0:T(8,128)} %add.19.refs_0_), channel_id=1, source_target_pairs={{0,2},{1,3},{2,4},{3,5},{4,6},{5,7},{6,0},{7,1},{8,10},{9,11},{10,... | collective-permute-start | bytes 393224 | tf_op jit(solution)/shard_map/ppermute | solution.py:826
  219.3 14.5 %collective-permute-start.21 = (f32[128,256]{1,0:T(8,128)}, f32[128,256]{1,0:T(8,128)}, u32[]{:S(2)}, u32[]{:S(2)}) collective-permute-start(f32[128,256]{1,0:T(8,128)} %add.19.refs_0_), channel_id=1, source_target_pairs={{0,4},{1,5},{2,6},{3,7},{4,0},{5,1},{6,2},{7,3},{8,12},{9,13},{10,... | collective-permute-start | bytes 393224 | tf_op jit(solution)/shard_map/ppermute | solution.py:826
  221.0 0.7 copy-start.3
  221.7 15.0 %collective-permute-start.22 = (f32[128,256]{1,0:T(8,128)}, f32[128,256]{1,0:T(8,128)}, u32[]{:S(2)}, u32[]{:S(2)}) collective-permute-start(f32[128,256]{1,0:T(8,128)} %add.19.refs_0_), channel_id=1, source_target_pairs={{0,6},{1,7},{2,0},{3,1},{4,2},{5,3},{6,4},{7,5},{8,14},{9,15},{10,... | collective-permute-start | bytes 393224 | tf_op jit(solution)/shard_map/ppermute | solution.py:826
  222.7 0.7 copy-start.5
  223.3 13.4 %collective-permute-start.23 = (f32[128,256]{1,0:T(8,128)}, f32[128,256]{1,0:T(8,128)}, u32[]{:S(2)}, u32[]{:S(2)}) collective-permute-start(f32[128,256]{1,0:T(8,128)} %add.19.refs_0_), channel_id=1, source_target_pairs={{0,1},{1,0},{2,3},{3,2},{4,5},{5,4},{6,7},{7,6},{8,9},{9,8},{10,11... | collective-permute-start | bytes 393224 | tf_op jit(solution)/shard_map/ppermute | solution.py:830
  225.1 1.0 copy-start.1
  226.1 0.9 copy-start.2
  227.0 0.9 copy-start.4
  227.9 0.9 copy-start.6
  228.8 0.9 copy-start.8
  229.7 0.7 copy-start.9
  231.7 6.7 %collective-permute-start.6 = (bf16[272,256]{1,0:T(8,128)(2,1)S(1)}, bf16[272,256]{1,0:T(8,128)(2,1)S(1)}, u32[]{:S(2)}, u32[]{:S(2)}) collective-permute-start(bf16[272,256]{1,0:T(8,128)(2,1)S(1)} %cold_update.1.refs_0_), channel_id=1, source_target_pairs={{0,6},{1,7},{2,0},{3,1},{4,2},{5,3},{6,4},{7,5},{8,14},{9,15},{10,... | collective-permute-start | bytes 417800 | tf_op jit(solution)/shard_map/ppermute | solution.py:826
  233.2 7.5 %collective-permute-start.4 = (bf16[272,256]{1,0:T(8,128)(2,1)S(1)}, bf16[272,256]{1,0:T(8,128)(2,1)S(1)}, u32[]{:S(2)}, u32[]{:S(2)}) collective-permute-start(bf16[272,256]{1,0:T(8,128)(2,1)S(1)} %cold_update.1.refs_0_), channel_id=1, source_target_pairs={{0,2},{1,3},{2,4},{3,5},{4,6},{5,7},{6,0},{7,1},{8,10},{9,11},{10,... | collective-permute-start | bytes 417800 | tf_op jit(solution)/shard_map/ppermute | solution.py:826
  233.8 9.7 %collective-permute-start.5 = (bf16[272,256]{1,0:T(8,128)(2,1)S(1)}, bf16[272,256]{1,0:T(8,128)(2,1)S(1)}, u32[]{:S(2)}, u32[]{:S(2)}) collective-permute-start(bf16[272,256]{1,0:T(8,128)(2,1)S(1)} %cold_update.1.refs_0_), channel_id=1, source_target_pairs={{0,4},{1,5},{2,6},{3,7},{4,0},{5,1},{6,2},{7,3},{8,12},{9,13},{10,... | collective-permute-start | bytes 417800 | tf_op jit(solution)/shard_map/ppermute | solution.py:826
  236.7 1.6 collective-permute-start.24
  236.7 6.8 %collective-permute-start.25 = (f32[128,256]{1,0:T(8,128)}, f32[128,256]{1,0:T(8,128)S(1)}, u32[]{:S(2)}, u32[]{:S(2)}) collective-permute-start(f32[128,256]{1,0:T(8,128)} %collective-permute-done.21.refs_2_), channel_id=1, source_target_pairs={{0,1},{1,0},{2,3},{3,2},{4,5},{5,4},{6,7},{7,6},{8,9},{9,8},{10,11... | collective-permute-start | bytes 393224 | tf_op jit(solution)/shard_map/ppermute | solution.py:830
  238.3 11.9 %collective-permute-start.7 = (bf16[272,256]{1,0:T(8,128)(2,1)S(1)}, bf16[272,256]{1,0:T(8,128)(2,1)S(1)}, u32[]{:S(2)}, u32[]{:S(2)}) collective-permute-start(bf16[272,256]{1,0:T(8,128)(2,1)S(1)} %cold_update.1.refs_0_), channel_id=1, source_target_pairs={{0,1},{1,0},{2,3},{3,2},{4,5},{5,4},{6,7},{7,6},{8,9},{9,8},{10,11... | collective-permute-start | bytes 417800 | tf_op jit(solution)/shard_map/ppermute | solution.py:830
  238.4 11.8 %collective-permute-start.10 = (bf16[272,256]{1,0:T(8,128)(2,1)S(1)}, bf16[272,256]{1,0:T(8,128)(2,1)S(1)}, u32[]{:S(2)}, u32[]{:S(2)}) collective-permute-start(bf16[272,256]{1,0:T(8,128)(2,1)S(1)} %collective-permute-done.6.refs_3_), channel_id=1, source_target_pairs={{0,1},{1,0},{2,3},{3,2},{4,5},{5,4},{6,7},{7,6},{8,9},{9,8},{10,11... | collective-permute-start | bytes 417800 | tf_op jit(solution)/shard_map/ppermute | solution.py:830
  240.7 9.5 %collective-permute-start.8 = (bf16[272,256]{1,0:T(8,128)(2,1)S(1)}, bf16[272,256]{1,0:T(8,128)(2,1)S(1)}, u32[]{:S(2)}, u32[]{:S(2)}) collective-permute-start(bf16[272,256]{1,0:T(8,128)(2,1)S(1)} %collective-permute-done.4.refs_1_), channel_id=1, source_target_pairs={{0,1},{1,0},{2,3},{3,2},{4,5},{5,4},{6,7},{7,6},{8,9},{9,8},{10,11... | collective-permute-start | bytes 417800 | tf_op jit(solution)/shard_map/ppermute | solution.py:830
  243.5 6.7 %collective-permute-start.9 = (bf16[272,256]{1,0:T(8,128)(2,1)S(1)}, bf16[272,256]{1,0:T(8,128)(2,1)S(1)}, u32[]{:S(2)}, u32[]{:S(2)}) collective-permute-start(bf16[272,256]{1,0:T(8,128)(2,1)S(1)} %collective-permute-done.5.refs_2_), channel_id=1, source_target_pairs={{0,1},{1,0},{2,3},{3,2},{4,5},{5,4},{6,7},{7,6},{8,9},{9,8},{10,11... | collective-permute-start | bytes 417800 | tf_op jit(solution)/shard_map/ppermute | solution.py:830
  243.5 1.7 collective-permute-start.26
  245.2 1.2 copy-start
  246.4 0.7 copy-start.10

commit v6 on v5

--- a/solution.py
+++ b/solution.py
@@ -29,6 +29,10 @@
 
 def as_one(same):
     return jnp.where(same, jnp.ones(same.shape, BF), jnp.zeros(same.shape, BF))
+
+
+def mine_of(at, k, flip):
+    return (((at >> 1) + k) & (N_X - 1)) * 2 + ((at & 1) ^ flip)
 
 
 def chunk_of(at, i):
@@ -320,7 +324,8 @@
     block = match.shape[1]
     size = res.shape[0] // N_DP
     subs = iota((block, samples), 0).astype(jnp.int16)
-    copies[0].wait()
+    for c in copies:
+        c.wait()
 
     def body(b, carry):
         at = pl.multiple_of(b * block, block)
@@ -331,38 +336,22 @@
                 mine = jnp.broadcast_to(row, (16, samples)).astype(jnp.int16)
                 same = subs == jnp.concatenate([mine] * (block // 16), axis=0)
                 match[m, :, f * samples : (f + 1) * samples] = as_one(same)
-
-            @pl.when(b == 0)
-            def _():
-                copies[1 + 2 * m].wait()
-                copies[2 + 2 * m].wait()
-
             for part in parts:
                 term = jnp.dot(match[m], part[...], preferred_element_type=F32)
                 total = term if total is None else total + term
         res[pl.ds(at, block), :] = total
-        for q in range(block // size):
-            chunk = b * (block // size) + q
+        return carry
+
+    lax.fori_loop(0, res.shape[0] // block, body, 0)
+    done = []
+    for k in range(N_X):
+        for flip, dst in ((0, outs[k]), (1, other.at[k])):
+            chunk = mine_of(at_ref[0], k, flip)
             src = res.at[pl.ds(pl.multiple_of(chunk * size, size), size), :]
-            place = ((chunk >> 1) - (at_ref[0] >> 1)) & (N_X - 1)
-            mine = (chunk & 1) == (at_ref[0] & 1)
-            for k in range(N_X):
-
-                @pl.when(mine & (place == k))
-                def _():
-                    pltpu.make_async_copy(src, outs[k], sems.at[5 + k]).start()
-
-            @pl.when(jnp.logical_not(mine))
-            def _():
-                pltpu.make_async_copy(src, other.at[place], sems.at[5 + N_X + place]).start()
-
-        return carry
-
-    lax.fori_loop(0, res.shape[0] // block, body, 0)
-    for k in range(N_X):
-        src = res.at[pl.ds(0, size), :]
-        pltpu.make_async_copy(src, outs[k], sems.at[5 + k]).wait()
-        pltpu.make_async_copy(src, other.at[k], sems.at[5 + N_X + k]).wait()
+            done.append(pltpu.make_async_copy(src, dst, sems.at[2 * k + flip]))
+            done[-1].start()
+    for c in done:
+        c.wait()
 
 
 def hot_scatter(dp_at, ids, hi0, lo0, hi1, lo1, count):
@@ -423,16 +412,12 @@
                     if other != m:
                         add_hits(ones_of(part, other, j))
         at = pl.ds(pl.multiple_of(b * block, block), block)
-
-        @pl.when(b == 0)
-        def _():
-            load.wait()
-
         res[at, :] = jnp.dot(match[...], table[...], preferred_element_type=F32).astype(BF)
         pltpu.make_async_copy(res.at[at, :], rows.at[at, :], sems.at[1 + b]).start()
         return carry
 
     steps = shards // per
+    load.wait()
     lax.fori_loop(0, steps, body, 0)
     if with_hits:
         total = jnp.sum(count_acc[...].astype(F32), axis=0, keepdims=True)
@@ -489,122 +474,59 @@
         match[:, i * 128 : (i + 1) * 128] = as_one(same)
 
 
-def owner_first_kernel(wanted, grads_h, out, grads, match, res, sems):
-    load = pltpu.make_async_copy(grads_h, grads, sems.at[0])
-    load.start()
-    block = match.shape[0]
-    tiles = id_tiles(wanted, 0)
-    subs = iota((block, 128), 0).astype(jnp.int16)
-    steps = res.shape[0] // block
-
-    def body(b, carry):
-        at = pl.multiple_of(b * block, block)
-        owner_match(tiles, at, match, subs)
-
-        @pl.when(b == 0)
-        def _():
-            load.wait()
-
-        rows = pl.ds(at, block)
-        res[rows, :] = jnp.dot(match[...], grads[...], preferred_element_type=F32)
-        pltpu.make_async_copy(res.at[rows, :], out.at[rows, :], sems.at[1 + b]).start()
-        return carry
-
-    lax.fori_loop(0, steps, body, 0)
-    for b in range(steps):
-        rows = pl.ds(b * block, block)
-        pltpu.make_async_copy(res.at[rows, :], out.at[rows, :], sems.at[1 + b]).wait()
-
-
-def owner_first(wanted, grads, count):
-    slots, width = grads.shape
-    return pl.pallas_call(
-        owner_first_kernel,
-        in_specs=[VMEM, HBM],
-        out_specs=HBM,
-        out_shape=jax.ShapeDtypeStruct((count, width), F32),
-        scratch_shapes=[
-            pltpu.VMEM((slots, width), BF),
-            pltpu.VMEM((256, slots), BF),
-            pltpu.VMEM((count, width), F32),
-            pltpu.SemaphoreType.DMA((1 + count // 256,)),
-        ],
-        compiler_params=params(),
-        name="owner_first",
-    )(wanted, grads)
-
-
-def owner_second_kernel(at_ref, wanted, hits, grads_h, prev_h, *refs):
-    outs = refs[:N_X]
-    other, grads, prev, match, res, sems = refs[N_X:]
-    size = match.shape[0]
-    load = pltpu.make_async_copy(grads_h, grads, sems.at[0])
-    load.start()
-    load_prev = pltpu.make_async_copy(prev_h, prev, sems.at[1])
-    load_prev.start()
-    tiles = id_tiles(wanted, 1)
+def owner_kernel(flip, at_ref, wanted, hits, *refs):
+    grads_h = refs[:MB]
+    outs = refs[MB : -4]
+    grads, match, res, sems = refs[-4:]
+    size = match.shape[1]
+    copies = load_all([(grads_h[m], grads.at[m]) for m in range(MB)], sems)
+    tiles = [id_tiles(wanted, m) for m in range(MB)]
     subs = iota((size, 128), 0).astype(jnp.int16)
+    for c in copies:
+        c.wait()
 
     def body(k, carry):
-        x = ((at_ref[0] >> 1) + k) & (N_X - 1)
-        chunk = x * 2 + ((at_ref[0] & 1) ^ (1 - (k >> 2)))
+        chunk = mine_of(at_ref[0], k, flip)
         at = pl.multiple_of(chunk * size, size)
-        owner_match(tiles, at, match, subs)
-
-        @pl.when(k == 0)
-        def _():
-            load.wait()
-
-        total = jnp.dot(match[...], grads[...], preferred_element_type=F32)
-
-        @pl.when(k == 0)
-        def _():
-            load_prev.wait()
-
-        total = total + prev[pl.ds(at, size), :]
+        total = None
+        for m in range(MB):
+            owner_match(tiles[m], at, match.at[m], subs)
+            term = jnp.dot(match[m], grads[m], preferred_element_type=F32)
+            total = term if total is None else total + term
         res[k, :size, :] = total.astype(BF)
         mine = hits[pl.ds(chunk, 1), :]
         res[k, size:, :] = jnp.broadcast_to(mine, (16, size)).astype(BF)
-
-        @pl.when(k < N_X)
-        def _():
-            place = k & (N_X - 1)
-            pltpu.make_async_copy(res.at[k], other.at[place], sems.at[2 + k]).start()
-
-        for j in range(N_X):
-
-            @pl.when(k == N_X + j)
-            def _():
-                pltpu.make_async_copy(res.at[k], outs[j], sems.at[2 + k]).start()
-
         return carry
 
-    lax.fori_loop(0, N_DP, body, 0)
-    for j in range(N_X):
-        pltpu.make_async_copy(res.at[j], other.at[j], sems.at[2 + j]).wait()
-        pltpu.make_async_copy(res.at[N_X + j], outs[j], sems.at[2 + N_X + j]).wait()
-
-
-def owner_second(dp_at, wanted, hits, grads, prev):
-    slots, width = grads.shape
-    count = prev.shape[0]
-    size = count // N_DP
-    return pl.pallas_call(
-        owner_second_kernel,
-        in_specs=[SMEM, VMEM, VMEM, HBM, HBM],
-        out_specs=(HBM,) * (N_X + 1),
-        out_shape=(jax.ShapeDtypeStruct((size + 16, width), BF),) * N_X
-        + (jax.ShapeDtypeStruct((N_X, size + 16, width), BF),),
+    lax.fori_loop(0, N_X, body, 0)
+    if flip:
+        done = load_all([(res, outs[0])], sems)
+    else:
+        done = load_all([(res.at[k], outs[k]) for k in range(N_X)], sems)
+    for c in done:
+        c.wait()
+
+
+def owner(flip, dp_at, wanted, hits, grads):
+    slots, width = grads[0].shape
+    size = hits.shape[1]
+    part = (size + 16, width)
+    whole = (jax.ShapeDtypeStruct((N_X,) + part, BF),)
+    each = (jax.ShapeDtypeStruct(part, BF),) * N_X
+    return pl.pallas_call(
+        lambda *refs: owner_kernel(flip, *refs),
+        in_specs=[SMEM, VMEM, VMEM] + [HBM] * MB,
+        out_specs=(HBM,) * (1 if flip else N_X),
+        out_shape=whole if flip else each,
         scratch_shapes=[
-            pltpu.VMEM((slots, width), BF),
-            pltpu.VMEM((count, width), F32),
-            pltpu.VMEM((size, slots), BF),
-            pltpu.VMEM((N_DP, size + 16, width), BF),
-            pltpu.SemaphoreType.DMA((2 + N_DP,)),
+            pltpu.VMEM((MB, slots, width), BF),
+            pltpu.VMEM((MB, size, slots), BF),
+            pltpu.VMEM((N_X,) + part, BF),
+            pltpu.SemaphoreType.DMA((MB + N_X,)),
         ],
         compiler_params=params(),
-        name="owner_second",
-    )(dp_at, wanted, hits, grads, prev)
+        name="owner_other" if flip else "owner_mine",
+    )(dp_at, wanted, hits, *grads)
 
 
 def to_col(row, eye):
@@ -651,14 +573,19 @@
     )(dp_at, table, bits)
 
 
-def cold_update_kernel(at_ref, table, accum, bits, *refs):
-    parts = refs[:N_X]
-    out = refs[N_X]
+def cold_update_kernel(at_ref, *refs):
+    ins = refs[: 3 + N_X]
+    out = refs[3 + N_X]
+    table, accum, bits, parts, res, sems = refs[4 + N_X :]
     size = table.shape[0]
+    spots = [table, accum, bits] + [parts.at[k] for k in range(N_X)]
+    copies = load_all(list(zip(ins, spots)), sems)
     eye = iota((size, size), 0) == iota((size, size), 1)
-    total = parts[0][...].astype(F32)
+    for c in copies:
+        c.wait()
+    total = parts[0].astype(F32)
     for k in range(1, N_X):
-        total = total + parts[k][...].astype(F32)
+        total = total + parts[k].astype(F32)
     touched = to_col(total[size : size + 1], eye)
     averaged = total[:size] / jnp.maximum(touched, 1.0)
     at = at_ref[0] * 2
@@ -667,23 +594,35 @@
     updated, accum_new = adagrad(table[...].astype(F32), old, averaged)
     grid_step = jnp.max(jnp.abs(updated), axis=-1, keepdims=True) / 8.0
     dither = bits[...].astype(F32) * (1.0 / 65280.0) - 0.5
-    out[:size, :] = jnp.where(touched > 0.5, updated + grid_step * dither, updated).astype(BF)
+    res[:size, :] = jnp.where(touched > 0.5, updated + grid_step * dither, updated).astype(BF)
     row = to_row(accum_new, eye)
     high = row.astype(BF).astype(F32)
     middle = (row - high).astype(BF).astype(F32)
     low = (row - high) - middle
     which = iota((16, size), 0)
     packed = jnp.where(which == 0, high, jnp.where(which == 1, middle, low))
-    out[size:, :] = packed.astype(BF)
+    res[size:, :] = packed.astype(BF)
+    done = pltpu.make_async_copy(res, out, sems.at[0])
+    done.start()
+    done.wait()
 
 
 def cold_update(dp_at, table, accum, bits, parts):
+    shape = parts[0].shape
     return pl.pallas_call(
         cold_update_kernel,
-        in_specs=[SMEM] + [VMEM] * (3 + N_X),
-        out_specs=VMEM,
-        out_shape=jax.ShapeDtypeStruct(parts[0].shape, BF),
-        compiler_params=small_params(),
+        in_specs=[SMEM] + [HBM] * (3 + N_X),
+        out_specs=HBM,
+        out_shape=jax.ShapeDtypeStruct(shape, BF),
+        scratch_shapes=[
+            pltpu.VMEM(table.shape, BF),
+            pltpu.VMEM(accum.shape, F32),
+            pltpu.VMEM(bits.shape, jnp.int32),
+            pltpu.VMEM((N_X,) + shape, BF),
+            pltpu.VMEM(shape, BF),
+            pltpu.SemaphoreType.DMA((3 + N_X,)),
+        ],
+        compiler_params=params(),
         name="cold_update",
     )(dp_at, table, accum, bits, *parts)
 
@@ -757,18 +696,30 @@
 
 
 def sum_parts_kernel(*refs):
-    parts = refs[:N_X]
-    out = refs[N_X]
-    out[...] = (parts[0][...] + parts[1][...]) + (parts[2][...] + parts[3][...])
+    parts_h = refs[:N_X]
+    out, parts, res, sems = refs[N_X:]
+    copies = load_all([(parts_h[k], parts.at[k]) for k in range(N_X)], sems)
+    for c in copies:
+        c.wait()
+    res[...] = (parts[0] + parts[1]) + (parts[2] + parts[3])
+    done = pltpu.make_async_copy(res, out, sems.at[0])
+    done.start()
+    done.wait()
 
 
 def sum_parts(parts):
+    shape = parts[0].shape
     return pl.pallas_call(
         sum_parts_kernel,
-        in_specs=[VMEM] * N_X,
-        out_specs=VMEM,
-        out_shape=jax.ShapeDtypeStruct(parts[0].shape, F32),
-        compiler_params=small_params(),
+        in_specs=[HBM] * N_X,
+        out_specs=HBM,
+        out_shape=jax.ShapeDtypeStruct(shape, F32),
+        scratch_shapes=[
+            pltpu.VMEM((N_X,) + shape, F32),
+            pltpu.VMEM(shape, F32),
+            pltpu.SemaphoreType.DMA((N_X,)),
+        ],
+        compiler_params=params(),
         name="sum_parts",
     )(*parts)
 
@@ -860,7 +811,7 @@
 ):
     shards = lax.axis_size("shard")
     capacity = requests.shape[1]
-    row_count, row_width = cold_table.shape
+    _, row_width = cold_table.shape
     hot_count = hot_table.shape[0]
     slots = shards * capacity
     dp_at = lax.axis_index("dp").astype(jnp.int32).reshape(1)
@@ -912,9 +863,9 @@
         dp_at, hot_table, hot_accum.reshape(N_DP, -1), hot_all
     )
 
-    first = owner_first(wanted, owned[0], row_count)
-    parts = owner_second(dp_at, wanted, hits, owned[1], first)
-    parts = to_owners(parts)
+    other = owner(1, dp_at, wanted, hits, owned)
+    mine = owner(0, dp_at, wanted, hits, owned)
+    parts = to_owners([*mine, *other])
     packed = cold_update(dp_at, own_table, cold_accum.reshape(-1, 128), own_bits, parts)
     parts = to_all(packed)
     cold_out, cold_accum_out = cold_join(dp_at, parts)

time: 255 us -> 247 us (0.969)
  waiting for transfers between devices: 49 us -> 61.3 us
  Pallas kernels: 108 us -> 97.6 us
  local copies, waits for them, and re-layouts: 11.9 us -> 4.47 us
  starting transfers between devices: 58.6 us -> 55.4 us
    all_to_all x4, waiting for transfers between devices: 23.7 us -> 32.3 us  [exchange(): return lax.all_to_all(value, axis, split_axis=0, concat_axis=0, tiled=True)]
    unnamed x29 -> x13, local copies, waits for them, and re-layouts: 11.8 us -> 4.37 us
    ppermute x5, starting transfers between devices: 12.2 us -> 7.43 us  [step(): hot_all = hot_all + lax.ppermute(hot_all, 'shard', perm)]
    pallas_call x1, Pallas kernels: 13.1 us -> 8.28 us  [hot_scatter(): pl.pallas_call(hot_scatter_kernel, in_specs=[SMEM] + [HBM] * 5, out_specs...]
    pallas_call x4, Pallas kernels: 19.9 us -> 16.2 us  [the longest x2 12.1 us: owner(): pl.pallas_call(lambda *refs: owner_kernel(flip, *refs), in_specs=[SMEM, V...]
  transfers between devices with their start and end apart: 31 -> 31, of which waited for: 12 -> 12; matrix products, arithmetic and copies ran while one was open for 2% -> 2% of each run, Pallas kernels for 40% -> 37%
where the time goes in v6:
time: 247 us; the launch traced here: 244 us
  Pallas kernels  97.6 us (40%)
  waiting for transfers between devices  61.3 us (25%)
  starting transfers between devices  55.4 us (22%)
  blocking collectives  20.2 us (8%)
  local copies, waits for them, and re-layouts  4.47 us (2%)
  other arithmetic  4.11 us (2%)
    pallas_call x2, Pallas kernels, backprop(): pl.pallas_call(lambda *refs: step_kernel(m, *refs), in_specs=[HBM] * 9, o...  42.7 us
    all_to_all x4, waiting for transfers between devices, exchange(): return lax.all_to_all(value, axis, split_axis=0, concat_axis=0, tiled=True)  32.3 us
    all_to_all x4, starting transfers between devices, exchange(): return lax.all_to_all(value, axis, split_axis=0, concat_axis=0, tiled=True)  26.8 us
    all_to_all x1, blocking collectives, exchange(): return lax.all_to_all(value, axis, split_axis=0, concat_axis=0, tiled=True)  20.2 us
    ppermute x12, starting transfers between devices, along_x(): return lax.ppermute(value, 'dp', perm)  19.7 us
    ppermute x5, waiting for transfers between devices, step(): hot_all = hot_all + lax.ppermute(hot_all, 'shard', perm)  18.2 us
    pallas_call x2, Pallas kernels, serve(): pl.pallas_call(lambda *refs: serve_kernel(m, with_hits, *refs), in_specs=...  12.7 us
    pallas_call x2, Pallas kernels, owner(): pl.pallas_call(lambda *refs: owner_kernel(flip, *refs), in_specs=[SMEM, V...  12.1 us
  transfers between devices with their start and end apart: 31, of which 12 were waited for; matrix products, arithmetic and copies ran while one was open for 2% of the time, Pallas kernels for 37%

profile of v6, /device:TPU:8, one launch (start us, length us, event | category | flops | bytes accessed | tf_op | source)
XLA Modules:
  0.0 244.2 jit_solution(5023981148561016197)
XLA Ops:
  0.6 0.8 copy.24
  1.4 0.9 fusion
  2.3 0.1 all_to_all.19
  2.4 20.2 %all_to_all.31 = s32[32,1,128]{2,1,0:T(1,128)} all-to-all(s32[32,1,128]{2,1,0:T(1,128)S(1)} %all_to_all.19), channel_id=1, replica_groups=mesh['shard'=32,'dp'=8] {'shard'}, dimensions={0} | all-to-all | bytes 32768 | tf_op jit(solution)/shard_map/all_to_all | solution.py:772
  22.5 6.8 %serve_rows.2 = (bf16[2048,256]{1,0:T(8,128)(2,1)}, f32[8,256]{1,0:T(8,128)}) custom-call(s32[32,128]{1,0:T(8,128)} %bitcast.27, bf16[2048,256]{1,0:T(8,128)(2,1)} %refs_1_.3), custom_call_target="tpu_custom_call" | custom-call | tf_op jit(solution)/shard_map/serve_rows/pallas_call | solution.py:439
  29.3 5.7 %all-to-all-start.3 = ((bf16[32,64,256]{2,1,0:T(8,128)(2,1)}), bf16[32,64,256]{2,1,0:T(8,128)(2,1)}, u32[]{:S(2)}, u32[]{:S(2)}) async-start(bf16[32,64,256]{2,1,0:T(8,128)(2,1)} %bitcast.26), calls=%async_computation.3 | async-start | bytes 2097152 | tf_op jit(solution)/shard_map/all_to_all | solution.py:772
  35.0 6.0 %serve_rows.3 = bf16[2048,256]{1,0:T(8,128)(2,1)} custom-call(s32[32,128]{1,0:T(8,128)} %bitcast.28, bf16[2048,256]{1,0:T(8,128)(2,1)} %refs_1_.3), custom_call_target="tpu_custom_call" | custom-call | tf_op jit(solution)/shard_map/serve_rows/pallas_call | solution.py:439
  41.0 20.9 %all-to-all-done.3 = bf16[32,64,256]{2,1,0:T(8,128)(2,1)} async-done(((bf16[32,64,256]{2,1,0:T(8,128)(2,1)}), bf16[32,64,256]{2,1,0:T(8,128)(2,1)}, u32[]{:S(2)}, u32[]{:S(2)}) %all-to-all-start.3) | async-done | bytes 1048608 | tf_op jit(solution)/shard_map/all_to_all | solution.py:772
  61.9 5.6 %all-to-all-start.1 = ((bf16[32,64,256]{2,1,0:T(8,128)(2,1)}), bf16[32,64,256]{2,1,0:T(8,128)(2,1)}, u32[]{:S(2)}, u32[]{:S(2)}) async-start(bf16[32,64,256]{2,1,0:T(8,128)(2,1)} %bitcast.23), calls=%async_computation.1 | async-start | bytes 2097152 | tf_op jit(solution)/shard_map/all_to_all | solution.py:772
  67.6 0.8 copy.27.later.refs_2_
  68.4 0.8 copy.26.hot_ids
  69.2 6.6 %hot_rows.1.refs_1_ = bf16[4096,256]{1,0:T(8,128)(2,1)} custom-call(s32[512,8]{1,0:T(8,128)} %copy.26.hot_ids, f32[1024,256]{1,0:T(8,128)} %table_h.3, s32[512,8]{1,0:T(8,128)} %copy.27.later.refs_2_), custom_call_target="tpu_custom_call" | custom-call | tf_op jit(solution)/shard_map/hot_rows/pallas_call | solution.py:92
  75.9 21.4 %train_step.3 = (bf16[2048,256]{1,0:T(8,128)(2,1)}, bf16[2048,256]{1,0:T(8,128)(2,1)}, bf16[2048,256]{1,0:T(8,128)(2,1)}) custom-call(bf16[2048,256]{1,0:T(8,128)(2,1)} %bitcast.14.refs_0_, bf16[4096,256]{1,0:T(8,128)(2,1)} %hot_rows.1.refs_1_, s32[512,8]{1,0:T(8,128)} %copy.27.later.refs_2_, s32[8,512]{1,0:T(8,128)} %bitcast.31, f32[1,512]{1,0:T(1,128)} %bitcast.36, ...), custom_call_target="tpu_custom_call" | custom-call | tf_op jit(solution)/shard_map/train_step/pallas_call | solution.py:287
  97.3 9.8 %all-to-all-start.4 = ((bf16[32,64,256]{2,1,0:T(8,128)(2,1)}), bf16[32,64,256]{2,1,0:T(8,128)(2,1)}, u32[]{:S(2)}, u32[]{:S(2)}) async-start(bf16[32,64,256]{2,1,0:T(8,128)(2,1)} %bitcast.25), calls=%async_computation.4 | async-start | bytes 2097152 | tf_op jit(solution)/shard_map/all_to_all | solution.py:772
  107.1 21.3 %train_step.2 = (bf16[2048,256]{1,0:T(8,128)(2,1)}, bf16[2048,256]{1,0:T(8,128)(2,1)}, bf16[2048,256]{1,0:T(8,128)(2,1)}) custom-call(bf16[2048,256]{1,0:T(8,128)(2,1)} %bitcast.6.refs_0_, bf16[4096,256]{1,0:T(8,128)(2,1)} %hot_rows.1.refs_1_, s32[512,8]{1,0:T(8,128)} %copy.27.later.refs_2_, s32[8,512]{1,0:T(8,128)} %bitcast.32, f32[1,512]{1,0:T(1,128)} %bitcast.37, ...), custom_call_target="tpu_custom_call" | custom-call | tf_op jit(solution)/shard_map/train_step/pallas_call | solution.py:287
  128.5 4.6 %all-to-all-done.4 = bf16[32,64,256]{2,1,0:T(8,128)(2,1)} async-done(((bf16[32,64,256]{2,1,0:T(8,128)(2,1)}), bf16[32,64,256]{2,1,0:T(8,128)(2,1)}, u32[]{:S(2)}, u32[]{:S(2)}) %all-to-all-start.4) | async-done | bytes 1048608 | tf_op jit(solution)/shard_map/all_to_all | solution.py:772
  133.1 5.6 %all-to-all-start.2 = ((bf16[32,64,256]{2,1,0:T(8,128)(2,1)}), bf16[32,64,256]{2,1,0:T(8,128)(2,1)}, u32[]{:S(2)}, u32[]{:S(2)}) async-start(bf16[32,64,256]{2,1,0:T(8,128)(2,1)} %bitcast.24), calls=%async_computation.2 | async-start | bytes 2097152 | tf_op jit(solution)/shard_map/all_to_all | solution.py:772
  138.7 8.3 %hot_scatter.1 = (f32[128,256]{1,0:T(8,128)}, f32[128,256]{1,0:T(8,128)}, f32[128,256]{1,0:T(8,128)}, f32[128,256]{1,0:T(8,128)}, f32[4,128,256]{2,1,0:T(8,128)}) custom-call(s32[1]{0:T(128)} %bitcast.at_ref.refs_0_, s32[8,512]{1,0:T(8,128)} %bitcast.33, bf16[2048,256]{1,0:T(8,128)(2,1)} %get-tuple-element.51.hi0, bf16[2048,256]{1,0:T(8,128)(2,1)} %get-tuple-element.52.lo0, ...), custom_call_target="tpu_custom_call" | custom-call | tf_op jit(solution)/shard_map/hot_scatter/pallas_call | solution.py:359
  147.1 2.2 collective-permute-done.11.refs_4_
  149.3 2.2 pair_sum.3
  151.5 1.6 collective-permute-start.12
  153.1 2.7 %collective-permute-start.13 = (f32[128,256]{1,0:T(8,128)}, f32[128,256]{1,0:T(8,128)}, u32[]{:S(2)}, u32[]{:S(2)}) collective-permute-start(f32[128,256]{1,0:T(8,128)} %get-tuple-element.62), channel_id=1, source_target_pairs={{0,4},{1,5},{2,6},{3,7},{4,0},{5,1},{6,2},{7,3},{8,12},{9,13},{10,... | collective-permute-start | bytes 393224 | tf_op jit(solution)/shard_map/ppermute | solution.py:777
  155.8 1.4 collective-permute-start.14
  157.2 6.8 %all-to-all-done.2 = bf16[32,64,256]{2,1,0:T(8,128)(2,1)} async-done(((bf16[32,64,256]{2,1,0:T(8,128)(2,1)}), bf16[32,64,256]{2,1,0:T(8,128)(2,1)}, u32[]{:S(2)}, u32[]{:S(2)}) %all-to-all-start.2) | async-done | bytes 1048608 | tf_op jit(solution)/shard_map/all_to_all | solution.py:772
  164.0 6.1 %owner_other.1 = bf16[4,272,256]{2,1,0:T(8,128)(2,1)} custom-call(s32[1]{0:T(128)} %bitcast.at_ref.refs_0_, s32[32,128]{1,0:T(8,128)} %bitcast.29, f32[8,256]{1,0:T(8,128)} %get-tuple-element.37.refs_2_, bf16[2048,256]{1,0:T(8,128)(2,1)} %bitcast.12.refs_3_, bf16[2048,256]{1,0:T(8,128)(2,1)} %bitcast.16.refs_4_), custom_call_target="tpu_custom_call" | custom-call | tf_op jit(solution)/shard_map/owner_other/pallas_call | solution.py:516
  170.1 0.1 collective-permute-start
  170.2 1.8 sum_parts.1
  172.1 0.9 collective-permute-start.15
  173.0 5.3 %collective-permute-done.15 = f32[128,256]{1,0:T(8,128)S(1)} collective-permute-done((f32[128,256]{1,0:T(8,128)}, f32[128,256]{1,0:T(8,128)S(1)}, u32[]{:S(2)}, u32[]{:S(2)}) %collective-permute-start.15) | collective-permute-done | bytes 131104 | tf_op jit(solution)/shard_map/ppermute | solution.py:859
  178.2 0.9 add.15
  179.2 2.2 collective-permute-start.16
  181.3 4.5 %collective-permute-done.16 = f32[128,256]{1,0:T(8,128)S(1)} collective-permute-done((f32[128,256]{1,0:T(8,128)S(1)}, f32[128,256]{1,0:T(8,128)S(1)}, u32[]{:S(2)}, u32[]{:S(2)}) %collective-permute-start.16) | collective-permute-done | bytes 131104 | tf_op jit(solution)/shard_map/ppermute | solution.py:859
  185.8 1.0 collective-permute-start.17
  186.8 4.1 %collective-permute-done.17 = f32[128,256]{1,0:T(8,128)S(1)} collective-permute-done((f32[128,256]{1,0:T(8,128)S(1)}, f32[128,256]{1,0:T(8,128)S(1)}, u32[]{:S(2)}, u32[]{:S(2)}) %collective-permute-start.17) | collective-permute-done | bytes 131104 | tf_op jit(solution)/shard_map/ppermute | solution.py:859
  190.8 0.7 add.17
  191.5 1.9 collective-permute-start.18
  193.4 6.1 %owner_mine.1 = (bf16[272,256]{1,0:T(8,128)(2,1)}, bf16[272,256]{1,0:T(8,128)(2,1)}, bf16[272,256]{1,0:T(8,128)(2,1)}, bf16[272,256]{1,0:T(8,128)(2,1)}) custom-call(s32[1]{0:T(128)} %bitcast.at_ref.refs_0_, s32[32,128]{1,0:T(8,128)} %bitcast.30, f32[8,256]{1,0:T(8,128)} %get-tuple-element.37.refs_2_, bf16[2048,256]{1,0:T(8,128)(2,1)} %bitcast.12.refs_3_, ...), custom_call_target="tpu_custom_call" | custom-call | tf_op jit(solution)/shard_map/owner_mine/pallas_call | solution.py:516
  199.5 2.3 pair_sum.2
  201.8 1.6 collective-permute-start.1
  203.4 1.0 add.18
  204.4 1.5 collective-permute-start.19
  205.8 2.7 %collective-permute-start.2 = (bf16[272,256]{1,0:T(8,128)(2,1)}, bf16[272,256]{1,0:T(8,128)(2,1)}, u32[]{:S(2)}, u32[]{:S(2)}) collective-permute-start(bf16[272,256]{1,0:T(8,128)(2,1)} %get-tuple-element.47), channel_id=1, source_target_pairs={{0,4},{1,5},{2,6},{3,7},{4,0},{5,1},{6,2},{7,3},{8,12},{9,13},{10,... | collective-permute-start | bytes 417800 | tf_op jit(solution)/shard_map/ppermute | solution.py:777
  208.5 1.4 collective-permute-start.3
  210.0 4.4 %collective-permute-done.19 = f32[128,256]{1,0:T(8,128)S(1)} collective-permute-done((f32[128,256]{1,0:T(8,128)S(1)}, f32[128,256]{1,0:T(8,128)S(1)}, u32[]{:S(2)}, u32[]{:S(2)}) %collective-permute-start.19) | collective-permute-done | bytes 131104 | tf_op jit(solution)/shard_map/ppermute | solution.py:859
  214.4 0.7 add.19.refs_0_
  215.0 1.5 collective-permute-start.20
  216.5 1.7 collective-permute-start.21
  218.3 2.1 collective-permute-start.22
  220.4 1.8 pick_rows.1
  222.2 2.3 cold_update.1.refs_0_
  224.5 0.3 collective-permute-start.6
  224.8 1.8 collective-permute-start.4
  226.6 0.8 collective-permute-start.5
  227.4 0.5 collective-permute-start.25
  227.9 1.0 collective-permute-done.24.refs_5_
  229.0 0.1 collective-permute-start.7
  229.1 2.2 collective-permute-done.6.refs_3_
  231.4 3.8 %collective-permute-done.4.refs_1_ = bf16[272,256]{1,0:T(8,128)(2,1)S(1)} collective-permute-done((bf16[272,256]{1,0:T(8,128)(2,1)}, bf16[272,256]{1,0:T(8,128)(2,1)S(1)}, u32[]{:S(2)}, u32[]{:S(2)}) %collective-permute-start.4) | collective-permute-done | bytes 139296 | tf_op jit(solution)/shard_map/ppermute | solution.py:777
  235.2 0.5 collective-permute-start.9
  235.8 1.5 collective-permute-done.26.refs_7_
  237.3 1.2 copy-done
  238.5 0.7 copy-done.2
  239.2 3.1 %hot_update.1 = (f32[1024,256]{1,0:T(8,128)}, f32[8,128]{1,0:T(8,128)}) custom-call(s32[1]{0:T(128)} %bitcast.at_ref.refs_0_, f32[1024,256]{1,0:T(8,128)S(1)} %copy-done, f32[8,128]{1,0:T(8,128)S(1)} %bitcast.22, f32[128,256]{1,0:T(8,128)} %add.19.refs_0_, f32[128,256]{1,0:T(8,128)} %collective-permute-done.20.refs_1_, ...), custom_call_target="tpu_custom_call" | custom-call | tf_op jit(solution)/shard_map/hot_update/pallas_call | solution.py:752
  242.3 1.6 cold_join.1
  (34 shorter events, 0.3 us)
Async XLA Ops:
  29.3 32.6 %all-to-all-start.3 = ((bf16[32,64,256]{2,1,0:T(8,128)(2,1)}), bf16[32,64,256]{2,1,0:T(8,128)(2,1)}, u32[]{:S(2)}, u32[]{:S(2)}) async-start(bf16[32,64,256]{2,1,0:T(8,128)(2,1)} %bitcast.26), calls=%async_computation.3 | async-start | bytes 2097152 | tf_op jit(solution)/shard_map/all_to_all | solution.py:772
  41.0 26.6 %copy-start.3 = (s32[512,8]{0,1:T(8,128)S(1)}, s32[512,8]{0,1:T(8,128)}, u32[]{:S(2)}) copy-start(s32[512,8]{0,1:T(8,128)} %param.25) | copy-start | bytes 49156
  41.0 27.4 %copy-start.4 = (s32[512,8]{0,1:T(8,128)S(1)}, s32[512,8]{0,1:T(8,128)}, u32[]{:S(2)}) copy-start(s32[512,8]{0,1:T(8,128)} %param.24) | copy-start | bytes 49156
  61.9 35.3 %all-to-all-start.1 = ((bf16[32,64,256]{2,1,0:T(8,128)(2,1)}), bf16[32,64,256]{2,1,0:T(8,128)(2,1)}, u32[]{:S(2)}, u32[]{:S(2)}) async-start(bf16[32,64,256]{2,1,0:T(8,128)(2,1)} %bitcast.23), calls=%async_computation.1 | async-start | bytes 2097152 | tf_op jit(solution)/shard_map/all_to_all | solution.py:772
  97.3 35.8 %all-to-all-start.4 = ((bf16[32,64,256]{2,1,0:T(8,128)(2,1)}), bf16[32,64,256]{2,1,0:T(8,128)(2,1)}, u32[]{:S(2)}, u32[]{:S(2)}) async-start(bf16[32,64,256]{2,1,0:T(8,128)(2,1)} %bitcast.25), calls=%async_computation.4 | async-start | bytes 2097152 | tf_op jit(solution)/shard_map/all_to_all | solution.py:772
  133.1 31.0 %all-to-all-start.2 = ((bf16[32,64,256]{2,1,0:T(8,128)(2,1)}), bf16[32,64,256]{2,1,0:T(8,128)(2,1)}, u32[]{:S(2)}, u32[]{:S(2)}) async-start(bf16[32,64,256]{2,1,0:T(8,128)(2,1)} %bitcast.24), calls=%async_computation.2 | async-start | bytes 2097152 | tf_op jit(solution)/shard_map/all_to_all | solution.py:772
  147.0 2.3 collective-permute-start.11
  151.5 18.7 %collective-permute-start.12 = (f32[128,256]{1,0:T(8,128)}, f32[128,256]{1,0:T(8,128)}, u32[]{:S(2)}, u32[]{:S(2)}) collective-permute-start(f32[128,256]{1,0:T(8,128)} %get-tuple-element.61), channel_id=1, source_target_pairs={{0,2},{1,3},{2,4},{3,5},{4,6},{5,7},{6,0},{7,1},{8,10},{9,11},{10,... | collective-permute-start | bytes 393224 | tf_op jit(solution)/shard_map/ppermute | solution.py:777
  153.1 17.1 %collective-permute-start.13 = (f32[128,256]{1,0:T(8,128)}, f32[128,256]{1,0:T(8,128)}, u32[]{:S(2)}, u32[]{:S(2)}) collective-permute-start(f32[128,256]{1,0:T(8,128)} %get-tuple-element.62), channel_id=1, source_target_pairs={{0,4},{1,5},{2,6},{3,7},{4,0},{5,1},{6,2},{7,3},{8,12},{9,13},{10,... | collective-permute-start | bytes 393224 | tf_op jit(solution)/shard_map/ppermute | solution.py:777
  155.8 14.4 %collective-permute-start.14 = (f32[128,256]{1,0:T(8,128)}, f32[128,256]{1,0:T(8,128)}, u32[]{:S(2)}, u32[]{:S(2)}) collective-permute-start(f32[128,256]{1,0:T(8,128)} %get-tuple-element.63), channel_id=1, source_target_pairs={{0,6},{1,7},{2,0},{3,1},{4,2},{5,3},{6,4},{7,5},{8,14},{9,15},{10,... | collective-permute-start | bytes 393224 | tf_op jit(solution)/shard_map/ppermute | solution.py:777
  170.1 29.4 %collective-permute-start = (bf16[4,272,256]{2,1,0:T(8,128)(2,1)}, bf16[4,272,256]{2,1,0:T(8,128)(2,1)}, u32[]{:S(2)}, u32[]{:S(2)}) collective-permute-start(bf16[4,272,256]{2,1,0:T(8,128)(2,1)} %owner_other.1), channel_id=1, source_target_pairs={{0,1},{1,0},{2,3},{3,2},{4,5},{5,4},{6,7},{7,6},{8,9},{9,8},{10,11... | collective-permute-start | bytes 1671176 | tf_op jit(solution)/shard_map/ppermute | solution.py:781
  172.1 6.2 %collective-permute-start.15 = (f32[128,256]{1,0:T(8,128)}, f32[128,256]{1,0:T(8,128)S(1)}, u32[]{:S(2)}, u32[]{:S(2)}) collective-permute-start(f32[128,256]{1,0:T(8,128)} %sum_parts.1), channel_id=1, source_target_pairs={{0,8},{8,0},{16,24},{24,16},{32,40},{40,32},{48,56},{56,48},{64,72... | collective-permute-start | bytes 393224 | tf_op jit(solution)/shard_map/ppermute | solution.py:859
  179.2 6.6 %collective-permute-start.16 = (f32[128,256]{1,0:T(8,128)S(1)}, f32[128,256]{1,0:T(8,128)S(1)}, u32[]{:S(2)}, u32[]{:S(2)}) collective-permute-start(f32[128,256]{1,0:T(8,128)S(1)} %add.15), channel_id=1, source_target_pairs={{0,16},{8,24},{16,0},{24,8},{32,48},{40,56},{48,32},{56,40},{64,80... | collective-permute-start | bytes 393224 | tf_op jit(solution)/shard_map/ppermute | solution.py:859
  185.8 5.1 %collective-permute-start.17 = (f32[128,256]{1,0:T(8,128)S(1)}, f32[128,256]{1,0:T(8,128)S(1)}, u32[]{:S(2)}, u32[]{:S(2)}) collective-permute-start(f32[128,256]{1,0:T(8,128)S(1)} %add.16), channel_id=1, source_target_pairs={{0,32},{8,40},{16,48},{24,56},{32,0},{40,8},{48,16},{56,24},{64,96... | collective-permute-start | bytes 393224 | tf_op jit(solution)/shard_map/ppermute | solution.py:859
  191.5 11.9 %collective-permute-start.18 = (f32[128,256]{1,0:T(8,128)}, f32[128,256]{1,0:T(8,128)}, u32[]{:S(2)}, u32[]{:S(2)}) collective-permute-start(f32[128,256]{1,0:T(8,128)} %add.17), channel_id=1, source_target_pairs={{0,64},{8,72},{16,80},{24,88},{32,96},{40,104},{48,112},{56,120},{... | collective-permute-start | bytes 393224 | tf_op jit(solution)/shard_map/ppermute | solution.py:859
  201.8 16.5 %collective-permute-start.1 = (bf16[272,256]{1,0:T(8,128)(2,1)}, bf16[272,256]{1,0:T(8,128)(2,1)}, u32[]{:S(2)}, u32[]{:S(2)}) collective-permute-start(bf16[272,256]{1,0:T(8,128)(2,1)} %get-tuple-element.46), channel_id=1, source_target_pairs={{0,2},{1,3},{2,4},{3,5},{4,6},{5,7},{6,0},{7,1},{8,10},{9,11},{10,... | collective-permute-start | bytes 417800 | tf_op jit(solution)/shard_map/ppermute | solution.py:777
  204.4 10.0 %collective-permute-start.19 = (f32[128,256]{1,0:T(8,128)S(1)}, f32[128,256]{1,0:T(8,128)S(1)}, u32[]{:S(2)}, u32[]{:S(2)}) collective-permute-start(f32[128,256]{1,0:T(8,128)S(1)} %add.18), channel_id=1, source_target_pairs={{0,128},{8,136},{16,144},{24,152},{32,160},{40,168},{48,176},{56,1... | collective-permute-start | bytes 393224 | tf_op jit(solution)/shard_map/ppermute | solution.py:859
  205.8 14.6 %collective-permute-start.2 = (bf16[272,256]{1,0:T(8,128)(2,1)}, bf16[272,256]{1,0:T(8,128)(2,1)}, u32[]{:S(2)}, u32[]{:S(2)}) collective-permute-start(bf16[272,256]{1,0:T(8,128)(2,1)} %get-tuple-element.47), channel_id=1, source_target_pairs={{0,4},{1,5},{2,6},{3,7},{4,0},{5,1},{6,2},{7,3},{8,12},{9,13},{10,... | collective-permute-start | bytes 417800 | tf_op jit(solution)/shard_map/ppermute | solution.py:777
  208.5 13.7 %collective-permute-start.3 = (bf16[272,256]{1,0:T(8,128)(2,1)}, bf16[272,256]{1,0:T(8,128)(2,1)}, u32[]{:S(2)}, u32[]{:S(2)}) collective-permute-start(bf16[272,256]{1,0:T(8,128)(2,1)} %get-tuple-element.48), channel_id=1, source_target_pairs={{0,6},{1,7},{2,0},{3,1},{4,2},{5,3},{6,4},{7,5},{8,14},{9,15},{10,... | collective-permute-start | bytes 417800 | tf_op jit(solution)/shard_map/ppermute | solution.py:777
  215.0 9.8 %collective-permute-start.20 = (f32[128,256]{1,0:T(8,128)}, f32[128,256]{1,0:T(8,128)}, u32[]{:S(2)}, u32[]{:S(2)}) collective-permute-start(f32[128,256]{1,0:T(8,128)} %add.19.refs_0_), channel_id=1, source_target_pairs={{0,2},{1,3},{2,4},{3,5},{4,6},{5,7},{6,0},{7,1},{8,10},{9,11},{10,... | collective-permute-start | bytes 393224 | tf_op jit(solution)/shard_map/ppermute | solution.py:777
  216.5 10.1 %collective-permute-start.21 = (f32[128,256]{1,0:T(8,128)}, f32[128,256]{1,0:T(8,128)}, u32[]{:S(2)}, u32[]{:S(2)}) collective-permute-start(f32[128,256]{1,0:T(8,128)} %add.19.refs_0_), channel_id=1, source_target_pairs={{0,4},{1,5},{2,6},{3,7},{4,0},{5,1},{6,2},{7,3},{8,12},{9,13},{10,... | collective-permute-start | bytes 393224 | tf_op jit(solution)/shard_map/ppermute | solution.py:777
  218.3 9.2 %collective-permute-start.22 = (f32[128,256]{1,0:T(8,128)}, f32[128,256]{1,0:T(8,128)}, u32[]{:S(2)}, u32[]{:S(2)}) collective-permute-start(f32[128,256]{1,0:T(8,128)} %add.19.refs_0_), channel_id=1, source_target_pairs={{0,6},{1,7},{2,0},{3,1},{4,2},{5,3},{6,4},{7,5},{8,14},{9,15},{10,... | collective-permute-start | bytes 393224 | tf_op jit(solution)/shard_map/ppermute | solution.py:777
  220.4 7.0 %collective-permute-start.23 = (f32[128,256]{1,0:T(8,128)}, f32[128,256]{1,0:T(8,128)}, u32[]{:S(2)}, u32[]{:S(2)}) collective-permute-start(f32[128,256]{1,0:T(8,128)} %add.19.refs_0_), channel_id=1, source_target_pairs={{0,1},{1,0},{2,3},{3,2},{4,5},{5,4},{6,7},{7,6},{8,9},{9,8},{10,11... | collective-permute-start | bytes 393224 | tf_op jit(solution)/shard_map/ppermute | solution.py:781
  224.5 6.8 %collective-permute-start.6 = (bf16[272,256]{1,0:T(8,128)(2,1)}, bf16[272,256]{1,0:T(8,128)(2,1)S(1)}, u32[]{:S(2)}, u32[]{:S(2)}) collective-permute-start(bf16[272,256]{1,0:T(8,128)(2,1)} %cold_update.1.refs_0_), channel_id=1, source_target_pairs={{0,6},{1,7},{2,0},{3,1},{4,2},{5,3},{6,4},{7,5},{8,14},{9,15},{10,... | collective-permute-start | bytes 417800 | tf_op jit(solution)/shard_map/ppermute | solution.py:777
  224.8 10.4 %collective-permute-start.4 = (bf16[272,256]{1,0:T(8,128)(2,1)}, bf16[272,256]{1,0:T(8,128)(2,1)S(1)}, u32[]{:S(2)}, u32[]{:S(2)}) collective-permute-start(bf16[272,256]{1,0:T(8,128)(2,1)} %cold_update.1.refs_0_), channel_id=1, source_target_pairs={{0,2},{1,3},{2,4},{3,5},{4,6},{5,7},{6,0},{7,1},{8,10},{9,11},{10,... | collective-permute-start | bytes 417800 | tf_op jit(solution)/shard_map/ppermute | solution.py:777
  226.6 8.6 %collective-permute-start.5 = (bf16[272,256]{1,0:T(8,128)(2,1)}, bf16[272,256]{1,0:T(8,128)(2,1)S(1)}, u32[]{:S(2)}, u32[]{:S(2)}) collective-permute-start(bf16[272,256]{1,0:T(8,128)(2,1)} %cold_update.1.refs_0_), channel_id=1, source_target_pairs={{0,4},{1,5},{2,6},{3,7},{4,0},{5,1},{6,2},{7,3},{8,12},{9,13},{10,... | collective-permute-start | bytes 417800 | tf_op jit(solution)/shard_map/ppermute | solution.py:777
  227.4 1.6 collective-permute-start.24
  227.4 8.3 %collective-permute-start.25 = (f32[128,256]{1,0:T(8,128)}, f32[128,256]{1,0:T(8,128)S(1)}, u32[]{:S(2)}, u32[]{:S(2)}) collective-permute-start(f32[128,256]{1,0:T(8,128)} %collective-permute-done.21.refs_2_), channel_id=1, source_target_pairs={{0,1},{1,0},{2,3},{3,2},{4,5},{5,4},{6,7},{7,6},{8,9},{9,8},{10,11... | collective-permute-start | bytes 393224 | tf_op jit(solution)/shard_map/ppermute | solution.py:781
  229.0 13.3 %collective-permute-start.7 = (bf16[272,256]{1,0:T(8,128)(2,1)}, bf16[272,256]{1,0:T(8,128)(2,1)S(1)}, u32[]{:S(2)}, u32[]{:S(2)}) collective-permute-start(bf16[272,256]{1,0:T(8,128)(2,1)} %cold_update.1.refs_0_), channel_id=1, source_target_pairs={{0,1},{1,0},{2,3},{3,2},{4,5},{5,4},{6,7},{7,6},{8,9},{9,8},{10,11... | collective-permute-start | bytes 417800 | tf_op jit(solution)/shard_map/ppermute | solution.py:781
  231.4 11.0 %collective-permute-start.10 = (bf16[272,256]{1,0:T(8,128)(2,1)S(1)}, bf16[272,256]{1,0:T(8,128)(2,1)S(1)}, u32[]{:S(2)}, u32[]{:S(2)}) collective-permute-start(bf16[272,256]{1,0:T(8,128)(2,1)S(1)} %collective-permute-done.6.refs_3_), channel_id=1, source_target_pairs={{0,1},{1,0},{2,3},{3,2},{4,5},{5,4},{6,7},{7,6},{8,9},{9,8},{10,11... | collective-permute-start | bytes 417800 | tf_op jit(solution)/shard_map/ppermute | solution.py:781
  235.2 7.1 %collective-permute-start.8 = (bf16[272,256]{1,0:T(8,128)(2,1)S(1)}, bf16[272,256]{1,0:T(8,128)(2,1)S(1)}, u32[]{:S(2)}, u32[]{:S(2)}) collective-permute-start(bf16[272,256]{1,0:T(8,128)(2,1)S(1)} %collective-permute-done.4.refs_1_), channel_id=1, source_target_pairs={{0,1},{1,0},{2,3},{3,2},{4,5},{5,4},{6,7},{7,6},{8,9},{9,8},{10,11... | collective-permute-start | bytes 417800 | tf_op jit(solution)/shard_map/ppermute | solution.py:781
  235.2 7.1 %collective-permute-start.9 = (bf16[272,256]{1,0:T(8,128)(2,1)S(1)}, bf16[272,256]{1,0:T(8,128)(2,1)S(1)}, u32[]{:S(2)}, u32[]{:S(2)}) collective-permute-start(bf16[272,256]{1,0:T(8,128)(2,1)S(1)} %collective-permute-done.5.refs_2_), channel_id=1, source_target_pairs={{0,1},{1,0},{2,3},{3,2},{4,5},{5,4},{6,7},{7,6},{8,9},{9,8},{10,11... | collective-permute-start | bytes 417800 | tf_op jit(solution)/shard_map/ppermute | solution.py:781
  235.7 1.6 collective-permute-start.26
  237.3 1.2 copy-start
  238.5 0.7 copy-start.2
  239.2 3.2 %copy-start.1 = (bf16[272,256]{1,0:T(8,128)(2,1)S(1)}, bf16[272,256]{1,0:T(8,128)(2,1)}, u32[]{:S(2)}) copy-start(bf16[272,256]{1,0:T(8,128)(2,1)} %cold_update.1.refs_0_) | copy-start | bytes 417796

commit v7 on v6

--- a/solution.py
+++ b/solution.py
@@ -20,7 +20,7 @@
 N_X = 4
 VMEM_LIMIT = 64 << 20
 learn_rate = 0.3
-UNROLL = 4
+UNROLL = 8
 
 
 def iota(shape, axis):
@@ -853,11 +853,11 @@
     hot_grads = hot_scatter(dp_at, hot_ids.T, *hot_parts, hot_count)
     hot_grads = to_owners(hot_grads)
     hot_all = sum_parts(hot_grads)
-    step_bit = 1
-    while step_bit < shards:
+    step_bit = shards // 2
+    while step_bit:
         perm = [(i, i ^ step_bit) for i in range(shards)]
         hot_all = hot_all + lax.ppermute(hot_all, "shard", perm)
-        step_bit *= 2
+        step_bit //= 2
     hot_all = to_all(hot_all)
     hot_out, hot_accum_out = hot_update(
         dp_at, hot_table, hot_accum.reshape(N_DP, -1), hot_all

time: 247 us -> 251 us (1.016)
  waiting for transfers between devices: 61.3 us -> 68.8 us
  Pallas kernels: 97.6 us -> 94.9 us
    ppermute x5, waiting for transfers between devices: 18.2 us -> 24.7 us  [step(): hot_all = hot_all + lax.ppermute(hot_all, 'shard', perm)]
    pallas_call x2, Pallas kernels: 42.7 us -> 40 us  [backprop(): pl.pallas_call(lambda *refs: step_kernel(m, *refs), in_specs=[HBM] * 9, o...]
  transfers between devices with their start and end apart: 31 -> 31, of which waited for: 12 -> 11; matrix products, arithmetic and copies ran while one was open for 2% -> 2% of each run, Pallas kernels for 37% -> 35%
where the time goes in v7:
time: 251 us; the launch traced here: 248 us
  Pallas kernels  94.9 us (38%)
  waiting for transfers between devices  68.8 us (27%)
  starting transfers between devices  54.8 us (22%)
  blocking collectives  20.2 us (8%)
  local copies, waits for them, and re-layouts  4.47 us (2%)
  other arithmetic  4.11 us (2%)
    pallas_call x2, Pallas kernels, backprop(): pl.pallas_call(lambda *refs: step_kernel(m, *refs), in_specs=[HBM] * 9, o...  40 us
    all_to_all x4, waiting for transfers between devices, exchange(): return lax.all_to_all(value, axis, split_axis=0, concat_axis=0, tiled=True)  33.6 us
    all_to_all x4, starting transfers between devices, exchange(): return lax.all_to_all(value, axis, split_axis=0, concat_axis=0, tiled=True)  26.8 us
    ppermute x5, waiting for transfers between devices, step(): hot_all = hot_all + lax.ppermute(hot_all, 'shard', perm)  24.7 us
    all_to_all x1, blocking collectives, exchange(): return lax.all_to_all(value, axis, split_axis=0, concat_axis=0, tiled=True)  20.2 us
    ppermute x12, starting transfers between devices, along_x(): return lax.ppermute(value, 'dp', perm)  19.9 us
    pallas_call x2, Pallas kernels, serve(): pl.pallas_call(lambda *refs: serve_kernel(m, with_hits, *refs), in_specs=...  12.7 us
    pallas_call x2, Pallas kernels, owner(): pl.pallas_call(lambda *refs: owner_kernel(flip, *refs), in_specs=[SMEM, V...  12.1 us
  transfers between devices with their start and end apart: 31, of which 11 were waited for; matrix products, arithmetic and copies ran while one was open for 2% of the time, Pallas kernels for 35%

profile of v7, /device:TPU:8, one launch (start us, length us, event | category | flops | bytes accessed | tf_op | source)
XLA Modules:
  0.0 248.4 jit_solution(18054728749785709551)
XLA Ops:
  0.6 0.8 copy.24
  1.4 0.9 fusion
  2.3 0.1 all_to_all.19
  2.4 20.2 %all_to_all.31 = s32[32,1,128]{2,1,0:T(1,128)} all-to-all(s32[32,1,128]{2,1,0:T(1,128)S(1)} %all_to_all.19), channel_id=1, replica_groups=mesh['shard'=32,'dp'=8] {'shard'}, dimensions={0} | all-to-all | bytes 32768 | tf_op jit(solution)/shard_map/all_to_all | solution.py:772
  22.5 6.8 %serve_rows.2 = (bf16[2048,256]{1,0:T(8,128)(2,1)}, f32[8,256]{1,0:T(8,128)}) custom-call(s32[32,128]{1,0:T(8,128)} %bitcast.27, bf16[2048,256]{1,0:T(8,128)(2,1)} %refs_1_.3), custom_call_target="tpu_custom_call" | custom-call | tf_op jit(solution)/shard_map/serve_rows/pallas_call | solution.py:439
  29.3 5.7 %all-to-all-start.3 = ((bf16[32,64,256]{2,1,0:T(8,128)(2,1)}), bf16[32,64,256]{2,1,0:T(8,128)(2,1)}, u32[]{:S(2)}, u32[]{:S(2)}) async-start(bf16[32,64,256]{2,1,0:T(8,128)(2,1)} %bitcast.26), calls=%async_computation.3 | async-start | bytes 2097152 | tf_op jit(solution)/shard_map/all_to_all | solution.py:772
  35.0 6.0 %serve_rows.3 = bf16[2048,256]{1,0:T(8,128)(2,1)} custom-call(s32[32,128]{1,0:T(8,128)} %bitcast.28, bf16[2048,256]{1,0:T(8,128)(2,1)} %refs_1_.3), custom_call_target="tpu_custom_call" | custom-call | tf_op jit(solution)/shard_map/serve_rows/pallas_call | solution.py:439
  41.0 20.9 %all-to-all-done.3 = bf16[32,64,256]{2,1,0:T(8,128)(2,1)} async-done(((bf16[32,64,256]{2,1,0:T(8,128)(2,1)}), bf16[32,64,256]{2,1,0:T(8,128)(2,1)}, u32[]{:S(2)}, u32[]{:S(2)}) %all-to-all-start.3) | async-done | bytes 1048608 | tf_op jit(solution)/shard_map/all_to_all | solution.py:772
  61.9 5.6 %all-to-all-start.1 = ((bf16[32,64,256]{2,1,0:T(8,128)(2,1)}), bf16[32,64,256]{2,1,0:T(8,128)(2,1)}, u32[]{:S(2)}, u32[]{:S(2)}) async-start(bf16[32,64,256]{2,1,0:T(8,128)(2,1)} %bitcast.23), calls=%async_computation.1 | async-start | bytes 2097152 | tf_op jit(solution)/shard_map/all_to_all | solution.py:772
  67.6 0.8 copy.27.later.refs_2_
  68.4 0.8 copy.26.hot_ids
  69.2 6.6 %hot_rows.1.refs_1_ = bf16[4096,256]{1,0:T(8,128)(2,1)} custom-call(s32[512,8]{1,0:T(8,128)} %copy.26.hot_ids, f32[1024,256]{1,0:T(8,128)} %table_h.3, s32[512,8]{1,0:T(8,128)} %copy.27.later.refs_2_), custom_call_target="tpu_custom_call" | custom-call | tf_op jit(solution)/shard_map/hot_rows/pallas_call | solution.py:92
  75.9 20.0 %train_step.3 = (bf16[2048,256]{1,0:T(8,128)(2,1)}, bf16[2048,256]{1,0:T(8,128)(2,1)}, bf16[2048,256]{1,0:T(8,128)(2,1)}) custom-call(bf16[2048,256]{1,0:T(8,128)(2,1)} %bitcast.14.refs_0_, bf16[4096,256]{1,0:T(8,128)(2,1)} %hot_rows.1.refs_1_, s32[512,8]{1,0:T(8,128)} %copy.27.later.refs_2_, s32[8,512]{1,0:T(8,128)} %bitcast.31, f32[1,512]{1,0:T(1,128)} %bitcast.36, ...), custom_call_target="tpu_custom_call" | custom-call | tf_op jit(solution)/shard_map/train_step/pallas_call | solution.py:287
  95.9 9.9 %all-to-all-start.4 = ((bf16[32,64,256]{2,1,0:T(8,128)(2,1)}), bf16[32,64,256]{2,1,0:T(8,128)(2,1)}, u32[]{:S(2)}, u32[]{:S(2)}) async-start(bf16[32,64,256]{2,1,0:T(8,128)(2,1)} %bitcast.25), calls=%async_computation.4 | async-start | bytes 2097152 | tf_op jit(solution)/shard_map/all_to_all | solution.py:772
  105.8 20.0 %train_step.2 = (bf16[2048,256]{1,0:T(8,128)(2,1)}, bf16[2048,256]{1,0:T(8,128)(2,1)}, bf16[2048,256]{1,0:T(8,128)(2,1)}) custom-call(bf16[2048,256]{1,0:T(8,128)(2,1)} %bitcast.6.refs_0_, bf16[4096,256]{1,0:T(8,128)(2,1)} %hot_rows.1.refs_1_, s32[512,8]{1,0:T(8,128)} %copy.27.later.refs_2_, s32[8,512]{1,0:T(8,128)} %bitcast.32, f32[1,512]{1,0:T(1,128)} %bitcast.37, ...), custom_call_target="tpu_custom_call" | custom-call | tf_op jit(solution)/shard_map/train_step/pallas_call | solution.py:287
  125.8 5.9 %all-to-all-done.4 = bf16[32,64,256]{2,1,0:T(8,128)(2,1)} async-done(((bf16[32,64,256]{2,1,0:T(8,128)(2,1)}), bf16[32,64,256]{2,1,0:T(8,128)(2,1)}, u32[]{:S(2)}, u32[]{:S(2)}) %all-to-all-start.4) | async-done | bytes 1048608 | tf_op jit(solution)/shard_map/all_to_all | solution.py:772
  131.7 5.6 %all-to-all-start.2 = ((bf16[32,64,256]{2,1,0:T(8,128)(2,1)}), bf16[32,64,256]{2,1,0:T(8,128)(2,1)}, u32[]{:S(2)}, u32[]{:S(2)}) async-start(bf16[32,64,256]{2,1,0:T(8,128)(2,1)} %bitcast.24), calls=%async_computation.2 | async-start | bytes 2097152 | tf_op jit(solution)/shard_map/all_to_all | solution.py:772
  137.3 8.3 %hot_scatter.1 = (f32[128,256]{1,0:T(8,128)}, f32[128,256]{1,0:T(8,128)}, f32[128,256]{1,0:T(8,128)}, f32[128,256]{1,0:T(8,128)}, f32[4,128,256]{2,1,0:T(8,128)}) custom-call(s32[1]{0:T(128)} %bitcast.at_ref.refs_0_, s32[8,512]{1,0:T(8,128)} %bitcast.33, bf16[2048,256]{1,0:T(8,128)(2,1)} %get-tuple-element.51.hi0, bf16[2048,256]{1,0:T(8,128)(2,1)} %get-tuple-element.52.lo0, ...), custom_call_target="tpu_custom_call" | custom-call | tf_op jit(solution)/shard_map/hot_scatter/pallas_call | solution.py:359
  145.6 0.1 collective-permute-start.11
  145.7 2.2 collective-permute-done.11.refs_4_
  148.0 2.2 pair_sum.3
  150.2 1.6 collective-permute-start.12
  151.7 2.7 %collective-permute-start.13 = (f32[128,256]{1,0:T(8,128)}, f32[128,256]{1,0:T(8,128)}, u32[]{:S(2)}, u32[]{:S(2)}) collective-permute-start(f32[128,256]{1,0:T(8,128)} %get-tuple-element.62), channel_id=1, source_target_pairs={{0,4},{1,5},{2,6},{3,7},{4,0},{5,1},{6,2},{7,3},{8,12},{9,13},{10,... | collective-permute-start | bytes 393224 | tf_op jit(solution)/shard_map/ppermute | solution.py:777
  154.5 1.4 collective-permute-start.14
  155.9 6.8 %all-to-all-done.2 = bf16[32,64,256]{2,1,0:T(8,128)(2,1)} async-done(((bf16[32,64,256]{2,1,0:T(8,128)(2,1)}), bf16[32,64,256]{2,1,0:T(8,128)(2,1)}, u32[]{:S(2)}, u32[]{:S(2)}) %all-to-all-start.2) | async-done | bytes 1048608 | tf_op jit(solution)/shard_map/all_to_all | solution.py:772
  162.7 6.1 %owner_other.1 = bf16[4,272,256]{2,1,0:T(8,128)(2,1)} custom-call(s32[1]{0:T(128)} %bitcast.at_ref.refs_0_, s32[32,128]{1,0:T(8,128)} %bitcast.29, f32[8,256]{1,0:T(8,128)} %get-tuple-element.37.refs_2_, bf16[2048,256]{1,0:T(8,128)(2,1)} %bitcast.12.refs_3_, bf16[2048,256]{1,0:T(8,128)(2,1)} %bitcast.16.refs_4_), custom_call_target="tpu_custom_call" | custom-call | tf_op jit(solution)/shard_map/owner_other/pallas_call | solution.py:516
  168.7 0.1 collective-permute-start
  168.9 1.8 sum_parts.1
  170.7 1.9 collective-permute-start.15
  172.6 11.0 %collective-permute-done.15 = f32[128,256]{1,0:T(8,128)S(1)} collective-permute-done((f32[128,256]{1,0:T(8,128)}, f32[128,256]{1,0:T(8,128)S(1)}, u32[]{:S(2)}, u32[]{:S(2)}) %collective-permute-start.15) | collective-permute-done | bytes 131104 | tf_op jit(solution)/shard_map/ppermute | solution.py:859
  183.6 0.9 add.15
  184.5 0.1 collective-permute-start.16
  184.6 8.8 %collective-permute-done.16 = f32[128,256]{1,0:T(8,128)S(1)} collective-permute-done((f32[128,256]{1,0:T(8,128)S(1)}, f32[128,256]{1,0:T(8,128)S(1)}, u32[]{:S(2)}, u32[]{:S(2)}) %collective-permute-start.16) | collective-permute-done | bytes 131104 | tf_op jit(solution)/shard_map/ppermute | solution.py:859
  193.4 0.1 collective-permute-start.17
  193.5 5.0 %collective-permute-done.17 = f32[128,256]{1,0:T(8,128)S(1)} collective-permute-done((f32[128,256]{1,0:T(8,128)S(1)}, f32[128,256]{1,0:T(8,128)S(1)}, u32[]{:S(2)}, u32[]{:S(2)}) %collective-permute-start.17) | collective-permute-done | bytes 131104 | tf_op jit(solution)/shard_map/ppermute | solution.py:859
  198.4 0.7 add.17
  199.1 1.4 collective-permute-start.18
  200.5 6.1 %owner_mine.1 = (bf16[272,256]{1,0:T(8,128)(2,1)}, bf16[272,256]{1,0:T(8,128)(2,1)}, bf16[272,256]{1,0:T(8,128)(2,1)}, bf16[272,256]{1,0:T(8,128)(2,1)}) custom-call(s32[1]{0:T(128)} %bitcast.at_ref.refs_0_, s32[32,128]{1,0:T(8,128)} %bitcast.30, f32[8,256]{1,0:T(8,128)} %get-tuple-element.37.refs_2_, bf16[2048,256]{1,0:T(8,128)(2,1)} %bitcast.12.refs_3_, ...), custom_call_target="tpu_custom_call" | custom-call | tf_op jit(solution)/shard_map/owner_mine/pallas_call | solution.py:516
  206.6 2.3 pair_sum.2
  208.9 1.6 collective-permute-start.1
  210.5 1.0 add.18
  211.5 3.1 %collective-permute-start.19 = (f32[128,256]{1,0:T(8,128)S(1)}, f32[128,256]{1,0:T(8,128)S(1)}, u32[]{:S(2)}, u32[]{:S(2)}) collective-permute-start(f32[128,256]{1,0:T(8,128)S(1)} %add.18), channel_id=1, source_target_pairs={{0,8},{8,0},{16,24},{24,16},{32,40},{40,32},{48,56},{56,48},{64,72... | collective-permute-start | bytes 393224 | tf_op jit(solution)/shard_map/ppermute | solution.py:859
  214.6 2.7 %collective-permute-start.2 = (bf16[272,256]{1,0:T(8,128)(2,1)}, bf16[272,256]{1,0:T(8,128)(2,1)}, u32[]{:S(2)}, u32[]{:S(2)}) collective-permute-start(bf16[272,256]{1,0:T(8,128)(2,1)} %get-tuple-element.47), channel_id=1, source_target_pairs={{0,4},{1,5},{2,6},{3,7},{4,0},{5,1},{6,2},{7,3},{8,12},{9,13},{10,... | collective-permute-start | bytes 417800 | tf_op jit(solution)/shard_map/ppermute | solution.py:777
  217.3 1.4 collective-permute-start.3
  218.7 0.7 add.19.refs_0_
  219.4 0.6 collective-permute-start.20
  220.0 1.4 collective-permute-start.21
  221.4 2.2 collective-permute-start.22
  223.6 1.8 pick_rows.1
  225.4 2.3 cold_update.1.refs_0_
  227.7 2.3 collective-permute-start.6
  229.9 2.0 collective-permute-start.5
  232.0 0.5 collective-permute-start.25
  232.5 1.0 collective-permute-done.24.refs_5_
  233.5 0.1 collective-permute-start.7
  233.7 0.8 collective-permute-done.6.refs_3_
  234.5 4.9 %collective-permute-done.4.refs_1_ = bf16[272,256]{1,0:T(8,128)(2,1)S(1)} collective-permute-done((bf16[272,256]{1,0:T(8,128)(2,1)}, bf16[272,256]{1,0:T(8,128)(2,1)S(1)}, u32[]{:S(2)}, u32[]{:S(2)}) %collective-permute-start.4) | collective-permute-done | bytes 139296 | tf_op jit(solution)/shard_map/ppermute | solution.py:777
  239.4 0.5 collective-permute-start.9
  239.9 0.1 collective-permute-start.26
  240.0 1.5 collective-permute-done.26.refs_7_
  241.5 1.2 copy-done
  242.7 0.7 copy-done.2
  243.4 3.1 %hot_update.1 = (f32[1024,256]{1,0:T(8,128)}, f32[8,128]{1,0:T(8,128)}) custom-call(s32[1]{0:T(128)} %bitcast.at_ref.refs_0_, f32[1024,256]{1,0:T(8,128)S(1)} %copy-done, f32[8,128]{1,0:T(8,128)S(1)} %bitcast.22, f32[128,256]{1,0:T(8,128)} %add.19.refs_0_, f32[128,256]{1,0:T(8,128)} %collective-permute-done.20.refs_1_, ...), custom_call_target="tpu_custom_call" | custom-call | tf_op jit(solution)/shard_map/hot_update/pallas_call | solution.py:752
  246.6 1.6 cold_join.1
  (34 shorter events, 0.1 us)
Async XLA Ops:
  29.3 32.6 %all-to-all-start.3 = ((bf16[32,64,256]{2,1,0:T(8,128)(2,1)}), bf16[32,64,256]{2,1,0:T(8,128)(2,1)}, u32[]{:S(2)}, u32[]{:S(2)}) async-start(bf16[32,64,256]{2,1,0:T(8,128)(2,1)} %bitcast.26), calls=%async_computation.3 | async-start | bytes 2097152 | tf_op jit(solution)/shard_map/all_to_all | solution.py:772
  41.0 26.6 %copy-start.3 = (s32[512,8]{0,1:T(8,128)S(1)}, s32[512,8]{0,1:T(8,128)}, u32[]{:S(2)}) copy-start(s32[512,8]{0,1:T(8,128)} %param.25) | copy-start | bytes 49156
  41.0 27.4 %copy-start.4 = (s32[512,8]{0,1:T(8,128)S(1)}, s32[512,8]{0,1:T(8,128)}, u32[]{:S(2)}) copy-start(s32[512,8]{0,1:T(8,128)} %param.24) | copy-start | bytes 49156
  61.9 34.0 %all-to-all-start.1 = ((bf16[32,64,256]{2,1,0:T(8,128)(2,1)}), bf16[32,64,256]{2,1,0:T(8,128)(2,1)}, u32[]{:S(2)}, u32[]{:S(2)}) async-start(bf16[32,64,256]{2,1,0:T(8,128)(2,1)} %bitcast.23), calls=%async_computation.1 | async-start | bytes 2097152 | tf_op jit(solution)/shard_map/all_to_all | solution.py:772
  95.9 35.8 %all-to-all-start.4 = ((bf16[32,64,256]{2,1,0:T(8,128)(2,1)}), bf16[32,64,256]{2,1,0:T(8,128)(2,1)}, u32[]{:S(2)}, u32[]{:S(2)}) async-start(bf16[32,64,256]{2,1,0:T(8,128)(2,1)} %bitcast.25), calls=%async_computation.4 | async-start | bytes 2097152 | tf_op jit(solution)/shard_map/all_to_all | solution.py:772
  131.7 30.9 %all-to-all-start.2 = ((bf16[32,64,256]{2,1,0:T(8,128)(2,1)}), bf16[32,64,256]{2,1,0:T(8,128)(2,1)}, u32[]{:S(2)}, u32[]{:S(2)}) async-start(bf16[32,64,256]{2,1,0:T(8,128)(2,1)} %bitcast.24), calls=%async_computation.2 | async-start | bytes 2097152 | tf_op jit(solution)/shard_map/all_to_all | solution.py:772
  145.6 2.3 collective-permute-start.11
  150.2 18.7 %collective-permute-start.12 = (f32[128,256]{1,0:T(8,128)}, f32[128,256]{1,0:T(8,128)}, u32[]{:S(2)}, u32[]{:S(2)}) collective-permute-start(f32[128,256]{1,0:T(8,128)} %get-tuple-element.61), channel_id=1, source_target_pairs={{0,2},{1,3},{2,4},{3,5},{4,6},{5,7},{6,0},{7,1},{8,10},{9,11},{10,... | collective-permute-start | bytes 393224 | tf_op jit(solution)/shard_map/ppermute | solution.py:777
  151.7 17.1 %collective-permute-start.13 = (f32[128,256]{1,0:T(8,128)}, f32[128,256]{1,0:T(8,128)}, u32[]{:S(2)}, u32[]{:S(2)}) collective-permute-start(f32[128,256]{1,0:T(8,128)} %get-tuple-element.62), channel_id=1, source_target_pairs={{0,4},{1,5},{2,6},{3,7},{4,0},{5,1},{6,2},{7,3},{8,12},{9,13},{10,... | collective-permute-start | bytes 393224 | tf_op jit(solution)/shard_map/ppermute | solution.py:777
  154.5 14.4 %collective-permute-start.14 = (f32[128,256]{1,0:T(8,128)}, f32[128,256]{1,0:T(8,128)}, u32[]{:S(2)}, u32[]{:S(2)}) collective-permute-start(f32[128,256]{1,0:T(8,128)} %get-tuple-element.63), channel_id=1, source_target_pairs={{0,6},{1,7},{2,0},{3,1},{4,2},{5,3},{6,4},{7,5},{8,14},{9,15},{10,... | collective-permute-start | bytes 393224 | tf_op jit(solution)/shard_map/ppermute | solution.py:777
  168.7 37.9 %collective-permute-start = (bf16[4,272,256]{2,1,0:T(8,128)(2,1)}, bf16[4,272,256]{2,1,0:T(8,128)(2,1)}, u32[]{:S(2)}, u32[]{:S(2)}) collective-permute-start(bf16[4,272,256]{2,1,0:T(8,128)(2,1)} %owner_other.1), channel_id=1, source_target_pairs={{0,1},{1,0},{2,3},{3,2},{4,5},{5,4},{6,7},{7,6},{8,9},{9,8},{10,11... | collective-permute-start | bytes 1671176 | tf_op jit(solution)/shard_map/ppermute | solution.py:781
  170.7 12.9 %collective-permute-start.15 = (f32[128,256]{1,0:T(8,128)}, f32[128,256]{1,0:T(8,128)S(1)}, u32[]{:S(2)}, u32[]{:S(2)}) collective-permute-start(f32[128,256]{1,0:T(8,128)} %sum_parts.1), channel_id=1, source_target_pairs={{0,128},{8,136},{16,144},{24,152},{32,160},{40,168},{48,176},{56,1... | collective-permute-start | bytes 393224 | tf_op jit(solution)/shard_map/ppermute | solution.py:859
  184.5 8.9 %collective-permute-start.16 = (f32[128,256]{1,0:T(8,128)S(1)}, f32[128,256]{1,0:T(8,128)S(1)}, u32[]{:S(2)}, u32[]{:S(2)}) collective-permute-start(f32[128,256]{1,0:T(8,128)S(1)} %add.15), channel_id=1, source_target_pairs={{0,64},{8,72},{16,80},{24,88},{32,96},{40,104},{48,112},{56,120},{... | collective-permute-start | bytes 393224 | tf_op jit(solution)/shard_map/ppermute | solution.py:859
  193.4 5.1 %collective-permute-start.17 = (f32[128,256]{1,0:T(8,128)S(1)}, f32[128,256]{1,0:T(8,128)S(1)}, u32[]{:S(2)}, u32[]{:S(2)}) collective-permute-start(f32[128,256]{1,0:T(8,128)S(1)} %add.16), channel_id=1, source_target_pairs={{0,32},{8,40},{16,48},{24,56},{32,0},{40,8},{48,16},{56,24},{64,96... | collective-permute-start | bytes 393224 | tf_op jit(solution)/shard_map/ppermute | solution.py:859
  199.1 11.4 %collective-permute-start.18 = (f32[128,256]{1,0:T(8,128)}, f32[128,256]{1,0:T(8,128)}, u32[]{:S(2)}, u32[]{:S(2)}) collective-permute-start(f32[128,256]{1,0:T(8,128)} %add.17), channel_id=1, source_target_pairs={{0,16},{8,24},{16,0},{24,8},{32,48},{40,56},{48,32},{56,40},{64,80... | collective-permute-start | bytes 393224 | tf_op jit(solution)/shard_map/ppermute | solution.py:859
  208.9 12.5 %collective-permute-start.1 = (bf16[272,256]{1,0:T(8,128)(2,1)}, bf16[272,256]{1,0:T(8,128)(2,1)}, u32[]{:S(2)}, u32[]{:S(2)}) collective-permute-start(bf16[272,256]{1,0:T(8,128)(2,1)} %get-tuple-element.46), channel_id=1, source_target_pairs={{0,2},{1,3},{2,4},{3,5},{4,6},{5,7},{6,0},{7,1},{8,10},{9,11},{10,... | collective-permute-start | bytes 417800 | tf_op jit(solution)/shard_map/ppermute | solution.py:777
  211.5 7.2 %collective-permute-start.19 = (f32[128,256]{1,0:T(8,128)S(1)}, f32[128,256]{1,0:T(8,128)S(1)}, u32[]{:S(2)}, u32[]{:S(2)}) collective-permute-start(f32[128,256]{1,0:T(8,128)S(1)} %add.18), channel_id=1, source_target_pairs={{0,8},{8,0},{16,24},{24,16},{32,40},{40,32},{48,56},{56,48},{64,72... | collective-permute-start | bytes 393224 | tf_op jit(solution)/shard_map/ppermute | solution.py:859
  214.6 9.0 %collective-permute-start.2 = (bf16[272,256]{1,0:T(8,128)(2,1)}, bf16[272,256]{1,0:T(8,128)(2,1)}, u32[]{:S(2)}, u32[]{:S(2)}) collective-permute-start(bf16[272,256]{1,0:T(8,128)(2,1)} %get-tuple-element.47), channel_id=1, source_target_pairs={{0,4},{1,5},{2,6},{3,7},{4,0},{5,1},{6,2},{7,3},{8,12},{9,13},{10,... | collective-permute-start | bytes 417800 | tf_op jit(solution)/shard_map/ppermute | solution.py:777
  217.3 8.0 %collective-permute-start.3 = (bf16[272,256]{1,0:T(8,128)(2,1)}, bf16[272,256]{1,0:T(8,128)(2,1)}, u32[]{:S(2)}, u32[]{:S(2)}) collective-permute-start(bf16[272,256]{1,0:T(8,128)(2,1)} %get-tuple-element.48), channel_id=1, source_target_pairs={{0,6},{1,7},{2,0},{3,1},{4,2},{5,3},{6,4},{7,5},{8,14},{9,15},{10,... | collective-permute-start | bytes 417800 | tf_op jit(solution)/shard_map/ppermute | solution.py:777
  219.4 10.5 %collective-permute-start.20 = (f32[128,256]{1,0:T(8,128)}, f32[128,256]{1,0:T(8,128)}, u32[]{:S(2)}, u32[]{:S(2)}) collective-permute-start(f32[128,256]{1,0:T(8,128)} %add.19.refs_0_), channel_id=1, source_target_pairs={{0,2},{1,3},{2,4},{3,5},{4,6},{5,7},{6,0},{7,1},{8,10},{9,11},{10,... | collective-permute-start | bytes 393224 | tf_op jit(solution)/shard_map/ppermute | solution.py:777
  220.0 9.9 %collective-permute-start.21 = (f32[128,256]{1,0:T(8,128)}, f32[128,256]{1,0:T(8,128)}, u32[]{:S(2)}, u32[]{:S(2)}) collective-permute-start(f32[128,256]{1,0:T(8,128)} %add.19.refs_0_), channel_id=1, source_target_pairs={{0,4},{1,5},{2,6},{3,7},{4,0},{5,1},{6,2},{7,3},{8,12},{9,13},{10,... | collective-permute-start | bytes 393224 | tf_op jit(solution)/shard_map/ppermute | solution.py:777
  221.4 10.6 %collective-permute-start.22 = (f32[128,256]{1,0:T(8,128)}, f32[128,256]{1,0:T(8,128)}, u32[]{:S(2)}, u32[]{:S(2)}) collective-permute-start(f32[128,256]{1,0:T(8,128)} %add.19.refs_0_), channel_id=1, source_target_pairs={{0,6},{1,7},{2,0},{3,1},{4,2},{5,3},{6,4},{7,5},{8,14},{9,15},{10,... | collective-permute-start | bytes 393224 | tf_op jit(solution)/shard_map/ppermute | solution.py:777
  223.6 8.4 %collective-permute-start.23 = (f32[128,256]{1,0:T(8,128)}, f32[128,256]{1,0:T(8,128)}, u32[]{:S(2)}, u32[]{:S(2)}) collective-permute-start(f32[128,256]{1,0:T(8,128)} %add.19.refs_0_), channel_id=1, source_target_pairs={{0,1},{1,0},{2,3},{3,2},{4,5},{5,4},{6,7},{7,6},{8,9},{9,8},{10,11... | collective-permute-start | bytes 393224 | tf_op jit(solution)/shard_map/ppermute | solution.py:781
  227.7 6.8 %collective-permute-start.6 = (bf16[272,256]{1,0:T(8,128)(2,1)}, bf16[272,256]{1,0:T(8,128)(2,1)S(1)}, u32[]{:S(2)}, u32[]{:S(2)}) collective-permute-start(bf16[272,256]{1,0:T(8,128)(2,1)} %cold_update.1.refs_0_), channel_id=1, source_target_pairs={{0,6},{1,7},{2,0},{3,1},{4,2},{5,3},{6,4},{7,5},{8,14},{9,15},{10,... | collective-permute-start | bytes 417800 | tf_op jit(solution)/shard_map/ppermute | solution.py:777
  229.9 9.5 %collective-permute-start.4 = (bf16[272,256]{1,0:T(8,128)(2,1)}, bf16[272,256]{1,0:T(8,128)(2,1)S(1)}, u32[]{:S(2)}, u32[]{:S(2)}) collective-permute-start(bf16[272,256]{1,0:T(8,128)(2,1)} %cold_update.1.refs_0_), channel_id=1, source_target_pairs={{0,2},{1,3},{2,4},{3,5},{4,6},{5,7},{6,0},{7,1},{8,10},{9,11},{10,... | collective-permute-start | bytes 417800 | tf_op jit(solution)/shard_map/ppermute | solution.py:777
  229.9 9.5 %collective-permute-start.5 = (bf16[272,256]{1,0:T(8,128)(2,1)}, bf16[272,256]{1,0:T(8,128)(2,1)S(1)}, u32[]{:S(2)}, u32[]{:S(2)}) collective-permute-start(bf16[272,256]{1,0:T(8,128)(2,1)} %cold_update.1.refs_0_), channel_id=1, source_target_pairs={{0,4},{1,5},{2,6},{3,7},{4,0},{5,1},{6,2},{7,3},{8,12},{9,13},{10,... | collective-permute-start | bytes 417800 | tf_op jit(solution)/shard_map/ppermute | solution.py:777
  232.0 1.6 collective-permute-start.24
  232.0 7.9 %collective-permute-start.25 = (f32[128,256]{1,0:T(8,128)}, f32[128,256]{1,0:T(8,128)S(1)}, u32[]{:S(2)}, u32[]{:S(2)}) collective-permute-start(f32[128,256]{1,0:T(8,128)} %collective-permute-done.21.refs_2_), channel_id=1, source_target_pairs={{0,1},{1,0},{2,3},{3,2},{4,5},{5,4},{6,7},{7,6},{8,9},{9,8},{10,11... | collective-permute-start | bytes 393224 | tf_op jit(solution)/shard_map/ppermute | solution.py:781
  233.5 13.0 %collective-permute-start.7 = (bf16[272,256]{1,0:T(8,128)(2,1)}, bf16[272,256]{1,0:T(8,128)(2,1)S(1)}, u32[]{:S(2)}, u32[]{:S(2)}) collective-permute-start(bf16[272,256]{1,0:T(8,128)(2,1)} %cold_update.1.refs_0_), channel_id=1, source_target_pairs={{0,1},{1,0},{2,3},{3,2},{4,5},{5,4},{6,7},{7,6},{8,9},{9,8},{10,11... | collective-permute-start | bytes 417800 | tf_op jit(solution)/shard_map/ppermute | solution.py:781
  234.5 12.0 %collective-permute-start.10 = (bf16[272,256]{1,0:T(8,128)(2,1)S(1)}, bf16[272,256]{1,0:T(8,128)(2,1)S(1)}, u32[]{:S(2)}, u32[]{:S(2)}) collective-permute-start(bf16[272,256]{1,0:T(8,128)(2,1)S(1)} %collective-permute-done.6.refs_3_), channel_id=1, source_target_pairs={{0,1},{1,0},{2,3},{3,2},{4,5},{5,4},{6,7},{7,6},{8,9},{9,8},{10,11... | collective-permute-start | bytes 417800 | tf_op jit(solution)/shard_map/ppermute | solution.py:781
  239.4 7.1 %collective-permute-start.8 = (bf16[272,256]{1,0:T(8,128)(2,1)S(1)}, bf16[272,256]{1,0:T(8,128)(2,1)S(1)}, u32[]{:S(2)}, u32[]{:S(2)}) collective-permute-start(bf16[272,256]{1,0:T(8,128)(2,1)S(1)} %collective-permute-done.4.refs_1_), channel_id=1, source_target_pairs={{0,1},{1,0},{2,3},{3,2},{4,5},{5,4},{6,7},{7,6},{8,9},{9,8},{10,11... | collective-permute-start | bytes 417800 | tf_op jit(solution)/shard_map/ppermute | solution.py:781
  239.4 7.1 %collective-permute-start.9 = (bf16[272,256]{1,0:T(8,128)(2,1)S(1)}, bf16[272,256]{1,0:T(8,128)(2,1)S(1)}, u32[]{:S(2)}, u32[]{:S(2)}) collective-permute-start(bf16[272,256]{1,0:T(8,128)(2,1)S(1)} %collective-permute-done.5.refs_2_), channel_id=1, source_target_pairs={{0,1},{1,0},{2,3},{3,2},{4,5},{5,4},{6,7},{7,6},{8,9},{9,8},{10,11... | collective-permute-start | bytes 417800 | tf_op jit(solution)/shard_map/ppermute | solution.py:781
  239.9 1.6 collective-permute-start.26
  241.5 1.2 copy-start
  242.7 0.7 copy-start.2
  243.4 3.2 %copy-start.1 = (bf16[272,256]{1,0:T(8,128)(2,1)S(1)}, bf16[272,256]{1,0:T(8,128)(2,1)}, u32[]{:S(2)}) copy-start(bf16[272,256]{1,0:T(8,128)(2,1)} %cold_update.1.refs_0_) | copy-start | bytes 417796

commit v8 on v7

--- a/solution.py
+++ b/solution.py
@@ -45,7 +45,7 @@
 
 
 def small_params():
-    return pltpu.CompilerParams(vmem_limit_bytes=20 << 20)
+    return pltpu.CompilerParams(vmem_limit_bytes=24 << 20)
 
 
 def load_all(pairs, sems):
@@ -524,7 +524,7 @@
             pltpu.VMEM((N_X,) + part, BF),
             pltpu.SemaphoreType.DMA((MB + N_X,)),
         ],
-        compiler_params=params(),
+        compiler_params=small_params(),
         name="owner_other" if flip else "owner_mine",
     )(dp_at, wanted, hits, *grads)
 
@@ -622,7 +622,7 @@
             pltpu.VMEM(shape, BF),
             pltpu.SemaphoreType.DMA((3 + N_X,)),
         ],
-        compiler_params=params(),
+        compiler_params=small_params(),
         name="cold_update",
     )(dp_at, table, accum, bits, *parts)
 
@@ -690,7 +690,7 @@
             pltpu.VMEM(other.shape, other.dtype),
             pltpu.SemaphoreType.DMA((N_X + 1,)),
         ],
-        compiler_params=params(),
+        compiler_params=small_params(),
         name="pair_sum",
     )(*mine, other)
 
@@ -719,7 +719,7 @@
             pltpu.VMEM(shape, F32),
             pltpu.SemaphoreType.DMA((N_X,)),
         ],
-        compiler_params=params(),
+        compiler_params=small_params(),
         name="sum_parts",
     )(*parts)
 

time: 251 us -> 254 us (1.012)
  local copies, waits for them, and re-layouts: 4.47 us -> 16.7 us
  Pallas kernels: 94.9 us -> 90.8 us
  waiting for transfers between devices: 68.8 us -> 64.8 us
    unnamed x13 -> x43, local copies, waits for them, and re-layouts: 4.37 us -> 16.6 us
    all_to_all x4, waiting for transfers between devices: 33.6 us -> 30.9 us  [exchange(): return lax.all_to_all(value, axis, split_axis=0, concat_axis=0, tiled=True)]
  transfers between devices with their start and end apart: 31 -> 31, of which waited for: 11 -> 12; matrix products, arithmetic and copies ran while one was open for 2% -> 1% of each run, Pallas kernels for 35% -> 33%
where the time goes in v8:
time: 254 us; the launch traced here: 250 us
  Pallas kernels  90.8 us (36%)
  waiting for transfers between devices  64.8 us (26%)
  starting transfers between devices  54.7 us (22%)
  blocking collectives  20.2 us (8%)
  local copies, waits for them, and re-layouts  16.7 us (7%)
    pallas_call x2, Pallas kernels, backprop(): pl.pallas_call(lambda *refs: step_kernel(m, *refs), in_specs=[HBM] * 9, o...  40 us
    all_to_all x4, waiting for transfers between devices, exchange(): return lax.all_to_all(value, axis, split_axis=0, concat_axis=0, tiled=True)  30.9 us
    all_to_all x4, starting transfers between devices, exchange(): return lax.all_to_all(value, axis, split_axis=0, concat_axis=0, tiled=True)  26.8 us
    ppermute x5, waiting for transfers between devices, step(): hot_all = hot_all + lax.ppermute(hot_all, 'shard', perm)  24.5 us
    all_to_all x1, blocking collectives, exchange(): return lax.all_to_all(value, axis, split_axis=0, concat_axis=0, tiled=True)  20.2 us
    ppermute x12, starting transfers between devices, along_x(): return lax.ppermute(value, 'dp', perm)  18.2 us
    unnamed x43, local copies, waits for them, and re-layouts  16.6 us
    pallas_call x2, Pallas kernels, serve(): pl.pallas_call(lambda *refs: serve_kernel(m, with_hits, *refs), in_specs=...  12.7 us
  transfers between devices with their start and end apart: 31, of which 12 were waited for; matrix products, arithmetic and copies ran while one was open for 1% of the time, Pallas kernels for 33%

profile of v8, /device:TPU:8, one launch (start us, length us, event | category | flops | bytes accessed | tf_op | source)
XLA Modules:
  0.0 249.9 jit_solution(17080626687882363459)
XLA Ops:
  0.6 0.8 copy.24
  1.4 0.9 fusion
  2.4 20.2 %all_to_all.31 = s32[32,1,128]{2,1,0:T(1,128)} all-to-all(s32[32,1,128]{2,1,0:T(1,128)S(1)} %all_to_all.19), channel_id=1, replica_groups=mesh['shard'=32,'dp'=8] {'shard'}, dimensions={0} | all-to-all | bytes 32768 | tf_op jit(solution)/shard_map/all_to_all | solution.py:772
  22.5 6.8 %serve_rows.2 = (bf16[2048,256]{1,0:T(8,128)(2,1)}, f32[8,256]{1,0:T(8,128)}) custom-call(s32[32,128]{1,0:T(8,128)} %bitcast.22, bf16[2048,256]{1,0:T(8,128)(2,1)} %refs_1_.3), custom_call_target="tpu_custom_call" | custom-call | tf_op jit(solution)/shard_map/serve_rows/pallas_call | solution.py:439
  29.3 5.7 %all-to-all-start.3 = ((bf16[32,64,256]{2,1,0:T(8,128)(2,1)}), bf16[32,64,256]{2,1,0:T(8,128)(2,1)}, u32[]{:S(2)}, u32[]{:S(2)}) async-start(bf16[32,64,256]{2,1,0:T(8,128)(2,1)} %bitcast.31), calls=%async_computation.3 | async-start | bytes 2097152 | tf_op jit(solution)/shard_map/all_to_all | solution.py:772
  35.0 6.0 %serve_rows.3 = bf16[2048,256]{1,0:T(8,128)(2,1)} custom-call(s32[32,128]{1,0:T(8,128)} %bitcast.23, bf16[2048,256]{1,0:T(8,128)(2,1)} %refs_1_.3), custom_call_target="tpu_custom_call" | custom-call | tf_op jit(solution)/shard_map/serve_rows/pallas_call | solution.py:439
  41.0 20.9 %all-to-all-done.3 = bf16[32,64,256]{2,1,0:T(8,128)(2,1)} async-done(((bf16[32,64,256]{2,1,0:T(8,128)(2,1)}), bf16[32,64,256]{2,1,0:T(8,128)(2,1)}, u32[]{:S(2)}, u32[]{:S(2)}) %all-to-all-start.3) | async-done | bytes 1048608 | tf_op jit(solution)/shard_map/all_to_all | solution.py:772
  61.9 5.6 %all-to-all-start.1 = ((bf16[32,64,256]{2,1,0:T(8,128)(2,1)}), bf16[32,64,256]{2,1,0:T(8,128)(2,1)}, u32[]{:S(2)}, u32[]{:S(2)}) async-start(bf16[32,64,256]{2,1,0:T(8,128)(2,1)} %bitcast.28), calls=%async_computation.1 | async-start | bytes 2097152 | tf_op jit(solution)/shard_map/all_to_all | solution.py:772
  67.6 0.8 copy.27.later.refs_2_
  68.4 0.8 copy.26.hot_ids
  69.2 6.6 %hot_rows.1.refs_1_ = bf16[4096,256]{1,0:T(8,128)(2,1)} custom-call(s32[512,8]{1,0:T(8,128)} %copy.26.hot_ids, f32[1024,256]{1,0:T(8,128)} %table_h.3, s32[512,8]{1,0:T(8,128)} %copy.27.later.refs_2_), custom_call_target="tpu_custom_call" | custom-call | tf_op jit(solution)/shard_map/hot_rows/pallas_call | solution.py:92
  75.9 20.0 %train_step.3 = (bf16[2048,256]{1,0:T(8,128)(2,1)}, bf16[2048,256]{1,0:T(8,128)(2,1)}, bf16[2048,256]{1,0:T(8,128)(2,1)}) custom-call(bf16[2048,256]{1,0:T(8,128)(2,1)} %bitcast.14.refs_0_, bf16[4096,256]{1,0:T(8,128)(2,1)} %hot_rows.1.refs_1_, s32[512,8]{1,0:T(8,128)} %copy.27.later.refs_2_, s32[8,512]{1,0:T(8,128)} %bitcast.32, f32[1,512]{1,0:T(1,128)} %bitcast.36, ...), custom_call_target="tpu_custom_call" | custom-call | tf_op jit(solution)/shard_map/train_step/pallas_call | solution.py:287
  95.9 9.9 %all-to-all-start.4 = ((bf16[32,64,256]{2,1,0:T(8,128)(2,1)}), bf16[32,64,256]{2,1,0:T(8,128)(2,1)}, u32[]{:S(2)}, u32[]{:S(2)}) async-start(bf16[32,64,256]{2,1,0:T(8,128)(2,1)} %bitcast.30), calls=%async_computation.4 | async-start | bytes 2097152 | tf_op jit(solution)/shard_map/all_to_all | solution.py:772
  105.8 20.0 %train_step.2 = (bf16[2048,256]{1,0:T(8,128)(2,1)}, bf16[2048,256]{1,0:T(8,128)(2,1)}, bf16[2048,256]{1,0:T(8,128)(2,1)}) custom-call(bf16[2048,256]{1,0:T(8,128)(2,1)} %bitcast.6.refs_0_, bf16[4096,256]{1,0:T(8,128)(2,1)} %hot_rows.1.refs_1_, s32[512,8]{1,0:T(8,128)} %copy.27.later.refs_2_, s32[8,512]{1,0:T(8,128)} %bitcast.33, f32[1,512]{1,0:T(1,128)} %bitcast.37, ...), custom_call_target="tpu_custom_call" | custom-call | tf_op jit(solution)/shard_map/train_step/pallas_call | solution.py:287
  125.8 6.0 %all-to-all-done.4 = bf16[32,64,256]{2,1,0:T(8,128)(2,1)} async-done(((bf16[32,64,256]{2,1,0:T(8,128)(2,1)}), bf16[32,64,256]{2,1,0:T(8,128)(2,1)}, u32[]{:S(2)}, u32[]{:S(2)}) %all-to-all-start.4) | async-done | bytes 1048608 | tf_op jit(solution)/shard_map/all_to_all | solution.py:772
  131.7 5.6 %all-to-all-start.2 = ((bf16[32,64,256]{2,1,0:T(8,128)(2,1)}), bf16[32,64,256]{2,1,0:T(8,128)(2,1)}, u32[]{:S(2)}, u32[]{:S(2)}) async-start(bf16[32,64,256]{2,1,0:T(8,128)(2,1)} %bitcast.29), calls=%async_computation.2 | async-start | bytes 2097152 | tf_op jit(solution)/shard_map/all_to_all | solution.py:772
  137.4 8.3 %hot_scatter.1 = (f32[128,256]{1,0:T(8,128)}, f32[128,256]{1,0:T(8,128)}, f32[128,256]{1,0:T(8,128)}, f32[128,256]{1,0:T(8,128)}, f32[4,128,256]{2,1,0:T(8,128)}) custom-call(s32[1]{0:T(128)} %bitcast.at_ref.refs_0_, s32[8,512]{1,0:T(8,128)} %bitcast.34, bf16[2048,256]{1,0:T(8,128)(2,1)} %get-tuple-element.51.hi0, bf16[2048,256]{1,0:T(8,128)(2,1)} %get-tuple-element.52.lo0, ...), custom_call_target="tpu_custom_call" | custom-call | tf_op jit(solution)/shard_map/hot_scatter/pallas_call | solution.py:359
  145.8 2.1 collective-permute-done.11.refs_4_
  147.9 0.9 copy-done.10
  148.8 0.9 copy-done.11
  149.7 0.9 copy-done.12
  150.6 0.9 copy-done.13
  151.5 1.5 pair_sum.3
  153.0 1.6 collective-permute-start.12
  154.5 2.7 %collective-permute-start.13 = (f32[128,256]{1,0:T(8,128)S(1)}, f32[128,256]{1,0:T(8,128)S(1)}, u32[]{:S(2)}, u32[]{:S(2)}) collective-permute-start(f32[128,256]{1,0:T(8,128)S(1)} %get-tuple-element.62), channel_id=1, source_target_pairs={{0,4},{1,5},{2,6},{3,7},{4,0},{5,1},{6,2},{7,3},{8,12},{9,13},{10,... | collective-permute-start | bytes 393224 | tf_op jit(solution)/shard_map/ppermute | solution.py:777
  157.3 1.4 collective-permute-start.14
  158.7 4.0 %all-to-all-done.2 = bf16[32,64,256]{2,1,0:T(8,128)(2,1)} async-done(((bf16[32,64,256]{2,1,0:T(8,128)(2,1)}), bf16[32,64,256]{2,1,0:T(8,128)(2,1)}, u32[]{:S(2)}, u32[]{:S(2)}) %all-to-all-start.2) | async-done | bytes 1048608 | tf_op jit(solution)/shard_map/all_to_all | solution.py:772
  162.7 0.7 copy-done.1
  163.4 0.7 copy-done.15
  164.1 4.6 %owner_other.1 = bf16[4,272,256]{2,1,0:T(8,128)(2,1)S(1)} custom-call(s32[1]{0:T(128)} %bitcast.at_ref.refs_0_, s32[32,128]{1,0:T(8,128)S(1)} %bitcast.24, f32[8,256]{1,0:T(8,128)S(1)} %copy-done.15, bf16[2048,256]{1,0:T(8,128)(2,1)} %bitcast.12.refs_3_, bf16[2048,256]{1,0:T(8,128)(2,1)} %bitcast.16.refs_4_), custom_call_target="tpu_custom_call" | custom-call | tf_op jit(solution)/shard_map/owner_other/pallas_call | solution.py:516
  168.9 0.9 sum_parts.1
  169.8 1.9 collective-permute-start.15
  171.7 10.8 %collective-permute-done.15 = f32[128,256]{1,0:T(8,128)S(1)} collective-permute-done((f32[128,256]{1,0:T(8,128)S(1)}, f32[128,256]{1,0:T(8,128)S(1)}, u32[]{:S(2)}, u32[]{:S(2)}) %collective-permute-start.15) | collective-permute-done | bytes 131104 | tf_op jit(solution)/shard_map/ppermute | solution.py:859
  182.6 8.8 %collective-permute-done.16 = f32[128,256]{1,0:T(8,128)S(1)} collective-permute-done((f32[128,256]{1,0:T(8,128)S(1)}, f32[128,256]{1,0:T(8,128)S(1)}, u32[]{:S(2)}, u32[]{:S(2)}) %collective-permute-start.16) | collective-permute-done | bytes 131104 | tf_op jit(solution)/shard_map/ppermute | solution.py:859
  191.5 5.0 %collective-permute-done.17 = f32[128,256]{1,0:T(8,128)S(1)} collective-permute-done((f32[128,256]{1,0:T(8,128)S(1)}, f32[128,256]{1,0:T(8,128)S(1)}, u32[]{:S(2)}, u32[]{:S(2)}) %collective-permute-start.17) | collective-permute-done | bytes 131104 | tf_op jit(solution)/shard_map/ppermute | solution.py:859
  196.5 1.8 collective-permute-start.18
  198.2 5.3 %owner_mine.1 = (bf16[272,256]{1,0:T(8,128)(2,1)S(1)}, bf16[272,256]{1,0:T(8,128)(2,1)S(1)}, bf16[272,256]{1,0:T(8,128)(2,1)S(1)}, bf16[272,256]{1,0:T(8,128)(2,1)S(1)}) custom-call(s32[1]{0:T(128)} %bitcast.at_ref.refs_0_, s32[32,128]{1,0:T(8,128)S(1)} %bitcast.25, f32[8,256]{1,0:T(8,128)S(1)} %copy-done.15, bf16[2048,256]{1,0:T(8,128)(2,1)} %bitcast.12.refs_3_, ...), custom_call_target="tpu_custom_call" | custom-call | tf_op jit(solution)/shard_map/owner_mine/pallas_call | solution.py:516
  203.5 2.2 pair_sum.2
  206.4 4.5 %collective-permute-start.19 = (f32[128,256]{1,0:T(8,128)S(1)}, f32[128,256]{1,0:T(8,128)S(1)}, u32[]{:S(2)}, u32[]{:S(2)}) collective-permute-start(f32[128,256]{1,0:T(8,128)S(1)} %add.18), channel_id=1, source_target_pairs={{0,8},{8,0},{16,24},{24,16},{32,40},{40,32},{48,56},{56,48},{64,72... | collective-permute-start | bytes 393224 | tf_op jit(solution)/shard_map/ppermute | solution.py:859
  210.9 2.7 %collective-permute-start.2 = (bf16[272,256]{1,0:T(8,128)(2,1)S(1)}, bf16[272,256]{1,0:T(8,128)(2,1)S(1)}, u32[]{:S(2)}, u32[]{:S(2)}) collective-permute-start(bf16[272,256]{1,0:T(8,128)(2,1)S(1)} %get-tuple-element.47), channel_id=1, source_target_pairs={{0,4},{1,5},{2,6},{3,7},{4,0},{5,1},{6,2},{7,3},{8,12},{9,13},{10,... | collective-permute-start | bytes 417800 | tf_op jit(solution)/shard_map/ppermute | solution.py:777
  213.7 1.4 collective-permute-start.3
  215.1 0.7 add.19.refs_0_
  216.4 1.4 collective-permute-start.21
  217.8 0.7 copy-done.6
  218.4 2.2 collective-permute-start.22
  221.2 1.8 pick_rows.1
  223.0 0.9 copy-done.3
  224.0 0.9 copy-done.5
  224.9 0.9 copy-done.7
  225.8 0.9 copy-done.9
  226.7 0.9 copy-done.14
  227.6 0.7 copy-done.16
  228.3 2.2 cold_update.1.refs_0_
  231.1 1.5 collective-permute-start.4
  232.6 2.0 collective-permute-start.5
  235.1 1.0 collective-permute-done.24.refs_5_
  236.3 0.8 collective-permute-done.6.refs_3_
  237.1 1.5 collective-permute-done.4.refs_1_
  238.7 2.7 %collective-permute-done.5.refs_2_ = bf16[272,256]{1,0:T(8,128)(2,1)S(1)} collective-permute-done((bf16[272,256]{1,0:T(8,128)(2,1)S(1)}, bf16[272,256]{1,0:T(8,128)(2,1)S(1)}, u32[]{:S(2)}, u32[]{:S(2)}) %collective-permute-start.5) | collective-permute-done | bytes 139296 | tf_op jit(solution)/shard_map/ppermute | solution.py:777
  241.9 1.2 collective-permute-done.26.refs_7_
  243.1 1.2 copy-done
  244.3 0.7 copy-done.17
  245.0 3.1 %hot_update.1 = (f32[1024,256]{1,0:T(8,128)}, f32[8,128]{1,0:T(8,128)}) custom-call(s32[1]{0:T(128)} %bitcast.at_ref.refs_0_, f32[1024,256]{1,0:T(8,128)S(1)} %copy-done, f32[8,128]{1,0:T(8,128)S(1)} %bitcast.27, f32[128,256]{1,0:T(8,128)} %add.19.refs_0_, f32[128,256]{1,0:T(8,128)} %collective-permute-done.20.refs_1_, ...), custom_call_target="tpu_custom_call" | custom-call | tf_op jit(solution)/shard_map/hot_update/pallas_call | solution.py:752
  248.1 1.6 cold_join.1
  (64 shorter events, 4.4 us)
Async XLA Ops:
  29.3 32.6 %all-to-all-start.3 = ((bf16[32,64,256]{2,1,0:T(8,128)(2,1)}), bf16[32,64,256]{2,1,0:T(8,128)(2,1)}, u32[]{:S(2)}, u32[]{:S(2)}) async-start(bf16[32,64,256]{2,1,0:T(8,128)(2,1)} %bitcast.31), calls=%async_computation.3 | async-start | bytes 2097152 | tf_op jit(solution)/shard_map/all_to_all | solution.py:772
  41.0 26.6 %copy-start.18 = (s32[512,8]{0,1:T(8,128)S(1)}, s32[512,8]{0,1:T(8,128)}, u32[]{:S(2)}) copy-start(s32[512,8]{0,1:T(8,128)} %param.25) | copy-start | bytes 49156
  41.0 27.4 %copy-start.19 = (s32[512,8]{0,1:T(8,128)S(1)}, s32[512,8]{0,1:T(8,128)}, u32[]{:S(2)}) copy-start(s32[512,8]{0,1:T(8,128)} %param.24) | copy-start | bytes 49156
  61.9 34.0 %all-to-all-start.1 = ((bf16[32,64,256]{2,1,0:T(8,128)(2,1)}), bf16[32,64,256]{2,1,0:T(8,128)(2,1)}, u32[]{:S(2)}, u32[]{:S(2)}) async-start(bf16[32,64,256]{2,1,0:T(8,128)(2,1)} %bitcast.28), calls=%async_computation.1 | async-start | bytes 2097152 | tf_op jit(solution)/shard_map/all_to_all | solution.py:772
  95.9 35.8 %all-to-all-start.4 = ((bf16[32,64,256]{2,1,0:T(8,128)(2,1)}), bf16[32,64,256]{2,1,0:T(8,128)(2,1)}, u32[]{:S(2)}, u32[]{:S(2)}) async-start(bf16[32,64,256]{2,1,0:T(8,128)(2,1)} %bitcast.30), calls=%async_computation.4 | async-start | bytes 2097152 | tf_op jit(solution)/shard_map/all_to_all | solution.py:772
  131.7 31.0 %all-to-all-start.2 = ((bf16[32,64,256]{2,1,0:T(8,128)(2,1)}), bf16[32,64,256]{2,1,0:T(8,128)(2,1)}, u32[]{:S(2)}, u32[]{:S(2)}) async-start(bf16[32,64,256]{2,1,0:T(8,128)(2,1)} %bitcast.29), calls=%async_computation.2 | async-start | bytes 2097152 | tf_op jit(solution)/shard_map/all_to_all | solution.py:772
  145.7 2.2 collective-permute-start.11
  147.9 0.9 copy-start.10
  148.8 0.9 copy-start.11
  149.7 0.9 copy-start.12
  150.6 0.9 copy-start.13
  153.0 15.9 %collective-permute-start.12 = (f32[128,256]{1,0:T(8,128)S(1)}, f32[128,256]{1,0:T(8,128)S(1)}, u32[]{:S(2)}, u32[]{:S(2)}) collective-permute-start(f32[128,256]{1,0:T(8,128)S(1)} %get-tuple-element.61), channel_id=1, source_target_pairs={{0,2},{1,3},{2,4},{3,5},{4,6},{5,7},{6,0},{7,1},{8,10},{9,11},{10,... | collective-permute-start | bytes 393224 | tf_op jit(solution)/shard_map/ppermute | solution.py:777
  154.5 14.3 %collective-permute-start.13 = (f32[128,256]{1,0:T(8,128)S(1)}, f32[128,256]{1,0:T(8,128)S(1)}, u32[]{:S(2)}, u32[]{:S(2)}) collective-permute-start(f32[128,256]{1,0:T(8,128)S(1)} %get-tuple-element.62), channel_id=1, source_target_pairs={{0,4},{1,5},{2,6},{3,7},{4,0},{5,1},{6,2},{7,3},{8,12},{9,13},{10,... | collective-permute-start | bytes 393224 | tf_op jit(solution)/shard_map/ppermute | solution.py:777
  157.3 11.6 %collective-permute-start.14 = (f32[128,256]{1,0:T(8,128)S(1)}, f32[128,256]{1,0:T(8,128)S(1)}, u32[]{:S(2)}, u32[]{:S(2)}) collective-permute-start(f32[128,256]{1,0:T(8,128)S(1)} %get-tuple-element.63), channel_id=1, source_target_pairs={{0,6},{1,7},{2,0},{3,1},{4,2},{5,3},{6,4},{7,5},{8,14},{9,15},{10,... | collective-permute-start | bytes 393224 | tf_op jit(solution)/shard_map/ppermute | solution.py:777
  162.7 0.7 copy-start.1
  163.4 0.7 copy-start.15
  164.1 34.1 %copy-start.2 = (s32[32,1,128]{2,1,0:T(1,128)S(1)}, s32[32,1,128]{2,1,0:T(1,128)}, u32[]{:S(2)}) copy-start(s32[32,1,128]{2,1,0:T(1,128)} %all_to_all.31) | copy-start | bytes 49156
  168.8 34.8 %collective-permute-start = (bf16[4,272,256]{2,1,0:T(8,128)(2,1)S(1)}, bf16[4,272,256]{2,1,0:T(8,128)(2,1)S(1)}, u32[]{:S(2)}, u32[]{:S(2)}) collective-permute-start(bf16[4,272,256]{2,1,0:T(8,128)(2,1)S(1)} %owner_other.1), channel_id=1, source_target_pairs={{0,1},{1,0},{2,3},{3,2},{4,5},{5,4},{6,7},{7,6},{8,9},{9,8},{10,11... | collective-permute-start | bytes 1671176 | tf_op jit(solution)/shard_map/ppermute | solution.py:781
  169.8 12.7 %collective-permute-start.15 = (f32[128,256]{1,0:T(8,128)S(1)}, f32[128,256]{1,0:T(8,128)S(1)}, u32[]{:S(2)}, u32[]{:S(2)}) collective-permute-start(f32[128,256]{1,0:T(8,128)S(1)} %sum_parts.1), channel_id=1, source_target_pairs={{0,128},{8,136},{16,144},{24,152},{32,160},{40,168},{48,176},{56,1... | collective-permute-start | bytes 393224 | tf_op jit(solution)/shard_map/ppermute | solution.py:859
  182.5 8.9 %collective-permute-start.16 = (f32[128,256]{1,0:T(8,128)S(1)}, f32[128,256]{1,0:T(8,128)S(1)}, u32[]{:S(2)}, u32[]{:S(2)}) collective-permute-start(f32[128,256]{1,0:T(8,128)S(1)} %add.15), channel_id=1, source_target_pairs={{0,64},{8,72},{16,80},{24,88},{32,96},{40,104},{48,112},{56,120},{... | collective-permute-start | bytes 393224 | tf_op jit(solution)/shard_map/ppermute | solution.py:859
  191.4 5.1 %collective-permute-start.17 = (f32[128,256]{1,0:T(8,128)S(1)}, f32[128,256]{1,0:T(8,128)S(1)}, u32[]{:S(2)}, u32[]{:S(2)}) collective-permute-start(f32[128,256]{1,0:T(8,128)S(1)} %add.16), channel_id=1, source_target_pairs={{0,32},{8,40},{16,48},{24,56},{32,0},{40,8},{48,16},{56,24},{64,96... | collective-permute-start | bytes 393224 | tf_op jit(solution)/shard_map/ppermute | solution.py:859
  196.5 9.9 %collective-permute-start.18 = (f32[128,256]{1,0:T(8,128)S(1)}, f32[128,256]{1,0:T(8,128)S(1)}, u32[]{:S(2)}, u32[]{:S(2)}) collective-permute-start(f32[128,256]{1,0:T(8,128)S(1)} %add.17), channel_id=1, source_target_pairs={{0,16},{8,24},{16,0},{24,8},{32,48},{40,56},{48,32},{56,40},{64,80... | collective-permute-start | bytes 393224 | tf_op jit(solution)/shard_map/ppermute | solution.py:859
  205.7 0.7 copy-start.4
  206.4 11.4 %collective-permute-start.1 = (bf16[272,256]{1,0:T(8,128)(2,1)S(1)}, bf16[272,256]{1,0:T(8,128)(2,1)S(1)}, u32[]{:S(2)}, u32[]{:S(2)}) collective-permute-start(bf16[272,256]{1,0:T(8,128)(2,1)S(1)} %get-tuple-element.46), channel_id=1, source_target_pairs={{0,2},{1,3},{2,4},{3,5},{4,6},{5,7},{6,0},{7,1},{8,10},{9,11},{10,... | collective-permute-start | bytes 417800 | tf_op jit(solution)/shard_map/ppermute | solution.py:777
  206.4 8.6 %collective-permute-start.19 = (f32[128,256]{1,0:T(8,128)S(1)}, f32[128,256]{1,0:T(8,128)S(1)}, u32[]{:S(2)}, u32[]{:S(2)}) collective-permute-start(f32[128,256]{1,0:T(8,128)S(1)} %add.18), channel_id=1, source_target_pairs={{0,8},{8,0},{16,24},{24,16},{32,40},{40,32},{48,56},{56,48},{64,72... | collective-permute-start | bytes 393224 | tf_op jit(solution)/shard_map/ppermute | solution.py:859
  210.9 9.7 %collective-permute-start.2 = (bf16[272,256]{1,0:T(8,128)(2,1)S(1)}, bf16[272,256]{1,0:T(8,128)(2,1)S(1)}, u32[]{:S(2)}, u32[]{:S(2)}) collective-permute-start(bf16[272,256]{1,0:T(8,128)(2,1)S(1)} %get-tuple-element.47), channel_id=1, source_target_pairs={{0,4},{1,5},{2,6},{3,7},{4,0},{5,1},{6,2},{7,3},{8,12},{9,13},{10,... | collective-permute-start | bytes 417800 | tf_op jit(solution)/shard_map/ppermute | solution.py:777
  213.7 9.4 %collective-permute-start.3 = (bf16[272,256]{1,0:T(8,128)(2,1)}, bf16[272,256]{1,0:T(8,128)(2,1)}, u32[]{:S(2)}, u32[]{:S(2)}) collective-permute-start(bf16[272,256]{1,0:T(8,128)(2,1)} %get-tuple-element.48), channel_id=1, source_target_pairs={{0,6},{1,7},{2,0},{3,1},{4,2},{5,3},{6,4},{7,5},{8,14},{9,15},{10,... | collective-permute-start | bytes 417800 | tf_op jit(solution)/shard_map/ppermute | solution.py:777
  215.7 15.4 %collective-permute-start.20 = (f32[128,256]{1,0:T(8,128)}, f32[128,256]{1,0:T(8,128)}, u32[]{:S(2)}, u32[]{:S(2)}) collective-permute-start(f32[128,256]{1,0:T(8,128)} %add.19.refs_0_), channel_id=1, source_target_pairs={{0,2},{1,3},{2,4},{3,5},{4,6},{5,7},{6,0},{7,1},{8,10},{9,11},{10,... | collective-permute-start | bytes 393224 | tf_op jit(solution)/shard_map/ppermute | solution.py:777
  216.4 16.3 %collective-permute-start.21 = (f32[128,256]{1,0:T(8,128)}, f32[128,256]{1,0:T(8,128)}, u32[]{:S(2)}, u32[]{:S(2)}) collective-permute-start(f32[128,256]{1,0:T(8,128)} %add.19.refs_0_), channel_id=1, source_target_pairs={{0,4},{1,5},{2,6},{3,7},{4,0},{5,1},{6,2},{7,3},{8,12},{9,13},{10,... | collective-permute-start | bytes 393224 | tf_op jit(solution)/shard_map/ppermute | solution.py:777
  217.8 0.7 copy-start.6
  218.4 16.2 %collective-permute-start.22 = (f32[128,256]{1,0:T(8,128)}, f32[128,256]{1,0:T(8,128)}, u32[]{:S(2)}, u32[]{:S(2)}) collective-permute-start(f32[128,256]{1,0:T(8,128)} %add.19.refs_0_), channel_id=1, source_target_pairs={{0,6},{1,7},{2,0},{3,1},{4,2},{5,3},{6,4},{7,5},{8,14},{9,15},{10,... | collective-permute-start | bytes 393224 | tf_op jit(solution)/shard_map/ppermute | solution.py:777
  220.6 0.6 copy-start.8
  221.2 13.4 %collective-permute-start.23 = (f32[128,256]{1,0:T(8,128)}, f32[128,256]{1,0:T(8,128)}, u32[]{:S(2)}, u32[]{:S(2)}) collective-permute-start(f32[128,256]{1,0:T(8,128)} %add.19.refs_0_), channel_id=1, source_target_pairs={{0,1},{1,0},{2,3},{3,2},{4,5},{5,4},{6,7},{7,6},{8,9},{9,8},{10,11... | collective-permute-start | bytes 393224 | tf_op jit(solution)/shard_map/ppermute | solution.py:781
  223.0 1.0 copy-start.3
  224.0 0.9 copy-start.5
  224.9 0.9 copy-start.7
  225.8 0.9 copy-start.9
  226.7 0.9 copy-start.14
  227.6 0.7 copy-start.16
  230.5 6.6 %collective-permute-start.6 = (bf16[272,256]{1,0:T(8,128)(2,1)S(1)}, bf16[272,256]{1,0:T(8,128)(2,1)S(1)}, u32[]{:S(2)}, u32[]{:S(2)}) collective-permute-start(bf16[272,256]{1,0:T(8,128)(2,1)S(1)} %cold_update.1.refs_0_), channel_id=1, source_target_pairs={{0,6},{1,7},{2,0},{3,1},{4,2},{5,3},{6,4},{7,5},{8,14},{9,15},{10,... | collective-permute-start | bytes 417800 | tf_op jit(solution)/shard_map/ppermute | solution.py:777
  231.1 7.5 %collective-permute-start.4 = (bf16[272,256]{1,0:T(8,128)(2,1)S(1)}, bf16[272,256]{1,0:T(8,128)(2,1)S(1)}, u32[]{:S(2)}, u32[]{:S(2)}) collective-permute-start(bf16[272,256]{1,0:T(8,128)(2,1)S(1)} %cold_update.1.refs_0_), channel_id=1, source_target_pairs={{0,2},{1,3},{2,4},{3,5},{4,6},{5,7},{6,0},{7,1},{8,10},{9,11},{10,... | collective-permute-start | bytes 417800 | tf_op jit(solution)/shard_map/ppermute | solution.py:777
  232.6 8.8 %collective-permute-start.5 = (bf16[272,256]{1,0:T(8,128)(2,1)S(1)}, bf16[272,256]{1,0:T(8,128)(2,1)S(1)}, u32[]{:S(2)}, u32[]{:S(2)}) collective-permute-start(bf16[272,256]{1,0:T(8,128)(2,1)S(1)} %cold_update.1.refs_0_), channel_id=1, source_target_pairs={{0,4},{1,5},{2,6},{3,7},{4,0},{5,1},{6,2},{7,3},{8,12},{9,13},{10,... | collective-permute-start | bytes 417800 | tf_op jit(solution)/shard_map/ppermute | solution.py:777
  234.6 1.6 collective-permute-start.24
  234.6 6.8 %collective-permute-start.25 = (f32[128,256]{1,0:T(8,128)}, f32[128,256]{1,0:T(8,128)S(1)}, u32[]{:S(2)}, u32[]{:S(2)}) collective-permute-start(f32[128,256]{1,0:T(8,128)} %collective-permute-done.21.refs_2_), channel_id=1, source_target_pairs={{0,1},{1,0},{2,3},{3,2},{4,5},{5,4},{6,7},{7,6},{8,9},{9,8},{10,11... | collective-permute-start | bytes 393224 | tf_op jit(solution)/shard_map/ppermute | solution.py:781
  236.2 11.9 %collective-permute-start.7 = (bf16[272,256]{1,0:T(8,128)(2,1)S(1)}, bf16[272,256]{1,0:T(8,128)(2,1)S(1)}, u32[]{:S(2)}, u32[]{:S(2)}) collective-permute-start(bf16[272,256]{1,0:T(8,128)(2,1)S(1)} %cold_update.1.refs_0_), channel_id=1, source_target_pairs={{0,1},{1,0},{2,3},{3,2},{4,5},{5,4},{6,7},{7,6},{8,9},{9,8},{10,11... | collective-permute-start | bytes 417800 | tf_op jit(solution)/shard_map/ppermute | solution.py:781
  237.1 11.0 %collective-permute-start.10 = (bf16[272,256]{1,0:T(8,128)(2,1)S(1)}, bf16[272,256]{1,0:T(8,128)(2,1)S(1)}, u32[]{:S(2)}, u32[]{:S(2)}) collective-permute-start(bf16[272,256]{1,0:T(8,128)(2,1)S(1)} %collective-permute-done.6.refs_3_), channel_id=1, source_target_pairs={{0,1},{1,0},{2,3},{3,2},{4,5},{5,4},{6,7},{7,6},{8,9},{9,8},{10,11... | collective-permute-start | bytes 417800 | tf_op jit(solution)/shard_map/ppermute | solution.py:781
  238.7 9.5 %collective-permute-start.8 = (bf16[272,256]{1,0:T(8,128)(2,1)S(1)}, bf16[272,256]{1,0:T(8,128)(2,1)S(1)}, u32[]{:S(2)}, u32[]{:S(2)}) collective-permute-start(bf16[272,256]{1,0:T(8,128)(2,1)S(1)} %collective-permute-done.4.refs_1_), channel_id=1, source_target_pairs={{0,1},{1,0},{2,3},{3,2},{4,5},{5,4},{6,7},{7,6},{8,9},{9,8},{10,11... | collective-permute-start | bytes 417800 | tf_op jit(solution)/shard_map/ppermute | solution.py:781
  241.4 6.7 %collective-permute-start.9 = (bf16[272,256]{1,0:T(8,128)(2,1)S(1)}, bf16[272,256]{1,0:T(8,128)(2,1)S(1)}, u32[]{:S(2)}, u32[]{:S(2)}) collective-permute-start(bf16[272,256]{1,0:T(8,128)(2,1)S(1)} %collective-permute-done.5.refs_2_), channel_id=1, source_target_pairs={{0,1},{1,0},{2,3},{3,2},{4,5},{5,4},{6,7},{7,6},{8,9},{9,8},{10,11... | collective-permute-start | bytes 417800 | tf_op jit(solution)/shard_map/ppermute | solution.py:781
  241.4 1.7 collective-permute-start.26
  243.1 1.2 copy-start
  244.3 0.7 copy-start.17

commit v9 on v8

--- a/solution.py
+++ b/solution.py
@@ -1,3 +1,5 @@
+import functools
+
 import jax
 import jax.numpy as jnp
 from jax import lax
@@ -20,7 +22,7 @@
 N_X = 4
 VMEM_LIMIT = 64 << 20
 learn_rate = 0.3
-UNROLL = 8
+UNROLL = 4
 
 
 def iota(shape, axis):
@@ -321,28 +323,29 @@
     other, ids, h0, l0, h1, l1, match, res, sems = refs[N_X:]
     copies = load_all([(ids_h, ids), (hi0, h0), (lo0, l0), (hi1, h1), (lo1, l1)], sems)
     samples = ids.shape[1] // MB
-    block = match.shape[1]
+    block = match.shape[0]
     size = res.shape[0] // N_DP
     subs = iota((block, samples), 0).astype(jnp.int16)
-    for c in copies:
-        c.wait()
-
-    def body(b, carry):
+    copies[0].wait()
+
+    def body(m, hi, lo, b, carry):
         at = pl.multiple_of(b * block, block)
-        total = None
-        for m, parts in enumerate(((h0, l0), (h1, l1))):
-            for f in range(F_COLD):
-                row = ids[f : f + 1, m * samples : (m + 1) * samples] - at
-                mine = jnp.broadcast_to(row, (16, samples)).astype(jnp.int16)
-                same = subs == jnp.concatenate([mine] * (block // 16), axis=0)
-                match[m, :, f * samples : (f + 1) * samples] = as_one(same)
-            for part in parts:
-                term = jnp.dot(match[m], part[...], preferred_element_type=F32)
-                total = term if total is None else total + term
+        for f in range(F_COLD):
+            row = ids[f : f + 1, m * samples : (m + 1) * samples] - at
+            mine = jnp.broadcast_to(row, (16, samples)).astype(jnp.int16)
+            same = subs == jnp.concatenate([mine] * (block // 16), axis=0)
+            match[:, f * samples : (f + 1) * samples] = as_one(same)
+        total = jnp.dot(match[...], hi[...], preferred_element_type=F32)
+        total = total + jnp.dot(match[...], lo[...], preferred_element_type=F32)
+        if m:
+            total = total + res[pl.ds(at, block), :]
         res[pl.ds(at, block), :] = total
         return carry
 
-    lax.fori_loop(0, res.shape[0] // block, body, 0)
+    for m, (hi, lo) in enumerate(((h0, l0), (h1, l1))):
+        copies[1 + 2 * m].wait()
+        copies[2 + 2 * m].wait()
+        lax.fori_loop(0, res.shape[0] // block, functools.partial(body, m, hi, lo), 0)
     done = []
     for k in range(N_X):
         for flip, dst in ((0, outs[k]), (1, other.at[k])):
@@ -365,7 +368,7 @@
         scratch_shapes=[pltpu.VMEM(ids.shape, jnp.int32)]
         + [pltpu.VMEM((rows, width), BF)] * 4
         + [
-            pltpu.VMEM((MB, 256, rows), BF),
+            pltpu.VMEM((256, rows), BF),
             pltpu.VMEM((count, width), F32),
             pltpu.SemaphoreType.DMA((5 + N_DP,)),
         ],
@@ -401,8 +404,7 @@
         tall = one[0:16] + one[16:32] + one[32:48] + one[48:64]
         count_acc[...] += tall
 
-    def body(b, carry):
-        part = pltpu.roll(turned, lanes - b * per, 1)
+    def build(part):
         for j in range(per):
             one = ones_of(part, m, j)
             match[j * capacity : (j + 1) * capacity, :] = one
@@ -411,14 +413,26 @@
                 for other in range(MB):
                     if other != m:
                         add_hits(ones_of(part, other, j))
+
+    def finish(b):
         at = pl.ds(pl.multiple_of(b * block, block), block)
         res[at, :] = jnp.dot(match[...], table[...], preferred_element_type=F32).astype(BF)
         pltpu.make_async_copy(res.at[at, :], rows.at[at, :], sems.at[1 + b]).start()
+
+    def body(b, carry):
+        build(pltpu.roll(turned, lanes - b * per, 1))
+        finish(b)
         return carry
 
     steps = shards // per
-    load.wait()
-    lax.fori_loop(0, steps, body, 0)
+    if with_hits:
+        load.wait()
+        lax.fori_loop(0, steps, body, 0)
+    else:
+        build(turned)
+        load.wait()
+        finish(0)
+        lax.fori_loop(1, steps, body, 0)
     if with_hits:
         total = jnp.sum(count_acc[...].astype(F32), axis=0, keepdims=True)
         size = count // N_DP
@@ -678,7 +692,7 @@
         c.wait()
 
 
-def pair_sum(mine, other):
+def pair_sum(mine, other, compiler_params):
     outs = tuple(jax.ShapeDtypeStruct(part.shape, part.dtype) for part in mine)
     return pl.pallas_call(
         pair_sum_kernel,
@@ -690,7 +704,7 @@
             pltpu.VMEM(other.shape, other.dtype),
             pltpu.SemaphoreType.DMA((N_X + 1,)),
         ],
-        compiler_params=small_params(),
+        compiler_params=compiler_params,
         name="pair_sum",
     )(*mine, other)
 
@@ -781,10 +795,10 @@
     return lax.ppermute(value, "dp", [(i, i ^ 1) for i in range(N_DP)])
 
 
-def to_owners(parts):
+def to_owners(parts, compiler_params):
     *mine, other = parts
     other = to_partner(other)
-    mine = pair_sum(mine, other)
+    mine = pair_sum(mine, other, compiler_params)
     return [mine[0]] + [along_x(mine[k], k) for k in range(1, N_X)]
 
 
@@ -851,7 +865,7 @@
         owned.append(rows.reshape(slots, row_width))
 
     hot_grads = hot_scatter(dp_at, hot_ids.T, *hot_parts, hot_count)
-    hot_grads = to_owners(hot_grads)
+    hot_grads = to_owners(hot_grads, params())
     hot_all = sum_parts(hot_grads)
     step_bit = shards // 2
     while step_bit:
@@ -865,7 +879,7 @@
 
     other = owner(1, dp_at, wanted, hits, owned)
     mine = owner(0, dp_at, wanted, hits, owned)
-    parts = to_owners([*mine, *other])
+    parts = to_owners([*mine, *other], small_params())
     packed = cold_update(dp_at, own_table, cold_accum.reshape(-1, 128), own_bits, parts)
     parts = to_all(packed)
     cold_out, cold_accum_out = cold_join(dp_at, parts)

time: 254 us -> 256 us (level)
  waiting for transfers between devices: 64.8 us -> 68.6 us
  local copies, waits for them, and re-layouts: 16.7 us -> 13.1 us
  Pallas kernels: 90.8 us -> 94.3 us
    unnamed x43 -> x37, local copies, waits for them, and re-layouts: 16.6 us -> 13 us
    ppermute x5, starting transfers between devices: 8.33 us -> 5.47 us  [step(): hot_all = hot_all + lax.ppermute(hot_all, 'shard', perm)]
    pallas_call x2, Pallas kernels: 40 us -> 42.7 us  [backprop(): pl.pallas_call(lambda *refs: step_kernel(m, *refs), in_specs=[HBM] * 9, o...]
  transfers between devices with their start and end apart: 31 -> 31, of which waited for: 12 -> 12; matrix products, arithmetic and copies ran while one was open for 1% -> 1% of each run, Pallas kernels for 33% -> 34%
where the time goes in v9:
time: 256 us; the launch traced here: 252 us
  Pallas kernels  94.3 us (37%)
  waiting for transfers between devices  68.6 us (27%)
  starting transfers between devices  53.2 us (21%)
  blocking collectives  20.2 us (8%)
  local copies, waits for them, and re-layouts  13.1 us (5%)
    pallas_call x2, Pallas kernels, backprop(): pl.pallas_call(lambda *refs: step_kernel(m, *refs), in_specs=[HBM] * 9, o...  42.7 us
    all_to_all x4, waiting for transfers between devices, exchange(): return lax.all_to_all(value, axis, split_axis=0, concat_axis=0, tiled=True)  33.4 us
    all_to_all x4, starting transfers between devices, exchange(): return lax.all_to_all(value, axis, split_axis=0, concat_axis=0, tiled=True)  26.6 us
    ppermute x5, waiting for transfers between devices, step(): hot_all = hot_all + lax.ppermute(hot_all, 'shard', perm)  25.6 us
    all_to_all x1, blocking collectives, exchange(): return lax.all_to_all(value, axis, split_axis=0, concat_axis=0, tiled=True)  20.2 us
    ppermute x12, starting transfers between devices, along_x(): return lax.ppermute(value, 'dp', perm)  19.7 us
    unnamed x37, local copies, waits for them, and re-layouts  13 us
    pallas_call x2, Pallas kernels, serve(): pl.pallas_call(lambda *refs: serve_kernel(m, with_hits, *refs), in_specs=...  12.8 us
  transfers between devices with their start and end apart: 31, of which 12 were waited for; matrix products, arithmetic and copies ran while one was open for 1% of the time, Pallas kernels for 34%

profile of v9, /device:TPU:8, one launch (start us, length us, event | category | flops | bytes accessed | tf_op | source)
XLA Modules:
  0.0 252.1 jit_solution(10422703571052231005)
XLA Ops:
  0.6 0.8 copy.24
  1.4 0.9 fusion
  2.4 20.2 %all_to_all.31 = s32[32,1,128]{2,1,0:T(1,128)} all-to-all(s32[32,1,128]{2,1,0:T(1,128)S(1)} %all_to_all.19), channel_id=1, replica_groups=mesh['shard'=32,'dp'=8] {'shard'}, dimensions={0} | all-to-all | bytes 32768 | tf_op jit(solution)/shard_map/all_to_all | solution.py:786
  22.5 6.8 %serve_rows.2 = (bf16[2048,256]{1,0:T(8,128)(2,1)}, f32[8,256]{1,0:T(8,128)}) custom-call(s32[32,128]{1,0:T(8,128)} %bitcast.22, bf16[2048,256]{1,0:T(8,128)(2,1)} %refs_1_.3), custom_call_target="tpu_custom_call" | custom-call | tf_op jit(solution)/shard_map/serve_rows/pallas_call | solution.py:453
  29.3 5.5 %all-to-all-start.3 = ((bf16[32,64,256]{2,1,0:T(8,128)(2,1)}), bf16[32,64,256]{2,1,0:T(8,128)(2,1)}, u32[]{:S(2)}, u32[]{:S(2)}) async-start(bf16[32,64,256]{2,1,0:T(8,128)(2,1)} %bitcast.31), calls=%async_computation.3 | async-start | bytes 2097152 | tf_op jit(solution)/shard_map/all_to_all | solution.py:786
  34.9 6.0 %serve_rows.3 = bf16[2048,256]{1,0:T(8,128)(2,1)} custom-call(s32[32,128]{1,0:T(8,128)} %bitcast.23, bf16[2048,256]{1,0:T(8,128)(2,1)} %refs_1_.3), custom_call_target="tpu_custom_call" | custom-call | tf_op jit(solution)/shard_map/serve_rows/pallas_call | solution.py:453
  40.9 21.2 %all-to-all-done.3 = bf16[32,64,256]{2,1,0:T(8,128)(2,1)} async-done(((bf16[32,64,256]{2,1,0:T(8,128)(2,1)}), bf16[32,64,256]{2,1,0:T(8,128)(2,1)}, u32[]{:S(2)}, u32[]{:S(2)}) %all-to-all-start.3) | async-done | bytes 1048608 | tf_op jit(solution)/shard_map/all_to_all | solution.py:786
  62.1 5.6 %all-to-all-start.1 = ((bf16[32,64,256]{2,1,0:T(8,128)(2,1)}), bf16[32,64,256]{2,1,0:T(8,128)(2,1)}, u32[]{:S(2)}, u32[]{:S(2)}) async-start(bf16[32,64,256]{2,1,0:T(8,128)(2,1)} %bitcast.28), calls=%async_computation.1 | async-start | bytes 2097152 | tf_op jit(solution)/shard_map/all_to_all | solution.py:786
  67.7 0.9 copy.27.later.refs_2_
  68.6 0.8 copy.26.hot_ids
  69.4 6.7 %hot_rows.1.refs_1_ = bf16[4096,256]{1,0:T(8,128)(2,1)} custom-call(s32[512,8]{1,0:T(8,128)} %copy.26.hot_ids, f32[1024,256]{1,0:T(8,128)} %table_h.3, s32[512,8]{1,0:T(8,128)} %copy.27.later.refs_2_), custom_call_target="tpu_custom_call" | custom-call | tf_op jit(solution)/shard_map/hot_rows/pallas_call | solution.py:94
  76.1 21.4 %train_step.3 = (bf16[2048,256]{1,0:T(8,128)(2,1)}, bf16[2048,256]{1,0:T(8,128)(2,1)}, bf16[2048,256]{1,0:T(8,128)(2,1)}) custom-call(bf16[2048,256]{1,0:T(8,128)(2,1)} %bitcast.14.refs_0_, bf16[4096,256]{1,0:T(8,128)(2,1)} %hot_rows.1.refs_1_, s32[512,8]{1,0:T(8,128)} %copy.27.later.refs_2_, s32[8,512]{1,0:T(8,128)} %bitcast.32, f32[1,512]{1,0:T(1,128)} %bitcast.36, ...), custom_call_target="tpu_custom_call" | custom-call | tf_op jit(solution)/shard_map/train_step/pallas_call | solution.py:289
  97.5 9.9 %all-to-all-start.4 = ((bf16[32,64,256]{2,1,0:T(8,128)(2,1)}), bf16[32,64,256]{2,1,0:T(8,128)(2,1)}, u32[]{:S(2)}, u32[]{:S(2)}) async-start(bf16[32,64,256]{2,1,0:T(8,128)(2,1)} %bitcast.30), calls=%async_computation.4 | async-start | bytes 2097152 | tf_op jit(solution)/shard_map/all_to_all | solution.py:786
  107.3 21.3 %train_step.2 = (bf16[2048,256]{1,0:T(8,128)(2,1)}, bf16[2048,256]{1,0:T(8,128)(2,1)}, bf16[2048,256]{1,0:T(8,128)(2,1)}) custom-call(bf16[2048,256]{1,0:T(8,128)(2,1)} %bitcast.6.refs_0_, bf16[4096,256]{1,0:T(8,128)(2,1)} %hot_rows.1.refs_1_, s32[512,8]{1,0:T(8,128)} %copy.27.later.refs_2_, s32[8,512]{1,0:T(8,128)} %bitcast.33, f32[1,512]{1,0:T(1,128)} %bitcast.37, ...), custom_call_target="tpu_custom_call" | custom-call | tf_op jit(solution)/shard_map/train_step/pallas_call | solution.py:289
  128.7 4.8 %all-to-all-done.4 = bf16[32,64,256]{2,1,0:T(8,128)(2,1)} async-done(((bf16[32,64,256]{2,1,0:T(8,128)(2,1)}), bf16[32,64,256]{2,1,0:T(8,128)(2,1)}, u32[]{:S(2)}, u32[]{:S(2)}) %all-to-all-start.4) | async-done | bytes 1048608 | tf_op jit(solution)/shard_map/all_to_all | solution.py:786
  133.4 5.6 %all-to-all-start.2 = ((bf16[32,64,256]{2,1,0:T(8,128)(2,1)}), bf16[32,64,256]{2,1,0:T(8,128)(2,1)}, u32[]{:S(2)}, u32[]{:S(2)}) async-start(bf16[32,64,256]{2,1,0:T(8,128)(2,1)} %bitcast.29), calls=%async_computation.2 | async-start | bytes 2097152 | tf_op jit(solution)/shard_map/all_to_all | solution.py:786
  139.1 8.3 %hot_scatter.1 = (f32[128,256]{1,0:T(8,128)}, f32[128,256]{1,0:T(8,128)}, f32[128,256]{1,0:T(8,128)}, f32[128,256]{1,0:T(8,128)}, f32[4,128,256]{2,1,0:T(8,128)}) custom-call(s32[1]{0:T(128)} %bitcast.at_ref.refs_0_, s32[8,512]{1,0:T(8,128)} %bitcast.34, bf16[2048,256]{1,0:T(8,128)(2,1)} %get-tuple-element.51.hi0, bf16[2048,256]{1,0:T(8,128)(2,1)} %get-tuple-element.52.lo0, ...), custom_call_target="tpu_custom_call" | custom-call | tf_op jit(solution)/shard_map/hot_scatter/pallas_call | solution.py:362
  147.5 2.2 collective-permute-done.11.refs_4_
  149.7 2.2 pair_sum.3
  151.9 1.6 collective-permute-start.12
  153.5 2.7 %collective-permute-start.13 = (f32[128,256]{1,0:T(8,128)}, f32[128,256]{1,0:T(8,128)S(1)}, u32[]{:S(2)}, u32[]{:S(2)}) collective-permute-start(f32[128,256]{1,0:T(8,128)} %get-tuple-element.62), channel_id=1, source_target_pairs={{0,4},{1,5},{2,6},{3,7},{4,0},{5,1},{6,2},{7,3},{8,12},{9,13},{10,... | collective-permute-start | bytes 393224 | tf_op jit(solution)/shard_map/ppermute | solution.py:791
  156.2 1.4 collective-permute-start.14
  157.7 7.4 %all-to-all-done.2 = bf16[32,64,256]{2,1,0:T(8,128)(2,1)} async-done(((bf16[32,64,256]{2,1,0:T(8,128)(2,1)}), bf16[32,64,256]{2,1,0:T(8,128)(2,1)}, u32[]{:S(2)}, u32[]{:S(2)}) %all-to-all-start.2) | async-done | bytes 1048608 | tf_op jit(solution)/shard_map/all_to_all | solution.py:786
  165.1 0.7 copy-done.1
  165.8 0.7 copy-done.12
  166.5 4.7 %owner_other.1 = bf16[4,272,256]{2,1,0:T(8,128)(2,1)S(1)} custom-call(s32[1]{0:T(128)} %bitcast.at_ref.refs_0_, s32[32,128]{1,0:T(8,128)S(1)} %bitcast.24, f32[8,256]{1,0:T(8,128)S(1)} %copy-done.12, bf16[2048,256]{1,0:T(8,128)(2,1)} %bitcast.12.refs_3_, bf16[2048,256]{1,0:T(8,128)(2,1)} %bitcast.16.refs_4_), custom_call_target="tpu_custom_call" | custom-call | tf_op jit(solution)/shard_map/owner_other/pallas_call | solution.py:530
  171.3 0.9 sum_parts.1
  172.2 1.5 collective-permute-start.15
  173.8 11.1 %collective-permute-done.15 = f32[128,256]{1,0:T(8,128)S(1)} collective-permute-done((f32[128,256]{1,0:T(8,128)S(1)}, f32[128,256]{1,0:T(8,128)S(1)}, u32[]{:S(2)}, u32[]{:S(2)}) %collective-permute-start.15) | collective-permute-done | bytes 131104 | tf_op jit(solution)/shard_map/ppermute | solution.py:873
  185.0 9.1 %collective-permute-done.16 = f32[128,256]{1,0:T(8,128)S(1)} collective-permute-done((f32[128,256]{1,0:T(8,128)S(1)}, f32[128,256]{1,0:T(8,128)S(1)}, u32[]{:S(2)}, u32[]{:S(2)}) %collective-permute-start.16) | collective-permute-done | bytes 131104 | tf_op jit(solution)/shard_map/ppermute | solution.py:873
  194.2 5.4 %collective-permute-done.17 = f32[128,256]{1,0:T(8,128)S(1)} collective-permute-done((f32[128,256]{1,0:T(8,128)S(1)}, f32[128,256]{1,0:T(8,128)S(1)}, u32[]{:S(2)}, u32[]{:S(2)}) %collective-permute-start.17) | collective-permute-done | bytes 131104 | tf_op jit(solution)/shard_map/ppermute | solution.py:873
  199.6 0.7 collective-permute-start.18
  200.3 5.3 %owner_mine.1 = (bf16[272,256]{1,0:T(8,128)(2,1)S(1)}, bf16[272,256]{1,0:T(8,128)(2,1)S(1)}, bf16[272,256]{1,0:T(8,128)(2,1)S(1)}, bf16[272,256]{1,0:T(8,128)(2,1)S(1)}) custom-call(s32[1]{0:T(128)} %bitcast.at_ref.refs_0_, s32[32,128]{1,0:T(8,128)S(1)} %bitcast.25, f32[8,256]{1,0:T(8,128)S(1)} %copy-done.12, bf16[2048,256]{1,0:T(8,128)(2,1)} %bitcast.12.refs_3_, ...), custom_call_target="tpu_custom_call" | custom-call | tf_op jit(solution)/shard_map/owner_mine/pallas_call | solution.py:530
  205.6 2.2 pair_sum.2
  207.8 0.6 copy-done.4
  208.4 1.5 collective-permute-start.1
  209.9 3.1 %collective-permute-start.19 = (f32[128,256]{1,0:T(8,128)S(1)}, f32[128,256]{1,0:T(8,128)S(1)}, u32[]{:S(2)}, u32[]{:S(2)}) collective-permute-start(f32[128,256]{1,0:T(8,128)S(1)} %add.18), channel_id=1, source_target_pairs={{0,8},{8,0},{16,24},{24,16},{32,40},{40,32},{48,56},{56,48},{64,72... | collective-permute-start | bytes 393224 | tf_op jit(solution)/shard_map/ppermute | solution.py:873
  213.0 2.8 %collective-permute-start.2 = (bf16[272,256]{1,0:T(8,128)(2,1)S(1)}, bf16[272,256]{1,0:T(8,128)(2,1)S(1)}, u32[]{:S(2)}, u32[]{:S(2)}) collective-permute-start(bf16[272,256]{1,0:T(8,128)(2,1)S(1)} %get-tuple-element.47), channel_id=1, source_target_pairs={{0,4},{1,5},{2,6},{3,7},{4,0},{5,1},{6,2},{7,3},{8,12},{9,13},{10,... | collective-permute-start | bytes 417800 | tf_op jit(solution)/shard_map/ppermute | solution.py:791
  215.8 1.4 collective-permute-start.3
  217.2 0.7 add.19.refs_0_
  218.5 1.4 collective-permute-start.21
  219.8 0.6 copy-done.6
  220.5 2.2 collective-permute-start.22
  222.7 0.7 copy-done.8
  223.4 1.8 pick_rows.1
  225.2 0.9 copy-done.3
  226.1 0.9 copy-done.5
  227.0 0.9 copy-done.7
  227.9 0.9 copy-done.9
  228.8 0.9 copy-done.11
  229.7 0.7 copy-done.13
  230.4 2.2 cold_update.1.refs_0_
  232.6 0.6 collective-permute-start.6
  233.3 1.5 collective-permute-start.4
  234.7 2.0 collective-permute-start.5
  237.3 1.0 collective-permute-done.24.refs_5_
  238.5 0.8 collective-permute-done.6.refs_3_
  239.3 1.5 collective-permute-done.4.refs_1_
  240.8 2.8 %collective-permute-done.5.refs_2_ = bf16[272,256]{1,0:T(8,128)(2,1)S(1)} collective-permute-done((bf16[272,256]{1,0:T(8,128)(2,1)S(1)}, bf16[272,256]{1,0:T(8,128)(2,1)S(1)}, u32[]{:S(2)}, u32[]{:S(2)}) %collective-permute-start.5) | collective-permute-done | bytes 139296 | tf_op jit(solution)/shard_map/ppermute | solution.py:791
  244.0 1.2 collective-permute-done.26.refs_7_
  245.2 1.2 copy-done
  246.5 0.7 copy-done.14
  247.1 3.1 %hot_update.1 = (f32[1024,256]{1,0:T(8,128)}, f32[8,128]{1,0:T(8,128)}) custom-call(s32[1]{0:T(128)} %bitcast.at_ref.refs_0_, f32[1024,256]{1,0:T(8,128)S(1)} %copy-done, f32[8,128]{1,0:T(8,128)S(1)} %bitcast.27, f32[128,256]{1,0:T(8,128)} %add.19.refs_0_, f32[128,256]{1,0:T(8,128)} %collective-permute-done.20.refs_1_, ...), custom_call_target="tpu_custom_call" | custom-call | tf_op jit(solution)/shard_map/hot_update/pallas_call | solution.py:766
  250.3 1.6 cold_join.1
  (58 shorter events, 2.4 us)
Async XLA Ops:
  29.3 32.8 %all-to-all-start.3 = ((bf16[32,64,256]{2,1,0:T(8,128)(2,1)}), bf16[32,64,256]{2,1,0:T(8,128)(2,1)}, u32[]{:S(2)}, u32[]{:S(2)}) async-start(bf16[32,64,256]{2,1,0:T(8,128)(2,1)} %bitcast.31), calls=%async_computation.3 | async-start | bytes 2097152 | tf_op jit(solution)/shard_map/all_to_all | solution.py:786
  40.8 26.9 %copy-start.15 = (s32[512,8]{0,1:T(8,128)S(1)}, s32[512,8]{0,1:T(8,128)}, u32[]{:S(2)}) copy-start(s32[512,8]{0,1:T(8,128)} %param.25) | copy-start | bytes 49156
  40.9 27.7 %copy-start.16 = (s32[512,8]{0,1:T(8,128)S(1)}, s32[512,8]{0,1:T(8,128)}, u32[]{:S(2)}) copy-start(s32[512,8]{0,1:T(8,128)} %param.24) | copy-start | bytes 49156
  62.1 35.4 %all-to-all-start.1 = ((bf16[32,64,256]{2,1,0:T(8,128)(2,1)}), bf16[32,64,256]{2,1,0:T(8,128)(2,1)}, u32[]{:S(2)}, u32[]{:S(2)}) async-start(bf16[32,64,256]{2,1,0:T(8,128)(2,1)} %bitcast.28), calls=%async_computation.1 | async-start | bytes 2097152 | tf_op jit(solution)/shard_map/all_to_all | solution.py:786
  97.5 36.0 %all-to-all-start.4 = ((bf16[32,64,256]{2,1,0:T(8,128)(2,1)}), bf16[32,64,256]{2,1,0:T(8,128)(2,1)}, u32[]{:S(2)}, u32[]{:S(2)}) async-start(bf16[32,64,256]{2,1,0:T(8,128)(2,1)} %bitcast.30), calls=%async_computation.4 | async-start | bytes 2097152 | tf_op jit(solution)/shard_map/all_to_all | solution.py:786
  133.4 31.6 %all-to-all-start.2 = ((bf16[32,64,256]{2,1,0:T(8,128)(2,1)}), bf16[32,64,256]{2,1,0:T(8,128)(2,1)}, u32[]{:S(2)}, u32[]{:S(2)}) async-start(bf16[32,64,256]{2,1,0:T(8,128)(2,1)} %bitcast.29), calls=%async_computation.2 | async-start | bytes 2097152 | tf_op jit(solution)/shard_map/all_to_all | solution.py:786
  147.4 2.3 collective-permute-start.11
  151.9 19.4 %collective-permute-start.12 = (f32[128,256]{1,0:T(8,128)}, f32[128,256]{1,0:T(8,128)S(1)}, u32[]{:S(2)}, u32[]{:S(2)}) collective-permute-start(f32[128,256]{1,0:T(8,128)} %get-tuple-element.61), channel_id=1, source_target_pairs={{0,2},{1,3},{2,4},{3,5},{4,6},{5,7},{6,0},{7,1},{8,10},{9,11},{10,... | collective-permute-start | bytes 393224 | tf_op jit(solution)/shard_map/ppermute | solution.py:791
  153.5 17.8 %collective-permute-start.13 = (f32[128,256]{1,0:T(8,128)}, f32[128,256]{1,0:T(8,128)S(1)}, u32[]{:S(2)}, u32[]{:S(2)}) collective-permute-start(f32[128,256]{1,0:T(8,128)} %get-tuple-element.62), channel_id=1, source_target_pairs={{0,4},{1,5},{2,6},{3,7},{4,0},{5,1},{6,2},{7,3},{8,12},{9,13},{10,... | collective-permute-start | bytes 393224 | tf_op jit(solution)/shard_map/ppermute | solution.py:791
  156.2 15.1 %collective-permute-start.14 = (f32[128,256]{1,0:T(8,128)}, f32[128,256]{1,0:T(8,128)S(1)}, u32[]{:S(2)}, u32[]{:S(2)}) collective-permute-start(f32[128,256]{1,0:T(8,128)} %get-tuple-element.63), channel_id=1, source_target_pairs={{0,6},{1,7},{2,0},{3,1},{4,2},{5,3},{6,4},{7,5},{8,14},{9,15},{10,... | collective-permute-start | bytes 393224 | tf_op jit(solution)/shard_map/ppermute | solution.py:791
  165.1 0.7 copy-start.1
  165.8 0.7 copy-start.12
  166.5 4.8 %copy-start.10 = (f32[128,256]{1,0:T(8,128)S(1)}, f32[128,256]{1,0:T(8,128)}, u32[]{:S(2)}) copy-start(f32[128,256]{1,0:T(8,128)} %get-tuple-element.60.refs_0_) | copy-start | bytes 393220
  166.5 33.8 %copy-start.2 = (s32[32,1,128]{2,1,0:T(1,128)S(1)}, s32[32,1,128]{2,1,0:T(1,128)}, u32[]{:S(2)}) copy-start(s32[32,1,128]{2,1,0:T(1,128)} %all_to_all.31) | copy-start | bytes 49156
  171.2 34.4 %collective-permute-start = (bf16[4,272,256]{2,1,0:T(8,128)(2,1)S(1)}, bf16[4,272,256]{2,1,0:T(8,128)(2,1)S(1)}, u32[]{:S(2)}, u32[]{:S(2)}) collective-permute-start(bf16[4,272,256]{2,1,0:T(8,128)(2,1)S(1)} %owner_other.1), channel_id=1, source_target_pairs={{0,1},{1,0},{2,3},{3,2},{4,5},{5,4},{6,7},{7,6},{8,9},{9,8},{10,11... | collective-permute-start | bytes 1671176 | tf_op jit(solution)/shard_map/ppermute | solution.py:795
  172.2 12.7 %collective-permute-start.15 = (f32[128,256]{1,0:T(8,128)S(1)}, f32[128,256]{1,0:T(8,128)S(1)}, u32[]{:S(2)}, u32[]{:S(2)}) collective-permute-start(f32[128,256]{1,0:T(8,128)S(1)} %sum_parts.1), channel_id=1, source_target_pairs={{0,128},{8,136},{16,144},{24,152},{32,160},{40,168},{48,176},{56,1... | collective-permute-start | bytes 393224 | tf_op jit(solution)/shard_map/ppermute | solution.py:873
  184.9 9.2 %collective-permute-start.16 = (f32[128,256]{1,0:T(8,128)S(1)}, f32[128,256]{1,0:T(8,128)S(1)}, u32[]{:S(2)}, u32[]{:S(2)}) collective-permute-start(f32[128,256]{1,0:T(8,128)S(1)} %add.15), channel_id=1, source_target_pairs={{0,64},{8,72},{16,80},{24,88},{32,96},{40,104},{48,112},{56,120},{... | collective-permute-start | bytes 393224 | tf_op jit(solution)/shard_map/ppermute | solution.py:873
  194.1 5.5 %collective-permute-start.17 = (f32[128,256]{1,0:T(8,128)S(1)}, f32[128,256]{1,0:T(8,128)S(1)}, u32[]{:S(2)}, u32[]{:S(2)}) collective-permute-start(f32[128,256]{1,0:T(8,128)S(1)} %add.16), channel_id=1, source_target_pairs={{0,32},{8,40},{16,48},{24,56},{32,0},{40,8},{48,16},{56,24},{64,96... | collective-permute-start | bytes 393224 | tf_op jit(solution)/shard_map/ppermute | solution.py:873
  199.6 10.3 %collective-permute-start.18 = (f32[128,256]{1,0:T(8,128)S(1)}, f32[128,256]{1,0:T(8,128)S(1)}, u32[]{:S(2)}, u32[]{:S(2)}) collective-permute-start(f32[128,256]{1,0:T(8,128)S(1)} %add.17), channel_id=1, source_target_pairs={{0,16},{8,24},{16,0},{24,8},{32,48},{40,56},{48,32},{56,40},{64,80... | collective-permute-start | bytes 393224 | tf_op jit(solution)/shard_map/ppermute | solution.py:873
  207.8 0.7 copy-start.4
  208.4 11.4 %collective-permute-start.1 = (bf16[272,256]{1,0:T(8,128)(2,1)S(1)}, bf16[272,256]{1,0:T(8,128)(2,1)S(1)}, u32[]{:S(2)}, u32[]{:S(2)}) collective-permute-start(bf16[272,256]{1,0:T(8,128)(2,1)S(1)} %get-tuple-element.46), channel_id=1, source_target_pairs={{0,2},{1,3},{2,4},{3,5},{4,6},{5,7},{6,0},{7,1},{8,10},{9,11},{10,... | collective-permute-start | bytes 417800 | tf_op jit(solution)/shard_map/ppermute | solution.py:791
  209.9 7.3 %collective-permute-start.19 = (f32[128,256]{1,0:T(8,128)S(1)}, f32[128,256]{1,0:T(8,128)S(1)}, u32[]{:S(2)}, u32[]{:S(2)}) collective-permute-start(f32[128,256]{1,0:T(8,128)S(1)} %add.18), channel_id=1, source_target_pairs={{0,8},{8,0},{16,24},{24,16},{32,40},{40,32},{48,56},{56,48},{64,72... | collective-permute-start | bytes 393224 | tf_op jit(solution)/shard_map/ppermute | solution.py:873
  213.0 9.7 %collective-permute-start.2 = (bf16[272,256]{1,0:T(8,128)(2,1)S(1)}, bf16[272,256]{1,0:T(8,128)(2,1)S(1)}, u32[]{:S(2)}, u32[]{:S(2)}) collective-permute-start(bf16[272,256]{1,0:T(8,128)(2,1)S(1)} %get-tuple-element.47), channel_id=1, source_target_pairs={{0,4},{1,5},{2,6},{3,7},{4,0},{5,1},{6,2},{7,3},{8,12},{9,13},{10,... | collective-permute-start | bytes 417800 | tf_op jit(solution)/shard_map/ppermute | solution.py:791
  215.8 9.4 %collective-permute-start.3 = (bf16[272,256]{1,0:T(8,128)(2,1)}, bf16[272,256]{1,0:T(8,128)(2,1)}, u32[]{:S(2)}, u32[]{:S(2)}) collective-permute-start(bf16[272,256]{1,0:T(8,128)(2,1)} %get-tuple-element.48), channel_id=1, source_target_pairs={{0,6},{1,7},{2,0},{3,1},{4,2},{5,3},{6,4},{7,5},{8,14},{9,15},{10,... | collective-permute-start | bytes 417800 | tf_op jit(solution)/shard_map/ppermute | solution.py:791
  217.9 15.4 %collective-permute-start.20 = (f32[128,256]{1,0:T(8,128)}, f32[128,256]{1,0:T(8,128)}, u32[]{:S(2)}, u32[]{:S(2)}) collective-permute-start(f32[128,256]{1,0:T(8,128)} %add.19.refs_0_), channel_id=1, source_target_pairs={{0,2},{1,3},{2,4},{3,5},{4,6},{5,7},{6,0},{7,1},{8,10},{9,11},{10,... | collective-permute-start | bytes 393224 | tf_op jit(solution)/shard_map/ppermute | solution.py:791
  218.5 16.3 %collective-permute-start.21 = (f32[128,256]{1,0:T(8,128)}, f32[128,256]{1,0:T(8,128)}, u32[]{:S(2)}, u32[]{:S(2)}) collective-permute-start(f32[128,256]{1,0:T(8,128)} %add.19.refs_0_), channel_id=1, source_target_pairs={{0,4},{1,5},{2,6},{3,7},{4,0},{5,1},{6,2},{7,3},{8,12},{9,13},{10,... | collective-permute-start | bytes 393224 | tf_op jit(solution)/shard_map/ppermute | solution.py:791
  219.8 0.7 copy-start.6
  220.5 16.3 %collective-permute-start.22 = (f32[128,256]{1,0:T(8,128)}, f32[128,256]{1,0:T(8,128)}, u32[]{:S(2)}, u32[]{:S(2)}) collective-permute-start(f32[128,256]{1,0:T(8,128)} %add.19.refs_0_), channel_id=1, source_target_pairs={{0,6},{1,7},{2,0},{3,1},{4,2},{5,3},{6,4},{7,5},{8,14},{9,15},{10,... | collective-permute-start | bytes 393224 | tf_op jit(solution)/shard_map/ppermute | solution.py:791
  222.7 0.7 copy-start.8
  223.4 13.4 %collective-permute-start.23 = (f32[128,256]{1,0:T(8,128)}, f32[128,256]{1,0:T(8,128)}, u32[]{:S(2)}, u32[]{:S(2)}) collective-permute-start(f32[128,256]{1,0:T(8,128)} %add.19.refs_0_), channel_id=1, source_target_pairs={{0,1},{1,0},{2,3},{3,2},{4,5},{5,4},{6,7},{7,6},{8,9},{9,8},{10,11... | collective-permute-start | bytes 393224 | tf_op jit(solution)/shard_map/ppermute | solution.py:795
  225.2 1.0 copy-start.3
  226.1 0.9 copy-start.5
  227.0 0.9 copy-start.7
  227.9 0.9 copy-start.9
  228.8 0.9 copy-start.11
  229.7 0.7 copy-start.13
  232.6 6.6 %collective-permute-start.6 = (bf16[272,256]{1,0:T(8,128)(2,1)S(1)}, bf16[272,256]{1,0:T(8,128)(2,1)S(1)}, u32[]{:S(2)}, u32[]{:S(2)}) collective-permute-start(bf16[272,256]{1,0:T(8,128)(2,1)S(1)} %cold_update.1.refs_0_), channel_id=1, source_target_pairs={{0,6},{1,7},{2,0},{3,1},{4,2},{5,3},{6,4},{7,5},{8,14},{9,15},{10,... | collective-permute-start | bytes 417800 | tf_op jit(solution)/shard_map/ppermute | solution.py:791
  233.3 7.5 %collective-permute-start.4 = (bf16[272,256]{1,0:T(8,128)(2,1)S(1)}, bf16[272,256]{1,0:T(8,128)(2,1)S(1)}, u32[]{:S(2)}, u32[]{:S(2)}) collective-permute-start(bf16[272,256]{1,0:T(8,128)(2,1)S(1)} %cold_update.1.refs_0_), channel_id=1, source_target_pairs={{0,2},{1,3},{2,4},{3,5},{4,6},{5,7},{6,0},{7,1},{8,10},{9,11},{10,... | collective-permute-start | bytes 417800 | tf_op jit(solution)/shard_map/ppermute | solution.py:791
  234.7 8.8 %collective-permute-start.5 = (bf16[272,256]{1,0:T(8,128)(2,1)S(1)}, bf16[272,256]{1,0:T(8,128)(2,1)S(1)}, u32[]{:S(2)}, u32[]{:S(2)}) collective-permute-start(bf16[272,256]{1,0:T(8,128)(2,1)S(1)} %cold_update.1.refs_0_), channel_id=1, source_target_pairs={{0,4},{1,5},{2,6},{3,7},{4,0},{5,1},{6,2},{7,3},{8,12},{9,13},{10,... | collective-permute-start | bytes 417800 | tf_op jit(solution)/shard_map/ppermute | solution.py:791
  236.8 1.6 collective-permute-start.24
  236.8 6.8 %collective-permute-start.25 = (f32[128,256]{1,0:T(8,128)}, f32[128,256]{1,0:T(8,128)S(1)}, u32[]{:S(2)}, u32[]{:S(2)}) collective-permute-start(f32[128,256]{1,0:T(8,128)} %collective-permute-done.21.refs_2_), channel_id=1, source_target_pairs={{0,1},{1,0},{2,3},{3,2},{4,5},{5,4},{6,7},{7,6},{8,9},{9,8},{10,11... | collective-permute-start | bytes 393224 | tf_op jit(solution)/shard_map/ppermute | solution.py:795
  238.3 11.9 %collective-permute-start.7 = (bf16[272,256]{1,0:T(8,128)(2,1)S(1)}, bf16[272,256]{1,0:T(8,128)(2,1)S(1)}, u32[]{:S(2)}, u32[]{:S(2)}) collective-permute-start(bf16[272,256]{1,0:T(8,128)(2,1)S(1)} %cold_update.1.refs_0_), channel_id=1, source_target_pairs={{0,1},{1,0},{2,3},{3,2},{4,5},{5,4},{6,7},{7,6},{8,9},{9,8},{10,11... | collective-permute-start | bytes 417800 | tf_op jit(solution)/shard_map/ppermute | solution.py:795
  239.3 11.0 %collective-permute-start.10 = (bf16[272,256]{1,0:T(8,128)(2,1)S(1)}, bf16[272,256]{1,0:T(8,128)(2,1)S(1)}, u32[]{:S(2)}, u32[]{:S(2)}) collective-permute-start(bf16[272,256]{1,0:T(8,128)(2,1)S(1)} %collective-permute-done.6.refs_3_), channel_id=1, source_target_pairs={{0,1},{1,0},{2,3},{3,2},{4,5},{5,4},{6,7},{7,6},{8,9},{9,8},{10,11... | collective-permute-start | bytes 417800 | tf_op jit(solution)/shard_map/ppermute | solution.py:795
  240.8 9.5 %collective-permute-start.8 = (bf16[272,256]{1,0:T(8,128)(2,1)S(1)}, bf16[272,256]{1,0:T(8,128)(2,1)S(1)}, u32[]{:S(2)}, u32[]{:S(2)}) collective-permute-start(bf16[272,256]{1,0:T(8,128)(2,1)S(1)} %collective-permute-done.4.refs_1_), channel_id=1, source_target_pairs={{0,1},{1,0},{2,3},{3,2},{4,5},{5,4},{6,7},{7,6},{8,9},{9,8},{10,11... | collective-permute-start | bytes 417800 | tf_op jit(solution)/shard_map/ppermute | solution.py:795
  243.5 6.7 %collective-permute-start.9 = (bf16[272,256]{1,0:T(8,128)(2,1)S(1)}, bf16[272,256]{1,0:T(8,128)(2,1)S(1)}, u32[]{:S(2)}, u32[]{:S(2)}) collective-permute-start(bf16[272,256]{1,0:T(8,128)(2,1)S(1)} %collective-permute-done.5.refs_2_), channel_id=1, source_target_pairs={{0,1},{1,0},{2,3},{3,2},{4,5},{5,4},{6,7},{7,6},{8,9},{9,8},{10,11... | collective-permute-start | bytes 417800 | tf_op jit(solution)/shard_map/ppermute | solution.py:795
  243.5 1.7 collective-permute-start.26
  245.2 1.2 copy-start
  246.5 0.7 copy-start.14
